TPU v7x, 32 devices: a whole 2x2x4 slice. The times are simulated.
32 devices in a mesh: dp: 4 (over z), ctx: 2 (over core), tp: 4 (over y, x).
Axes of the slice: x: 2, y: 2, z: 4, core: 2. Of those that a mesh axis runs over, the one named last changes fastest.
Arguments:
- block_in: bfloat16 [8192, 2048], P(('dp', 'ctx')), may hold values from -6 to 6
- query_proj: bfloat16 [2048, 2048], P('dp', 'tp'), may hold values from -0.125 to 0.125
- forget_proj: bfloat16 [2048, 2048], P('dp', 'tp'), may hold values from -0.0625 to 0.0625
- value_proj: bfloat16 [2048, 2048], P('dp', 'tp'), may hold values from -0.125 to 0.125
- outgate_proj: bfloat16 [2048, 2048], P('dp', 'tp'), may hold values from -0.125 to 0.125
- out_proj: bfloat16 [2048, 2048], P('tp', 'dp'), may hold values from -0.125 to 0.125
- ffn_gate: bfloat16 [2048, 5632], P('dp', 'tp'), may hold values from -0.125 to 0.125
- ffn_up: bfloat16 [2048, 5632], P('dp', 'tp'), may hold values from -0.125 to 0.125
- ffn_down: bfloat16 [5632, 2048], P('tp', 'dp'), may hold values from -0.078125 to 0.078125
- first_gain: float32 [2048], replicated, may hold values from 0.5 to 1.5
- second_gain: float32 [2048], replicated, may hold values from 0.5 to 1.5
- group_gain: float32 [2048], P('tp'), may hold values from 0.5 to 1.5
- forget_bias: float32 [2048], P('tp'), may hold values from 3 to 12
- bound_table: float32 [24, 2048], P(None, 'tp'), may hold values from -4 to 4
- layer_index: int32 [1], replicated, may hold values from 1 to 23
- second_start: int32 [4], P('dp'), may hold values from 1 to 2048, as said below
- cotangent: bfloat16 [8192, 2048], P(('dp', 'ctx')), may hold values from -6 to 6
Outputs:
- block_out: bfloat16 [8192, 2048], P(('dp', 'ctx'))
- input_grad: float32 [8192, 2048], P(('dp', 'ctx'))
- query_grad: float32 [2048, 2048], P('dp', 'tp')
- forget_grad: float32 [2048, 2048], P('dp', 'tp')
- value_grad: float32 [2048, 2048], P('dp', 'tp')
- outgate_grad: float32 [2048, 2048], P('dp', 'tp')
- out_proj_grad: float32 [2048, 2048], P('tp', 'dp')
- ffn_gate_grad: float32 [2048, 5632], P('dp', 'tp')
- ffn_up_grad: float32 [2048, 5632], P('dp', 'tp')
- ffn_down_grad: float32 [5632, 2048], P('tp', 'dp')
- first_gain_grad: float32 [2048], replicated
- second_gain_grad: float32 [2048], replicated
- group_gain_grad: float32 [2048], P('tp')
- forget_bias_grad: float32 [2048], P('tp')
- bound_table_grad: float32 [24, 2048], P(None, 'tp')
Inputs may be any that keep to these rules, and one draw needn't show every extreme that they name: second_start[p] is 2048 where pack p is one whole sequence, and otherwise the position inside the pack where its second sequence begins; pack 0 is always one whole sequence and pack 1 always holds two. layer_index names a row of bound_table other than the first.
All inputs are finite; a program needn't handle non-finite values.
Results may differ from a plain program's by a relative error of at most 0.018.
Values may be sent and summed in bfloat16 or wider, within the bound.
No kernel may reach another device: no remote copies, remote signals or barrier semaphores. Data moves between devices by JAX's collectives and lax.ppermute only.
A program may use at most 384 MiB of HBM per device.

v0:
```python
import jax
import jax.numpy as jnp
from jax import lax
from jax.sharding import PartitionSpec as P

HEAD = 128
BLOCK = 32


HIGH = lax.Precision.HIGHEST
EPS_NORM = 1e-06
EPS_GROUP = 1e-05


def carried_in(value, axis, join, neutral):
    count, mine = (lax.axis_size(axis), lax.axis_index(axis))
    pieces = jax.tree.map(lambda part: lax.all_gather(part, axis), value)
    total = jax.tree.map(
        lambda part, zero: jnp.full_like(part, 0) + jnp.asarray(zero, part.dtype), value, neutral
    )

    def hop(position, total):
        longer = join(total, jax.tree.map(lambda part: part[position], pieces))
        return jax.tree.map(lambda new, old: jnp.where(position < mine, new, old), longer, total)

    return lax.fori_loop(0, count - 1, hop, total)


def carried_in_2(array, axis, combine, identity):
    peers, index = (lax.axis_size(axis), lax.axis_index(axis))
    everything = jax.tree.map(
        lambda part, kind: lax.all_gather(part.astype(kind), axis),
        array,
        jax.tree.map(lambda a: jnp.bfloat16 if a.dtype == jnp.float32 else a.dtype, array),
    )
    start = jax.tree.map(
        lambda part, zero: jnp.broadcast_to(jnp.asarray(zero, part.dtype), part.shape),
        array,
        identity,
    )

    def hop(k, before):
        at = peers - 1 - k
        reached = at > index
        new = combine(
            before, jax.tree.map(lambda part, own: part[at].astype(own.dtype), everything, array)
        )
        return jax.tree.map(lambda a, b: jnp.where(reached, a, b), new, before)

    return lax.fori_loop(0, peers, hop, start)


def rms_norm(rows_in, gain_vec):
    return (
        rows_in
        * lax.rsqrt(jnp.mean(rows_in * rows_in, axis=-1, keepdims=True) + EPS_NORM)
        * gain_vec
    )


def head_norm(mixed, pre_gate, gain_vec, head_count):
    row_count = mixed.shape[0]
    grouped = mixed.reshape(row_count, head_count, -1)
    scaled = grouped * lax.rsqrt(jnp.mean(grouped * grouped, axis=-1, keepdims=True) + EPS_GROUP)
    return scaled.reshape(row_count, -1) * gain_vec * jax.nn.silu(pre_gate)


def lower_bound(bound_rows, which_layer):
    weights = jax.nn.softmax(bound_rows, axis=0)
    rising = jnp.cumsum(weights, axis=0) - weights[0:1]
    picked = (
        lax.broadcasted_iota(jnp.int32, (bound_rows.shape[0], 1), 0) == which_layer[0]
    ).astype(bound_rows.dtype)
    return jnp.sum(rising * picked, axis=0)


def gate_values(pre_query, pre_forget, bias_vec, bound_vec):
    shifted = pre_forget + bias_vec
    forget = bound_vec + (1.0 - bound_vec) * jax.nn.sigmoid(shifted)
    return (jax.nn.silu(pre_query), (1.0 - bound_vec) * jax.nn.sigmoid(-shifted), jnp.log(forget))


def chain_link(earlier, later):
    return (earlier[0] * later[0], later[0][..., None] * earlier[1] + later[1])


def contract_last(left_side, right_side):
    return lax.dot_general(
        left_side, right_side, (((1,), (1,)), ((), ())), preferred_element_type=jnp.float32
    )


def contract_first(left_side, right_side):
    return lax.dot_general(
        left_side, right_side, (((0,), (0,)), ((), ())), preferred_element_type=jnp.float32
    )


def block_parts(queries, key_rows, values, log_forget, doc_ids, prev_doc, block_len):
    length, head_count, feature = queries.shape
    block_count = length // block_len
    blocked = (block_count, block_len, head_count, feature)
    queries = queries.reshape(blocked)
    key_rows = key_rows.reshape(blocked)
    values = values.reshape(blocked)
    decays = jnp.cumsum(log_forget.reshape(blocked), axis=1)
    doc_ids = doc_ids.reshape(block_count, block_len)
    before = jnp.concatenate([jnp.reshape(prev_doc, (1,)), doc_ids[:-1, block_len - 1]])
    middle = decays[:, block_len // 2 : block_len // 2 + 1]
    final_decay = decays[:, block_len - 1 :]
    scores = jnp.einsum(
        "nthc,nshc->nhts",
        queries * jnp.exp(decays - middle),
        key_rows * jnp.exp(middle - decays),
        precision=HIGH,
    )
    causal = lax.broadcasted_iota(jnp.int32, (block_len, block_len), 0) >= lax.broadcasted_iota(
        jnp.int32, (block_len, block_len), 1
    )
    allowed = causal[None] & (doc_ids[:, :, None] == doc_ids[:, None, :])
    scores = jnp.where(allowed[:, None], scores, 0.0)
    inside = jnp.einsum("nhts,nshe->nthe", scores, values, precision=HIGH)
    in_tail = (doc_ids == doc_ids[:, block_len - 1 :]).astype(decays.dtype)
    ending = key_rows * jnp.exp(final_decay - decays) * in_tail[:, :, None, None]
    states = jnp.einsum("nshc,nshe->nhce", ending, values, precision=HIGH)
    kept_flag = (doc_ids[:, block_len - 1] == before).astype(decays.dtype)
    carried = jnp.exp(final_decay[:, 0]) * kept_flag[:, None, None]
    entering = (doc_ids == before[:, None]).astype(decays.dtype)
    reached = queries * jnp.exp(decays) * entering[:, :, None, None]
    prefix_decay, prefix_state = lax.associative_scan(chain_link, (carried, states), axis=0)
    return (inside, reached, prefix_decay, prefix_state)


def finish(pieces, state_in):
    inside, reached, prefix_decay, prefix_state = pieces
    state_ends = prefix_decay[..., None] * state_in[None] + prefix_state
    state_starts = jnp.concatenate([state_in[None], state_ends[:-1]], axis=0)
    outside = jnp.einsum("nthc,nhce->nthe", reached, state_starts, precision=HIGH)
    summed = inside + outside
    block_count, block_len, head_count, feature = summed.shape
    return (summed.reshape(block_count * block_len, head_count, feature), state_ends[-1])


def body(
    block_in,
    query_proj,
    forget_proj,
    value_proj,
    outgate_proj,
    out_proj,
    ffn_gate,
    ffn_up,
    ffn_down,
    first_gain,
    second_gain,
    group_gain,
    forget_bias,
    bound_table,
    layer_index,
    second_start,
    cotangent,
):
    row_count = block_in.shape[0]
    local_width = query_proj.shape[1]
    head_count = local_width // HEAD
    hidden_width = ffn_gate.shape[1]
    inputs = block_in.astype(jnp.float32)
    first_low = rms_norm(inputs, first_gain).astype(jnp.bfloat16)
    mix_local = jnp.concatenate([query_proj, forget_proj, value_proj, outgate_proj], axis=1)
    ffn_local = jnp.concatenate([ffn_gate, ffn_up], axis=1)
    mix_full, out_full = (
        lax.all_gather(mix_local, "dp", axis=0, tiled=True),
        lax.all_gather(out_proj, "dp", axis=1, tiled=True),
    )
    projected = jnp.dot(first_low, mix_full, preferred_element_type=jnp.float32)
    pre_query = projected[:, :local_width]
    pre_forget = projected[:, local_width : 2 * local_width]
    pre_value = projected[:, 2 * local_width : 3 * local_width]
    pre_outgate = projected[:, 3 * local_width :]
    bound_vec = lower_bound(bound_table, layer_index)
    queries, key_rows, log_forget = gate_values(pre_query, pre_forget, forget_bias, bound_vec)
    offset = lax.axis_index("ctx") * row_count
    doc_ids = (offset + lax.iota(jnp.int32, row_count) >= second_start[0]).astype(jnp.int32)
    prev_doc = (offset - 1 >= second_start[0]).astype(jnp.int32)

    def to_heads(flat):
        return flat.reshape(row_count, head_count, HEAD)

    def mixer(queries_in, keys_in, values_in, logs_in, state_in):
        return finish(
            block_parts(queries_in, keys_in, values_in, logs_in, doc_ids, prev_doc, BLOCK), state_in
        )

    pieces = block_parts(
        to_heads(queries),
        to_heads(key_rows),
        to_heads(pre_value),
        to_heads(log_forget),
        doc_ids,
        prev_doc,
        BLOCK,
    )
    identity = (
        jnp.ones((head_count, HEAD), jnp.float32),
        jnp.zeros((head_count, HEAD, HEAD), jnp.float32),
    )
    shard_decay = pieces[2][-1]
    entry_pair = carried_in((shard_decay, pieces[3][-1]), "ctx", chain_link, identity)
    state_in = entry_pair[1]
    mixed, _ = finish(pieces, state_in)
    mixed_flat = mixed.reshape(row_count, local_width)
    gated_low = head_norm(mixed_flat, pre_outgate, group_gain, head_count).astype(jnp.bfloat16)
    mix_partial = jnp.dot(gated_low, out_full, preferred_element_type=jnp.float32)
    resid = inputs + lax.psum(mix_partial, "tp")
    second_low = rms_norm(resid, second_gain).astype(jnp.bfloat16)
    ffn_full, down_full = (
        lax.all_gather(ffn_local, "dp", axis=0, tiled=True),
        lax.all_gather(ffn_down, "dp", axis=1, tiled=True),
    )
    gate_up = jnp.dot(second_low, ffn_full, preferred_element_type=jnp.float32)
    pre_gate = gate_up[:, :hidden_width]
    pre_up = gate_up[:, hidden_width:]
    hidden_low = (jax.nn.silu(pre_gate) * pre_up).astype(jnp.bfloat16)
    ffn_partial = jnp.dot(hidden_low, down_full, preferred_element_type=jnp.float32)
    block_out = (
        resid + lax.psum(ffn_partial.astype(jnp.bfloat16), "tp").astype(jnp.float32)
    ).astype(jnp.bfloat16)
    mix_full, out_full, ffn_full, down_full = (
        lax.all_gather(mix_local, "dp", axis=0, tiled=True),
        lax.all_gather(out_proj, "dp", axis=1, tiled=True),
        lax.all_gather(ffn_local, "dp", axis=0, tiled=True),
        lax.all_gather(ffn_down, "dp", axis=1, tiled=True),
    )
    cotangent_full = cotangent.astype(jnp.float32)
    hidden_grad = contract_last(cotangent, down_full)
    down_weight_grad = contract_first(hidden_low, cotangent)
    _, act_pull = jax.vjp(lambda gate_in, up_in: jax.nn.silu(gate_in) * up_in, pre_gate, pre_up)
    gate_grad, up_grad = act_pull(hidden_grad)
    gate_up_grad = jnp.concatenate([gate_grad, up_grad], axis=1).astype(jnp.bfloat16)
    second_part = contract_last(gate_up_grad, ffn_full)
    ffn_weight_grad = contract_first(second_low, gate_up_grad)
    second_total = lax.psum(second_part, "tp")
    _, second_pull = jax.vjp(rms_norm, resid, second_gain)
    resid_part, second_gain_grad = second_pull(second_total)
    resid_grad = cotangent_full + resid_part
    resid_low = resid_grad.astype(jnp.bfloat16)
    gated_grad = contract_last(resid_low, out_full)
    out_weight_grad = contract_first(gated_low, resid_low)
    _, head_pull = jax.vjp(
        lambda mixed_in, gate_in, gain_in: head_norm(mixed_in, gate_in, gain_in, head_count),
        mixed_flat,
        pre_outgate,
        group_gain,
    )
    mixed_grad, outgate_pre_grad, group_gain_grad = head_pull(gated_grad)
    _, mixer_pull = jax.vjp(
        mixer,
        to_heads(queries),
        to_heads(key_rows),
        to_heads(pre_value),
        to_heads(log_forget),
        state_in,
    )
    first_pass = mixer_pull(
        (to_heads(mixed_grad), jnp.zeros((head_count, HEAD, HEAD), jnp.float32))
    )
    after_pair = carried_in_2((shard_decay, first_pass[4]), "ctx", chain_link, identity)
    second_pass = mixer_pull((jnp.zeros((row_count, head_count, HEAD), jnp.float32), after_pair[1]))
    query_rec_grad = (first_pass[0] + second_pass[0]).reshape(row_count, local_width)
    key_rec_grad = (first_pass[1] + second_pass[1]).reshape(row_count, local_width)
    value_rec_grad = (first_pass[2] + second_pass[2]).reshape(row_count, local_width)
    log_rec_grad = (first_pass[3] + second_pass[3]).reshape(row_count, local_width)
    _, gate_pull = jax.vjp(gate_values, pre_query, pre_forget, forget_bias, bound_vec)
    query_pre_grad, forget_pre_grad, forget_bias_grad, bound_grad = gate_pull(
        (query_rec_grad, key_rec_grad, log_rec_grad)
    )
    _, table_pull = jax.vjp(lambda rows_in: lower_bound(rows_in, layer_index), bound_table)
    (table_grad,) = table_pull(bound_grad)
    proj_grad = jnp.concatenate(
        [query_pre_grad, forget_pre_grad, value_rec_grad, outgate_pre_grad], axis=1
    ).astype(jnp.bfloat16)
    first_part = contract_last(proj_grad, mix_full)
    mix_weight_grad = contract_first(first_low, proj_grad)
    first_total = lax.psum(first_part.astype(jnp.bfloat16), "tp").astype(jnp.float32)
    _, first_pull = jax.vjp(rms_norm, inputs, first_gain)
    input_part, first_gain_grad = first_pull(first_total)
    input_grad = resid_grad + input_part
    mix_summed, out_summed, ffn_summed, down_summed = (
        lax.psum_scatter(
            mix_weight_grad.astype(jnp.bfloat16), ("dp", "ctx"), scatter_dimension=0, tiled=True
        ).astype(jnp.float32),
        lax.psum_scatter(
            out_weight_grad.astype(jnp.bfloat16), ("dp", "ctx"), scatter_dimension=1, tiled=True
        ).astype(jnp.float32),
        lax.psum_scatter(
            ffn_weight_grad.astype(jnp.bfloat16), ("dp", "ctx"), scatter_dimension=0, tiled=True
        ).astype(jnp.float32),
        lax.psum_scatter(
            down_weight_grad.astype(jnp.bfloat16), ("dp", "ctx"), scatter_dimension=1, tiled=True
        ).astype(jnp.float32),
    )
    mix_shard, out_shard, ffn_shard, down_shard = (
        lax.all_gather(mix_summed.astype(jnp.bfloat16), "ctx", axis=0, tiled=True).astype(
            mix_summed.dtype
        ),
        lax.all_gather(out_summed.astype(jnp.bfloat16), "ctx", axis=1, tiled=True).astype(
            out_summed.dtype
        ),
        lax.all_gather(ffn_summed.astype(jnp.bfloat16), "ctx", axis=0, tiled=True).astype(
            ffn_summed.dtype
        ),
        lax.all_gather(down_summed.astype(jnp.bfloat16), "ctx", axis=1, tiled=True).astype(
            down_summed.dtype
        ),
    )
    first_sum, second_sum, group_sum, bias_sum, table_sum = (
        lax.psum(first_gain_grad.astype(jnp.bfloat16), ("dp", "ctx")).astype(jnp.float32),
        lax.psum(second_gain_grad.astype(jnp.bfloat16), ("dp", "ctx")).astype(jnp.float32),
        lax.psum(group_gain_grad.astype(jnp.bfloat16), ("dp", "ctx")).astype(jnp.float32),
        lax.psum(forget_bias_grad.astype(jnp.bfloat16), ("dp", "ctx")).astype(jnp.float32),
        lax.psum(table_grad.astype(jnp.bfloat16), ("dp", "ctx")).astype(jnp.float32),
    )
    return (
        block_out,
        input_grad,
        mix_shard[:, :local_width],
        mix_shard[:, local_width : 2 * local_width],
        mix_shard[:, 2 * local_width : 3 * local_width],
        mix_shard[:, 3 * local_width :],
        out_shard,
        ffn_shard[:, :hidden_width],
        ffn_shard[:, hidden_width:],
        down_shard,
        first_sum,
        second_sum,
        group_sum,
        bias_sum,
        table_sum,
    )


def solution(mesh):
    return jax.shard_map(
        body,
        mesh=mesh,
        in_specs=(
            P(("dp", "ctx"), None),
            P("dp", "tp"),
            P("dp", "tp"),
            P("dp", "tp"),
            P("dp", "tp"),
            P("tp", "dp"),
            P("dp", "tp"),
            P("dp", "tp"),
            P("tp", "dp"),
            P(),
            P(),
            P("tp"),
            P("tp"),
            P(None, "tp"),
            P(),
            P("dp"),
            P(("dp", "ctx"), None),
        ),
        out_specs=(
            P(("dp", "ctx"), None),
            P(("dp", "ctx"), None),
            P("dp", "tp"),
            P("dp", "tp"),
            P("dp", "tp"),
            P("dp", "tp"),
            P("tp", "dp"),
            P("dp", "tp"),
            P("dp", "tp"),
            P("tp", "dp"),
            P(),
            P(),
            P("tp"),
            P("tp"),
            P(None, "tp"),
        ),
        check_vma=False,
    )
```

profile of v0, /device:TPU:0, one launch (start us, length us, event | category | flops | bytes accessed | tf_op | source)
XLA Modules:
  0.0 2218.8 jit_solution(17821822070272523341)
XLA Ops:
  17.0 145.9 %all-gather.8.cloned.1.call-done = bf16[2048,2048]{1,0:T(8,128)(2,1)} async-done(((bf16[512,2048]{1,0:T(8,128)(2,1)}), bf16[2048,2048]{1,0:T(8,128)(2,1)}) %all-gather.8.cloned.1.call-update) | async-done | bytes 8388624 | tf_op jit(solution)/shard_map/all_gather | solution.py:172
  162.8 12.6 fusion.115
  209.9 13.7 fusion.85
  268.4 18.6 pad.557
  287.0 12.1 pad.558
  312.1 35.5 %pad.734 = f32[31,4,128,128]{2,3,1,0:T(8,128)} pad(f32[16,4,128,128]{2,3,1,0:T(8,128)} %pad_maximum_fusion.5, f32[]{:T(128)} %constant.113.clone.1), padding=0_0_1x0_0_0x0_0_0x0_0_0 | pad | bytes 12320772 | tf_op jit(solution)/shard_map/slice | solution.py:137
  347.6 35.6 %pad.559 = f32[32,4,128,128]{2,3,1,0:T(8,128)} pad(f32[16,4,128,128]{2,3,1,0:T(8,128)} %pad_maximum_fusion.5, f32[]{:T(128)} %constant.113.clone.1), padding=0_1_1x0_0_0x0_0_0x0_0_0 | pad | bytes 12582916 | tf_op jit(solution)/shard_map/pad | solution.py:130
  385.0 35.6 %pad.1005 = f32[32,4,128,128]{2,3,1,0:T(8,128)} pad(f32[16,4,128,128]{2,3,1,0:T(8,128)} %add.591, f32[]{:T(128)} %constant.113.clone.1), padding=1_0_1x0_0_0x0_0_0x0_0_0 | pad | bytes 12582916
  438.1 12.0 multiply_add_fusion
  450.2 16.1 fusion.19
  499.8 166.2 %all-reduce.122.cloned.1.call-done = f32[1024,2048]{1,0:T(8,128)} async-done(((f32[1024,2048]{1,0:T(8,128)}), f32[1024,2048]{1,0:T(8,128)}) %all-reduce.122.cloned.1.call-update) | async-done | bytes 8388624 | tf_op jit(solution)/shard_map/psum | solution.py:214
  675.0 194.9 %all-gather.12.cloned.1.call-done = bf16[2048,2816]{1,0:T(8,128)(2,1)} async-done(((bf16[512,2816]{1,0:T(8,128)(2,1)}), bf16[2048,2816]{1,0:T(8,128)(2,1)}) %all-gather.12.cloned.1.call-update) | async-done | bytes 11534352 | tf_op jit(solution)/shard_map/all_gather | solution.py:217
  869.9 20.0 fusion.177
  889.9 86.4 %all-gather.14.cloned.1.call-done = bf16[1408,2048]{1,0:T(8,128)(2,1)} async-done(((bf16[1408,512]{1,0:T(8,128)(2,1)}), bf16[1408,2048]{1,0:T(8,128)(2,1)}) %all-gather.14.cloned.1.call-update) | async-done | bytes 5767184 | tf_op jit(solution)/shard_map/all_gather | solution.py:218
  976.3 16.2 fusion.15
  995.1 16.8 fusion.20
  1012.0 10.5 convolution_convert_fusion.1
  1024.9 11.3 fusion.17
  1054.8 18.7 convolution_convert_fusion
  1073.5 11.1 convolution_convert_fusion.4
  1084.6 97.8 %all-reduce.124.cloned.1.call-done = f32[1024,2048]{1,0:T(8,128)} async-done(((f32[1024,2048]{1,0:T(8,128)}), f32[1024,2048]{1,0:T(8,128)}) %all-reduce.124.cloned.1.call-update) | async-done | bytes 8388624 | tf_op jit(solution)/shard_map/psum | solution.py:242
  1214.6 13.5 fusion.78
  1364.9 10.2 pad.622
  1401.0 12.0 pad.589
  1413.1 18.5 pad.623
  1435.8 18.6 pad.624
  1454.4 12.1 pad.590
  1466.5 16.7 pad.568
  1483.2 10.8 pad.602
  1494.0 15.5 multiply_reduce_fusion.5
  1510.5 35.6 %pad.625 = f32[32,4,128,128]{2,3,1,0:T(8,128)} pad(f32[16,4,128,128]{2,3,1,0:T(8,128)} %get-tuple-element.256, f32[]{:T(128)} %constant.113.clone.1), padding=1_0_1x0_0_0x0_0_0x0_0_0 | pad | bytes 12582916 | tf_op jit(solution)/shard_map/transpose(jvp())/pad | solution.py:130
  1546.0 35.5 %pad.591 = f32[32,4,128,128]{2,3,1,0:T(8,128)} pad(f32[16,4,128,128]{2,3,1,0:T(8,128)} %get-tuple-element.255, f32[]{:T(128)} %constant.113.clone.1), padding=1_0_1x0_0_0x0_0_0x0_0_0 | pad | bytes 12582916 | tf_op jit(solution)/shard_map/transpose(jvp())/pad | solution.py:130
  1590.3 35.6 %pad.592 = f32[32,4,128,128]{2,3,1,0:T(8,128)} pad(f32[16,4,128,128]{2,3,1,0:T(8,128)} %get-tuple-element.375, f32[]{:T(128)} %constant.113.clone.1), padding=0_1_1x0_0_0x0_0_0x0_0_0 | pad | bytes 12582916 | tf_op jit(solution)/shard_map/transpose(jvp())/pad | solution.py:130
  1625.9 35.7 %pad.626 = f32[32,4,128,128]{2,3,1,0:T(8,128)} pad(f32[16,4,128,128]{2,3,1,0:T(8,128)} %get-tuple-element.376, f32[]{:T(128)} %constant.113.clone.1), padding=0_1_1x0_0_0x0_0_0x0_0_0 | pad | bytes 12582916 | tf_op jit(solution)/shard_map/transpose(jvp())/pad | solution.py:130
  1661.7 33.6 %pad.562 = f32[32,4,128,128]{2,3,1,0:T(8,128)} pad(f32[15,4,128,128]{2,3,1,0:T(8,128)} %get-tuple-element.290, f32[]{:T(128)} %constant.113.clone.1), padding=2_1_1x0_0_0x0_0_0x0_0_0 | pad | bytes 12320772 | tf_op jit(solution)/shard_map/transpose(jvp())/pad | solution.py:130
  1695.3 33.7 %pad.597 = f32[32,4,128,128]{2,3,1,0:T(8,128)} pad(f32[15,4,128,128]{2,3,1,0:T(8,128)} %get-tuple-element.291, f32[]{:T(128)} %constant.113.clone.1), padding=2_1_1x0_0_0x0_0_0x0_0_0 | pad | bytes 12320772 | tf_op jit(solution)/shard_map/transpose(jvp())/pad | solution.py:130
  1729.0 10.8 fusion.18
  1752.8 10.0 add_add_fusion.3
  1771.4 15.1 fusion.83
  1786.5 9.8 add_add_fusion.2
  1810.3 19.3 fusion.176
  1830.9 11.6 fusion.41
  1842.6 13.5 fusion.81
  1877.1 12.9 convolution_convert_fusion.3
  1890.7 14.5 convolution_convert_fusion.2
  1913.4 152.0 %all-reduce.126.cloned.1.call-done = (bf16[1024,2048]{1,0:T(8,128)(2,1)}, bf16[1024,2048]{1,0:T(8,128)(2,1)}) async-done(((bf16[1024,2048]{1,0:T(8,128)(2,1)}, bf16[1024,2048]{1,0:T(8,128)(2,1)}), (bf16[1024,2048]{1,0:T(8,128)(2,1)}, bf16[1024,2048]{1,0:T(8,128)(2,1)})) %all-reduce.126.cloned.1.call-update) | async-done | bytes 8388624 | tf_op jit(solution)/shard_map/psum | solution.py:226
  2073.8 84.8 %reduce-scatter.5.cloned.1.call-done = bf16[256,2048]{1,0:T(8,128)(2,1)} async-done(((bf16[2048,2048]{1,0:T(8,128)(2,1)}), bf16[256,2048]{1,0:T(8,128)(2,1)}) %reduce-scatter.5.cloned.1.call-update) | async-done | bytes 1048592 | tf_op jit(solution)/shard_map/reduce_scatter | solution.py:289
  2164.6 26.3 %all-reduce.116 = (bf16[2048]{0:T(1024)(128)(2,1)S(1)}, bf16[2048]{0:T(1024)(128)(2,1)S(1)}, bf16[512]{0:T(512)(128)(2,1)S(1)}, bf16[512]{0:T(512)(128)(2,1)S(1)}, bf16[24,512]{1,0:T(8,128)(2,1)S(1)}) all-reduce(bf16[2048]{0:T(1024)(128)(2,1)S(1)} %get-tuple-element.200, ...), channel_id=1, replica_groups=mesh['dp'=4,'ctx'=2,'tp'=4] {'dp','ctx'}, use_global_device_ids=true, to_apply=%region_51.52 | all-reduce | flops 17408 | bytes 69632 | tf_op jit(solution)/shard_map/psum | solution.py:317
  (808 shorter events, 494.5 us)
Async XLA Ops:
  7.2 155.7 %all-gather.8.cloned.1.call-start = ((), (), s32[]{:S(2)}) async-start(), calls=%async_computation.4 | async-start | bytes 10485760 | tf_op jit(solution)/shard_map/all_gather | solution.py:172
  10.4 477.5 %all-gather.10.cloned.1.call-start = ((), (), s32[]{:S(2)}) async-start(), calls=%async_computation.5 | async-start | bytes 2621440 | tf_op jit(solution)/shard_map/all_gather | solution.py:173
  11.1 654.9 %all-reduce.122.cloned.1.call-start = ((), (), s32[]{:S(2)}) async-start(), calls=%async_computation.6 | async-start | bytes 16777216 | tf_op jit(solution)/shard_map/psum | solution.py:214
  12.7 150.1 %copy-start.194 = (f32[2048]{0:T(1024)S(1)}, f32[2048]{0:T(1024)}, u32[]{:S(2)}) copy-start(f32[2048]{0:T(1024)} %param.28) | copy-start | bytes 24580
  16.4 159.0 %copy-start.171 = (f32[1024]{0:T(1024)}, f32[1024]{0:T(1024)S(1)}, u32[]{:S(2)}) copy-start(f32[1024]{0:T(1024)S(1)} %fusion.149) | copy-start | bytes 12292
  16.6 158.8 %copy-start.178 = (f32[512]{0:T(512)}, f32[512]{0:T(512)S(1)}, u32[]{:S(2)}) copy-start(f32[512]{0:T(512)S(1)} %multiply_reduce_fusion.28) | copy-start | bytes 6148
  16.6 158.8 %copy-start.196 = (f32[512]{0:T(512)}, f32[512]{0:T(512)S(1)}, u32[]{:S(2)}) copy-start(f32[512]{0:T(512)S(1)} %broadcast_subtract_fusion) | copy-start | bytes 6148
  16.7 169.4 %copy-start.214 = (f32[32]{0:T(128)}, f32[32]{0:T(128)S(1)}, u32[]{:S(2)}) copy-start(f32[32]{0:T(128)S(1)} %get-tuple-element.269) | copy-start | bytes 388
  16.9 1024.1 %copy-start.73 = (pred[32,32,32]{2,1,0:T(8,128)(4,1)}, pred[32,32,32]{2,1,0:T(8,128)(4,1)S(1)}, u32[]{:S(2)}) copy-start(pred[32,32,32]{2,1,0:T(8,128)(4,1)S(1)} %compare_and_fusion) | copy-start | bytes 98308
  16.9 189.3 %copy-start.131 = (f32[32,32]{0,1:T(8,128)}, f32[32,32]{0,1:T(8,128)S(1)}, u32[]{:S(2)}) copy-start(f32[32,32]{0,1:T(8,128)S(1)} %get-tuple-element.440) | copy-start | bytes 12292
  16.9 415.8 %copy-start.129 = (f32[32,32]{0,1:T(8,128)}, f32[32,32]{0,1:T(8,128)S(1)}, u32[]{:S(2)}) copy-start(f32[32,32]{0,1:T(8,128)S(1)} %get-tuple-element.439) | copy-start | bytes 12292
  17.0 158.5 %copy-start.204 = (f32[512]{0:T(512)S(1)}, f32[512]{0:T(512)}, u32[]{:S(2)}) copy-start(f32[512]{0:T(512)} %param.31) | copy-start | bytes 6148
  184.2 22.0 copy-start
  187.5 36.2 %copy-start.125 = (f32[16,4,128]{2,1,0:T(4,128)}, f32[16,4,128]{2,1,0:T(4,128)S(1)}, u32[]{:S(2)}) copy-start(f32[16,4,128]{2,1,0:T(4,128)S(1)} %get-tuple-element.356) | copy-start | bytes 98308
  187.5 39.7 %copy-start.142 = (f32[8,4,128]{2,1,0:T(4,128)}, f32[8,4,128]{2,1,0:T(4,128)S(1)}, u32[]{:S(2)}) copy-start(f32[8,4,128]{2,1,0:T(4,128)S(1)} %get-tuple-element.380) | copy-start | bytes 49156
  187.6 42.5 %copy-start.155 = (f32[4,4,128]{2,1,0:T(4,128)}, f32[4,4,128]{2,1,0:T(4,128)S(1)}, u32[]{:S(2)}) copy-start(f32[4,4,128]{2,1,0:T(4,128)S(1)} %get-tuple-element.402) | copy-start | bytes 24580
  187.6 42.6 %copy-start.165 = (f32[2,4,128]{2,1,0:T(4,128)}, f32[2,4,128]{2,1,0:T(4,128)S(1)}, u32[]{:S(2)}) copy-start(f32[2,4,128]{2,1,0:T(4,128)S(1)} %get-tuple-element.421) | copy-start | bytes 12292
  187.7 42.6 %copy-start.198 = (f32[4,128]{1,0:T(4,128)}, f32[4,128]{1,0:T(4,128)S(1)}, u32[]{:S(2)}) copy-start(f32[4,128]{1,0:T(4,128)S(1)} %get-tuple-element.431) | copy-start | bytes 6148
  347.6 35.6 %copy-start.206 = (f32[1,4,128]{2,1,0:T(4,128)S(1)}, f32[1,4,128]{2,1,0:T(4,128)}, u32[]{:S(2)}) copy-start(f32[1,4,128]{2,1,0:T(4,128)} %get-tuple-element.266) | copy-start | bytes 6148
  424.2 600.7 %copy-start.88 = (f32[1,4,128,128]{2,3,1,0:T(8,128)}, f32[1,4,128,128]{2,3,1,0:T(8,128)S(1)}, u32[]{:S(2)}) copy-start(f32[1,4,128,128]{2,3,1,0:T(8,128)S(1)} %add_select_fusion) | copy-start | bytes 786436
  495.5 374.3 %all-gather.12.cloned.1.call-start = ((), (), s32[]{:S(2)}) async-start(), calls=%async_computation.7 | async-start | bytes 14417920 | tf_op jit(solution)/shard_map/all_gather | solution.py:217
  499.2 477.1 %all-gather.14.cloned.1.call-start = ((), (), s32[]{:S(2)}) async-start(), calls=%async_computation.8 | async-start | bytes 7208960 | tf_op jit(solution)/shard_map/all_gather | solution.py:218
  499.7 370.1 %copy-start.177 = (f32[2048]{0:T(1024)S(1)}, f32[2048]{0:T(1024)}, u32[]{:S(2)}) copy-start(f32[2048]{0:T(1024)} %param.29) | copy-start | bytes 24580
  499.8 682.7 %all-reduce.124.cloned.1.call-start = ((), (), s32[]{:S(2)}) async-start(), calls=%async_computation.9 | async-start | bytes 16777216 | tf_op jit(solution)/shard_map/psum | solution.py:242
  1011.9 865.1 %reduce-scatter.11.cloned.1.call-start = ((), (), s32[]{:S(2)}) async-start(), calls=%async_computation.15 | async-start | bytes 6488064 | tf_op jit(solution)/shard_map/reduce_scatter | solution.py:298
  1022.5 882.9 %reduce-scatter.9.cloned.1.call-start = ((), (), s32[]{:S(2)}) async-start(), calls=%async_computation.13 | async-start | bytes 12976128 | tf_op jit(solution)/shard_map/reduce_scatter | solution.py:295
  1073.5 833.1 %reduce-scatter.7.cloned.1.call-start = ((), (), s32[]{:S(2)}) async-start(), calls=%async_computation.12 | async-start | bytes 2359296 | tf_op jit(solution)/shard_map/reduce_scatter | solution.py:292
  1265.8 31.7 %copy-start.157 = (f32[8,4,128]{2,1,0:T(4,128)}, f32[8,4,128]{2,1,0:T(4,128)S(1)}, u32[]{:S(2)}) copy-start(f32[8,4,128]{2,1,0:T(4,128)S(1)} %slice.479) | copy-start | bytes 49156
  1265.9 31.7 %copy-start.158 = (f32[8,4,128]{2,1,0:T(4,128)}, f32[8,4,128]{2,1,0:T(4,128)S(1)}, u32[]{:S(2)}) copy-start(f32[8,4,128]{2,1,0:T(4,128)S(1)} %slice.471) | copy-start | bytes 49156
  1546.0 35.5 %copy-start.126 = (f32[16,4,128]{2,1,0:T(4,128)S(1)}, f32[16,4,128]{2,1,0:T(4,128)}, u32[]{:S(2)}) copy-start(f32[16,4,128]{2,1,0:T(4,128)} %copy-done.125) | copy-start | bytes 98308
  1695.3 33.7 %copy-start.24 = (f32[32,4,128,32]{2,3,1,0:T(8,128)S(1)}, f32[32,4,128,32]{2,3,1,0:T(8,128)}, u32[]{:S(2)}) copy-start(f32[32,4,128,32]{2,3,1,0:T(8,128)} %copy-done.23) | copy-start | bytes 6291460
  1695.3 33.7 %copy-start.89 = (f32[1,4,128,128]{2,3,1,0:T(8,128)S(1)}, f32[1,4,128,128]{2,3,1,0:T(8,128)}, u32[]{:S(2)}) copy-start(f32[1,4,128,128]{2,3,1,0:T(8,128)} %copy-done.88) | copy-start | bytes 786436
  1771.4 33.5 %slice-start.1 = ((s8[8388608]{0:T(1024)(128)(4,1)}), s8[4194304]{0:T(1024)(128)(4,1)S(1)}, s32[]{:S(2)}) async-start(s8[8388608]{0:T(1024)(128)(4,1)} %bitcast.242), calls=%async_computation.19 | async-start | bytes 8388608
  1808.7 20.9 copy-start.134
  1808.7 20.9 copy-start.135
  1808.7 20.9 slice-start.17
  1808.7 20.9 slice-start.18
  1808.8 20.9 copy-start.215
  1808.8 101.3 %all-gather.20.cloned.1.call-start = ((), (), s32[]{:S(2)}) async-start(), calls=%async_computation.16 | async-start | bytes 2162688 | tf_op jit(solution)/shard_map/all_gather | solution.py:312
  1810.3 20.6 copy-start.48
  1810.3 20.6 copy-start.49
  1810.3 20.6 copy-start.54
  1810.3 20.6 copy-start.55
  1877.1 188.4 %all-reduce.126.cloned.1.call-start = ((), (), s32[]{:S(2)}) async-start(), calls=%async_computation.17 | async-start | bytes 16777216 | tf_op jit(solution)/shard_map/psum | solution.py:226
  1890.0 268.6 %reduce-scatter.5.cloned.1.call-start = ((), (), s32[]{:S(2)}) async-start(), calls=%async_computation.10 | async-start | bytes 9437184 | tf_op jit(solution)/shard_map/reduce_scatter | solution.py:289
  1905.3 298.1 %all-gather.18.cloned.1.call-start = ((), (), s32[]{:S(2)}) async-start(), calls=%async_computation.14 | async-start | bytes 4325376 | tf_op jit(solution)/shard_map/all_gather | solution.py:309
  1906.0 302.0 %all-gather.16.cloned.1.call-start = ((), (), s32[]{:S(2)}) async-start(), calls=%async_computation.11 | async-start | bytes 3145728 | tf_op jit(solution)/shard_map/all_gather | solution.py:303
  2158.6 35.2 %copy-start.168 = (f32[1024]{0:T(1024)S(1)}, f32[1024]{0:T(1024)}, u32[]{:S(2)}) copy-start(f32[1024]{0:T(1024)} %copy-done.167) | copy-start | bytes 12292
  (213 other events, 1256.3 us)
Sparse Core Ops, SparseCore 0:
  10.5 152.3 all-gather.7
  164.4 44.1 all-gather.9
  495.6 170.3 all-reduce.121
  668.1 201.7 all-gather.11
  871.3 104.8 all-gather.13
  1012.0 170.3 all-reduce.123
  1184.7 65.5 reduce-scatter.10
  1252.6 117.6 reduce-scatter.8
  1808.8 36.2 reduce-scatter.6
  1877.2 10.0 all-gather.19
  1891.6 173.7 all-reduce.125
  2068.3 90.2 reduce-scatter.4
  2160.2 10.1 all-gather.17
  2171.8 11.7 all-gather.15
where the time goes:
time: 2250 us; the launch traced here: 2220 us
  waiting for transfers between devices  930 us (41%)
  local copies, waits for them, and re-layouts  640 us (28%)
  matrix products  319 us (14%)
  other arithmetic  275 us (12%)
  blocking collectives  36.4 us (2%)
    pad x74, local copies, waits for them, and re-layouts, block_parts(): lax.associative_scan(chain_link, (carried, states), axis=0)  483 us
    all_gather x1, waiting for transfers between devices, body(): lax.all_gather(ffn_local, 'dp', axis=0, tiled=True)  195 us
    psum x1, waiting for transfers between devices, body(): resid = inputs + lax.psum(mix_partial, 'tp')  166 us
    psum x1, waiting for transfers between devices, body(): lax.psum(ffn_partial.astype(jnp.bfloat16), 'tp').astype(jnp.float32)  152 us
    all_gather x1, waiting for transfers between devices, body(): lax.all_gather(mix_local, 'dp', axis=0, tiled=True)  146 us
    psum x1, waiting for transfers between devices, body(): second_total = lax.psum(second_part, 'tp')  97.8 us
    all_gather x1, waiting for transfers between devices, body(): lax.all_gather(ffn_down, 'dp', axis=1, tiled=True)  86.4 us
    reduce_scatter x1, waiting for transfers between devices, body(): lax.psum_scatter(mix_weight_grad.astype(jnp.bfloat16), ('dp', 'ctx'), sca...  84.8 us
  transfers between devices with their start and end apart: 14, of which 7 were waited for; matrix products, arithmetic and copies ran while one was open for 51% of the time, Pallas kernels for 0%

commit v1 on v0

v1 whole, which is shorter than its diff:
```python
import functools

import jax
import jax.numpy as jnp
from jax import lax
from jax.experimental import pallas as pl
from jax.experimental.pallas import tpu as pltpu
from jax.sharding import PartitionSpec as P

HEAD = 128
SUB = 32
CHUNK = 128
EPS_NORM = 1e-06
EPS_GROUP = 1e-05
F32 = jnp.float32
BF16 = jnp.bfloat16


def dot_nn(a, b):
    return lax.dot_general(a, b, (((1,), (0,)), ((), ())), preferred_element_type=F32)


def dot_nt(a, b):
    return lax.dot_general(a, b, (((1,), (1,)), ((), ())), preferred_element_type=F32)


def dot_tn(a, b):
    return lax.dot_general(a, b, (((0,), (0,)), ((), ())), preferred_element_type=F32)


def sigmoid_pair(x):
    small = jnp.exp(-jnp.abs(x))
    inv = 1.0 / (1.0 + small)
    rest = small * inv
    up = x >= 0.0
    return jnp.where(up, inv, rest), jnp.where(up, rest, inv)


def tri_dot(tri, x):
    high = x.astype(BF16)
    low = (x - high.astype(F32)).astype(BF16)
    return dot_nn(tri, high) + dot_nn(tri, low)


def triangle(upper):
    rows = lax.broadcasted_iota(jnp.int32, (CHUNK, CHUNK), 0)
    cols = lax.broadcasted_iota(jnp.int32, (CHUNK, CHUNK), 1)
    keep = rows <= cols if upper else rows >= cols
    return jnp.where(keep, 1.0, 0.0).astype(BF16)


def chunk_masks(start, split):
    rows = lax.broadcasted_iota(jnp.int32, (CHUNK, CHUNK), 0)
    cols = lax.broadcasted_iota(jnp.int32, (CHUNK, CHUNK), 1)
    local = split - start
    causal = rows >= cols
    same = (rows >= local) == (cols >= local)
    token = lax.broadcasted_iota(jnp.int32, (CHUNK, HEAD), 0)
    before = start > split
    enter = jnp.where(jnp.logical_or(token < local, before), 1.0, 0.0)
    last = CHUNK - 1 >= local
    tail = jnp.where((token >= local) == last, 1.0, 0.0)
    kept = jnp.where(jnp.logical_or(jnp.logical_not(last), before), 1.0, 0.0)
    return causal & same, enter, tail, kept


def decays(log_forget, tri):
    b = tri_dot(tri, log_forget)
    return b


def key_rows(k, b, kd, k_end_sub, mids, ends):
    out = []
    count = CHUNK // SUB
    for i in range(count):
        parts = []
        for j in range(i):
            part = k_end_sub[j * SUB : (j + 1) * SUB]
            parts.append(part * jnp.exp(mids[i] - ends[j]))
        parts.append(kd[i * SUB : (i + 1) * SUB])
        if i < count - 1:
            parts.append(jnp.zeros(((count - 1 - i) * SUB, HEAD), F32))
        out.append(jnp.concatenate(parts, axis=0).astype(BF16))
    return out


def spread(rows_list):
    return jnp.concatenate([jnp.broadcast_to(r, (SUB, HEAD)) for r in rows_list], axis=0)


def chunk_common(q, k, log_forget, tri):
    count = CHUNK // SUB
    b = tri_dot(tri, log_forget)
    mids = [b[i * SUB + SUB // 2 : i * SUB + SUB // 2 + 1] for i in range(count)]
    ends = [b[(i + 1) * SUB - 1 : (i + 1) * SUB] for i in range(count)]
    mid = spread(mids)
    end = spread(ends)
    to_mid = jnp.exp(b - mid)
    from_mid = jnp.exp(mid - b)
    to_end = jnp.exp(end - b)
    whole = jnp.exp(b)
    final = ends[-1]
    to_final = jnp.exp(final - b)
    qd = (q * to_mid).astype(BF16)
    keys = key_rows(k, b, k * from_mid, k * to_end, mids, ends)
    return b, mids, ends, to_mid, from_mid, to_end, whole, final, to_final, qd, keys


def scores_of(qd, keys):
    count = CHUNK // SUB
    return jnp.concatenate(
        [dot_nt(qd[i * SUB : (i + 1) * SUB], keys[i]) for i in range(count)], axis=0
    )


def forward_kernel(
    heads, chunks, split_ref, pre_ref, bias_ref, bound_ref, gain_ref, gated_ref, mixed_ref, states_ref, state
):
    step = pl.program_id(0)
    width = heads * HEAD

    @pl.when(step == 0)
    def _():
        state[...] = jnp.zeros_like(state)

    split = split_ref[0]
    tri = triangle(False)
    for n in range(chunks):
        start = (step * chunks + n) * CHUNK
        allowed, enter, tail, kept = chunk_masks(start, split)
        rows = slice(n * CHUNK, (n + 1) * CHUNK)
        for h in range(heads):
            cols = slice(h * HEAD, (h + 1) * HEAD)

            def part(which):
                return pre_ref[rows, which * width + h * HEAD : which * width + (h + 1) * HEAD]

            pre_q = part(0)
            q = pre_q * sigmoid_pair(pre_q)[0]
            bound = bound_ref[:, cols]
            plus, minus = sigmoid_pair(part(1) + bias_ref[:, cols])
            k = (1.0 - bound) * minus
            log_forget = jnp.log(bound + (1.0 - bound) * plus)
            _, _, _, _, _, _, whole, final, to_final, qd, keys = chunk_common(q, k, log_forget, tri)
            v = part(2).astype(BF16)
            scores = jnp.where(allowed, scores_of(qd, keys), 0.0).astype(BF16)
            old = state[h]
            states_ref[n, h] = old
            mixed = dot_nn(scores, v) + dot_nt((q * whole * enter).astype(BF16), old.astype(BF16))
            ending = (k * to_final * tail).astype(BF16)
            state[h] = old * (jnp.exp(final) * kept) + dot_tn(v, ending)
            mixed_ref[rows, cols] = mixed
            scale = lax.rsqrt(jnp.mean(mixed * mixed, axis=-1, keepdims=True) + EPS_GROUP)
            pre_g = part(3)
            gate = pre_g * sigmoid_pair(pre_g)[0]
            gated_ref[rows, cols] = (mixed * scale * gain_ref[:, cols] * gate).astype(BF16)


def mixer_forward(pre, bias, bound, gain, split, chunks=2):
    tokens, wide = pre.shape
    width = wide // 4
    heads = width // HEAD
    block = chunks * CHUNK
    steps = tokens // block
    row = pl.BlockSpec((1, width), lambda i: (0, 0))
    return pl.pallas_call(
        functools.partial(forward_kernel, heads, chunks),
        grid=(steps,),
        in_specs=[
            pl.BlockSpec(memory_space=pltpu.SMEM),
            pl.BlockSpec((block, wide), lambda i: (i, 0)),
            row,
            row,
            row,
        ],
        out_specs=[
            pl.BlockSpec((block, width), lambda i: (i, 0)),
            pl.BlockSpec((block, width), lambda i: (i, 0)),
            pl.BlockSpec((chunks, heads, HEAD, HEAD), lambda i: (i, 0, 0, 0)),
        ],
        out_shape=[
            jax.ShapeDtypeStruct((tokens, width), BF16),
            jax.ShapeDtypeStruct((tokens, width), F32),
            jax.ShapeDtypeStruct((tokens // CHUNK, heads, HEAD, HEAD), F32),
        ],
        scratch_shapes=[pltpu.VMEM((heads, HEAD, HEAD), F32)],
        compiler_params=pltpu.CompilerParams(
            dimension_semantics=("arbitrary",), vmem_limit_bytes=32 << 20
        ),
        cost_estimate=pl.CostEstimate(
            flops=tokens * width * 2048, bytes_accessed=tokens * width * 30, transcendentals=tokens * width * 12
        ),
        name="mixer_forward",
    )(split, pre, bias[None], bound[None], gain[None])


def backward_kernel(
    heads,
    chunks,
    split_ref,
    pre_ref,
    mixed_ref,
    grad_ref,
    states_ref,
    bias_ref,
    bound_ref,
    gain_ref,
    out_ref,
    sums_ref,
    adjoint,
    later,
):
    step = pl.program_id(0)
    steps = pl.num_programs(0)
    width = heads * HEAD
    count = CHUNK // SUB

    @pl.when(step == 0)
    def _():
        adjoint[...] = jnp.zeros_like(adjoint)
        later[...] = jnp.zeros_like(later)
        sums_ref[...] = jnp.zeros_like(sums_ref)

    split = split_ref[0]
    tri = triangle(False)
    tri_up = triangle(True)
    for n in reversed(range(chunks)):
        start = ((steps - 1 - step) * chunks + n) * CHUNK
        allowed, enter, tail, kept = chunk_masks(start, split)
        rows = slice(n * CHUNK, (n + 1) * CHUNK)
        for h in range(heads):
            cols = slice(h * HEAD, (h + 1) * HEAD)

            def part(which):
                return pre_ref[rows, which * width + h * HEAD : which * width + (h + 1) * HEAD]

            def store(which, value):
                out_ref[rows, which * width + h * HEAD : which * width + (h + 1) * HEAD] = value.astype(BF16)

            pre_q = part(0)
            sig_q, sig_nq = sigmoid_pair(pre_q)
            q = pre_q * sig_q
            bound = bound_ref[:, cols]
            plus, minus = sigmoid_pair(part(1) + bias_ref[:, cols])
            k = (1.0 - bound) * minus
            forget = bound + (1.0 - bound) * plus
            _, mids, ends, to_mid, from_mid, to_end, whole, final, to_final, qd, keys = chunk_common(
                q, k, jnp.log(forget), tri
            )
            v = part(2).astype(BF16)

            mixed = mixed_ref[rows, cols]
            grad = grad_ref[rows, cols].astype(F32)
            gain = gain_ref[:, cols]
            scale = lax.rsqrt(jnp.mean(mixed * mixed, axis=-1, keepdims=True) + EPS_GROUP)
            pre_g = part(3)
            sig_g, sig_ng = sigmoid_pair(pre_g)
            gate = pre_g * sig_g
            unit = mixed * scale
            u = grad * gain * gate
            moment = jnp.mean(u * unit, axis=-1, keepdims=True)
            mixed_grad = scale * (u - unit * moment)
            gu = grad * unit
            gain_sum = jnp.sum(gu * gate, axis=0, keepdims=True)
            store(3, gu * gain * (sig_g * (1.0 + pre_g * sig_ng)))

            do = mixed_grad.astype(BF16)
            old = states_ref[n, h]
            lam = adjoint[h]
            old_low = old.astype(BF16)
            lam_low = lam.astype(BF16)
            scores = jnp.where(allowed, scores_of(qd, keys), 0.0).astype(BF16)
            pair = jnp.where(allowed, dot_nt(do, v), 0.0).astype(BF16)
            reach = whole * enter
            remain = to_final * tail
            ending = (k * remain).astype(BF16)
            store(2, dot_tn(scores, do) + dot_nt(ending, lam_low))

            q_rows = []
            k_rows = [None] * count
            for i in range(count):
                pair_i = pair[i * SUB : (i + 1) * SUB]
                q_rows.append(dot_nn(pair_i, keys[i]))
                back = dot_tn(pair_i, qd[i * SUB : (i + 1) * SUB])
                for j in range(i + 1):
                    piece = back[j * SUB : (j + 1) * SUB]
                    if j == i:
                        piece = piece * from_mid[j * SUB : (j + 1) * SUB]
                        k_rows[j] = (k_rows[j], piece)
                    else:
                        piece = piece * jnp.exp(mids[i] - ends[j])
                        first = k_rows[j]
                        k_rows[j] = piece if first is None else first + piece
                diagonal = k_rows[i][1]
                k_rows[i] = None
                if i == 0:
                    diagonals = []
                diagonals.append(diagonal)
            k_intra = []
            for j in range(count):
                piece = diagonals[j]
                if k_rows[j] is not None:
                    piece = piece + k_rows[j] * to_end[j * SUB : (j + 1) * SUB]
                k_intra.append(piece)
            dq = jnp.concatenate(q_rows, axis=0) * to_mid + dot_nn(do, old_low) * reach
            dk = jnp.concatenate(k_intra, axis=0) + dot_nn(v, lam_low) * remain
            anchor = jnp.sum(lam * later[h], axis=0, keepdims=True)
            dlog = tri_dot(tri_up, q * dq - k * dk) + anchor
            adjoint[h] = lam * (jnp.exp(final) * kept) + dot_tn(do, (q * reach).astype(BF16))
            later[h] = old

            store(0, dq * (sig_q * (1.0 + pre_q * sig_nq)))
            drive = minus * (dlog / forget - dk)
            forget_grad = (1.0 - bound) * plus * drive
            store(1, forget_grad)
            sums_ref[0:1, cols] += gain_sum
            sums_ref[1:2, cols] += jnp.sum(forget_grad, axis=0, keepdims=True)
            sums_ref[2:3, cols] += jnp.sum(drive, axis=0, keepdims=True)


def mixer_backward(pre, mixed, grad, states, bias, bound, gain, split, chunks=1):
    tokens, wide = pre.shape
    width = wide // 4
    heads = width // HEAD
    block = chunks * CHUNK
    steps = tokens // block
    row = pl.BlockSpec((1, width), lambda i: (0, 0))
    narrow = pl.BlockSpec((block, width), lambda i: (steps - 1 - i, 0))
    return pl.pallas_call(
        functools.partial(backward_kernel, heads, chunks),
        grid=(steps,),
        in_specs=[
            pl.BlockSpec(memory_space=pltpu.SMEM),
            pl.BlockSpec((block, wide), lambda i: (steps - 1 - i, 0)),
            narrow,
            narrow,
            pl.BlockSpec((chunks, heads, HEAD, HEAD), lambda i: (steps - 1 - i, 0, 0, 0)),
            row,
            row,
            row,
        ],
        out_specs=[
            pl.BlockSpec((block, wide), lambda i: (steps - 1 - i, 0)),
            pl.BlockSpec((8, width), lambda i: (0, 0)),
        ],
        out_shape=[
            jax.ShapeDtypeStruct((tokens, wide), BF16),
            jax.ShapeDtypeStruct((8, width), F32),
        ],
        scratch_shapes=[pltpu.VMEM((heads, HEAD, HEAD), F32), pltpu.VMEM((heads, HEAD, HEAD), F32)],
        compiler_params=pltpu.CompilerParams(
            dimension_semantics=("arbitrary",), vmem_limit_bytes=32 << 20
        ),
        cost_estimate=pl.CostEstimate(
            flops=tokens * width * 5120, bytes_accessed=tokens * width * 34, transcendentals=tokens * width * 14
        ),
        name="mixer_backward",
    )(split, pre, mixed, grad, states, bias[None], bound[None], gain[None])


def rms_rows(rows_in):
    return lax.rsqrt(jnp.mean(rows_in * rows_in, axis=-1, keepdims=True) + EPS_NORM)


def norm_back(grad, rows_in, gain_vec):
    inv = rms_rows(rows_in)
    u = grad * gain_vec
    moment = jnp.mean(u * rows_in, axis=-1, keepdims=True)
    return inv * u - rows_in * (inv * inv * inv * moment), jnp.sum(grad * rows_in * inv, axis=0)


def gather(part, axes, dim):
    return lax.all_gather(part, axes, axis=dim, tiled=True)


def scatter(whole, axes, dim):
    return lax.psum_scatter(whole, axes, scatter_dimension=dim, tiled=True)


def matmul(left_side, right_side):
    return jnp.dot(left_side, right_side, preferred_element_type=F32)


def body(
    block_in,
    query_proj,
    forget_proj,
    value_proj,
    outgate_proj,
    out_proj,
    ffn_gate,
    ffn_up,
    ffn_down,
    first_gain,
    second_gain,
    group_gain,
    forget_bias,
    bound_table,
    layer_index,
    second_start,
    cotangent,
):
    ctx_count, ctx_at = lax.axis_size("ctx"), lax.axis_index("ctx")
    tp_count, tp_at = lax.axis_size("tp"), lax.axis_index("tp")
    row_count = block_in.shape[0]
    local_width = query_proj.shape[1]
    width = local_width // ctx_count
    hidden_width = ffn_gate.shape[1]
    shard_rows = row_count // tp_count

    def own_half(array, dim):
        size = array.shape[dim] // ctx_count
        return lax.dynamic_slice_in_dim(array, ctx_at * size, size, dim)

    def own_rows(array):
        return lax.dynamic_slice_in_dim(array, tp_at * shard_rows, shard_rows, 0)

    mix_full = gather(
        jnp.concatenate(
            [own_half(w, 1) for w in (query_proj, forget_proj, value_proj, outgate_proj)], axis=1
        ),
        "dp",
        0,
    )
    out_full = gather(own_half(out_proj, 0), "dp", 1)
    down_full = gather(own_half(ffn_down, 1), ("dp", "ctx"), 1)
    ffn_full = gather(own_half(jnp.concatenate([ffn_gate, ffn_up], axis=1), 0), ("dp", "ctx"), 0)

    inputs = block_in.astype(F32)
    first_low = (inputs * rms_rows(inputs) * first_gain).astype(BF16)
    first_all = gather(first_low, "ctx", 0)
    table = own_half(bound_table, 1)
    weights = jax.nn.softmax(table, axis=0)
    rows = lax.broadcasted_iota(jnp.int32, (table.shape[0], 1), 0)
    counted = jnp.where((rows >= 1) & (rows <= layer_index[0]), 1.0, 0.0)
    bound = jnp.sum(weights * counted, axis=0)
    bias = own_half(forget_bias, 0)
    gain = own_half(group_gain, 0)
    pre = matmul(first_all, mix_full)
    gated, mixed, states = mixer_forward(pre, bias, bound, gain, second_start)
    out_part = matmul(gated, out_full).astype(BF16)
    resid = own_rows(block_in).astype(F32) + scatter(out_part, ("ctx", "tp"), 0).astype(F32)

    second_low = gather((resid * rms_rows(resid) * second_gain).astype(BF16), "tp", 0)
    gate_up = matmul(second_low, ffn_full)
    pre_gate = gate_up[:, :hidden_width]
    pre_up = gate_up[:, hidden_width:]
    sig = jax.nn.sigmoid(pre_gate)
    hidden = (pre_gate * sig * pre_up).astype(BF16)
    ffn_part = matmul(hidden, down_full).astype(BF16)
    block_out = gather((resid + scatter(ffn_part, "tp", 0).astype(F32)).astype(BF16), "tp", 0)

    hidden_grad = dot_nt(cotangent, down_full)
    gate_grad = hidden_grad * pre_up * sig * (1.0 + pre_gate * (1.0 - sig))
    up_grad = hidden_grad * (pre_gate * sig)
    gate_up_grad = jnp.concatenate([gate_grad.astype(BF16), up_grad.astype(BF16)], axis=1)
    second_part = dot_nt(gate_up_grad, ffn_full).astype(BF16)
    down_sum = scatter(dot_tn(hidden, cotangent).astype(BF16), ("dp", "ctx"), 1)
    ffn_sum = scatter(dot_tn(second_low, gate_up_grad).astype(BF16), ("dp", "ctx"), 0)
    second_total = scatter(second_part, "tp", 0).astype(F32)
    resid_part, second_gain_grad = norm_back(second_total, resid, second_gain)
    resid_grad = own_rows(cotangent).astype(F32) + resid_part
    resid_low = gather(resid_grad.astype(BF16), ("ctx", "tp"), 0)

    gated_grad = dot_nt(resid_low, out_full)
    out_sum = scatter(dot_tn(gated, resid_low).astype(BF16), "dp", 1)
    proj_grad, sums = mixer_backward(pre, mixed, gated_grad, states, bias, bound, gain, second_start)
    first_part = dot_nt(proj_grad, mix_full).astype(BF16)
    mix_sum = scatter(dot_tn(first_all, proj_grad).astype(BF16), "dp", 0)
    first_total = scatter(first_part, ("ctx", "tp"), 0).astype(F32)
    input_part, first_gain_grad = norm_back(first_total, own_rows(block_in).astype(F32), first_gain)
    input_grad = gather((resid_grad + input_part).astype(BF16), "tp", 0).astype(F32)

    head_sums = gather(jnp.sum(gather(sums[:3], "dp", 0).reshape(-1, 3, width), axis=0), "ctx", 1)
    gains = jnp.stack([first_gain_grad, second_gain_grad])
    gain_sums = jnp.sum(gather(gains[None], ("dp", "ctx", "tp"), 0), axis=0)
    all_weights = jax.nn.softmax(bound_table, axis=0)
    all_bound = jnp.sum(all_weights * counted, axis=0)
    table_grad = all_weights * (counted - all_bound) * head_sums[2]

    mix_both = gather(mix_sum[None], "ctx", 0)

    def columns(which):
        parts = [mix_both[c, :, which * width : (which + 1) * width] for c in range(ctx_count)]
        return jnp.concatenate(parts, axis=1).astype(F32)

    ffn_shard = gather(ffn_sum, "ctx", 0).astype(F32)
    return (
        block_out,
        input_grad,
        columns(0),
        columns(1),
        columns(2),
        columns(3),
        gather(out_sum, "ctx", 0).astype(F32),
        ffn_shard[:, :hidden_width],
        ffn_shard[:, hidden_width:],
        gather(down_sum, "ctx", 1).astype(F32),
        gain_sums[0],
        gain_sums[1],
        head_sums[0],
        head_sums[1],
        table_grad,
    )


def solution(mesh):
    return jax.shard_map(
        body,
        mesh=mesh,
        in_specs=(
            P(("dp", "ctx"), None),
            P("dp", "tp"),
            P("dp", "tp"),
            P("dp", "tp"),
            P("dp", "tp"),
            P("tp", "dp"),
            P("dp", "tp"),
            P("dp", "tp"),
            P("tp", "dp"),
            P(),
            P(),
            P("tp"),
            P("tp"),
            P(None, "tp"),
            P(),
            P("dp"),
            P(("dp", "ctx"), None),
        ),
        out_specs=(
            P(("dp", "ctx"), None),
            P(("dp", "ctx"), None),
            P("dp", "tp"),
            P("dp", "tp"),
            P("dp", "tp"),
            P("dp", "tp"),
            P("tp", "dp"),
            P("dp", "tp"),
            P("dp", "tp"),
            P("tp", "dp"),
            P(),
            P(),
            P("tp"),
            P("tp"),
            P(None, "tp"),
        ),
        check_vma=False,
    )
```

time: 2250 us -> 1020 us (0.45); the launches traced: 2220 us -> 1010 us
  local copies, waits for them, and re-layouts: 640 us -> 33.6 us
  waiting for transfers between devices: 930 us -> 644 us
  other arithmetic: 275 us -> 44.6 us
  matrix products: 319 us -> 150 us
  blocking collectives: 36.4 us -> 87.7 us
  Pallas kernels: 0 us -> 33.6 us
    pad x74 -> x0, local copies, waits for them, and re-layouts: 483 us -> none  [block_parts(): lax.associative_scan(chain_link, (carried, states), axis=0)]
    psum x3 -> x0, waiting for transfers between devices: 416 us -> none  [the longest x1 166 us: body(): resid = inputs + lax.psum(mix_partial, 'tp')]
    reduce_scatter x4 -> x8, waiting for transfers between devices: 84.8 us -> 393 us  [scatter(): return lax.psum_scatter(whole, axes, scatter_dimension=dim, tiled=True)]
    all_gather x7 -> x12, waiting for transfers between devices: 427 us -> 249 us  [gather(): return lax.all_gather(part, axes, axis=dim, tiled=True)]
    dot_general x31 -> x12, matrix products: 310 us -> 150 us  [the longest x4 51.9 us: dot_nt(): lax.dot_general(a, b, (((1,), (1,)), ((), ())), preferred_element_type=F32)]
    reduce_sum x23 -> x10, other arithmetic: 105 us -> 10.3 us  [the longest x2 5.2 us: rms_rows(): jnp.mean(rows_in * rows_in, axis=-1, keepdims=True) + EPS_NORM]
    all_gather x5 -> x4, blocking collectives: 10.1 us -> 87.7 us  [gather(): return lax.all_gather(part, axes, axis=dim, tiled=True)]
    add x22 -> x0, other arithmetic: 59.4 us -> none  [the longest x10 15 us: block_parts(): lax.associative_scan(chain_link, (carried, states), axis=0)]
  transfers between devices with their start and end apart: 14 -> 20, of which waited for: 7 -> 14; matrix products, arithmetic and copies ran while one was open for 51% -> 16% of each run, Pallas kernels for 0% -> 3%
where the time goes in v1:
time: 1020 us; the launch traced here: 1010 us
  waiting for transfers between devices  644 us (63%)
  matrix products  150 us (15%)
  blocking collectives  87.7 us (9%)
  other arithmetic  44.6 us (4%)
  local copies, waits for them, and re-layouts  33.6 us (3%)
  Pallas kernels  33.6 us (3%)
  between operations  17.8 us (2%)
    reduce_scatter x8, waiting for transfers between devices, scatter(): return lax.psum_scatter(whole, axes, scatter_dimension=dim, tiled=True)  393 us
    all_gather x12, waiting for transfers between devices, gather(): return lax.all_gather(part, axes, axis=dim, tiled=True)  249 us
    all_gather x4, blocking collectives, gather(): return lax.all_gather(part, axes, axis=dim, tiled=True)  87.7 us
    dot_general x4, matrix products, dot_nt(): lax.dot_general(a, b, (((1,), (1,)), ((), ())), preferred_element_type=F32)  51.9 us
    dot_general x4, matrix products, dot_tn(): lax.dot_general(a, b, (((0,), (0,)), ((), ())), preferred_element_type=F32)  49.3 us
    dot_general x4, matrix products, matmul(): return jnp.dot(left_side, right_side, preferred_element_type=F32)  49 us
    pallas_call x1, Pallas kernels, mixer_backward(): pl.pallas_call(functools.partial(backward_kernel, heads, chunks), grid=(s...  22.2 us
    unnamed x62, local copies, waits for them, and re-layouts  22.1 us
  transfers between devices with their start and end apart: 20, of which 14 were waited for; matrix products, arithmetic and copies ran while one was open for 16% of the time, Pallas kernels for 3%

profile of v1, /device:TPU:0, one launch (start us, length us, event | category | flops | bytes accessed | tf_op | source)
XLA Modules:
  0.0 1013.6 jit_solution(16739948848391542412)
XLA Ops:
  11.5 3.2 fusion
  15.0 3.0 fusion.2
  21.5 73.6 %all-gather.19.cloned.1.call-done = bf16[2048,1024]{1,0:T(8,128)(2,1)} async-done(((bf16[512,1024]{1,0:T(8,128)(2,1)}), bf16[2048,1024]{1,0:T(8,128)(2,1)}) %all-gather.19.cloned.1.call-update) | async-done | bytes 4194320 | tf_op jit(solution)/shard_map/all_gather | solution.py:373
  95.1 20.5 %all-gather.17.cloned.1.call-done = bf16[2048,2048]{1,0:T(8,128)(2,1)} async-done(((bf16[1024,2048]{1,0:T(8,128)(2,1)}), bf16[2048,2048]{1,0:T(8,128)(2,1)}) %all-gather.17.cloned.1.call-update) | async-done | bytes 8388624 | tf_op jit(solution)/shard_map/all_gather | solution.py:373
  115.6 12.5 %fusion.35.pre_ref = f32[2048,1024]{1,0:T(8,128)S(1)} fusion(bf16[2048,2048]{1,0:T(8,128)(2,1)} %all-gather.17.cloned.1.call-done, bf16[2048,1024]{1,0:T(8,128)(2,1)} %all-gather.19.cloned.1.call-done), kind=kOutput, calls=%fused_computation.97 | convolution fusion | flops 8589934592 | bytes 20971520 | tf_op jit(solution)/shard_map/dot_general | solution.py:381
  128.1 11.4 %mixer_forward.1 = (bf16[2048,256]{1,0:T(8,128)(2,1)S(1)}, f32[2048,256]{1,0:T(8,128)S(1)}, f32[16,2,128,128]{3,2,1,0:T(8,128)S(1)}) custom-call(s32[1]{0:T(128)S(6)} %copy.37.split_ref, f32[2048,1024]{1,0:T(8,128)S(1)} %fusion.35.pre_ref, f32[1,256]{1,0:T(1,128)S(1)} %bitcast.68, f32[1,256]{1,0:T(1,128)S(1)} %bitcast.66, f32[1,256]{1,0:T(1,128)S(1)} %bitcast.70), custom_call_target="tpu_custom_call" | custom-call | flops 1073741824 | bytes 15728640 | tf_op jit(solution)/shard_map/mixer_forward/pallas_call | solution.py:166
  139.5 3.4 copy-done.4
  146.9 6.9 convolution_convert_fusion.3
  155.2 2.3 fusion.23
  157.6 69.4 %reduce-scatter.9.cloned.1.call-done = bf16[256,2048]{1,0:T(8,128)(2,1)} async-done(((bf16[2048,2048]{1,0:T(8,128)(2,1)}), bf16[256,2048]{1,0:T(8,128)(2,1)}) %reduce-scatter.9.cloned.1.call-update) | async-done | bytes 1048592 | tf_op jit(solution)/shard_map/reduce_scatter | solution.py:377
  227.0 2.0 multiply_reduce_fusion
  229.0 2.9 multiply_convert_fusion.1
  233.5 32.3 %all-gather.25.cloned.1.call-done = bf16[2048,2816]{1,0:T(8,128)(2,1)} async-done(((bf16[256,2816]{1,0:T(8,128)(2,1)}), bf16[2048,2816]{1,0:T(8,128)(2,1)}) %all-gather.25.cloned.1.call-update) | async-done | bytes 11534352 | tf_op jit(solution)/shard_map/all_gather | solution.py:373
  265.8 53.3 %all-gather.23.cloned.1.call-done = bf16[1024,2048]{1,0:T(8,128)(2,1)} async-done(((bf16[256,2048]{1,0:T(8,128)(2,1)}), bf16[1024,2048]{1,0:T(8,128)(2,1)}) %all-gather.23.cloned.1.call-update) | async-done | bytes 4194320 | tf_op jit(solution)/shard_map/all_gather | solution.py:373
  319.1 18.8 %fusion.36 = f32[1024,2816]{1,0:T(8,128)} fusion(bf16[1024,2048]{1,0:T(8,128)(2,1)} %all-gather.23.cloned.1.call-done, bf16[2048,2816]{1,0:T(8,128)(2,1)} %all-gather.25.cloned.1.call-done), kind=kOutput, calls=%fused_computation.98 | convolution fusion | flops 11811160064 | bytes 27262976 | tf_op jit(solution)/shard_map/dot_general | solution.py:381
  337.9 44.1 %all-gather.27.cloned.1.call-done = bf16[1408,2048]{1,0:T(8,128)(2,1)} async-done(((bf16[1408,256]{1,0:T(8,128)(2,1)}), bf16[1408,2048]{1,0:T(8,128)(2,1)}) %all-gather.27.cloned.1.call-update) | async-done | bytes 5767184 | tf_op jit(solution)/shard_map/all_gather | solution.py:373
  382.0 15.6 %fusion.5 = (bf16[1024,1408]{1,0:T(8,128)(2,1)S(1)}, bf16[1024,1408]{1,0:T(8,128)(2,1)S(1)}, bf16[1024,1408]{1,0:T(8,128)(2,1)}) fusion(f32[1024,2816]{1,0:T(8,128)} %fusion.36, bf16[1408,2048]{1,0:T(8,128)(2,1)} %all-gather.27.cloned.1.call-done, bf16[1024,2048]{1,0:T(8,128)(2,1)} %param.33), kind=kOutput, calls=%fused_computation.14 | convolution fusion | flops 5927206912 | bytes 30146560 | tf_op jit(solution)/shard_map/dot_general | solution.py:24
  400.1 16.2 %convolution_convert_fusion.4 = bf16[1024,2048]{1,0:T(8,128)(2,1)} fusion(bf16[2048,2816]{1,0:T(8,128)(2,1)} %all-gather.25.cloned.1.call-done, bf16[1024,1408]{1,0:T(8,128)(2,1)S(1)} %get-tuple-element.31, bf16[1024,1408]{1,0:T(8,128)(2,1)S(1)} %get-tuple-element.30), kind=kOutput, calls=%fused_computation.24 | convolution fusion | flops 11824791552 | bytes 21495808 | tf_op jit(solution)/shard_map/dot_general | solution.py:24
  416.4 50.8 %reduce-scatter.13.cloned.1.call-done = bf16[256,2048]{1,0:T(8,128)(2,1)} async-done(((bf16[1024,2048]{1,0:T(8,128)(2,1)}), bf16[256,2048]{1,0:T(8,128)(2,1)}) %reduce-scatter.13.cloned.1.call-update) | async-done | bytes 1048592 | tf_op jit(solution)/shard_map/reduce_scatter | solution.py:377
  467.2 2.5 fusion.18
  469.7 3.6 fusion.31
  473.6 10.5 %convolution_convert_fusion.1 = bf16[1408,2048]{1,0:T(8,128)(2,1)} fusion(bf16[1024,1408]{1,0:T(8,128)(2,1)} %get-tuple-element.32, bf16[1024,2048]{1,0:T(8,128)(2,1)} %param.33), kind=kOutput, calls=%fused_computation.6 | convolution fusion | flops 5908463616 | bytes 12845056 | tf_op jit(solution)/shard_map/dot_general | solution.py:28
  484.1 19.2 %convolution_convert_fusion = bf16[2048,2816]{1,0:T(8,128)(2,1)} fusion(bf16[1024,2048]{1,0:T(8,128)(2,1)} %all-gather.23.cloned.1.call-done, bf16[1024,1408]{1,0:T(8,128)(2,1)} %copy-done.29, bf16[1024,1408]{1,0:T(8,128)(2,1)} %copy-done.28), kind=kOutput, calls=%fused_computation | convolution fusion | flops 11828461568 | bytes 21495808 | tf_op jit(solution)/shard_map/dot_general | solution.py:28
  503.6 24.3 %all-gather.31.cloned.1.call-done = bf16[2048,2048]{1,0:T(8,128)(2,1)} async-done(((bf16[256,2048]{1,0:T(8,128)(2,1)}), bf16[2048,2048]{1,0:T(8,128)(2,1)}) %all-gather.31.cloned.1.call-update) | async-done | bytes 8388624 | tf_op jit(solution)/shard_map/all_gather | solution.py:373
  527.9 6.0 fusion.37.grad_ref
  534.0 3.4 copy-done.5
  537.4 22.2 %mixer_backward.1 = (bf16[2048,1024]{1,0:T(8,128)(2,1)S(1)}, f32[8,256]{1,0:T(8,128)S(1)}) custom-call(s32[1]{0:T(128)S(6)} %copy.37.split_ref, f32[2048,1024]{1,0:T(8,128)S(1)} %copy-done.5, f32[2048,256]{1,0:T(8,128)S(1)} %copy-done.7, f32[2048,256]{1,0:T(8,128)S(1)} %fusion.37.grad_ref, f32[16,2,128,128]{3,2,1,0:T(8,128)S(1)} %copy-done.9, ...), custom_call_target="tpu_custom_call" | custom-call | flops 2684354560 | bytes 17825792 | tf_op jit(solution)/shard_map/mixer_backward/pallas_call | solution.py:329
  559.6 2.0 copy-done.10
  561.6 12.7 %convolution_convert_fusion.6 = bf16[2048,1024]{1,0:T(8,128)(2,1)} fusion(bf16[2048,2048]{1,0:T(8,128)(2,1)} %all-gather.17.cloned.1.call-done, bf16[2048,1024]{1,0:T(8,128)(2,1)S(1)} %get-tuple-element.23), kind=kOutput, calls=%fused_computation.26 | convolution fusion | flops 8592031744 | bytes 16777216 | tf_op jit(solution)/shard_map/dot_general | solution.py:28
  574.4 14.1 %convolution_convert_fusion.2 = bf16[2048,2048]{1,0:T(8,128)(2,1)} fusion(bf16[2048,1024]{1,0:T(8,128)(2,1)} %copy-done.10, bf16[2048,1024]{1,0:T(8,128)(2,1)} %all-gather.19.cloned.1.call-done), kind=kOutput, calls=%fused_computation.7 | convolution fusion | flops 8594128896 | bytes 16777216 | tf_op jit(solution)/shard_map/dot_general | solution.py:24
  588.9 10.9 %convolution_convert_fusion.5 = bf16[1024,2048]{1,0:T(8,128)(2,1)} fusion(bf16[1024,1408]{1,0:T(8,128)(2,1)} %get-tuple-element.32, bf16[1408,2048]{1,0:T(8,128)(2,1)} %all-gather.27.cloned.1.call-done), kind=kOutput, calls=%fused_computation.25 | convolution fusion | flops 5907677184 | bytes 12845056 | tf_op jit(solution)/shard_map/dot_general | solution.py:381
  601.0 6.8 convolution_convert_fusion.7
  607.9 60.9 %reduce-scatter.21.cloned.1.call-done = bf16[256,2816]{1,0:T(8,128)(2,1)} async-done(((bf16[2048,2816]{1,0:T(8,128)(2,1)}), bf16[256,2816]{1,0:T(8,128)(2,1)}) %reduce-scatter.21.cloned.1.call-update) | async-done | bytes 1441808 | tf_op jit(solution)/shard_map/reduce_scatter | solution.py:377
  668.9 77.3 %reduce-scatter.17.cloned.1.call-done = bf16[512,1024]{1,0:T(8,128)(2,1)} async-done(((bf16[2048,1024]{1,0:T(8,128)(2,1)}), bf16[512,1024]{1,0:T(8,128)(2,1)}) %reduce-scatter.17.cloned.1.call-update) | async-done | bytes 1048592 | tf_op jit(solution)/shard_map/reduce_scatter | solution.py:377
  746.3 76.4 %reduce-scatter.15.cloned.1.call-done = bf16[256,2048]{1,0:T(8,128)(2,1)} async-done(((bf16[2048,2048]{1,0:T(8,128)(2,1)}), bf16[256,2048]{1,0:T(8,128)(2,1)}) %reduce-scatter.15.cloned.1.call-update) | async-done | bytes 1048592 | tf_op jit(solution)/shard_map/reduce_scatter | solution.py:377
  822.7 2.2 fusion.22
  824.9 53.8 %reduce-scatter.11.cloned.1.call-done = bf16[256,2048]{1,0:T(8,128)(2,1)} async-done(((bf16[1024,2048]{1,0:T(8,128)(2,1)}), bf16[256,2048]{1,0:T(8,128)(2,1)}) %reduce-scatter.11.cloned.1.call-update) | async-done | bytes 1048592 | tf_op jit(solution)/shard_map/reduce_scatter | solution.py:377
  878.7 5.0 fusion.13
  884.4 3.3 convert_element_type.124
  887.8 13.6 %all-gather.3 = f32[4,3,256]{2,1,0:T(4,128)S(1)} all-gather(f32[1,3,256]{2,1,0:T(4,128)S(1)} %slice_bitcast_fusion.8), channel_id=1, replica_groups=mesh['dp'=4,'ctx'=2,'tp'=4] {'dp'}, dimensions={0}, use_global_device_ids=true | all-gather | bytes 15360 | tf_op jit(solution)/shard_map/all_gather | solution.py:373
  901.4 1.8 all_gather.63
  904.5 4.6 reduce-scatter.19.cloned.1.call-done
  909.1 2.4 all_gather.58
  912.6 4.7 fusion.32
  917.3 1.7 slice_bitcast_fusion.1
  923.4 70.0 %all-gather.2 = f32[32,2,2048]{2,1,0:T(2,128)S(1)} all-gather(f32[1,2,2048]{2,1,0:T(2,128)S(1)} %maximum_bitcast_fusion), channel_id=3, replica_groups=mesh['dp'=4,'ctx'=2,'tp'=4] {'dp','ctx','tp'}, dimensions={0}, use_global_device_ids=true | all-gather | bytes 540672 | tf_op jit(solution)/shard_map/all_gather | solution.py:373
  994.1 6.7 convert_element_type.113
  1000.8 4.9 copy.38
  (135 shorter events, 26.0 us)
Async XLA Ops:
  8.0 224.0 %copy-start = (bf16[1408,512]{1,0:T(8,128)(2,1)S(1)}, bf16[1408,512]{1,0:T(8,128)(2,1)}, u32[]{:S(2)}) copy-start(bf16[1408,512]{1,0:T(8,128)(2,1)} %param.25) | copy-start | bytes 4325380
  8.0 87.1 %all-gather.19.cloned.1.call-start = ((), (), s32[]{:S(2)}) async-start(), calls=%async_computation.9 | async-start | bytes 5242880 | tf_op jit(solution)/shard_map/all_gather | solution.py:373
  9.3 5.5 copy-start.22
  11.5 104.2 %all-gather.17.cloned.1.call-start = ((), (), s32[]{:S(2)}) async-start(), calls=%async_computation.8 | async-start | bytes 12582912 | tf_op jit(solution)/shard_map/all_gather | solution.py:373
  11.5 3.5 copy-start.11
  18.0 1.8 copy-start.15
  18.0 2.6 copy-start.26
  18.0 2.7 copy-start.27
  18.1 128.9 %all-gather.21.cloned.1.call-start = ((), (), s32[]{:S(2)}) async-start(), calls=%async_computation.10 | async-start | bytes 1310720 | tf_op jit(solution)/shard_map/all_gather | solution.py:373
  19.8 207.2 %reduce-scatter.9.cloned.1.call-start = ((), (), s32[]{:S(2)}) async-start(), calls=%async_computation.11 | async-start | bytes 9437184 | tf_op jit(solution)/shard_map/reduce_scatter | solution.py:377
  139.5 3.4 copy-start.4
  142.9 1.3 copy-start.6
  144.3 1.4 copy-start.8
  145.6 8.2 copy-start.2
  153.8 1.4 copy-start.17
  153.9 75.2 %copy-start.20 = (f32[2048]{0:T(1024)S(1)}, f32[2048]{0:T(1024)}, u32[]{:S(2)}) copy-start(f32[2048]{0:T(1024)} %param.27) | copy-start | bytes 24580
  153.9 112.0 %all-gather.25.cloned.1.call-start = ((), (), s32[]{:S(2)}) async-start(), calls=%async_computation.13 | async-start | bytes 12976128 | tf_op jit(solution)/shard_map/all_gather | solution.py:373
  157.5 161.6 %all-gather.23.cloned.1.call-start = ((), (), s32[]{:S(2)}) async-start(), calls=%async_computation.12 | async-start | bytes 5242880 | tf_op jit(solution)/shard_map/all_gather | solution.py:373
  232.0 150.0 %all-gather.27.cloned.1.call-start = ((), (), s32[]{:S(2)}) async-start(), calls=%async_computation.14 | async-start | bytes 6488064 | tf_op jit(solution)/shard_map/all_gather | solution.py:373
  233.0 234.2 %reduce-scatter.13.cloned.1.call-start = ((), (), s32[]{:S(2)}) async-start(), calls=%async_computation.17 | async-start | bytes 5242880 | tf_op jit(solution)/shard_map/reduce_scatter | solution.py:377
  397.5 1.6 copy-start.28
  397.5 2.5 copy-start.29
  416.3 50.9 %copy-start.12 = (bf16[256,2048]{1,0:T(8,128)(2,1)S(1)}, bf16[256,2048]{1,0:T(8,128)(2,1)}, u32[]{:S(2)}) copy-start(bf16[256,2048]{1,0:T(8,128)(2,1)} %reduce-scatter.9.cloned.1.call-done) | copy-start | bytes 3145732
  416.3 111.6 %all-gather.31.cloned.1.call-start = ((), (), s32[]{:S(2)}) async-start(), calls=%async_computation.18 | async-start | bytes 9437184 | tf_op jit(solution)/shard_map/all_gather | solution.py:373
  473.4 126.5 %reduce-scatter.23.cloned.1.call-start = ((), (), s32[]{:S(2)}) async-start(), calls=%async_computation.25 | async-start | bytes 6488064 | tf_op jit(solution)/shard_map/reduce_scatter | solution.py:377
  484.1 184.7 %reduce-scatter.21.cloned.1.call-start = ((), (), s32[]{:S(2)}) async-start(), calls=%async_computation.23 | async-start | bytes 12976128 | tf_op jit(solution)/shard_map/reduce_scatter | solution.py:377
  503.3 24.6 %copy-start.18 = (bf16[256,2048]{1,0:T(8,128)(2,1)S(1)}, bf16[256,2048]{1,0:T(8,128)(2,1)}, u32[]{:S(2)}) copy-start(bf16[256,2048]{1,0:T(8,128)(2,1)} %all-gather.21.cloned.1.call-done) | copy-start | bytes 3145732
  503.4 30.6 %copy-start.7 = (f32[2048,256]{1,0:T(8,128)S(1)}, f32[2048,256]{1,0:T(8,128)}, u32[]{:S(2)}) copy-start(f32[2048,256]{1,0:T(8,128)} %copy-done.6) | copy-start | bytes 6291460
  503.4 242.8 %reduce-scatter.17.cloned.1.call-start = ((), (), s32[]{:S(2)}) async-start(), calls=%async_computation.21 | async-start | bytes 5242880 | tf_op jit(solution)/shard_map/reduce_scatter | solution.py:377
  527.9 6.0 copy-start.9
  534.0 3.5 copy-start.5
  559.6 2.0 copy-start.10
  574.4 248.3 %reduce-scatter.15.cloned.1.call-start = ((), (), s32[]{:S(2)}) async-start(), calls=%async_computation.19 | async-start | bytes 9437184 | tf_op jit(solution)/shard_map/reduce_scatter | solution.py:377
  588.6 290.1 %reduce-scatter.11.cloned.1.call-start = ((), (), s32[]{:S(2)}) async-start(), calls=%async_computation.15 | async-start | bytes 5242880 | tf_op jit(solution)/shard_map/reduce_scatter | solution.py:377
  599.8 1.2 copy-start.3
  599.8 284.7 %all-gather.37.cloned.1.call-start = ((), (), s32[]{:S(2)}) async-start(), calls=%async_computation.26 | async-start | bytes 2162688 | tf_op jit(solution)/shard_map/all_gather | solution.py:373
  600.4 222.4 %copy-start.23 = (f32[2048]{0:T(1024)S(1)}, f32[2048]{0:T(1024)}, u32[]{:S(2)}) copy-start(f32[2048]{0:T(1024)} %param.26) | copy-start | bytes 24580
  600.4 308.8 %reduce-scatter.19.cloned.1.call-start = ((), (), s32[]{:S(2)}) async-start(), calls=%async_computation.22 | async-start | bytes 1310720 | tf_op jit(solution)/shard_map/reduce_scatter | solution.py:377
  607.8 270.9 %copy-start.13 = (bf16[256,2048]{1,0:T(8,128)(2,1)S(1)}, bf16[256,2048]{1,0:T(8,128)(2,1)}, u32[]{:S(2)}) copy-start(bf16[256,2048]{1,0:T(8,128)(2,1)} %reduce-scatter.9.cloned.1.call-done) | copy-start | bytes 3145732
  607.8 270.9 %copy-start.14 = (bf16[256,2048]{1,0:T(8,128)(2,1)S(1)}, bf16[256,2048]{1,0:T(8,128)(2,1)}, u32[]{:S(2)}) copy-start(bf16[256,2048]{1,0:T(8,128)(2,1)} %reduce-scatter.13.cloned.1.call-done) | copy-start | bytes 3145732
  607.8 270.9 %copy-start.21 = (f32[2048]{0:T(1024)S(1)}, f32[2048]{0:T(1024)}, u32[]{:S(2)}) copy-start(f32[2048]{0:T(1024)} %param.27) | copy-start | bytes 24580
  607.9 304.8 %all-gather.35.cloned.1.call-start = ((), (), s32[]{:S(2)}) async-start(), calls=%async_computation.24 | async-start | bytes 4325376 | tf_op jit(solution)/shard_map/all_gather | solution.py:373
  668.8 248.5 %all-gather.39.cloned.1.call-start = ((), (), s32[]{:S(2)}) async-start(), calls=%async_computation.27 | async-start | bytes 3145728 | tf_op jit(solution)/shard_map/all_gather | solution.py:373
  746.2 247.9 %all-gather.33.cloned.1.call-start = ((), (), s32[]{:S(2)}) async-start(), calls=%async_computation.20 | async-start | bytes 5242880 | tf_op jit(solution)/shard_map/all_gather | solution.py:373
  824.9 59.4 %copy-start.16 = (f32[24,512]{1,0:T(8,128)S(1)}, f32[24,512]{1,0:T(8,128)}, u32[]{:S(2)}) copy-start(f32[24,512]{1,0:T(8,128)} %param.30) | copy-start | bytes 147460
  824.9 59.4 %copy-start.25 = (f32[24]{0:T(128)S(1)}, f32[24]{0:T(128)}, u32[]{:S(2)}) copy-start(f32[24]{0:T(128)} %copy-done.24) | copy-start | bytes 292
  883.7 117.1 %all-gather.29.cloned.1.call-start = ((), (), s32[]{:S(2)}) async-start(), calls=%async_computation.16 | async-start | bytes 5242880 | tf_op jit(solution)/shard_map/all_gather | solution.py:373
  1000.8 4.9 copy-start.1
  (2 other events, 1.9 us)
Sparse Core Ops, SparseCore 0:
  11.6 83.4 all-gather.18
  97.2 18.3 all-gather.16
  117.8 29.0 all-gather.20
  154.0 73.0 reduce-scatter.8
  473.5 54.4 all-gather.30
  601.8 9.5 all-gather.36
  668.9 10.1 all-gather.34
  746.3 11.2 all-gather.38
  883.8 55.1 all-gather.32
  940.8 57.0 all-gather.28
Sparse Core Ops, SparseCore 1:
  157.6 108.1 all-gather.24
  268.3 50.8 all-gather.22
  321.2 60.6 all-gather.26
  416.4 50.7 reduce-scatter.12
  484.2 64.6 reduce-scatter.22
  551.2 117.5 reduce-scatter.20
  671.0 75.2 reduce-scatter.16
  750.5 72.2 reduce-scatter.14
  826.1 52.5 reduce-scatter.10
  881.7 27.4 reduce-scatter.18

commit v2 on v1

--- a/solution.py
+++ b/solution.py
@@ -13,7 +13,13 @@
 EPS_NORM = 1e-06
 EPS_GROUP = 1e-05
 F32 = jnp.float32
+VMEM = 58 << 20
+UNREAD = pl.BlockSpec(memory_space=pl.ANY)
 BF16 = jnp.bfloat16
+
+
+def cost(flops):
+    return pl.CostEstimate(flops=2 * flops, bytes_accessed=1 << 20, transcendentals=0)
 
 
 def dot_nn(a, b):
@@ -62,11 +68,6 @@
     tail = jnp.where((token >= local) == last, 1.0, 0.0)
     kept = jnp.where(jnp.logical_or(jnp.logical_not(last), before), 1.0, 0.0)
     return causal & same, enter, tail, kept
-
-
-def decays(log_forget, tri):
-    b = tri_dot(tri, log_forget)
-    return b
 
 
 def key_rows(k, b, kd, k_end_sub, mids, ends):
@@ -114,7 +115,18 @@
 
 
 def forward_kernel(
-    heads, chunks, split_ref, pre_ref, bias_ref, bound_ref, gain_ref, gated_ref, mixed_ref, states_ref, state
+    heads,
+    chunks,
+    order_ref,
+    split_ref,
+    pre_ref,
+    bias_ref,
+    bound_ref,
+    gain_ref,
+    gated_ref,
+    mixed_ref,
+    states_ref,
+    state,
 ):
     step = pl.program_id(0)
     width = heads * HEAD
@@ -156,47 +168,51 @@
             gated_ref[rows, cols] = (mixed * scale * gain_ref[:, cols] * gate).astype(BF16)
 
 
-def mixer_forward(pre, bias, bound, gain, split, chunks=2):
+def mixer_forward(pre, bias, bound, gain, split, order):
     tokens, wide = pre.shape
     width = wide // 4
     heads = width // HEAD
-    block = chunks * CHUNK
-    steps = tokens // block
-    row = pl.BlockSpec((1, width), lambda i: (0, 0))
-    return pl.pallas_call(
-        functools.partial(forward_kernel, heads, chunks),
+    steps = order.shape[0]
+    block = tokens // steps
+    chunks = block // CHUNK
+    row = pl.BlockSpec((1, width), lambda i, order: (0, 0))
+    grid_spec = pltpu.PrefetchScalarGridSpec(
+        num_scalar_prefetch=1,
         grid=(steps,),
         in_specs=[
             pl.BlockSpec(memory_space=pltpu.SMEM),
-            pl.BlockSpec((block, wide), lambda i: (i, 0)),
+            pl.BlockSpec((block, wide), lambda i, order: (order[i], 0)),
             row,
             row,
             row,
         ],
         out_specs=[
-            pl.BlockSpec((block, width), lambda i: (i, 0)),
-            pl.BlockSpec((block, width), lambda i: (i, 0)),
-            pl.BlockSpec((chunks, heads, HEAD, HEAD), lambda i: (i, 0, 0, 0)),
+            pl.BlockSpec((block, width), lambda i, order: (order[i], 0)),
+            pl.BlockSpec((block, width), lambda i, order: (i, 0)),
+            pl.BlockSpec((chunks, heads, HEAD, HEAD), lambda i, order: (i, 0, 0, 0)),
         ],
+        scratch_shapes=[pltpu.VMEM((heads, HEAD, HEAD), F32)],
+    )
+    return pl.pallas_call(
+        functools.partial(forward_kernel, heads, chunks),
+        grid_spec=grid_spec,
         out_shape=[
             jax.ShapeDtypeStruct((tokens, width), BF16),
             jax.ShapeDtypeStruct((tokens, width), F32),
             jax.ShapeDtypeStruct((tokens // CHUNK, heads, HEAD, HEAD), F32),
         ],
-        scratch_shapes=[pltpu.VMEM((heads, HEAD, HEAD), F32)],
         compiler_params=pltpu.CompilerParams(
-            dimension_semantics=("arbitrary",), vmem_limit_bytes=32 << 20
+            dimension_semantics=("arbitrary",), vmem_limit_bytes=VMEM
         ),
-        cost_estimate=pl.CostEstimate(
-            flops=tokens * width * 2048, bytes_accessed=tokens * width * 30, transcendentals=tokens * width * 12
-        ),
+        cost_estimate=cost(tokens * width * 14000),
         name="mixer_forward",
-    )(split, pre, bias[None], bound[None], gain[None])
+    )(order, split, pre, bias[None], bound[None], gain[None])
 
 
 def backward_kernel(
     heads,
     chunks,
+    order_ref,
     split_ref,
     pre_ref,
     mixed_ref,
@@ -318,44 +334,176 @@
             sums_ref[2:3, cols] += jnp.sum(drive, axis=0, keepdims=True)
 
 
-def mixer_backward(pre, mixed, grad, states, bias, bound, gain, split, chunks=1):
+def mixer_backward(pre, mixed, grad, states, bias, bound, gain, split, order):
     tokens, wide = pre.shape
     width = wide // 4
     heads = width // HEAD
-    block = chunks * CHUNK
-    steps = tokens // block
-    row = pl.BlockSpec((1, width), lambda i: (0, 0))
-    narrow = pl.BlockSpec((block, width), lambda i: (steps - 1 - i, 0))
-    return pl.pallas_call(
-        functools.partial(backward_kernel, heads, chunks),
+    steps = order.shape[0]
+    block = tokens // steps
+    chunks = block // CHUNK
+    row = pl.BlockSpec((1, width), lambda i, order: (0, 0))
+    placed = lambda i, order: (order[steps - 1 - i], 0)
+    grid_spec = pltpu.PrefetchScalarGridSpec(
+        num_scalar_prefetch=1,
         grid=(steps,),
         in_specs=[
             pl.BlockSpec(memory_space=pltpu.SMEM),
-            pl.BlockSpec((block, wide), lambda i: (steps - 1 - i, 0)),
-            narrow,
-            narrow,
-            pl.BlockSpec((chunks, heads, HEAD, HEAD), lambda i: (steps - 1 - i, 0, 0, 0)),
+            pl.BlockSpec((block, wide), placed),
+            pl.BlockSpec((block, width), lambda i, order: (steps - 1 - i, 0)),
+            pl.BlockSpec((block, width), placed),
+            pl.BlockSpec((chunks, heads, HEAD, HEAD), lambda i, order: (steps - 1 - i, 0, 0, 0)),
             row,
             row,
             row,
         ],
         out_specs=[
-            pl.BlockSpec((block, wide), lambda i: (steps - 1 - i, 0)),
-            pl.BlockSpec((8, width), lambda i: (0, 0)),
+            pl.BlockSpec((block, wide), placed),
+            pl.BlockSpec((8, width), lambda i, order: (0, 0)),
         ],
+        scratch_shapes=[pltpu.VMEM((heads, HEAD, HEAD), F32), pltpu.VMEM((heads, HEAD, HEAD), F32)],
+    )
+    return pl.pallas_call(
+        functools.partial(backward_kernel, heads, chunks),
+        grid_spec=grid_spec,
         out_shape=[
             jax.ShapeDtypeStruct((tokens, wide), BF16),
             jax.ShapeDtypeStruct((8, width), F32),
         ],
-        scratch_shapes=[pltpu.VMEM((heads, HEAD, HEAD), F32), pltpu.VMEM((heads, HEAD, HEAD), F32)],
         compiler_params=pltpu.CompilerParams(
-            dimension_semantics=("arbitrary",), vmem_limit_bytes=32 << 20
+            dimension_semantics=("arbitrary",), vmem_limit_bytes=VMEM
         ),
-        cost_estimate=pl.CostEstimate(
-            flops=tokens * width * 5120, bytes_accessed=tokens * width * 34, transcendentals=tokens * width * 14
+        cost_estimate=cost(tokens * width * 22000),
+        name="mixer_backward",
+    )(order, split, pre, mixed, grad, states, bias[None], bound[None], gain[None])
+
+
+def product_kernel(dims, a_ref, b_ref, *refs):
+    out_ref = refs[-1]
+    dot = lax.dot_general(a_ref[...], b_ref[...], (dims, ((), ())), preferred_element_type=F32)
+    out_ref[...] = dot.astype(out_ref.dtype)
+
+
+def product_add_kernel(dims, a_ref, b_ref, add_ref, *refs):
+    out_ref = refs[-1]
+    dot = lax.dot_general(a_ref[...], b_ref[...], (dims, ((), ())), preferred_element_type=F32)
+    out_ref[...] = (dot + add_ref[...].astype(F32)).astype(out_ref.dtype)
+
+
+NN = ((1,), (0,))
+NT = ((1,), (1,))
+TN = ((0,), (0,))
+
+
+def product(a, b, dims, kind, rows=None, cols=None, a_half=None, add=None, wait=()):
+    count = a.shape[1 - dims[0][0]] if a_half is None else a.shape[0] // 2
+    depth = a.shape[dims[0][0]]
+    wide = b.shape[1 - dims[1][0]]
+    tile_rows = rows or count
+    tile_cols = cols or wide
+    by_rows = rows is not None
+    shift = (a_half or 0) * (count // tile_rows)
+
+    def at_row(i):
+        return (i if by_rows else 0) + shift
+
+    def at_col(i):
+        return 0 if by_rows else i
+
+    if dims[0][0] == 1:
+        a_spec = pl.BlockSpec((tile_rows, depth), lambda i: (at_row(i), 0))
+    else:
+        a_spec = pl.BlockSpec((depth, tile_rows), lambda i: (0, at_row(i)))
+    if dims[1][0] == 0:
+        b_spec = pl.BlockSpec((depth, tile_cols), lambda i: (0, at_col(i)))
+    else:
+        b_spec = pl.BlockSpec((tile_cols, depth), lambda i: (at_col(i), 0))
+    out_spec = pl.BlockSpec((tile_rows, tile_cols), lambda i: (at_row(i) - shift, at_col(i)))
+    kernel = product_kernel if add is None else product_add_kernel
+    return pl.pallas_call(
+        functools.partial(kernel, dims),
+        grid=(count // tile_rows * (wide // tile_cols),),
+        in_specs=[a_spec, b_spec] + ([] if add is None else [out_spec]) + [UNREAD] * len(wait),
+        out_specs=out_spec,
+        out_shape=jax.ShapeDtypeStruct((count, wide), kind),
+        compiler_params=pltpu.CompilerParams(
+            dimension_semantics=("arbitrary",), vmem_limit_bytes=VMEM
         ),
-        name="mixer_backward",
-    )(split, pre, mixed, grad, states, bias[None], bound[None], gain[None])
+        cost_estimate=cost(2 * count * wide * depth),
+        name="product",
+    )(a, b, *([] if add is None else [add]), *wait)
+
+
+def weight_sum_kernel(own_ref, other_ref, b_ref, weight_ref, right_ref, *refs):
+    out_ref, sum_ref = refs[-2:]
+    half = own_ref.shape[0]
+    wide = b_ref.shape[1]
+    dot = dot_tn(own_ref[...], b_ref[:half]) + dot_tn(other_ref[...], b_ref[half:])
+    out_ref[:, :wide] = dot.astype(out_ref.dtype)
+    total = jnp.sum(dot * weight_ref[...].astype(F32), axis=1, keepdims=True)
+    sum_ref[...] = jnp.broadcast_to(total, sum_ref.shape)
+    start = 0
+    more = None
+    for ref in refs[:-2]:
+        size = ref.shape[0]
+        if start < right_ref.shape[0]:
+            term = dot_tn(ref[...], right_ref[start : start + size])
+            more = term if more is None else more + term
+            start += size
+    out_ref[:, wide:] = more.astype(out_ref.dtype)
+
+
+def weight_sum_product(own, other, b, weight, blocks, right, rows=256, wait=()):
+    half, count = own.shape
+    depth, wide = b.shape
+    extra = right.shape[1]
+    a_spec = pl.BlockSpec((half, rows), lambda i: (0, i))
+    out, total = pl.pallas_call(
+        weight_sum_kernel,
+        grid=(count // rows,),
+        in_specs=[
+            a_spec,
+            a_spec,
+            pl.BlockSpec((depth, wide), lambda i: (0, 0)),
+            pl.BlockSpec((rows, wide), lambda i: (i, 0)),
+            pl.BlockSpec((depth, extra), lambda i: (0, 0)),
+        ]
+        + [pl.BlockSpec((block.shape[0], rows), lambda i: (0, i)) for block in blocks]
+        + [UNREAD] * len(wait),
+        out_specs=[
+            pl.BlockSpec((rows, wide + extra), lambda i: (i, 0)),
+            pl.BlockSpec((rows, HEAD), lambda i: (i, 0)),
+        ],
+        out_shape=[
+            jax.ShapeDtypeStruct((count, wide + extra), BF16),
+            jax.ShapeDtypeStruct((count, HEAD), F32),
+        ],
+        compiler_params=pltpu.CompilerParams(
+            dimension_semantics=("arbitrary",), vmem_limit_bytes=VMEM
+        ),
+        cost_estimate=cost(2 * count * (wide + extra) * depth),
+        name="weight_sum_product",
+    )(own, other, b, weight, right, *blocks, *wait)
+    return out, total[:, 0]
+
+
+def blocks_product_kernel(b_ref, *refs):
+    out_ref = refs[-1]
+    start = 0
+    for ref in refs[:-1]:
+        size = ref.shape[0]
+        out_ref[start : start + size] = dot_nt(ref[...], b_ref[...])
+        start += size
+
+
+def blocks_product(blocks, b):
+    count = sum(block.shape[0] for block in blocks)
+    return pl.pallas_call(
+        blocks_product_kernel,
+        out_shape=jax.ShapeDtypeStruct((count, b.shape[0]), F32),
+        compiler_params=pltpu.CompilerParams(vmem_limit_bytes=VMEM),
+        cost_estimate=cost(2 * count * b.size),
+        name="blocks_product",
+    )(b, *blocks)
 
 
 def rms_rows(rows_in):
@@ -379,6 +527,106 @@
 
 def matmul(left_side, right_side):
     return jnp.dot(left_side, right_side, preferred_element_type=F32)
+
+
+def after(value, *others):
+    return lax.optimization_barrier((value, *others))[0]
+
+
+def small_sum(part, axis):
+    count = lax.axis_size(axis)
+    if count <= 4:
+        got = [lax.ppermute(part, axis, [(i, i ^ m) for i in range(count)]) for m in range(1, count)]
+        return sum(got, part)
+    mask = 1
+    while mask < count:
+        part = part + lax.ppermute(part, axis, [(i, i ^ mask) for i in range(count)])
+        mask *= 2
+    return part
+
+
+def together(*values):
+    return lax.optimization_barrier(values)
+
+
+def swap(part):
+    return lax.ppermute(part, "ctx", [(0, 1), (1, 0)])
+
+
+def in_order(own, dim):
+    other = swap(own)
+    first = lax.axis_index("ctx") == 0
+    return jnp.concatenate([jnp.where(first, own, other), jnp.where(first, other, own)], axis=dim)
+
+
+def partner(part, mask):
+    return lax.ppermute(part, "tp", [(i, i ^ mask) for i in range(lax.axis_size("tp"))])
+
+
+def blocks_of(array, count):
+    size = array.shape[0] // count
+    return [array[m * size : (m + 1) * size] for m in range(count)]
+
+
+def relative(array, count, at):
+    size = array.shape[0] // count
+    return jnp.concatenate(
+        [lax.dynamic_slice_in_dim(array, (at ^ m) * size, size, 0) for m in range(count)], axis=0
+    )
+
+
+def piece(part, block, which):
+    half = part.shape[0] // 8
+    start = (2 * block + which) * half
+    return part[start : start + half]
+
+
+def sum_first(part):
+    near = partner(jnp.concatenate([piece(part, 1, 0), piece(part, 3, 0)], axis=0), 1)
+    far = partner(jnp.concatenate([piece(part, 2, 1), piece(part, 3, 1)], axis=0), 2)
+    return near, far
+
+
+def sum_second(part, near, far):
+    half = near.shape[0] // 2
+    near, far = together(near, far)
+    pass_far = (piece(part, 2, 0).astype(F32) + near[half:].astype(F32)).astype(BF16)
+    pass_near = (piece(part, 1, 1).astype(F32) + far[half:].astype(F32)).astype(BF16)
+    pass_far, pass_near = together(pass_far, pass_near)
+    return together(partner(pass_far, 2), partner(pass_near, 1))
+
+
+def sum_total(part, first, second):
+    half = second[0].shape[0]
+    halves = [
+        piece(part, 0, which).astype(F32) + first[which][:half].astype(F32) + second[which].astype(F32)
+        for which in (0, 1)
+    ]
+    return jnp.concatenate(halves, axis=0)
+
+
+def gather_first(own):
+    return partner(own, 1), partner(own, 2)
+
+
+def gather_second(near, far):
+    half = near.shape[0] // 2
+    far_half, near_half = together(far[:half], near[half:])
+    return partner(far_half, 1), partner(near_half, 2)
+
+
+def gather_blocks(own, first, second):
+    return [own, *first, jnp.concatenate(second, axis=0)]
+
+
+def placed_blocks(own, first, second, kind):
+    count, at = lax.axis_size("tp"), lax.axis_index("tp")
+    size, width = own.shape
+    out = jnp.zeros((count * size, width), kind)
+    starts = [at * size, (at ^ 1) * size, (at ^ 2) * size, (at ^ 3) * size, (at ^ 3) * size + size // 2]
+    for block, start in zip([own, *first, *second], starts):
+        out = lax.dynamic_update_slice_in_dim(out, block.astype(kind), start, 0)
+    return out
 
 
 def body(
@@ -402,7 +650,7 @@
 ):
     ctx_count, ctx_at = lax.axis_size("ctx"), lax.axis_index("ctx")
     tp_count, tp_at = lax.axis_size("tp"), lax.axis_index("tp")
-    row_count = block_in.shape[0]
+    row_count, model = block_in.shape
     local_width = query_proj.shape[1]
     width = local_width // ctx_count
     hidden_width = ffn_gate.shape[1]
@@ -412,8 +660,13 @@
         size = array.shape[dim] // ctx_count
         return lax.dynamic_slice_in_dim(array, ctx_at * size, size, dim)
 
-    def own_rows(array):
-        return lax.dynamic_slice_in_dim(array, tp_at * shard_rows, shard_rows, 0)
+    def sum_over_chip(rows_in, right_side, dot):
+        other = swap(dot(rows_in[row_count:], right_side).astype(BF16))
+        own = dot(rows_in[:row_count], right_side)
+        return (own + other.astype(F32)).astype(BF16)
+
+    blocks = ctx_count * tp_count
+    order = lax.iota(jnp.int32, blocks) ^ (ctx_at * tp_count + tp_at)
 
     mix_full = gather(
         jnp.concatenate(
@@ -423,12 +676,13 @@
         0,
     )
     out_full = gather(own_half(out_proj, 0), "dp", 1)
+    ffn_full = gather(own_half(jnp.concatenate([ffn_gate, ffn_up], axis=1), 0), ("dp", "ctx"), 0)
     down_full = gather(own_half(ffn_down, 1), ("dp", "ctx"), 1)
-    ffn_full = gather(own_half(jnp.concatenate([ffn_gate, ffn_up], axis=1), 0), ("dp", "ctx"), 0)
-
-    inputs = block_in.astype(F32)
+
+    inputs = relative(block_in, tp_count, tp_at).astype(F32)
     first_low = (inputs * rms_rows(inputs) * first_gain).astype(BF16)
-    first_all = gather(first_low, "ctx", 0)
+    first_swapped = swap(first_low)
+    first_all = jnp.concatenate([first_low, first_swapped], axis=0)
     table = own_half(bound_table, 1)
     weights = jax.nn.softmax(table, axis=0)
     rows = lax.broadcasted_iota(jnp.int32, (table.shape[0], 1), 0)
@@ -437,54 +691,101 @@
     bias = own_half(forget_bias, 0)
     gain = own_half(group_gain, 0)
     pre = matmul(first_all, mix_full)
-    gated, mixed, states = mixer_forward(pre, bias, bound, gain, second_start)
-    out_part = matmul(gated, out_full).astype(BF16)
-    resid = own_rows(block_in).astype(F32) + scatter(out_part, ("ctx", "tp"), 0).astype(F32)
-
-    second_low = gather((resid * rms_rows(resid) * second_gain).astype(BF16), "tp", 0)
+    gated, mixed, states = mixer_forward(pre, bias, bound, gain, second_start, order)
+    inputs_own = inputs[:shard_rows]
+    out_part = sum_over_chip(gated, out_full, dot_nn)
+    first = sum_first(out_part)
+    second = sum_second(out_part, *first)
+    resid = inputs_own + sum_total(out_part, first, second)
+
+    second_own = (resid * rms_rows(resid) * second_gain).astype(BF16)
+    first = gather_first(second_own)
+    second_low = jnp.concatenate(
+        gather_blocks(second_own, first, gather_second(*first)), axis=0
+    )
+    cotangent_rel = relative(cotangent, tp_count, tp_at)
     gate_up = matmul(second_low, ffn_full)
     pre_gate = gate_up[:, :hidden_width]
     pre_up = gate_up[:, hidden_width:]
     sig = jax.nn.sigmoid(pre_gate)
     hidden = (pre_gate * sig * pre_up).astype(BF16)
-    ffn_part = matmul(hidden, down_full).astype(BF16)
-    block_out = gather((resid + scatter(ffn_part, "tp", 0).astype(F32)).astype(BF16), "tp", 0)
-
-    hidden_grad = dot_nt(cotangent, down_full)
-    gate_grad = hidden_grad * pre_up * sig * (1.0 + pre_gate * (1.0 - sig))
-    up_grad = hidden_grad * (pre_gate * sig)
-    gate_up_grad = jnp.concatenate([gate_grad.astype(BF16), up_grad.astype(BF16)], axis=1)
-    second_part = dot_nt(gate_up_grad, ffn_full).astype(BF16)
-    down_sum = scatter(dot_tn(hidden, cotangent).astype(BF16), ("dp", "ctx"), 1)
-    ffn_sum = scatter(dot_tn(second_low, gate_up_grad).astype(BF16), ("dp", "ctx"), 0)
-    second_total = scatter(second_part, "tp", 0).astype(F32)
-    resid_part, second_gain_grad = norm_back(second_total, resid, second_gain)
-    resid_grad = own_rows(cotangent).astype(F32) + resid_part
-    resid_low = gather(resid_grad.astype(BF16), ("ctx", "tp"), 0)
-
-    gated_grad = dot_nt(resid_low, out_full)
-    out_sum = scatter(dot_tn(gated, resid_low).astype(BF16), "dp", 1)
-    proj_grad, sums = mixer_backward(pre, mixed, gated_grad, states, bias, bound, gain, second_start)
-    first_part = dot_nt(proj_grad, mix_full).astype(BF16)
-    mix_sum = scatter(dot_tn(first_all, proj_grad).astype(BF16), "dp", 0)
-    first_total = scatter(first_part, ("ctx", "tp"), 0).astype(F32)
-    input_part, first_gain_grad = norm_back(first_total, own_rows(block_in).astype(F32), first_gain)
-    input_grad = gather((resid_grad + input_part).astype(BF16), "tp", 0).astype(F32)
-
-    head_sums = gather(jnp.sum(gather(sums[:3], "dp", 0).reshape(-1, 3, width), axis=0), "ctx", 1)
-    gains = jnp.stack([first_gain_grad, second_gain_grad])
-    gain_sums = jnp.sum(gather(gains[None], ("dp", "ctx", "tp"), 0), axis=0)
+
+    down_grad = dot_tn(hidden, cotangent_rel).astype(BF16)
+    down_sum = scatter(down_grad, ("dp", "ctx"), 1)
+    ffn_part = matmul(after(hidden, down_grad), down_full).astype(BF16)
+    ffn_first = sum_first(ffn_part)
+    hidden_grad = dot_nt(after(cotangent_rel, ffn_part), down_full)
+    gate_grad = (hidden_grad * pre_up * sig * (1.0 + pre_gate * (1.0 - sig))).astype(BF16)
+    up_grad = (hidden_grad * (pre_gate * sig)).astype(BF16)
+    ffn_second = sum_second(after(ffn_part, gate_grad), *ffn_first)
+    gate_up_grad = jnp.concatenate([gate_grad, up_grad], axis=1)
+    second_part = dot_nt(after(gate_up_grad, *ffn_first), ffn_full).astype(BF16)
+    ffn_total = sum_total(ffn_part, ffn_first, ffn_second)
+    second_part = after(second_part, *ffn_second)
+    first = sum_first(second_part)
+    gate_weight_grad = product(second_low, gate_grad, TN, BF16, rows=256)
+    gate_sum = scatter(gate_weight_grad, ("dp", "ctx"), 0)
+    second = sum_second(second_part, *first)
+    second_total = sum_total(second_part, first, second)
+    resid_part, second_gain_grad = norm_back(
+        after(second_total, down_sum), resid, second_gain
+    )
+    resid_grad = cotangent_rel[:shard_rows].astype(F32) + resid_part
+    resid_own = resid_grad.astype(BF16)
+    first = gather_first(resid_own)
+    up_weight_grad = product(second_low, up_grad, TN, BF16, rows=256)
+    up_sum = scatter(up_weight_grad, ("dp", "ctx"), 0)
+    resid_second = gather_second(*first)
+    resid_blocks = [resid_own, *first, *resid_second]
+    resid_blocks = resid_blocks + [swap(block) for block in resid_blocks]
+
+    block_own = after((resid + ffn_total).astype(BF16), *resid_second)
+    block_first = gather_first(block_own)
+
+    gated_grad = blocks_product(resid_blocks, out_full)
+    proj_grad, sums = mixer_backward(pre, mixed, gated_grad, states, bias, bound, gain, second_start, order)
+    first_other = product(after(proj_grad, *block_first), mix_full, NT, BF16, cols=256, a_half=1)
+    block_second = gather_second(*[after(block, proj_grad) for block in block_first])
+    first_part = product(
+        after(proj_grad, first_other), mix_full, NT, BF16, cols=256, a_half=0, add=swap(first_other)
+    )
+    first_part = after(first_part, *block_second)
+    first = sum_first(first_part)
+    mix_grad, first_sum = weight_sum_product(
+        first_low, first_swapped, after(proj_grad, first_part), mix_full, resid_blocks, gated, wait=[gate_sum, up_sum]
+    )
+    mix_sum = scatter(mix_grad, "dp", 0)
+    block_own = after(block_own, first_part)
+    block_out = placed_blocks(block_own, block_first, block_second, BF16)
+    final_first = first
+    second = sum_second(first_part, *first)
+    input_part, _ = norm_back(sum_total(first_part, first, second), inputs_own, first_gain)
+    input_own = (resid_grad + input_part).astype(BF16)
+    first = gather_first(input_own)
+    input_grad = placed_blocks(input_own, first, gather_second(*first), F32)
+
+    first_gain_grad = first_sum / first_gain
+    first_gain_grad = first_sum / first_gain
+    gains = jnp.concatenate([first_gain_grad, second_gain_grad]).reshape(-1, HEAD)
+    gains = after(gains, *final_first)
+    gains = small_sum(gains + swap(gains), "tp")
+    heads = sums[:3].reshape(-1, HEAD)
+    small = small_sum(jnp.concatenate([heads, gains]), "dp")
+    cut = heads.shape[0]
+    head_sums = in_order(small[:cut].reshape(3, width), 1)
+    gain_sums = small[cut:].reshape(-1)
     all_weights = jax.nn.softmax(bound_table, axis=0)
     all_bound = jnp.sum(all_weights * counted, axis=0)
     table_grad = all_weights * (counted - all_bound) * head_sums[2]
 
-    mix_both = gather(mix_sum[None], "ctx", 0)
+    mix_other = swap(mix_sum)
+    first_core = ctx_at == 0
+    mix_pair = [jnp.where(first_core, mix_sum, mix_other), jnp.where(first_core, mix_other, mix_sum)]
 
     def columns(which):
-        parts = [mix_both[c, :, which * width : (which + 1) * width] for c in range(ctx_count)]
-        return jnp.concatenate(parts, axis=1).astype(F32)
-
-    ffn_shard = gather(ffn_sum, "ctx", 0).astype(F32)
+        cols = slice(which * width, (which + 1) * width)
+        return jnp.concatenate([part[:, cols] for part in mix_pair], axis=1).astype(F32)
+
     return (
         block_out,
         input_grad,
@@ -492,12 +793,12 @@
         columns(1),
         columns(2),
         columns(3),
-        gather(out_sum, "ctx", 0).astype(F32),
-        ffn_shard[:, :hidden_width],
-        ffn_shard[:, hidden_width:],
-        gather(down_sum, "ctx", 1).astype(F32),
-        gain_sums[0],
-        gain_sums[1],
+        jnp.concatenate([mix_pair[0][:, 4 * width :].T, mix_pair[1][:, 4 * width :].T], axis=0).astype(F32),
+        in_order(after(gate_sum, *final_first), 0).astype(F32),
+        in_order(after(up_sum, *final_first), 0).astype(F32),
+        in_order(after(down_sum, *final_first), 1).astype(F32),
+        gain_sums[:model],
+        gain_sums[model:],
         head_sums[0],
         head_sums[1],
         table_grad,

time: 1020 us -> 687 us (0.67)
  waiting for transfers between devices: 644 us -> 281 us
  blocking collectives: 87.7 us -> 0 us
  Pallas kernels: 33.6 us -> 120 us
  matrix products: 150 us -> 84.2 us
  starting transfers between devices: 1.94 us -> 45.9 us
  other arithmetic: 44.6 us -> 83.3 us
  local copies, waits for them, and re-layouts: 33.6 us -> 47.1 us
    reduce_scatter x8 -> x4, waiting for transfers between devices: 393 us -> 0.01 us  [scatter(): return lax.psum_scatter(whole, axes, scatter_dimension=dim, tiled=True)]
    ppermute x0 -> x52, waiting for transfers between devices: none -> 194 us  [the longest x32 178 us: partner(): lax.ppermute(part, 'tp', [(i, i ^ mask) for i in range(lax.axis_size('tp'...]
    all_gather x12 -> x4, waiting for transfers between devices: 249 us -> 87.1 us  [gather(): return lax.all_gather(part, axes, axis=dim, tiled=True)]
    all_gather x4 -> x0, blocking collectives: 87.7 us -> none  [gather(): return lax.all_gather(part, axes, axis=dim, tiled=True)]
    pallas_call x2 -> x8, Pallas kernels: 33.6 us -> 120 us  [the longest x4 45.6 us: product(): pl.pallas_call(functools.partial(kernel, dims), grid=(count // tile_rows...]
    ppermute x0 -> x52, starting transfers between devices: none -> 45.6 us  [the longest x32 35.3 us: partner(): lax.ppermute(part, 'tp', [(i, i ^ mask) for i in range(lax.axis_size('tp'...]
    dot_general x4 -> x1, matrix products: 49.3 us -> 8.12 us  [dot_tn(): lax.dot_general(a, b, (((0,), (0,)), ((), ())), preferred_element_type=F32)]
    dot_general x4 -> x2, matrix products: 51.9 us -> 28.2 us  [dot_nt(): lax.dot_general(a, b, (((1,), (1,)), ((), ())), preferred_element_type=F32)]
  transfers between devices with their start and end apart: 20 -> 60, of which waited for: 14 -> 35; matrix products, arithmetic and copies ran while one was open for 16% -> 28% of each run, Pallas kernels for 3% -> 15%
where the time goes in v2:
time: 687 us; the launch traced here: 678 us
  waiting for transfers between devices  281 us (41%)
  Pallas kernels  120 us (17%)
  matrix products  84.2 us (12%)
  other arithmetic  83.3 us (12%)
  local copies, waits for them, and re-layouts  47.1 us (7%)
  starting transfers between devices  45.9 us (7%)
  between operations  16.6 us (2%)
    ppermute x32, waiting for transfers between devices, partner(): lax.ppermute(part, 'tp', [(i, i ^ mask) for i in range(lax.axis_size('tp'...  178 us
    all_gather x4, waiting for transfers between devices, gather(): return lax.all_gather(part, axes, axis=dim, tiled=True)  87.1 us
    pallas_call x4, Pallas kernels, product(): pl.pallas_call(functools.partial(kernel, dims), grid=(count // tile_rows...  45.6 us
    dot_general x3, matrix products, matmul(): return jnp.dot(left_side, right_side, preferred_element_type=F32)  43.4 us
    ppermute x32, starting transfers between devices, partner(): lax.ppermute(part, 'tp', [(i, i ^ mask) for i in range(lax.axis_size('tp'...  35.3 us
    dot_general x2, matrix products, dot_nt(): lax.dot_general(a, b, (((1,), (1,)), ((), ())), preferred_element_type=F32)  28.2 us
    pallas_call x1, Pallas kernels, mixer_forward(): pl.pallas_call(functools.partial(forward_kernel, heads, chunks), grid_spe...  24.4 us
    pallas_call x1, Pallas kernels, mixer_backward(): pl.pallas_call(functools.partial(backward_kernel, heads, chunks), grid_sp...  22.9 us
  transfers between devices with their start and end apart: 60, of which 35 were waited for; matrix products, arithmetic and copies ran while one was open for 28% of the time, Pallas kernels for 15%

profile of v2, /device:TPU:0, one launch (start us, length us, event | category | flops | bytes accessed | tf_op | source)
XLA Modules:
  0.0 677.8 jit_solution(4334085365829295234)
XLA Ops:
  12.5 2.3 fusion.6
  14.9 2.5 constant_dynamic-slice_fusion.13
  18.5 8.5 %multiply_convert_fusion.own_ref = bf16[1024,2048]{1,0:T(8,128)(2,1)} fusion(f32[2048]{0:T(1024)S(1)} %copy-done.45, f32[1024]{0:T(1024)S(1)} %add_rsqrt_fusion, bf16[256,2048]{1,0:T(8,128)(2,1)S(1)} %get-tuple-element.209, bf16[256,2048]{1,0:T(8,128)(2,1)S(1)} %get-tuple-element.210, bf16[256,2048]{1,0:T(8,128)(2,1)S(1)} %get-tuple-element.208, ...), kind=kLoop, calls=%fused_computation.5 | loop fusion | flops 23068672 | bytes 8400896 | tf_op jit(solution)/shard_map/convert_element_type | solution.py:683
  31.4 3.3 collective-permute-done.other_ref
  34.7 59.6 %all-gather.5.cloned.1.call-done.b_ref.weight_ref = bf16[2048,1024]{1,0:T(8,128)(2,1)} async-done(((bf16[512,1024]{1,0:T(8,128)(2,1)}), bf16[2048,1024]{1,0:T(8,128)(2,1)}) %all-gather.5.cloned.1.call-update) | async-done | bytes 4194320 | tf_op jit(solution)/shard_map/all_gather | solution.py:521
  94.3 15.1 %fusion.pre_ref = f32[2048,1024]{1,0:T(8,128)} fusion(bf16[2048,1024]{1,0:T(8,128)(2,1)} %all-gather.5.cloned.1.call-done.b_ref.weight_ref, bf16[1024,2048]{1,0:T(8,128)(2,1)} %collective-permute-done.other_ref, bf16[1024,2048]{1,0:T(8,128)(2,1)} %multiply_convert_fusion.own_ref), kind=kOutput, calls=%fused_computation | convolution fusion | flops 8606711808 | bytes 20971520 | tf_op jit(solution)/shard_map/dot_general | solution.py:529
  109.4 24.4 %mixer_forward.1 = (bf16[2048,256]{1,0:T(8,128)(2,1)}, f32[2048,256]{1,0:T(8,128)}, f32[16,2,128,128]{3,2,1,0:T(8,128)}) custom-call(s32[8]{0:T(128)} %iota_xor_fusion.order_ref, s32[1]{0:T(128)S(6)} %copy.49.split_ref, f32[2048,1024]{1,0:T(8,128)} %fusion.pre_ref, f32[1,256]{1,0:T(1,128)} %bitcast.37, f32[1,256]{1,0:T(1,128)} %bitcast.35, f32[1,256]{1,0:T(1,128)} %bitcast.39), custom_call_target="tpu_custom_call" | custom-call | flops 14680064000 | bytes 1048576 | tf_op jit(solution)/shard_map/mixer_forward/pallas_call | solution.py:196
  133.9 3.2 convolution_convert_fusion.3
  137.3 7.1 %collective-permute-done.1 = bf16[1024,2048]{1,0:T(8,128)(2,1)S(1)} collective-permute-done((bf16[1024,2048]{1,0:T(8,128)(2,1)S(1)}, bf16[1024,2048]{1,0:T(8,128)(2,1)S(1)}, u32[]{:S(2)}, u32[]{:S(2)}) %collective-permute-start.1) | collective-permute-done | bytes 4194336 | tf_op jit(solution)/shard_map/ppermute | solution.py:553
  148.9 22.3 %collective-permute-done.3 = bf16[256,2048]{1,0:T(8,128)(2,1)S(1)} collective-permute-done((bf16[256,2048]{1,0:T(8,128)(2,1)S(1)}, bf16[256,2048]{1,0:T(8,128)(2,1)S(1)}, u32[]{:S(2)}, u32[]{:S(2)}) %collective-permute-start.3) | collective-permute-done | bytes 1048608 | tf_op jit(solution)/shard_map/ppermute | solution.py:563
  176.8 2.6 maximum_convert_fusion
  179.4 7.6 %collective-permute-done.4 = bf16[128,2048]{1,0:T(8,128)(2,1)} collective-permute-done((bf16[128,2048]{1,0:T(8,128)(2,1)}, bf16[128,2048]{1,0:T(8,128)(2,1)}, u32[]{:S(2)}, u32[]{:S(2)}) %collective-permute-start.4) | collective-permute-done | bytes 524320 | tf_op jit(solution)/shard_map/ppermute | solution.py:563
  194.3 20.2 %collective-permute-done.7 = bf16[256,2048]{1,0:T(8,128)(2,1)S(1)} collective-permute-done((bf16[256,2048]{1,0:T(8,128)(2,1)S(1)}, bf16[256,2048]{1,0:T(8,128)(2,1)S(1)}, u32[]{:S(2)}, u32[]{:S(2)}) %collective-permute-start.7) | collective-permute-done | bytes 1048608 | tf_op jit(solution)/shard_map/ppermute | solution.py:563
  222.2 4.5 collective-permute-done.8
  230.1 2.7 all-gather.9.cloned.1.call-done
  232.8 17.2 %fusion.23 = f32[1024,2816]{1,0:T(8,128)S(1)} fusion(bf16[1024,2048]{1,0:T(8,128)(2,1)} %constant_dynamic-update-slice_fusion.a_ref, bf16[2048,2816]{1,0:T(8,128)(2,1)} %all-gather.9.cloned.1.call-done), kind=kOutput, calls=%fused_computation.147 | convolution fusion | flops 11811160064 | bytes 27262976 | tf_op jit(solution)/shard_map/dot_general | solution.py:529
  251.8 3.2 copy-done.9
  256.6 8.1 %convolution_convert_fusion = bf16[1408,2048]{1,0:T(8,128)(2,1)} fusion(bf16[1024,1408]{1,0:T(8,128)(2,1)S(1)} %multiply_convert_fusion.3, bf16[256,2048]{1,0:T(8,128)(2,1)S(1)} %copy-done.19, bf16[256,2048]{1,0:T(8,128)(2,1)S(1)} %copy-done.20, bf16[256,2048]{1,0:T(8,128)(2,1)S(1)} %copy-done.18, bf16[256,2048]{1,0:T(8,128)(2,1)S(1)} %get-tuple-element.195), kind=kOutput, calls=%fused_computation.7 | convolution fusion | flops 5925240832 | bytes 12845056 | tf_op jit(solution)/shard_map/dot_general | solution.py:34
  264.8 3.8 pad_maximum_fusion.1
  268.6 24.8 %all-gather.11.cloned.1.call-done = bf16[1408,2048]{1,0:T(8,128)(2,1)} async-done(((bf16[1408,256]{1,0:T(8,128)(2,1)}), bf16[1408,2048]{1,0:T(8,128)(2,1)}) %all-gather.11.cloned.1.call-update) | async-done | bytes 5767184 | tf_op jit(solution)/shard_map/all_gather | solution.py:521
  293.4 11.1 %convolution_convert_fusion.2 = bf16[1024,2048]{1,0:T(8,128)(2,1)} fusion(bf16[1024,1408]{1,0:T(8,128)(2,1)} %copy-done.21, bf16[1408,2048]{1,0:T(8,128)(2,1)} %all-gather.11.cloned.1.call-done), kind=kOutput, calls=%fused_computation.17 | convolution fusion | flops 5907677184 | bytes 12845056 | tf_op jit(solution)/shard_map/dot_general | solution.py:529
  304.5 12.6 %multiply_convert_fusion.1 = (bf16[1024,1408]{1,0:T(8,128)(2,1)}, bf16[1024,1408]{1,0:T(8,128)(2,1)}) fusion(f32[1024,2816]{1,0:T(8,128)} %copy-done.9, bf16[1024,2048]{1,0:T(8,128)(2,1)S(1)} %copy-done.16, bf16[1408,2048]{1,0:T(8,128)(2,1)S(1)} %copy-done.53), kind=kOutput, calls=%fused_computation.9 | convolution fusion | flops 5924323328 | bytes 27262976 | tf_op jit(solution)/shard_map/dot_general | solution.py:30
  317.1 12.0 %product.6 = bf16[2048,1408]{1,0:T(8,128)(2,1)} custom-call(bf16[1024,2048]{1,0:T(8,128)(2,1)} %constant_dynamic-update-slice_fusion.a_ref, bf16[1024,1408]{1,0:T(8,128)(2,1)} %get-tuple-element.170.b_ref), custom_call_target="tpu_custom_call" | custom-call | flops 11811160064 | bytes 1048576 | tf_op jit(solution)/shard_map/product/pallas_call | solution.py:422
  336.6 21.2 %collective-permute-done.11 = bf16[256,2048]{1,0:T(8,128)(2,1)} collective-permute-done((bf16[256,2048]{1,0:T(8,128)(2,1)}, bf16[256,2048]{1,0:T(8,128)(2,1)}, u32[]{:S(2)}, u32[]{:S(2)}) %collective-permute-start.11) | collective-permute-done | bytes 1048608 | tf_op jit(solution)/shard_map/ppermute | solution.py:563
  364.2 15.6 %convolution_convert_fusion.1 = bf16[1024,2048]{1,0:T(8,128)(2,1)S(1)} fusion(bf16[1024,2816]{1,0:T(8,128)(2,1)S(1)} %pad_maximum_fusion, bf16[2048,2816]{1,0:T(8,128)(2,1)} %all-gather.9.cloned.1.call-done), kind=kOutput, calls=%fused_computation.16 | convolution fusion | flops 11813257216 | bytes 21495808 | tf_op jit(solution)/shard_map/dot_general | solution.py:30
  385.7 12.0 %product.7 = bf16[2048,1408]{1,0:T(8,128)(2,1)} custom-call(bf16[1024,2048]{1,0:T(8,128)(2,1)} %constant_dynamic-update-slice_fusion.a_ref, bf16[1024,1408]{1,0:T(8,128)(2,1)} %get-tuple-element.169.b_ref), custom_call_target="tpu_custom_call" | custom-call | flops 11811160064 | bytes 1048576 | tf_op jit(solution)/shard_map/product/pallas_call | solution.py:422
  397.7 8.6 %collective-permute-done.15 = bf16[256,2048]{1,0:T(8,128)(2,1)} collective-permute-done((bf16[256,2048]{1,0:T(8,128)(2,1)}, bf16[256,2048]{1,0:T(8,128)(2,1)}, u32[]{:S(2)}, u32[]{:S(2)}) %collective-permute-start.15) | collective-permute-done | bytes 1048608 | tf_op jit(solution)/shard_map/ppermute | solution.py:563
  411.4 3.8 convert_add_fusion.5
  415.2 5.7 collective-permute-done.16
  425.6 2.3 multiply_reduce_fusion.1
  430.4 21.6 %collective-permute-done.18.refs_2_ = bf16[256,2048]{1,0:T(8,128)(2,1)S(1)} collective-permute-done((bf16[256,2048]{1,0:T(8,128)(2,1)S(1)}, bf16[256,2048]{1,0:T(8,128)(2,1)S(1)}, u32[]{:S(2)}, u32[]{:S(2)}) %collective-permute-start.18) | collective-permute-done | bytes 1048608 | tf_op jit(solution)/shard_map/ppermute | solution.py:563
  455.4 7.0 %collective-permute-done.20.refs_3_ = bf16[128,2048]{1,0:T(8,128)(2,1)S(1)} collective-permute-done((bf16[128,2048]{1,0:T(8,128)(2,1)S(1)}, bf16[128,2048]{1,0:T(8,128)(2,1)S(1)}, u32[]{:S(2)}, u32[]{:S(2)}) %collective-permute-start.20) | collective-permute-done | bytes 524320 | tf_op jit(solution)/shard_map/ppermute | solution.py:563
  467.1 8.1 %blocks_product.1.grad_ref = f32[2048,256]{1,0:T(8,128)} custom-call(bf16[256,2048]{1,0:T(8,128)(2,1)} %all-gather.7.cloned.1.call-done.b_ref, bf16[256,2048]{1,0:T(8,128)(2,1)} %copy-done.31, bf16[256,2048]{1,0:T(8,128)(2,1)} %copy-done.44, bf16[256,2048]{1,0:T(8,128)(2,1)} %copy-done.43, bf16[128,2048]{1,0:T(8,128)(2,1)} %copy-done.56, ...), custom_call_target="tpu_custom_call" | custom-call | flops 4294967296 | bytes 1048576 | tf_op jit(solution)/shard_map/blocks_product/pallas_call | solution.py:500
  475.2 22.9 %mixer_backward.1 = (bf16[2048,1024]{1,0:T(8,128)(2,1)}, f32[8,256]{1,0:T(8,128)}) custom-call(s32[8]{0:T(128)} %iota_xor_fusion.order_ref, s32[1]{0:T(128)S(6)} %copy.49.split_ref, f32[2048,1024]{1,0:T(8,128)} %fusion.pre_ref, f32[2048,256]{1,0:T(8,128)} %get-tuple-element.102.mixed_ref, f32[2048,256]{1,0:T(8,128)} %blocks_product.1.grad_ref, ...), custom_call_target="tpu_custom_call" | custom-call | flops 23068672000 | bytes 1048576 | tf_op jit(solution)/shard_map/mixer_backward/pallas_call | solution.py:365
  498.1 10.5 %product.4 = bf16[1024,2048]{1,0:T(8,128)(2,1)} custom-call(bf16[2048,1024]{1,0:T(8,128)(2,1)} %get-tuple-element.121.a_ref.b_ref, bf16[2048,1024]{1,0:T(8,128)(2,1)} %all-gather.5.cloned.1.call-done.b_ref.weight_ref), custom_call_target="tpu_custom_call" | custom-call | flops 8589934592 | bytes 1048576 | tf_op jit(solution)/shard_map/product/pallas_call | solution.py:422
  511.8 4.4 collective-permute-done.29.add_ref
  516.1 11.1 %product.5 = bf16[1024,2048]{1,0:T(8,128)(2,1)} custom-call(bf16[2048,1024]{1,0:T(8,128)(2,1)} %get-tuple-element.121.a_ref.b_ref, bf16[2048,1024]{1,0:T(8,128)(2,1)} %all-gather.5.cloned.1.call-done.b_ref.weight_ref, bf16[1024,2048]{1,0:T(8,128)(2,1)} %collective-permute-done.29.add_ref), custom_call_target="tpu_custom_call" | custom-call | flops 8589934592 | bytes 1048576 | tf_op jit(solution)/shard_map/product/pallas_call | solution.py:422
  528.0 18.5 %weight_sum_product.1 = (bf16[2048,1280]{1,0:T(8,128)(2,1)}, f32[2048,128]{1,0:T(8,128)}) custom-call(bf16[1024,2048]{1,0:T(8,128)(2,1)} %multiply_convert_fusion.own_ref, bf16[1024,2048]{1,0:T(8,128)(2,1)} %collective-permute-done.other_ref, bf16[2048,1024]{1,0:T(8,128)(2,1)} %get-tuple-element.121.a_ref.b_ref, ...), custom_call_target="tpu_custom_call" | custom-call | flops 21474836480 | bytes 1048576 | tf_op jit(solution)/shard_map/weight_sum_product/pallas_call | solution.py:460
  551.9 2.5 broadcast_in_dim.18
  556.5 2.3 constant_dynamic-update-slice_fusion.7
  558.8 15.9 %collective-permute-done.33 = bf16[256,2048]{1,0:T(8,128)(2,1)S(1)} collective-permute-done((bf16[256,2048]{1,0:T(8,128)(2,1)S(1)}, bf16[256,2048]{1,0:T(8,128)(2,1)S(1)}, u32[]{:S(2)}, u32[]{:S(2)}) %collective-permute-start.33) | collective-permute-done | bytes 1048608 | tf_op jit(solution)/shard_map/ppermute | solution.py:563
  584.6 2.8 collective-permute-start.50
  587.4 2.6 add_convert_fusion.2
  595.0 9.7 %collective-permute-done.34 = bf16[128,2048]{1,0:T(8,128)(2,1)} collective-permute-done((bf16[128,2048]{1,0:T(8,128)(2,1)}, bf16[128,2048]{1,0:T(8,128)(2,1)}, u32[]{:S(2)}, u32[]{:S(2)}) %collective-permute-start.34) | collective-permute-done | bytes 524320 | tf_op jit(solution)/shard_map/ppermute | solution.py:563
  611.2 4.5 broadcast_in_dim.24
  615.7 4.0 convert_dynamic-update-slice_fusion.2
  631.8 12.3 %collective-permute-done.37 = bf16[256,2048]{1,0:T(8,128)(2,1)S(1)} collective-permute-done((bf16[256,2048]{1,0:T(8,128)(2,1)S(1)}, bf16[256,2048]{1,0:T(8,128)(2,1)S(1)}, u32[]{:S(2)}, u32[]{:S(2)}) %collective-permute-start.37) | collective-permute-done | bytes 1048608 | tf_op jit(solution)/shard_map/ppermute | solution.py:563
  650.1 6.7 collective-permute-done.38
  (324 shorter events, 145.9 us)
Async XLA Ops:
  7.2 87.1 %all-gather.5.cloned.1.call-start = ((), (), s32[]{:S(2)}) async-start(), calls=%async_computation.4 | async-start | bytes 5242880 | tf_op jit(solution)/shard_map/all_gather | solution.py:521
  10.7 123.2 %all-gather.7.cloned.1.call-start = ((), (), s32[]{:S(2)}) async-start(), calls=%async_computation.5 | async-start | bytes 1310720 | tf_op jit(solution)/shard_map/all_gather | solution.py:521
  12.4 220.3 %all-gather.9.cloned.1.call-start = ((), (), s32[]{:S(2)}) async-start(), calls=%async_computation.6 | async-start | bytes 12976128 | tf_op jit(solution)/shard_map/all_gather | solution.py:521
  14.8 278.5 %all-gather.11.cloned.1.call-start = ((), (), s32[]{:S(2)}) async-start(), calls=%async_computation.7 | async-start | bytes 6488064 | tf_op jit(solution)/shard_map/all_gather | solution.py:521
  27.0 7.6 %collective-permute-start = (bf16[1024,2048]{1,0:T(8,128)(2,1)}, bf16[1024,2048]{1,0:T(8,128)(2,1)}, u32[]{:S(2)}, u32[]{:S(2)}) collective-permute-start(bf16[1024,2048]{1,0:T(8,128)(2,1)} %multiply_convert_fusion.own_ref), channel_id=1, source_target_pairs={{0,4},{4,0},{1,5},{5,1},{2,6},{6,2},{3,7},{7,3},{8,12},{12,8},{9,1... | collective-permute-start | bytes 12582920 | tf_op jit(solution)/shard_map/ppermute | solution.py:553
  146.0 25.3 %collective-permute-start.3 = (bf16[256,2048]{1,0:T(8,128)(2,1)S(1)}, bf16[256,2048]{1,0:T(8,128)(2,1)S(1)}, u32[]{:S(2)}, u32[]{:S(2)}) collective-permute-start(bf16[256,2048]{1,0:T(8,128)(2,1)S(1)} %pad_maximum_fusion.5), channel_id=1, source_target_pairs={{0,2},{1,3},{2,0},{3,1},{4,6},{5,7},{6,4},{7,5},{8,10},{9,11},{10,... | collective-permute-start | bytes 3145736 | tf_op jit(solution)/shard_map/ppermute | solution.py:563
  147.4 25.0 %collective-permute-start.2 = (bf16[256,2048]{1,0:T(8,128)(2,1)S(1)}, bf16[256,2048]{1,0:T(8,128)(2,1)S(1)}, u32[]{:S(2)}, u32[]{:S(2)}) collective-permute-start(bf16[256,2048]{1,0:T(8,128)(2,1)S(1)} %pad_maximum_fusion.4), channel_id=1, source_target_pairs={{0,1},{1,0},{2,3},{3,2},{4,5},{5,4},{6,7},{7,6},{8,9},{9,8},{10,11... | collective-permute-start | bytes 3145736 | tf_op jit(solution)/shard_map/ppermute | solution.py:563
  173.8 13.2 %collective-permute-start.4 = (bf16[128,2048]{1,0:T(8,128)(2,1)}, bf16[128,2048]{1,0:T(8,128)(2,1)}, u32[]{:S(2)}, u32[]{:S(2)}) collective-permute-start(bf16[128,2048]{1,0:T(8,128)(2,1)} %get-tuple-element.75), channel_id=1, source_target_pairs={{0,2},{1,3},{2,0},{3,1},{4,6},{5,7},{6,4},{7,5},{8,10},{9,11},{10,... | collective-permute-start | bytes 1572872 | tf_op jit(solution)/shard_map/ppermute | solution.py:563
  174.6 13.0 %collective-permute-start.5 = (bf16[128,2048]{1,0:T(8,128)(2,1)}, bf16[128,2048]{1,0:T(8,128)(2,1)}, u32[]{:S(2)}, u32[]{:S(2)}) collective-permute-start(bf16[128,2048]{1,0:T(8,128)(2,1)} %get-tuple-element.76), channel_id=1, source_target_pairs={{0,1},{1,0},{2,3},{3,2},{4,5},{5,4},{6,7},{7,6},{8,9},{9,8},{10,11... | collective-permute-start | bytes 1572872 | tf_op jit(solution)/shard_map/ppermute | solution.py:563
  176.8 248.8 %reduce-scatter.5.cloned.1.call-start = ((), (), s32[]{:S(2)}) async-start(), calls=%async_computation.8 | async-start | bytes 6488064 | tf_op jit(solution)/shard_map/reduce_scatter | solution.py:525
  191.6 23.0 %collective-permute-start.7 = (bf16[256,2048]{1,0:T(8,128)(2,1)S(1)}, bf16[256,2048]{1,0:T(8,128)(2,1)S(1)}, u32[]{:S(2)}, u32[]{:S(2)}) collective-permute-start(bf16[256,2048]{1,0:T(8,128)(2,1)S(1)} %get-tuple-element.166), channel_id=1, source_target_pairs={{0,2},{1,3},{2,0},{3,1},{4,6},{5,7},{6,4},{7,5},{8,10},{9,11},{10,... | collective-permute-start | bytes 3145736 | tf_op jit(solution)/shard_map/ppermute | solution.py:563
  192.8 23.1 %collective-permute-start.6 = (bf16[256,2048]{1,0:T(8,128)(2,1)S(1)}, bf16[256,2048]{1,0:T(8,128)(2,1)S(1)}, u32[]{:S(2)}, u32[]{:S(2)}) collective-permute-start(bf16[256,2048]{1,0:T(8,128)(2,1)S(1)} %get-tuple-element.166), channel_id=1, source_target_pairs={{0,1},{1,0},{2,3},{3,2},{4,5},{5,4},{6,7},{7,6},{8,9},{9,8},{10,11... | collective-permute-start | bytes 3145736 | tf_op jit(solution)/shard_map/ppermute | solution.py:563
  216.0 10.8 %collective-permute-start.8 = (bf16[128,2048]{1,0:T(8,128)(2,1)S(1)}, bf16[128,2048]{1,0:T(8,128)(2,1)S(1)}, u32[]{:S(2)}, u32[]{:S(2)}) collective-permute-start(bf16[128,2048]{1,0:T(8,128)(2,1)S(1)} %slice.338), channel_id=1, source_target_pairs={{0,1},{1,0},{2,3},{3,2},{4,5},{5,4},{6,7},{7,6},{8,9},{9,8},{10,11... | collective-permute-start | bytes 1572872 | tf_op jit(solution)/shard_map/ppermute | solution.py:563
  219.3 10.0 %collective-permute-start.9 = (bf16[128,2048]{1,0:T(8,128)(2,1)S(1)}, bf16[128,2048]{1,0:T(8,128)(2,1)S(1)}, u32[]{:S(2)}, u32[]{:S(2)}) collective-permute-start(bf16[128,2048]{1,0:T(8,128)(2,1)S(1)} %slice.339), channel_id=1, source_target_pairs={{0,2},{1,3},{2,0},{3,1},{4,6},{5,7},{6,4},{7,5},{8,10},{9,11},{10,... | collective-permute-start | bytes 1572872 | tf_op jit(solution)/shard_map/ppermute | solution.py:563
  264.7 263.3 %reduce-scatter.7.cloned.1.call-start = ((), (), s32[]{:S(2)}) async-start(), calls=%async_computation.9 | async-start | bytes 6488064 | tf_op jit(solution)/shard_map/reduce_scatter | solution.py:525
  329.2 198.8 %reduce-scatter.9.cloned.1.call-start = ((), (), s32[]{:S(2)}) async-start(), calls=%async_computation.10 | async-start | bytes 6488064 | tf_op jit(solution)/shard_map/reduce_scatter | solution.py:525
  332.2 25.6 %collective-permute-start.11 = (bf16[256,2048]{1,0:T(8,128)(2,1)}, bf16[256,2048]{1,0:T(8,128)(2,1)}, u32[]{:S(2)}, u32[]{:S(2)}) collective-permute-start(bf16[256,2048]{1,0:T(8,128)(2,1)} %pad_maximum_fusion.7), channel_id=1, source_target_pairs={{0,2},{1,3},{2,0},{3,1},{4,6},{5,7},{6,4},{7,5},{8,10},{9,11},{10,... | collective-permute-start | bytes 3145736 | tf_op jit(solution)/shard_map/ppermute | solution.py:563
  334.7 25.2 %collective-permute-start.10 = (bf16[256,2048]{1,0:T(8,128)(2,1)}, bf16[256,2048]{1,0:T(8,128)(2,1)S(1)}, u32[]{:S(2)}, u32[]{:S(2)}) collective-permute-start(bf16[256,2048]{1,0:T(8,128)(2,1)} %pad_maximum_fusion.6), channel_id=1, source_target_pairs={{0,1},{1,0},{2,3},{3,2},{4,5},{5,4},{6,7},{7,6},{8,9},{9,8},{10,11... | collective-permute-start | bytes 3145736 | tf_op jit(solution)/shard_map/ppermute | solution.py:563
  362.1 17.7 %collective-permute-start.12 = (bf16[128,2048]{1,0:T(8,128)(2,1)S(1)}, bf16[128,2048]{1,0:T(8,128)(2,1)S(1)}, u32[]{:S(2)}, u32[]{:S(2)}) collective-permute-start(bf16[128,2048]{1,0:T(8,128)(2,1)S(1)} %get-tuple-element.86), channel_id=1, source_target_pairs={{0,2},{1,3},{2,0},{3,1},{4,6},{5,7},{6,4},{7,5},{8,10},{9,11},{10,... | collective-permute-start | bytes 1572872 | tf_op jit(solution)/shard_map/ppermute | solution.py:563
  362.7 18.0 %collective-permute-start.13 = (bf16[128,2048]{1,0:T(8,128)(2,1)S(1)}, bf16[128,2048]{1,0:T(8,128)(2,1)}, u32[]{:S(2)}, u32[]{:S(2)}) collective-permute-start(bf16[128,2048]{1,0:T(8,128)(2,1)S(1)} %get-tuple-element.87), channel_id=1, source_target_pairs={{0,1},{1,0},{2,3},{3,2},{4,5},{5,4},{6,7},{7,6},{8,9},{9,8},{10,11... | collective-permute-start | bytes 1572872 | tf_op jit(solution)/shard_map/ppermute | solution.py:563
  382.3 24.0 %collective-permute-start.15 = (bf16[256,2048]{1,0:T(8,128)(2,1)}, bf16[256,2048]{1,0:T(8,128)(2,1)}, u32[]{:S(2)}, u32[]{:S(2)}) collective-permute-start(bf16[256,2048]{1,0:T(8,128)(2,1)} %pad_maximum_fusion.9), channel_id=1, source_target_pairs={{0,2},{1,3},{2,0},{3,1},{4,6},{5,7},{6,4},{7,5},{8,10},{9,11},{10,... | collective-permute-start | bytes 3145736 | tf_op jit(solution)/shard_map/ppermute | solution.py:563
  385.1 23.1 %collective-permute-start.14 = (bf16[256,2048]{1,0:T(8,128)(2,1)}, bf16[256,2048]{1,0:T(8,128)(2,1)}, u32[]{:S(2)}, u32[]{:S(2)}) collective-permute-start(bf16[256,2048]{1,0:T(8,128)(2,1)} %pad_maximum_fusion.8), channel_id=1, source_target_pairs={{0,1},{1,0},{2,3},{3,2},{4,5},{5,4},{6,7},{7,6},{8,9},{9,8},{10,11... | collective-permute-start | bytes 3145736 | tf_op jit(solution)/shard_map/ppermute | solution.py:563
  397.7 250.9 %reduce-scatter.11.cloned.1.call-start = ((), (), s32[]{:S(2)}) async-start(), calls=%async_computation.11 | async-start | bytes 6553600 | tf_op jit(solution)/shard_map/reduce_scatter | solution.py:525
  410.2 10.7 %collective-permute-start.16 = (bf16[128,2048]{1,0:T(8,128)(2,1)S(1)}, bf16[128,2048]{1,0:T(8,128)(2,1)S(1)}, u32[]{:S(2)}, u32[]{:S(2)}) collective-permute-start(bf16[128,2048]{1,0:T(8,128)(2,1)S(1)} %get-tuple-element.94), channel_id=1, source_target_pairs={{0,2},{1,3},{2,0},{3,1},{4,6},{5,7},{6,4},{7,5},{8,10},{9,11},{10,... | collective-permute-start | bytes 1572872 | tf_op jit(solution)/shard_map/ppermute | solution.py:563
  411.2 10.9 %collective-permute-start.17 = (bf16[128,2048]{1,0:T(8,128)(2,1)S(1)}, bf16[128,2048]{1,0:T(8,128)(2,1)S(1)}, u32[]{:S(2)}, u32[]{:S(2)}) collective-permute-start(bf16[128,2048]{1,0:T(8,128)(2,1)S(1)} %get-tuple-element.95), channel_id=1, source_target_pairs={{0,1},{1,0},{2,3},{3,2},{4,5},{5,4},{6,7},{7,6},{8,9},{9,8},{10,11... | collective-permute-start | bytes 1572872 | tf_op jit(solution)/shard_map/ppermute | solution.py:563
  429.2 22.9 %collective-permute-start.18 = (bf16[256,2048]{1,0:T(8,128)(2,1)S(1)}, bf16[256,2048]{1,0:T(8,128)(2,1)S(1)}, u32[]{:S(2)}, u32[]{:S(2)}) collective-permute-start(bf16[256,2048]{1,0:T(8,128)(2,1)S(1)} %get-tuple-element.213.refs_0_), channel_id=1, source_target_pairs={{0,2},{1,3},{2,0},{3,1},{4,6},{5,7},{6,4},{7,5},{8,10},{9,11},{10,... | collective-permute-start | bytes 3145736 | tf_op jit(solution)/shard_map/ppermute | solution.py:563
  429.9 23.1 %collective-permute-start.19 = (bf16[256,2048]{1,0:T(8,128)(2,1)S(1)}, bf16[256,2048]{1,0:T(8,128)(2,1)S(1)}, u32[]{:S(2)}, u32[]{:S(2)}) collective-permute-start(bf16[256,2048]{1,0:T(8,128)(2,1)S(1)} %get-tuple-element.213.refs_0_), channel_id=1, source_target_pairs={{0,1},{1,0},{2,3},{3,2},{4,5},{5,4},{6,7},{7,6},{8,9},{9,8},{10,11... | collective-permute-start | bytes 3145736 | tf_op jit(solution)/shard_map/ppermute | solution.py:563
  430.4 32.4 %collective-permute-start.22 = (bf16[256,2048]{1,0:T(8,128)(2,1)S(1)}, bf16[256,2048]{1,0:T(8,128)(2,1)S(1)}, u32[]{:S(2)}, u32[]{:S(2)}) collective-permute-start(bf16[256,2048]{1,0:T(8,128)(2,1)S(1)} %get-tuple-element.213.refs_0_), channel_id=1, source_target_pairs={{0,4},{4,0},{1,5},{5,1},{2,6},{6,2},{3,7},{7,3},{8,12},{12,8},{9,1... | collective-permute-start | bytes 3145736 | tf_op jit(solution)/shard_map/ppermute | solution.py:553
  453.1 9.2 %collective-permute-start.20 = (bf16[128,2048]{1,0:T(8,128)(2,1)S(1)}, bf16[128,2048]{1,0:T(8,128)(2,1)S(1)}, u32[]{:S(2)}, u32[]{:S(2)}) collective-permute-start(bf16[128,2048]{1,0:T(8,128)(2,1)S(1)} %slice.352), channel_id=1, source_target_pairs={{0,1},{1,0},{2,3},{3,2},{4,5},{5,4},{6,7},{7,6},{8,9},{9,8},{10,11... | collective-permute-start | bytes 1572872 | tf_op jit(solution)/shard_map/ppermute | solution.py:563
  453.2 9.2 %collective-permute-start.21 = (bf16[128,2048]{1,0:T(8,128)(2,1)S(1)}, bf16[128,2048]{1,0:T(8,128)(2,1)S(1)}, u32[]{:S(2)}, u32[]{:S(2)}) collective-permute-start(bf16[128,2048]{1,0:T(8,128)(2,1)S(1)} %slice.353), channel_id=1, source_target_pairs={{0,2},{1,3},{2,0},{3,1},{4,6},{5,7},{6,4},{7,5},{8,10},{9,11},{10,... | collective-permute-start | bytes 1572872 | tf_op jit(solution)/shard_map/ppermute | solution.py:563
  454.8 11.1 %collective-permute-start.23 = (bf16[256,2048]{1,0:T(8,128)(2,1)S(1)}, bf16[256,2048]{1,0:T(8,128)(2,1)S(1)}, u32[]{:S(2)}, u32[]{:S(2)}) collective-permute-start(bf16[256,2048]{1,0:T(8,128)(2,1)S(1)} %collective-permute-done.19.refs_1_), channel_id=1, source_target_pairs={{0,4},{4,0},{1,5},{5,1},{2,6},{6,2},{3,7},{7,3},{8,12},{12,8},{9,1... | collective-permute-start | bytes 3145736 | tf_op jit(solution)/shard_map/ppermute | solution.py:553
  454.8 12.1 %collective-permute-start.24 = (bf16[256,2048]{1,0:T(8,128)(2,1)S(1)}, bf16[256,2048]{1,0:T(8,128)(2,1)}, u32[]{:S(2)}, u32[]{:S(2)}) collective-permute-start(bf16[256,2048]{1,0:T(8,128)(2,1)S(1)} %collective-permute-done.18.refs_2_), channel_id=1, source_target_pairs={{0,4},{4,0},{1,5},{5,1},{2,6},{6,2},{3,7},{7,3},{8,12},{12,8},{9,1... | collective-permute-start | bytes 3145736 | tf_op jit(solution)/shard_map/ppermute | solution.py:553
  462.8 35.3 %collective-permute-start.27 = (bf16[256,2048]{1,0:T(8,128)(2,1)S(1)}, bf16[256,2048]{1,0:T(8,128)(2,1)S(1)}, u32[]{:S(2)}, u32[]{:S(2)}) collective-permute-start(bf16[256,2048]{1,0:T(8,128)(2,1)S(1)} %get-tuple-element.112), channel_id=1, source_target_pairs={{0,1},{1,0},{2,3},{3,2},{4,5},{5,4},{6,7},{7,6},{8,9},{9,8},{10,11... | collective-permute-start | bytes 3145736 | tf_op jit(solution)/shard_map/ppermute | solution.py:563
  464.5 33.7 %collective-permute-start.28 = (bf16[256,2048]{1,0:T(8,128)(2,1)S(1)}, bf16[256,2048]{1,0:T(8,128)(2,1)}, u32[]{:S(2)}, u32[]{:S(2)}) collective-permute-start(bf16[256,2048]{1,0:T(8,128)(2,1)S(1)} %get-tuple-element.112), channel_id=1, source_target_pairs={{0,2},{1,3},{2,0},{3,1},{4,6},{5,7},{6,4},{7,5},{8,10},{9,11},{10,... | collective-permute-start | bytes 3145736 | tf_op jit(solution)/shard_map/ppermute | solution.py:563
  509.8 17.4 %collective-permute-start.30 = (bf16[128,2048]{1,0:T(8,128)(2,1)S(1)}, bf16[128,2048]{1,0:T(8,128)(2,1)S(1)}, u32[]{:S(2)}, u32[]{:S(2)}) collective-permute-start(bf16[128,2048]{1,0:T(8,128)(2,1)S(1)} %slice.291), channel_id=1, source_target_pairs={{0,1},{1,0},{2,3},{3,2},{4,5},{5,4},{6,7},{7,6},{8,9},{9,8},{10,11... | collective-permute-start | bytes 1572872 | tf_op jit(solution)/shard_map/ppermute | solution.py:563
  510.3 17.7 %collective-permute-start.31 = (bf16[128,2048]{1,0:T(8,128)(2,1)S(1)}, bf16[128,2048]{1,0:T(8,128)(2,1)}, u32[]{:S(2)}, u32[]{:S(2)}) collective-permute-start(bf16[128,2048]{1,0:T(8,128)(2,1)S(1)} %slice.292), channel_id=1, source_target_pairs={{0,2},{1,3},{2,0},{3,1},{4,6},{5,7},{6,4},{7,5},{8,10},{9,11},{10,... | collective-permute-start | bytes 1572872 | tf_op jit(solution)/shard_map/ppermute | solution.py:563
  549.4 25.3 %collective-permute-start.33 = (bf16[256,2048]{1,0:T(8,128)(2,1)S(1)}, bf16[256,2048]{1,0:T(8,128)(2,1)S(1)}, u32[]{:S(2)}, u32[]{:S(2)}) collective-permute-start(bf16[256,2048]{1,0:T(8,128)(2,1)S(1)} %pad_maximum_fusion.11), channel_id=1, source_target_pairs={{0,2},{1,3},{2,0},{3,1},{4,6},{5,7},{6,4},{7,5},{8,10},{9,11},{10,... | collective-permute-start | bytes 3145736 | tf_op jit(solution)/shard_map/ppermute | solution.py:563
  550.3 25.0 %collective-permute-start.32 = (bf16[256,2048]{1,0:T(8,128)(2,1)S(1)}, bf16[256,2048]{1,0:T(8,128)(2,1)S(1)}, u32[]{:S(2)}, u32[]{:S(2)}) collective-permute-start(bf16[256,2048]{1,0:T(8,128)(2,1)S(1)} %pad_maximum_fusion.10), channel_id=1, source_target_pairs={{0,1},{1,0},{2,3},{3,2},{4,5},{5,4},{6,7},{7,6},{8,9},{9,8},{10,11... | collective-permute-start | bytes 3145736 | tf_op jit(solution)/shard_map/ppermute | solution.py:563
  581.8 40.1 %collective-permute-start.43 = (bf16[1408,256]{1,0:T(8,128)(2,1)}, bf16[1408,256]{1,0:T(8,128)(2,1)}, u32[]{:S(2)}, u32[]{:S(2)}) collective-permute-start(bf16[1408,256]{1,0:T(8,128)(2,1)} %reduce-scatter.5.cloned.1.call-done), channel_id=1, source_target_pairs={{0,4},{4,0},{1,5},{5,1},{2,6},{6,2},{3,7},{7,3},{8,12},{12,8},{9,1... | collective-permute-start | bytes 2162696 | tf_op jit(solution)/shard_map/ppermute | solution.py:553
  581.8 41.5 %collective-permute-start.42 = (bf16[256,1408]{1,0:T(8,128)(2,1)}, bf16[256,1408]{1,0:T(8,128)(2,1)}, u32[]{:S(2)}, u32[]{:S(2)}) collective-permute-start(bf16[256,1408]{1,0:T(8,128)(2,1)} %reduce-scatter.9.cloned.1.call-done.refs_11_), channel_id=1, source_target_pairs={{0,4},{4,0},{1,5},{5,1},{2,6},{6,2},{3,7},{7,3},{8,12},{12,8},{9,1... | collective-permute-start | bytes 2162696 | tf_op jit(solution)/shard_map/ppermute | solution.py:553
  589.9 38.6 %collective-permute-start.41 = (bf16[256,1408]{1,0:T(8,128)(2,1)}, bf16[256,1408]{1,0:T(8,128)(2,1)}, u32[]{:S(2)}, u32[]{:S(2)}) collective-permute-start(bf16[256,1408]{1,0:T(8,128)(2,1)} %reduce-scatter.7.cloned.1.call-done.refs_10_), channel_id=1, source_target_pairs={{0,4},{4,0},{1,5},{5,1},{2,6},{6,2},{3,7},{7,3},{8,12},{12,8},{9,1... | collective-permute-start | bytes 2162696 | tf_op jit(solution)/shard_map/ppermute | solution.py:553
  590.0 14.6 %collective-permute-start.34 = (bf16[128,2048]{1,0:T(8,128)(2,1)}, bf16[128,2048]{1,0:T(8,128)(2,1)}, u32[]{:S(2)}, u32[]{:S(2)}) collective-permute-start(bf16[128,2048]{1,0:T(8,128)(2,1)} %get-tuple-element.115), channel_id=1, source_target_pairs={{0,2},{1,3},{2,0},{3,1},{4,6},{5,7},{6,4},{7,5},{8,10},{9,11},{10,... | collective-permute-start | bytes 1572872 | tf_op jit(solution)/shard_map/ppermute | solution.py:563
  592.7 14.2 %collective-permute-start.35 = (bf16[128,2048]{1,0:T(8,128)(2,1)}, bf16[128,2048]{1,0:T(8,128)(2,1)S(1)}, u32[]{:S(2)}, u32[]{:S(2)}) collective-permute-start(bf16[128,2048]{1,0:T(8,128)(2,1)} %get-tuple-element.116), channel_id=1, source_target_pairs={{0,1},{1,0},{2,3},{3,2},{4,5},{5,4},{6,7},{7,6},{8,9},{9,8},{10,11... | collective-permute-start | bytes 1572872 | tf_op jit(solution)/shard_map/ppermute | solution.py:563
  619.6 24.5 %collective-permute-start.37 = (bf16[256,2048]{1,0:T(8,128)(2,1)S(1)}, bf16[256,2048]{1,0:T(8,128)(2,1)S(1)}, u32[]{:S(2)}, u32[]{:S(2)}) collective-permute-start(bf16[256,2048]{1,0:T(8,128)(2,1)S(1)} %get-tuple-element.164), channel_id=1, source_target_pairs={{0,2},{1,3},{2,0},{3,1},{4,6},{5,7},{6,4},{7,5},{8,10},{9,11},{10,... | collective-permute-start | bytes 3145736 | tf_op jit(solution)/shard_map/ppermute | solution.py:563
  620.5 24.2 %collective-permute-start.36 = (bf16[256,2048]{1,0:T(8,128)(2,1)S(1)}, bf16[256,2048]{1,0:T(8,128)(2,1)S(1)}, u32[]{:S(2)}, u32[]{:S(2)}) collective-permute-start(bf16[256,2048]{1,0:T(8,128)(2,1)S(1)} %get-tuple-element.164), channel_id=1, source_target_pairs={{0,1},{1,0},{2,3},{3,2},{4,5},{5,4},{6,7},{7,6},{8,9},{9,8},{10,11... | collective-permute-start | bytes 3145736 | tf_op jit(solution)/shard_map/ppermute | solution.py:563
  644.7 12.1 %collective-permute-start.38 = (bf16[128,2048]{1,0:T(8,128)(2,1)S(1)}, bf16[128,2048]{1,0:T(8,128)(2,1)S(1)}, u32[]{:S(2)}, u32[]{:S(2)}) collective-permute-start(bf16[128,2048]{1,0:T(8,128)(2,1)S(1)} %slice.356), channel_id=1, source_target_pairs={{0,1},{1,0},{2,3},{3,2},{4,5},{5,4},{6,7},{7,6},{8,9},{9,8},{10,11... | collective-permute-start | bytes 1572872 | tf_op jit(solution)/shard_map/ppermute | solution.py:563
  646.2 11.8 %collective-permute-start.39 = (bf16[128,2048]{1,0:T(8,128)(2,1)S(1)}, bf16[128,2048]{1,0:T(8,128)(2,1)S(1)}, u32[]{:S(2)}, u32[]{:S(2)}) collective-permute-start(bf16[128,2048]{1,0:T(8,128)(2,1)S(1)} %slice.357), channel_id=1, source_target_pairs={{0,2},{1,3},{2,0},{3,1},{4,6},{5,7},{6,4},{7,5},{8,10},{9,11},{10,... | collective-permute-start | bytes 1572872 | tf_op jit(solution)/shard_map/ppermute | solution.py:563
  648.6 10.6 %collective-permute-start.40 = (bf16[512,1280]{1,0:T(8,128)(2,1)}, bf16[512,1280]{1,0:T(8,128)(2,1)S(1)}, u32[]{:S(2)}, u32[]{:S(2)}) collective-permute-start(bf16[512,1280]{1,0:T(8,128)(2,1)} %reduce-scatter.11.cloned.1.call-done), channel_id=1, source_target_pairs={{0,4},{4,0},{1,5},{5,1},{2,6},{6,2},{3,7},{7,3},{8,12},{12,8},{9,1... | collective-permute-start | bytes 3932168 | tf_op jit(solution)/shard_map/ppermute | solution.py:553
  (72 other events, 804.4 us)
Sparse Core Ops, SparseCore 0:
  10.8 83.4 all-gather.4
  96.5 26.4 all-gather.6
  125.2 107.5 all-gather.8
  234.2 59.1 all-gather.10
  295.5 63.0 reduce-scatter.4
  360.8 63.1 reduce-scatter.6
  426.3 63.2 reduce-scatter.8
  546.7 92.2 reduce-scatter.10

commit v3 on v2

--- a/solution.py
+++ b/solution.py
@@ -377,16 +377,15 @@
     )(order, split, pre, mixed, grad, states, bias[None], bound[None], gain[None])
 
 
-def product_kernel(dims, a_ref, b_ref, *refs):
-    out_ref = refs[-1]
+def blocks_of(array, count):
+    size = array.shape[0] // count
+    return [array[m * size : (m + 1) * size] for m in range(count)]
+
+
+def product_kernel(dims, parts, a_ref, b_ref, *refs):
     dot = lax.dot_general(a_ref[...], b_ref[...], (dims, ((), ())), preferred_element_type=F32)
-    out_ref[...] = dot.astype(out_ref.dtype)
-
-
-def product_add_kernel(dims, a_ref, b_ref, add_ref, *refs):
-    out_ref = refs[-1]
-    dot = lax.dot_general(a_ref[...], b_ref[...], (dims, ((), ())), preferred_element_type=F32)
-    out_ref[...] = (dot + add_ref[...].astype(F32)).astype(out_ref.dtype)
+    for block, out_ref in zip(blocks_of(dot, parts), refs[len(refs) - parts :]):
+        out_ref[...] = block.astype(out_ref.dtype)
 
 
 NN = ((1,), (0,))
@@ -394,7 +393,7 @@
 TN = ((0,), (0,))
 
 
-def product(a, b, dims, kind, rows=None, cols=None, a_half=None, add=None, wait=()):
+def product(a, b, dims, kind, rows=None, cols=None, a_half=None, parts=1, wait=()):
     count = a.shape[1 - dims[0][0]] if a_half is None else a.shape[0] // 2
     depth = a.shape[dims[0][0]]
     wide = b.shape[1 - dims[1][0]]
@@ -417,20 +416,20 @@
         b_spec = pl.BlockSpec((depth, tile_cols), lambda i: (0, at_col(i)))
     else:
         b_spec = pl.BlockSpec((tile_cols, depth), lambda i: (at_col(i), 0))
-    out_spec = pl.BlockSpec((tile_rows, tile_cols), lambda i: (at_row(i) - shift, at_col(i)))
-    kernel = product_kernel if add is None else product_add_kernel
-    return pl.pallas_call(
-        functools.partial(kernel, dims),
+    out_spec = pl.BlockSpec((tile_rows // parts, tile_cols), lambda i: (at_row(i) - shift, at_col(i)))
+    out = pl.pallas_call(
+        functools.partial(product_kernel, dims, parts),
         grid=(count // tile_rows * (wide // tile_cols),),
-        in_specs=[a_spec, b_spec] + ([] if add is None else [out_spec]) + [UNREAD] * len(wait),
-        out_specs=out_spec,
-        out_shape=jax.ShapeDtypeStruct((count, wide), kind),
+        in_specs=[a_spec, b_spec] + [UNREAD] * len(wait),
+        out_specs=[out_spec] * parts,
+        out_shape=[jax.ShapeDtypeStruct((count // parts, wide), kind)] * parts,
         compiler_params=pltpu.CompilerParams(
             dimension_semantics=("arbitrary",), vmem_limit_bytes=VMEM
         ),
         cost_estimate=cost(2 * count * wide * depth),
         name="product",
-    )(a, b, *([] if add is None else [add]), *wait)
+    )(a, b, *wait)
+    return out[0] if parts == 1 else out
 
 
 def weight_sum_kernel(own_ref, other_ref, b_ref, weight_ref, right_ref, *refs):
@@ -506,6 +505,39 @@
     )(b, *blocks)
 
 
+def joined_columns_kernel(width, at_ref, own_ref, other_ref, *out_refs):
+    def store(ref):
+        for which in range(4):
+            out_refs[which][...] = ref[:, which * width : (which + 1) * width].astype(F32)
+        out_refs[4][...] = ref[:, 4 * width :].astype(F32).T
+
+    mine = pl.program_id(0) == at_ref[0]
+    pl.when(mine)(lambda: store(own_ref))
+    pl.when(jnp.logical_not(mine))(lambda: store(other_ref))
+
+
+def joined_columns(own, other, at, width):
+    rows = own.shape[0]
+    whole = pl.BlockSpec(own.shape, lambda i, at: (0, 0))
+    beside = pl.BlockSpec((rows, width), lambda i, at: (0, i))
+    return pl.pallas_call(
+        functools.partial(joined_columns_kernel, width),
+        grid_spec=pltpu.PrefetchScalarGridSpec(
+            num_scalar_prefetch=1,
+            grid=(2,),
+            in_specs=[whole, whole],
+            out_specs=[beside] * 4 + [pl.BlockSpec((width, rows), lambda i, at: (i, 0))],
+        ),
+        out_shape=[jax.ShapeDtypeStruct((rows, 2 * width), F32)] * 4
+        + [jax.ShapeDtypeStruct((2 * width, rows), F32)],
+        compiler_params=pltpu.CompilerParams(
+            dimension_semantics=("arbitrary",), vmem_limit_bytes=VMEM
+        ),
+        cost_estimate=cost(1 << 20),
+        name="joined_columns",
+    )(at.astype(jnp.int32).reshape(1), own, other)
+
+
 def rms_rows(rows_in):
     return lax.rsqrt(jnp.mean(rows_in * rows_in, axis=-1, keepdims=True) + EPS_NORM)
 
@@ -563,11 +595,6 @@
     return lax.ppermute(part, "tp", [(i, i ^ mask) for i in range(lax.axis_size("tp"))])
 
 
-def blocks_of(array, count):
-    size = array.shape[0] // count
-    return [array[m * size : (m + 1) * size] for m in range(count)]
-
-
 def relative(array, count, at):
     size = array.shape[0] // count
     return jnp.concatenate(
@@ -575,31 +602,30 @@
     )
 
 
-def piece(part, block, which):
-    half = part.shape[0] // 8
-    start = (2 * block + which) * half
-    return part[start : start + half]
-
-
-def sum_first(part):
-    near = partner(jnp.concatenate([piece(part, 1, 0), piece(part, 3, 0)], axis=0), 1)
-    far = partner(jnp.concatenate([piece(part, 2, 1), piece(part, 3, 1)], axis=0), 2)
+def piece(parts, block, which):
+    half = parts[block].shape[0] // 2
+    return parts[block][which * half : (which + 1) * half]
+
+
+def sum_first(parts):
+    near = partner(jnp.concatenate([piece(parts, 1, 0), piece(parts, 3, 0)], axis=0), 1)
+    far = partner(jnp.concatenate([piece(parts, 2, 1), piece(parts, 3, 1)], axis=0), 2)
     return near, far
 
 
-def sum_second(part, near, far):
+def sum_second(parts, near, far):
     half = near.shape[0] // 2
     near, far = together(near, far)
-    pass_far = (piece(part, 2, 0).astype(F32) + near[half:].astype(F32)).astype(BF16)
-    pass_near = (piece(part, 1, 1).astype(F32) + far[half:].astype(F32)).astype(BF16)
+    pass_far = (piece(parts, 2, 0).astype(F32) + near[half:].astype(F32)).astype(BF16)
+    pass_near = (piece(parts, 1, 1).astype(F32) + far[half:].astype(F32)).astype(BF16)
     pass_far, pass_near = together(pass_far, pass_near)
     return together(partner(pass_far, 2), partner(pass_near, 1))
 
 
-def sum_total(part, first, second):
+def sum_total(parts, first, second):
     half = second[0].shape[0]
     halves = [
-        piece(part, 0, which).astype(F32) + first[which][:half].astype(F32) + second[which].astype(F32)
+        piece(parts, 0, which).astype(F32) + first[which][:half].astype(F32) + second[which].astype(F32)
         for which in (0, 1)
     ]
     return jnp.concatenate(halves, axis=0)
@@ -611,22 +637,46 @@
 
 def gather_second(near, far):
     half = near.shape[0] // 2
-    far_half, near_half = together(far[:half], near[half:])
-    return partner(far_half, 1), partner(near_half, 2)
+    return partner(far[:half], 1), partner(near[half:], 2)
 
 
 def gather_blocks(own, first, second):
     return [own, *first, jnp.concatenate(second, axis=0)]
 
 
-def placed_blocks(own, first, second, kind):
-    count, at = lax.axis_size("tp"), lax.axis_index("tp")
+def placed_kernel(at_ref, own_ref, near_ref, far_ref, top_ref, bottom_ref, out_ref):
+    step = pl.program_id(0)
+    half = top_ref.shape[0]
+    for which, ref in enumerate((own_ref, near_ref, far_ref)):
+
+        @pl.when(step == which)
+        def _(ref=ref):
+            out_ref[...] = ref[...].astype(out_ref.dtype)
+
+    @pl.when(step == 3)
+    def _():
+        out_ref[:half] = top_ref[...].astype(out_ref.dtype)
+        out_ref[half:] = bottom_ref[...].astype(out_ref.dtype)
+
+
+def placed_blocks(own, near, far, top, bottom, at, kind):
     size, width = own.shape
-    out = jnp.zeros((count * size, width), kind)
-    starts = [at * size, (at ^ 1) * size, (at ^ 2) * size, (at ^ 3) * size, (at ^ 3) * size + size // 2]
-    for block, start in zip([own, *first, *second], starts):
-        out = lax.dynamic_update_slice_in_dim(out, block.astype(kind), start, 0)
-    return out
+    inputs = [own, near, far, top, bottom]
+    return pl.pallas_call(
+        placed_kernel,
+        grid_spec=pltpu.PrefetchScalarGridSpec(
+            num_scalar_prefetch=1,
+            grid=(4,),
+            in_specs=[pl.BlockSpec(part.shape, lambda i, at: (0, 0)) for part in inputs],
+            out_specs=pl.BlockSpec((size, width), lambda i, at: (i ^ at[0], 0)),
+        ),
+        out_shape=jax.ShapeDtypeStruct((4 * size, width), kind),
+        compiler_params=pltpu.CompilerParams(
+            dimension_semantics=("arbitrary",), vmem_limit_bytes=VMEM
+        ),
+        cost_estimate=cost(1 << 20),
+        name="placed_blocks",
+    )(at.astype(jnp.int32).reshape(1), *inputs)
 
 
 def body(
@@ -693,7 +743,7 @@
     pre = matmul(first_all, mix_full)
     gated, mixed, states = mixer_forward(pre, bias, bound, gain, second_start, order)
     inputs_own = inputs[:shard_rows]
-    out_part = sum_over_chip(gated, out_full, dot_nn)
+    out_part = blocks_of(sum_over_chip(gated, out_full, dot_nn), tp_count)
     first = sum_first(out_part)
     second = sum_second(out_part, *first)
     resid = inputs_own + sum_total(out_part, first, second)
@@ -712,19 +762,15 @@
 
     down_grad = dot_tn(hidden, cotangent_rel).astype(BF16)
     down_sum = scatter(down_grad, ("dp", "ctx"), 1)
-    ffn_part = matmul(after(hidden, down_grad), down_full).astype(BF16)
-    ffn_first = sum_first(ffn_part)
-    hidden_grad = dot_nt(after(cotangent_rel, ffn_part), down_full)
+    hidden_grad = dot_nt(after(cotangent_rel, down_grad), down_full)
     gate_grad = (hidden_grad * pre_up * sig * (1.0 + pre_gate * (1.0 - sig))).astype(BF16)
     up_grad = (hidden_grad * (pre_gate * sig)).astype(BF16)
-    ffn_second = sum_second(after(ffn_part, gate_grad), *ffn_first)
     gate_up_grad = jnp.concatenate([gate_grad, up_grad], axis=1)
-    second_part = dot_nt(after(gate_up_grad, *ffn_first), ffn_full).astype(BF16)
-    ffn_total = sum_total(ffn_part, ffn_first, ffn_second)
-    second_part = after(second_part, *ffn_second)
+    second_part = blocks_of(dot_nt(gate_up_grad, ffn_full).astype(BF16), tp_count)
     first = sum_first(second_part)
+    ffn_part = matmul(after(hidden, *second_part), down_full).astype(BF16)
     gate_weight_grad = product(second_low, gate_grad, TN, BF16, rows=256)
-    gate_sum = scatter(gate_weight_grad, ("dp", "ctx"), 0)
+    gate_sum = scatter(after(gate_weight_grad, *first), ("dp", "ctx"), 0)
     second = sum_second(second_part, *first)
     second_total = sum_total(second_part, first, second)
     resid_part, second_gain_grad = norm_back(
@@ -734,40 +780,42 @@
     resid_own = resid_grad.astype(BF16)
     first = gather_first(resid_own)
     up_weight_grad = product(second_low, up_grad, TN, BF16, rows=256)
-    up_sum = scatter(up_weight_grad, ("dp", "ctx"), 0)
+    up_sum = scatter(after(up_weight_grad, *first), ("dp", "ctx"), 0)
     resid_second = gather_second(*first)
     resid_blocks = [resid_own, *first, *resid_second]
     resid_blocks = resid_blocks + [swap(block) for block in resid_blocks]
 
-    block_own = after((resid + ffn_total).astype(BF16), *resid_second)
-    block_first = gather_first(block_own)
-
+    ffn_part = blocks_of(after(ffn_part, *resid_second), tp_count)
+    ffn_first = sum_first(ffn_part)
     gated_grad = blocks_product(resid_blocks, out_full)
     proj_grad, sums = mixer_backward(pre, mixed, gated_grad, states, bias, bound, gain, second_start, order)
-    first_other = product(after(proj_grad, *block_first), mix_full, NT, BF16, cols=256, a_half=1)
-    block_second = gather_second(*[after(block, proj_grad) for block in block_first])
-    first_part = product(
-        after(proj_grad, first_other), mix_full, NT, BF16, cols=256, a_half=0, add=swap(first_other)
-    )
-    first_part = after(first_part, *block_second)
+    first_other = product(proj_grad, mix_full, NT, BF16, cols=256, a_half=1, parts=tp_count, wait=ffn_first)
+    ffn_second = sum_second([after(block, proj_grad) for block in ffn_part], *ffn_first)
+    block_own = (resid + sum_total(ffn_part, ffn_first, ffn_second)).astype(BF16)
+    first_own = product(
+        proj_grad, mix_full, NT, BF16, cols=256, a_half=0, parts=tp_count, wait=[first_other[0], block_own]
+    )
+    block_first = gather_first(block_own)
+    first_part = [
+        after((own.astype(F32) + swap(other).astype(F32)).astype(BF16), *block_first)
+        for own, other in zip(first_own, first_other)
+    ]
     first = sum_first(first_part)
     mix_grad, first_sum = weight_sum_product(
-        first_low, first_swapped, after(proj_grad, first_part), mix_full, resid_blocks, gated, wait=[gate_sum, up_sum]
-    )
-    mix_sum = scatter(mix_grad, "dp", 0)
-    block_own = after(block_own, first_part)
-    block_out = placed_blocks(block_own, block_first, block_second, BF16)
+        first_low, first_swapped, proj_grad, mix_full, resid_blocks, gated, wait=[gate_sum, up_sum]
+    )
+    mix_sum = scatter(after(mix_grad, *first), "dp", 0)
     final_first = first
     second = sum_second(first_part, *first)
     input_part, _ = norm_back(sum_total(first_part, first, second), inputs_own, first_gain)
     input_own = (resid_grad + input_part).astype(BF16)
-    first = gather_first(input_own)
-    input_grad = placed_blocks(input_own, first, gather_second(*first), F32)
-
-    first_gain_grad = first_sum / first_gain
-    first_gain_grad = first_sum / first_gain
-    gains = jnp.concatenate([first_gain_grad, second_gain_grad]).reshape(-1, HEAD)
-    gains = after(gains, *final_first)
+    block_second = gather_second(*[after(block, input_own) for block in block_first])
+    first = together(*gather_first(input_own), *block_second)[:2]
+    input_grad = placed_blocks(input_own, *first, *gather_second(*first), tp_at, F32)
+    block_out = placed_blocks(block_own, *block_first, *after(block_second, *first), tp_at, BF16)
+
+    gains = jnp.concatenate([first_sum / first_gain, second_gain_grad]).reshape(-1, HEAD)
+    gains = after(gains, *first)
     gains = small_sum(gains + swap(gains), "tp")
     heads = sums[:3].reshape(-1, HEAD)
     small = small_sum(jnp.concatenate([heads, gains]), "dp")
@@ -778,22 +826,13 @@
     all_bound = jnp.sum(all_weights * counted, axis=0)
     table_grad = all_weights * (counted - all_bound) * head_sums[2]
 
-    mix_other = swap(mix_sum)
-    first_core = ctx_at == 0
-    mix_pair = [jnp.where(first_core, mix_sum, mix_other), jnp.where(first_core, mix_other, mix_sum)]
-
-    def columns(which):
-        cols = slice(which * width, (which + 1) * width)
-        return jnp.concatenate([part[:, cols] for part in mix_pair], axis=1).astype(F32)
+    *mix_shards, out_shard = joined_columns(mix_sum, swap(mix_sum), ctx_at, width)
 
     return (
         block_out,
         input_grad,
-        columns(0),
-        columns(1),
-        columns(2),
-        columns(3),
-        jnp.concatenate([mix_pair[0][:, 4 * width :].T, mix_pair[1][:, 4 * width :].T], axis=0).astype(F32),
+        *mix_shards,
+        out_shard,
         in_order(after(gate_sum, *final_first), 0).astype(F32),
         in_order(after(up_sum, *final_first), 0).astype(F32),
         in_order(after(down_sum, *final_first), 1).astype(F32),

time: 687 us -> 648 us (0.943)
  waiting for transfers between devices: 281 us -> 245 us
  local copies, waits for them, and re-layouts: 47.1 us -> 30.8 us
  matrix products: 84.2 us -> 95.7 us
    ppermute x32, waiting for transfers between devices: 178 us -> 143 us  [partner(): lax.ppermute(part, 'tp', [(i, i ^ mask) for i in range(lax.axis_size('tp'...]
    pallas_call x4 -> x7, Pallas kernels: 45.6 us -> 58.3 us  [the longest x4 43.5 us: product(): pl.pallas_call(functools.partial(product_kernel, dims, parts), grid=(coun...]
    dot_general x1, matrix products: 8.12 us -> 18.6 us  [dot_tn(): lax.dot_general(a, b, (((0,), (0,)), ((), ())), preferred_element_type=F32)]
    pallas_call x1, Pallas kernels: 24.4 us -> 14.5 us  [mixer_forward(): pl.pallas_call(functools.partial(forward_kernel, heads, chunks), grid_spe...]
    dynamic_update_slice x5 -> x0, other arithmetic: 9.23 us -> none  [placed_blocks(): out = lax.dynamic_update_slice_in_dim(out, block.astype(kind), start, 0)]
    dynamic_update_slice x5 -> x0, local copies, waits for them, and re-layouts: 7.19 us -> none  [placed_blocks(): out = lax.dynamic_update_slice_in_dim(out, block.astype(kind), start, 0)]
    broadcast_in_dim x2 -> x0, local copies, waits for them, and re-layouts: 6.99 us -> none  [placed_blocks(): out = jnp.zeros((count * size, width), kind)]
    convert_element_type x9 -> x12, other arithmetic: 16.4 us -> 20.8 us  [the longest x4 7.61 us: body(): (own.astype(F32) + swap(other).astype(F32)).astype(BF16)]
  transfers between devices with their start and end apart: 60 -> 63, of which waited for: 35 -> 32; matrix products, arithmetic and copies ran while one was open for 28% -> 30% of each run, Pallas kernels for 15% -> 18%
where the time goes in v3:
time: 648 us; the launch traced here: 639 us
  waiting for transfers between devices  245 us (38%)
  Pallas kernels  122 us (19%)
  matrix products  95.7 us (15%)
  other arithmetic  80 us (12%)
  starting transfers between devices  48.1 us (7%)
  local copies, waits for them, and re-layouts  30.8 us (5%)
  between operations  17 us (3%)
    ppermute x32, waiting for transfers between devices, partner(): lax.ppermute(part, 'tp', [(i, i ^ mask) for i in range(lax.axis_size('tp'...  143 us
    all_gather x4, waiting for transfers between devices, gather(): return lax.all_gather(part, axes, axis=dim, tiled=True)  89 us
    pallas_call x4, Pallas kernels, product(): pl.pallas_call(functools.partial(product_kernel, dims, parts), grid=(coun...  43.5 us
    dot_general x3, matrix products, matmul(): return jnp.dot(left_side, right_side, preferred_element_type=F32)  41.9 us
    ppermute x32, starting transfers between devices, partner(): lax.ppermute(part, 'tp', [(i, i ^ mask) for i in range(lax.axis_size('tp'...  36.5 us
    dot_general x2, matrix products, dot_nt(): lax.dot_general(a, b, (((1,), (1,)), ((), ())), preferred_element_type=F32)  31.1 us
    pallas_call x1, Pallas kernels, mixer_backward(): pl.pallas_call(functools.partial(backward_kernel, heads, chunks), grid_sp...  22.8 us
    pallas_call x1, Pallas kernels, weight_sum_product(): pl.pallas_call(weight_sum_kernel, grid=(count // rows,), in_specs=[a_spec...  18.8 us
  transfers between devices with their start and end apart: 63, of which 32 were waited for; matrix products, arithmetic and copies ran while one was open for 30% of the time, Pallas kernels for 18%

profile of v3, /device:TPU:0, one launch (start us, length us, event | category | flops | bytes accessed | tf_op | source)
XLA Modules:
  0.0 638.6 jit_solution(11597797743554188391)
XLA Ops:
  11.6 2.3 fusion.13
  14.0 2.5 constant_dynamic-slice_fusion.13
  17.6 8.5 %multiply_convert_fusion.own_ref = bf16[1024,2048]{1,0:T(8,128)(2,1)} fusion(f32[2048]{0:T(1024)S(1)} %copy-done.40, f32[1024]{0:T(1024)S(1)} %add_rsqrt_fusion, bf16[256,2048]{1,0:T(8,128)(2,1)S(1)} %get-tuple-element.187, bf16[256,2048]{1,0:T(8,128)(2,1)S(1)} %get-tuple-element.188, bf16[256,2048]{1,0:T(8,128)(2,1)S(1)} %get-tuple-element.186, ...), kind=kLoop, calls=%fused_computation.5 | loop fusion | flops 23068672 | bytes 8400896 | tf_op jit(solution)/shard_map/convert_element_type | solution.py:733
  33.6 60.7 %all-gather.5.cloned.1.call-done.b_ref.weight_ref = bf16[2048,1024]{1,0:T(8,128)(2,1)} async-done(((bf16[512,1024]{1,0:T(8,128)(2,1)}), bf16[2048,1024]{1,0:T(8,128)(2,1)}) %all-gather.5.cloned.1.call-update) | async-done | bytes 4194320 | tf_op jit(solution)/shard_map/all_gather | solution.py:553
  94.3 15.1 %fusion.pre_ref = f32[2048,1024]{1,0:T(8,128)} fusion(bf16[2048,1024]{1,0:T(8,128)(2,1)} %all-gather.5.cloned.1.call-done.b_ref.weight_ref, bf16[1024,2048]{1,0:T(8,128)(2,1)} %collective-permute-done.other_ref, bf16[1024,2048]{1,0:T(8,128)(2,1)} %multiply_convert_fusion.own_ref), kind=kOutput, calls=%fused_computation | convolution fusion | flops 8606711808 | bytes 20971520 | tf_op jit(solution)/shard_map/dot_general | solution.py:561
  109.4 14.5 %mixer_forward.1 = (bf16[2048,256]{1,0:T(8,128)(2,1)}, f32[2048,256]{1,0:T(8,128)}, f32[16,2,128,128]{3,2,1,0:T(8,128)}) custom-call(s32[8]{0:T(128)} %iota_xor_fusion.order_ref, s32[1]{0:T(128)S(6)} %copy.37.split_ref, f32[2048,1024]{1,0:T(8,128)} %fusion.pre_ref, f32[1,256]{1,0:T(1,128)} %bitcast.34, f32[1,256]{1,0:T(1,128)} %bitcast.32, f32[1,256]{1,0:T(1,128)} %bitcast.36), custom_call_target="tpu_custom_call" | custom-call | flops 14680064000 | bytes 1048576 | tf_op jit(solution)/shard_map/mixer_forward/pallas_call | solution.py:196
  124.0 2.8 convolution_convert_fusion.2
  126.9 7.1 %collective-permute-done.1 = bf16[1024,2048]{1,0:T(8,128)(2,1)S(1)} collective-permute-done((bf16[1024,2048]{1,0:T(8,128)(2,1)S(1)}, bf16[1024,2048]{1,0:T(8,128)(2,1)S(1)}, u32[]{:S(2)}, u32[]{:S(2)}) %collective-permute-start.1) | collective-permute-done | bytes 4194336 | tf_op jit(solution)/shard_map/ppermute | solution.py:585
  138.9 22.0 %collective-permute-done.3 = bf16[256,2048]{1,0:T(8,128)(2,1)S(1)} collective-permute-done((bf16[256,2048]{1,0:T(8,128)(2,1)S(1)}, bf16[256,2048]{1,0:T(8,128)(2,1)S(1)}, u32[]{:S(2)}, u32[]{:S(2)}) %collective-permute-start.3) | collective-permute-done | bytes 1048608 | tf_op jit(solution)/shard_map/ppermute | solution.py:595
  166.8 5.0 maximum_convert_fusion
  171.8 5.2 collective-permute-done.4
  177.4 2.1 convert_add_fusion.7
  184.3 20.2 %collective-permute-done.7 = bf16[256,2048]{1,0:T(8,128)(2,1)S(1)} collective-permute-done((bf16[256,2048]{1,0:T(8,128)(2,1)S(1)}, bf16[256,2048]{1,0:T(8,128)(2,1)S(1)}, u32[]{:S(2)}, u32[]{:S(2)}) %collective-permute-start.7) | collective-permute-done | bytes 1048608 | tf_op jit(solution)/shard_map/ppermute | solution.py:595
  211.4 5.2 collective-permute-done.8
  219.6 13.2 %all-gather.9.cloned.1.call-done = bf16[2048,2816]{1,0:T(8,128)(2,1)} async-done(((bf16[256,2816]{1,0:T(8,128)(2,1)}), bf16[2048,2816]{1,0:T(8,128)(2,1)}) %all-gather.9.cloned.1.call-update) | async-done | bytes 11534352 | tf_op jit(solution)/shard_map/all_gather | solution.py:553
  232.8 17.2 %fusion.32 = f32[1024,2816]{1,0:T(8,128)S(1)} fusion(bf16[1024,2048]{1,0:T(8,128)(2,1)} %constant_dynamic-update-slice_fusion.a_ref, bf16[2048,2816]{1,0:T(8,128)(2,1)} %all-gather.9.cloned.1.call-done), kind=kOutput, calls=%fused_computation.137 | convolution fusion | flops 11811160064 | bytes 27262976 | tf_op jit(solution)/shard_map/dot_general | solution.py:561
  251.8 3.1 copy-done.8
  256.6 18.6 %convolution_convert_fusion = bf16[1408,2048]{1,0:T(8,128)(2,1)} fusion(bf16[1024,1408]{1,0:T(8,128)(2,1)S(1)} %multiply_convert_fusion.3, bf16[256,2048]{1,0:T(8,128)(2,1)S(1)} %copy-done.17, bf16[256,2048]{1,0:T(8,128)(2,1)S(1)} %copy-done.18, bf16[256,2048]{1,0:T(8,128)(2,1)S(1)} %copy-done.16, bf16[256,2048]{1,0:T(8,128)(2,1)S(1)} %get-tuple-element.173), kind=kOutput, calls=%fused_computation.7 | convolution fusion | flops 5925240832 | bytes 12845056 | tf_op jit(solution)/shard_map/dot_general | solution.py:34
  275.2 3.6 pad_maximum_fusion
  278.8 15.2 %all-gather.11.cloned.1.call-done = bf16[1408,2048]{1,0:T(8,128)(2,1)} async-done(((bf16[1408,256]{1,0:T(8,128)(2,1)}), bf16[1408,2048]{1,0:T(8,128)(2,1)}) %all-gather.11.cloned.1.call-update) | async-done | bytes 5767184 | tf_op jit(solution)/shard_map/all_gather | solution.py:553
  294.0 15.2 %multiply_convert_fusion.2 = (bf16[1024,1408]{1,0:T(8,128)(2,1)}, bf16[1024,1408]{1,0:T(8,128)(2,1)S(1)}) fusion(f32[1024,2816]{1,0:T(8,128)} %copy-done.8, bf16[1024,2048]{1,0:T(8,128)(2,1)} %pad_maximum_fusion, bf16[1408,2048]{1,0:T(8,128)(2,1)} %all-gather.11.cloned.1.call-done), kind=kOutput, calls=%fused_computation.13 | convolution fusion | flops 5924323328 | bytes 27262976 | tf_op jit(solution)/shard_map/dot_general | solution.py:30
  310.7 15.9 %fusion.9 = bf16[1024,2048]{1,0:T(8,128)(2,1)S(1)} fusion(bf16[2048,2816]{1,0:T(8,128)(2,1)} %all-gather.9.cloned.1.call-done, bf16[1024,1408]{1,0:T(8,128)(2,1)S(1)} %get-tuple-element.156.b_ref, bf16[1024,1408]{1,0:T(8,128)(2,1)} %get-tuple-element.155.b_ref), kind=kOutput, calls=%fused_computation.19 | convolution fusion | flops 11824791552 | bytes 21495808 | tf_op jit(solution)/shard_map/dot_general | solution.py:30
  332.3 12.0 %product.6 = bf16[2048,1408]{1,0:T(8,128)(2,1)} custom-call(bf16[1024,2048]{1,0:T(8,128)(2,1)} %constant_dynamic-update-slice_fusion.a_ref, bf16[1024,1408]{1,0:T(8,128)(2,1)} %get-tuple-element.155.b_ref), custom_call_target="tpu_custom_call" | custom-call | flops 11811160064 | bytes 1048576 | tf_op jit(solution)/shard_map/product/pallas_call | solution.py:420
  344.2 9.6 %collective-permute-done.11 = bf16[256,2048]{1,0:T(8,128)(2,1)} collective-permute-done((bf16[256,2048]{1,0:T(8,128)(2,1)}, bf16[256,2048]{1,0:T(8,128)(2,1)}, u32[]{:S(2)}, u32[]{:S(2)}) %collective-permute-start.11) | collective-permute-done | bytes 1048608 | tf_op jit(solution)/shard_map/ppermute | solution.py:595
  353.9 2.2 collective-permute-done.10
  360.2 10.9 %collective-permute-done.12 = bf16[128,2048]{1,0:T(8,128)(2,1)S(1)} collective-permute-done((bf16[128,2048]{1,0:T(8,128)(2,1)S(1)}, bf16[128,2048]{1,0:T(8,128)(2,1)S(1)}, u32[]{:S(2)}, u32[]{:S(2)}) %collective-permute-start.12) | collective-permute-done | bytes 524320 | tf_op jit(solution)/shard_map/ppermute | solution.py:595
  371.4 2.1 convert_add_fusion.5
  374.9 2.3 multiply_reduce_fusion.1
  381.7 12.0 %product.7 = bf16[2048,1408]{1,0:T(8,128)(2,1)} custom-call(bf16[1024,2048]{1,0:T(8,128)(2,1)} %constant_dynamic-update-slice_fusion.a_ref, bf16[1024,1408]{1,0:T(8,128)(2,1)} %copy-done.50), custom_call_target="tpu_custom_call" | custom-call | flops 11811160064 | bytes 1048576 | tf_op jit(solution)/shard_map/product/pallas_call | solution.py:420
  393.8 8.4 %collective-permute-done.14.refs_2_ = bf16[256,2048]{1,0:T(8,128)(2,1)} collective-permute-done((bf16[256,2048]{1,0:T(8,128)(2,1)}, bf16[256,2048]{1,0:T(8,128)(2,1)}, u32[]{:S(2)}, u32[]{:S(2)}) %collective-permute-start.14) | collective-permute-done | bytes 1048608 | tf_op jit(solution)/shard_map/ppermute | solution.py:595
  409.4 9.6 %convolution_convert_fusion.1 = bf16[1024,2048]{1,0:T(8,128)(2,1)S(1)} fusion(bf16[1024,1408]{1,0:T(8,128)(2,1)} %copy-done.19, bf16[1408,2048]{1,0:T(8,128)(2,1)} %all-gather.11.cloned.1.call-done), kind=kOutput, calls=%fused_computation.20 | convolution fusion | flops 5907677184 | bytes 12845056 | tf_op jit(solution)/shard_map/dot_general | solution.py:561
  426.7 8.0 %blocks_product.1.grad_ref = f32[2048,256]{1,0:T(8,128)} custom-call(bf16[256,2048]{1,0:T(8,128)(2,1)} %all-gather.7.cloned.1.call-done.b_ref, bf16[256,2048]{1,0:T(8,128)(2,1)} %fusion.26.refs_0_, bf16[256,2048]{1,0:T(8,128)(2,1)} %collective-permute-done.16.refs_1_, bf16[256,2048]{1,0:T(8,128)(2,1)} %collective-permute-done.14.refs_2_, ...), custom_call_target="tpu_custom_call" | custom-call | flops 4294967296 | bytes 1048576 | tf_op jit(solution)/shard_map/blocks_product/pallas_call | solution.py:499
  434.7 22.8 %mixer_backward.1 = (bf16[2048,1024]{1,0:T(8,128)(2,1)}, f32[8,256]{1,0:T(8,128)}) custom-call(s32[8]{0:T(128)} %iota_xor_fusion.order_ref, s32[1]{0:T(128)S(6)} %copy.37.split_ref, f32[2048,1024]{1,0:T(8,128)} %fusion.pre_ref, f32[2048,256]{1,0:T(8,128)} %get-tuple-element.97.mixed_ref, f32[2048,256]{1,0:T(8,128)} %blocks_product.1.grad_ref, ...), custom_call_target="tpu_custom_call" | custom-call | flops 23068672000 | bytes 1048576 | tf_op jit(solution)/shard_map/mixer_backward/pallas_call | solution.py:365
  462.6 9.7 %product.4 = (bf16[256,2048]{1,0:T(8,128)(2,1)}, bf16[256,2048]{1,0:T(8,128)(2,1)}, bf16[256,2048]{1,0:T(8,128)(2,1)}, bf16[256,2048]{1,0:T(8,128)(2,1)}) custom-call(bf16[2048,1024]{1,0:T(8,128)(2,1)} %get-tuple-element.99.a_ref.b_ref, bf16[2048,1024]{1,0:T(8,128)(2,1)} %all-gather.5.cloned.1.call-done.b_ref.weight_ref, ...), custom_call_target="tpu_custom_call" | custom-call | flops 8589934592 | bytes 1048576 | tf_op jit(solution)/shard_map/product/pallas_call | solution.py:420
  475.9 2.1 convert_add_fusion.3
  479.7 9.8 %product.5 = (bf16[256,2048]{1,0:T(8,128)(2,1)}, bf16[256,2048]{1,0:T(8,128)(2,1)}, bf16[256,2048]{1,0:T(8,128)(2,1)}, bf16[256,2048]{1,0:T(8,128)(2,1)}) custom-call(bf16[2048,1024]{1,0:T(8,128)(2,1)} %get-tuple-element.99.a_ref.b_ref, bf16[2048,1024]{1,0:T(8,128)(2,1)} %all-gather.5.cloned.1.call-done.b_ref.weight_ref, ...), custom_call_target="tpu_custom_call" | custom-call | flops 8589934592 | bytes 1048576 | tf_op jit(solution)/shard_map/product/pallas_call | solution.py:420
  491.6 2.3 add_convert_fusion.3
  495.6 7.2 %collective-permute-done.27.near_ref = bf16[256,2048]{1,0:T(8,128)(2,1)} collective-permute-done((bf16[256,2048]{1,0:T(8,128)(2,1)S(1)}, bf16[256,2048]{1,0:T(8,128)(2,1)}, u32[]{:S(2)}, u32[]{:S(2)}) %collective-permute-start.27) | collective-permute-done | bytes 1048608 | tf_op jit(solution)/shard_map/ppermute | solution.py:595
  507.6 18.8 %weight_sum_product.1 = (bf16[2048,1280]{1,0:T(8,128)(2,1)}, f32[2048,128]{1,0:T(8,128)}) custom-call(bf16[1024,2048]{1,0:T(8,128)(2,1)} %multiply_convert_fusion.own_ref, bf16[1024,2048]{1,0:T(8,128)(2,1)} %collective-permute-done.other_ref, bf16[2048,1024]{1,0:T(8,128)(2,1)} %get-tuple-element.99.a_ref.b_ref, ...), custom_call_target="tpu_custom_call" | custom-call | flops 21474836480 | bytes 1048576 | tf_op jit(solution)/shard_map/weight_sum_product/pallas_call | solution.py:459
  536.5 9.8 %collective-permute-done.35 = bf16[128,2048]{1,0:T(8,128)(2,1)S(1)} collective-permute-done((bf16[128,2048]{1,0:T(8,128)(2,1)S(1)}, bf16[128,2048]{1,0:T(8,128)(2,1)S(1)}, u32[]{:S(2)}, u32[]{:S(2)}) %collective-permute-start.35) | collective-permute-done | bytes 524320 | tf_op jit(solution)/shard_map/ppermute | solution.py:595
  549.1 2.1 multiply_reduce_fusion.3
  551.3 3.6 add_convert_fusion.1.own_ref
  563.0 29.1 %collective-permute-done.38.bottom_ref = bf16[128,2048]{1,0:T(8,128)(2,1)S(1)} collective-permute-done((bf16[128,2048]{1,0:T(8,128)(2,1)S(1)}, bf16[128,2048]{1,0:T(8,128)(2,1)S(1)}, u32[]{:S(2)}, u32[]{:S(2)}) %collective-permute-start.38) | collective-permute-done | bytes 524320 | tf_op jit(solution)/shard_map/ppermute | solution.py:595
  595.1 2.2 collective-permute-start.50
  602.5 2.8 collective-permute-start.53
  607.0 4.7 placed_blocks.2
  614.2 5.8 placed_blocks.3
  627.1 4.3 joined_columns.1
  (304 shorter events, 132.3 us)
Async XLA Ops:
  7.2 87.1 %all-gather.5.cloned.1.call-start = ((), (), s32[]{:S(2)}) async-start(), calls=%async_computation.4 | async-start | bytes 5242880 | tf_op jit(solution)/shard_map/all_gather | solution.py:553
  10.7 113.3 %all-gather.7.cloned.1.call-start = ((), (), s32[]{:S(2)}) async-start(), calls=%async_computation.5 | async-start | bytes 1310720 | tf_op jit(solution)/shard_map/all_gather | solution.py:553
  11.5 221.3 %all-gather.9.cloned.1.call-start = ((), (), s32[]{:S(2)}) async-start(), calls=%async_computation.6 | async-start | bytes 12976128 | tf_op jit(solution)/shard_map/all_gather | solution.py:553
  13.9 280.1 %all-gather.11.cloned.1.call-start = ((), (), s32[]{:S(2)}) async-start(), calls=%async_computation.7 | async-start | bytes 6488064 | tf_op jit(solution)/shard_map/all_gather | solution.py:553
  135.7 25.3 %collective-permute-start.3 = (bf16[256,2048]{1,0:T(8,128)(2,1)S(1)}, bf16[256,2048]{1,0:T(8,128)(2,1)S(1)}, u32[]{:S(2)}, u32[]{:S(2)}) collective-permute-start(bf16[256,2048]{1,0:T(8,128)(2,1)S(1)} %pad_maximum_fusion.4), channel_id=1, source_target_pairs={{0,2},{1,3},{2,0},{3,1},{4,6},{5,7},{6,4},{7,5},{8,10},{9,11},{10,... | collective-permute-start | bytes 3145736 | tf_op jit(solution)/shard_map/ppermute | solution.py:595
  137.4 25.0 %collective-permute-start.2 = (bf16[256,2048]{1,0:T(8,128)(2,1)S(1)}, bf16[256,2048]{1,0:T(8,128)(2,1)S(1)}, u32[]{:S(2)}, u32[]{:S(2)}) collective-permute-start(bf16[256,2048]{1,0:T(8,128)(2,1)S(1)} %pad_maximum_fusion.3), channel_id=1, source_target_pairs={{0,1},{1,0},{2,3},{3,2},{4,5},{5,4},{6,7},{7,6},{8,9},{9,8},{10,11... | collective-permute-start | bytes 3145736 | tf_op jit(solution)/shard_map/ppermute | solution.py:595
  163.8 13.2 %collective-permute-start.4 = (bf16[128,2048]{1,0:T(8,128)(2,1)}, bf16[128,2048]{1,0:T(8,128)(2,1)}, u32[]{:S(2)}, u32[]{:S(2)}) collective-permute-start(bf16[128,2048]{1,0:T(8,128)(2,1)} %get-tuple-element.84), channel_id=1, source_target_pairs={{0,2},{1,3},{2,0},{3,1},{4,6},{5,7},{6,4},{7,5},{8,10},{9,11},{10,... | collective-permute-start | bytes 1572872 | tf_op jit(solution)/shard_map/ppermute | solution.py:595
  164.3 13.1 %collective-permute-start.5 = (bf16[128,2048]{1,0:T(8,128)(2,1)}, bf16[128,2048]{1,0:T(8,128)(2,1)}, u32[]{:S(2)}, u32[]{:S(2)}) collective-permute-start(bf16[128,2048]{1,0:T(8,128)(2,1)} %get-tuple-element.85), channel_id=1, source_target_pairs={{0,1},{1,0},{2,3},{3,2},{4,5},{5,4},{6,7},{7,6},{8,9},{9,8},{10,11... | collective-permute-start | bytes 1572872 | tf_op jit(solution)/shard_map/ppermute | solution.py:595
  166.7 208.2 %reduce-scatter.5.cloned.1.call-start = ((), (), s32[]{:S(2)}) async-start(), calls=%async_computation.8 | async-start | bytes 6488064 | tf_op jit(solution)/shard_map/reduce_scatter | solution.py:557
  181.5 23.1 %collective-permute-start.7 = (bf16[256,2048]{1,0:T(8,128)(2,1)S(1)}, bf16[256,2048]{1,0:T(8,128)(2,1)S(1)}, u32[]{:S(2)}, u32[]{:S(2)}) collective-permute-start(bf16[256,2048]{1,0:T(8,128)(2,1)S(1)} %get-tuple-element.152), channel_id=1, source_target_pairs={{0,2},{1,3},{2,0},{3,1},{4,6},{5,7},{6,4},{7,5},{8,10},{9,11},{10,... | collective-permute-start | bytes 3145736 | tf_op jit(solution)/shard_map/ppermute | solution.py:595
  182.8 25.1 %collective-permute-start.6 = (bf16[256,2048]{1,0:T(8,128)(2,1)S(1)}, bf16[256,2048]{1,0:T(8,128)(2,1)S(1)}, u32[]{:S(2)}, u32[]{:S(2)}) collective-permute-start(bf16[256,2048]{1,0:T(8,128)(2,1)S(1)} %get-tuple-element.152), channel_id=1, source_target_pairs={{0,1},{1,0},{2,3},{3,2},{4,5},{5,4},{6,7},{7,6},{8,9},{9,8},{10,11... | collective-permute-start | bytes 3145736 | tf_op jit(solution)/shard_map/ppermute | solution.py:595
  204.6 12.1 %collective-permute-start.8 = (bf16[128,2048]{1,0:T(8,128)(2,1)S(1)}, bf16[128,2048]{1,0:T(8,128)(2,1)S(1)}, u32[]{:S(2)}, u32[]{:S(2)}) collective-permute-start(bf16[128,2048]{1,0:T(8,128)(2,1)S(1)} %slice.338), channel_id=1, source_target_pairs={{0,1},{1,0},{2,3},{3,2},{4,5},{5,4},{6,7},{7,6},{8,9},{9,8},{10,11... | collective-permute-start | bytes 1572872 | tf_op jit(solution)/shard_map/ppermute | solution.py:595
  208.0 10.8 %collective-permute-start.9 = (bf16[128,2048]{1,0:T(8,128)(2,1)S(1)}, bf16[128,2048]{1,0:T(8,128)(2,1)S(1)}, u32[]{:S(2)}, u32[]{:S(2)}) collective-permute-start(bf16[128,2048]{1,0:T(8,128)(2,1)S(1)} %slice.339), channel_id=1, source_target_pairs={{0,2},{1,3},{2,0},{3,1},{4,6},{5,7},{6,4},{7,5},{8,10},{9,11},{10,... | collective-permute-start | bytes 1572872 | tf_op jit(solution)/shard_map/ppermute | solution.py:595
  275.2 232.4 %reduce-scatter.7.cloned.1.call-start = ((), (), s32[]{:S(2)}) async-start(), calls=%async_computation.9 | async-start | bytes 6488064 | tf_op jit(solution)/shard_map/reduce_scatter | solution.py:557
  328.3 25.6 %collective-permute-start.11 = (bf16[256,2048]{1,0:T(8,128)(2,1)}, bf16[256,2048]{1,0:T(8,128)(2,1)}, u32[]{:S(2)}, u32[]{:S(2)}) collective-permute-start(bf16[256,2048]{1,0:T(8,128)(2,1)} %pad_maximum_fusion.6), channel_id=1, source_target_pairs={{0,2},{1,3},{2,0},{3,1},{4,6},{5,7},{6,4},{7,5},{8,10},{9,11},{10,... | collective-permute-start | bytes 3145736 | tf_op jit(solution)/shard_map/ppermute | solution.py:595
  330.8 25.3 %collective-permute-start.10 = (bf16[256,2048]{1,0:T(8,128)(2,1)}, bf16[256,2048]{1,0:T(8,128)(2,1)}, u32[]{:S(2)}, u32[]{:S(2)}) collective-permute-start(bf16[256,2048]{1,0:T(8,128)(2,1)} %pad_maximum_fusion.5), channel_id=1, source_target_pairs={{0,1},{1,0},{2,3},{3,2},{4,5},{5,4},{6,7},{7,6},{8,9},{9,8},{10,11... | collective-permute-start | bytes 3145736 | tf_op jit(solution)/shard_map/ppermute | solution.py:595
  356.1 151.4 %reduce-scatter.9.cloned.1.call-start = ((), (), s32[]{:S(2)}) async-start(), calls=%async_computation.10 | async-start | bytes 6488064 | tf_op jit(solution)/shard_map/reduce_scatter | solution.py:557
  358.2 12.9 %collective-permute-start.12 = (bf16[128,2048]{1,0:T(8,128)(2,1)S(1)}, bf16[128,2048]{1,0:T(8,128)(2,1)S(1)}, u32[]{:S(2)}, u32[]{:S(2)}) collective-permute-start(bf16[128,2048]{1,0:T(8,128)(2,1)S(1)} %get-tuple-element.91), channel_id=1, source_target_pairs={{0,2},{1,3},{2,0},{3,1},{4,6},{5,7},{6,4},{7,5},{8,10},{9,11},{10,... | collective-permute-start | bytes 1572872 | tf_op jit(solution)/shard_map/ppermute | solution.py:595
  358.7 12.7 %collective-permute-start.13 = (bf16[128,2048]{1,0:T(8,128)(2,1)S(1)}, bf16[128,2048]{1,0:T(8,128)(2,1)S(1)}, u32[]{:S(2)}, u32[]{:S(2)}) collective-permute-start(bf16[128,2048]{1,0:T(8,128)(2,1)S(1)} %get-tuple-element.92), channel_id=1, source_target_pairs={{0,1},{1,0},{2,3},{3,2},{4,5},{5,4},{6,7},{7,6},{8,9},{9,8},{10,11... | collective-permute-start | bytes 1572872 | tf_op jit(solution)/shard_map/ppermute | solution.py:595
  378.8 23.3 %collective-permute-start.14 = (bf16[256,2048]{1,0:T(8,128)(2,1)}, bf16[256,2048]{1,0:T(8,128)(2,1)}, u32[]{:S(2)}, u32[]{:S(2)}) collective-permute-start(bf16[256,2048]{1,0:T(8,128)(2,1)} %fusion.26.refs_0_), channel_id=1, source_target_pairs={{0,2},{1,3},{2,0},{3,1},{4,6},{5,7},{6,4},{7,5},{8,10},{9,11},{10,... | collective-permute-start | bytes 3145736 | tf_op jit(solution)/shard_map/ppermute | solution.py:595
  380.3 23.0 %collective-permute-start.16 = (bf16[256,2048]{1,0:T(8,128)(2,1)}, bf16[256,2048]{1,0:T(8,128)(2,1)}, u32[]{:S(2)}, u32[]{:S(2)}) collective-permute-start(bf16[256,2048]{1,0:T(8,128)(2,1)} %fusion.26.refs_0_), channel_id=1, source_target_pairs={{0,1},{1,0},{2,3},{3,2},{4,5},{5,4},{6,7},{7,6},{8,9},{9,8},{10,11... | collective-permute-start | bytes 3145736 | tf_op jit(solution)/shard_map/ppermute | solution.py:595
  405.1 14.6 %collective-permute-start.15 = (bf16[128,2048]{1,0:T(8,128)(2,1)}, bf16[128,2048]{1,0:T(8,128)(2,1)}, u32[]{:S(2)}, u32[]{:S(2)}) collective-permute-start(bf16[128,2048]{1,0:T(8,128)(2,1)} %slice.352), channel_id=1, source_target_pairs={{0,1},{1,0},{2,3},{3,2},{4,5},{5,4},{6,7},{7,6},{8,9},{9,8},{10,11... | collective-permute-start | bytes 1572872 | tf_op jit(solution)/shard_map/ppermute | solution.py:595
  408.5 11.3 %collective-permute-start.17 = (bf16[128,2048]{1,0:T(8,128)(2,1)}, bf16[128,2048]{1,0:T(8,128)(2,1)}, u32[]{:S(2)}, u32[]{:S(2)}) collective-permute-start(bf16[128,2048]{1,0:T(8,128)(2,1)} %slice.353), channel_id=1, source_target_pairs={{0,2},{1,3},{2,0},{3,1},{4,6},{5,7},{6,4},{7,5},{8,10},{9,11},{10,... | collective-permute-start | bytes 1572872 | tf_op jit(solution)/shard_map/ppermute | solution.py:595
  409.2 213.6 %reduce-scatter.11.cloned.1.call-start = ((), (), s32[]{:S(2)}) async-start(), calls=%async_computation.11 | async-start | bytes 6553600 | tf_op jit(solution)/shard_map/reduce_scatter | solution.py:557
  422.8 34.6 %collective-permute-start.24 = (bf16[256,2048]{1,0:T(8,128)(2,1)}, bf16[256,2048]{1,0:T(8,128)(2,1)}, u32[]{:S(2)}, u32[]{:S(2)}) collective-permute-start(bf16[256,2048]{1,0:T(8,128)(2,1)} %pad_maximum_fusion.8), channel_id=1, source_target_pairs={{0,2},{1,3},{2,0},{3,1},{4,6},{5,7},{6,4},{7,5},{8,10},{9,11},{10,... | collective-permute-start | bytes 3145736 | tf_op jit(solution)/shard_map/ppermute | solution.py:595
  424.2 33.3 %collective-permute-start.18 = (bf16[256,2048]{1,0:T(8,128)(2,1)}, bf16[256,2048]{1,0:T(8,128)(2,1)}, u32[]{:S(2)}, u32[]{:S(2)}) collective-permute-start(bf16[256,2048]{1,0:T(8,128)(2,1)} %pad_maximum_fusion.7), channel_id=1, source_target_pairs={{0,1},{1,0},{2,3},{3,2},{4,5},{5,4},{6,7},{7,6},{8,9},{9,8},{10,11... | collective-permute-start | bytes 3145736 | tf_op jit(solution)/shard_map/ppermute | solution.py:595
  460.6 14.1 %collective-permute-start.25 = (bf16[128,2048]{1,0:T(8,128)(2,1)S(1)}, bf16[128,2048]{1,0:T(8,128)(2,1)S(1)}, u32[]{:S(2)}, u32[]{:S(2)}) collective-permute-start(bf16[128,2048]{1,0:T(8,128)(2,1)S(1)} %add_convert_fusion.9), channel_id=1, source_target_pairs={{0,2},{1,3},{2,0},{3,1},{4,6},{5,7},{6,4},{7,5},{8,10},{9,11},{10,... | collective-permute-start | bytes 1572872 | tf_op jit(solution)/shard_map/ppermute | solution.py:595
  462.0 14.0 %collective-permute-start.26 = (bf16[128,2048]{1,0:T(8,128)(2,1)}, bf16[128,2048]{1,0:T(8,128)(2,1)S(1)}, u32[]{:S(2)}, u32[]{:S(2)}) collective-permute-start(bf16[128,2048]{1,0:T(8,128)(2,1)} %add_convert_fusion.8), channel_id=1, source_target_pairs={{0,1},{1,0},{2,3},{3,2},{4,5},{5,4},{6,7},{7,6},{8,9},{9,8},{10,11... | collective-permute-start | bytes 1572872 | tf_op jit(solution)/shard_map/ppermute | solution.py:595
  472.2 17.3 %collective-permute-start.33 = (bf16[256,2048]{1,0:T(8,128)(2,1)}, bf16[256,2048]{1,0:T(8,128)(2,1)}, u32[]{:S(2)}, u32[]{:S(2)}) collective-permute-start(bf16[256,2048]{1,0:T(8,128)(2,1)} %get-tuple-element.118), channel_id=1, source_target_pairs={{0,4},{4,0},{1,5},{5,1},{2,6},{6,2},{3,7},{7,3},{8,12},{12,8},{9,1... | collective-permute-start | bytes 3145736 | tf_op jit(solution)/shard_map/ppermute | solution.py:585
  472.2 19.4 %collective-permute-start.31 = (bf16[256,2048]{1,0:T(8,128)(2,1)}, bf16[256,2048]{1,0:T(8,128)(2,1)}, u32[]{:S(2)}, u32[]{:S(2)}) collective-permute-start(bf16[256,2048]{1,0:T(8,128)(2,1)} %get-tuple-element.115), channel_id=1, source_target_pairs={{0,4},{4,0},{1,5},{5,1},{2,6},{6,2},{3,7},{7,3},{8,12},{12,8},{9,1... | collective-permute-start | bytes 3145736 | tf_op jit(solution)/shard_map/ppermute | solution.py:585
  472.7 21.2 %collective-permute-start.30 = (bf16[256,2048]{1,0:T(8,128)(2,1)}, bf16[256,2048]{1,0:T(8,128)(2,1)}, u32[]{:S(2)}, u32[]{:S(2)}) collective-permute-start(bf16[256,2048]{1,0:T(8,128)(2,1)} %get-tuple-element.112), channel_id=1, source_target_pairs={{0,4},{4,0},{1,5},{5,1},{2,6},{6,2},{3,7},{7,3},{8,12},{12,8},{9,1... | collective-permute-start | bytes 3145736 | tf_op jit(solution)/shard_map/ppermute | solution.py:585
  478.5 24.3 %collective-permute-start.27 = (bf16[256,2048]{1,0:T(8,128)(2,1)S(1)}, bf16[256,2048]{1,0:T(8,128)(2,1)}, u32[]{:S(2)}, u32[]{:S(2)}) collective-permute-start(bf16[256,2048]{1,0:T(8,128)(2,1)S(1)} %fusion.12.refs_1_.own_ref), channel_id=1, source_target_pairs={{0,1},{1,0},{2,3},{3,2},{4,5},{5,4},{6,7},{7,6},{8,9},{9,8},{10,11... | collective-permute-start | bytes 3145736 | tf_op jit(solution)/shard_map/ppermute | solution.py:595
  479.0 24.0 %collective-permute-start.28 = (bf16[256,2048]{1,0:T(8,128)(2,1)S(1)}, bf16[256,2048]{1,0:T(8,128)(2,1)}, u32[]{:S(2)}, u32[]{:S(2)}) collective-permute-start(bf16[256,2048]{1,0:T(8,128)(2,1)S(1)} %fusion.12.refs_1_.own_ref), channel_id=1, source_target_pairs={{0,2},{1,3},{2,0},{3,1},{4,6},{5,7},{6,4},{7,5},{8,10},{9,11},{10,... | collective-permute-start | bytes 3145736 | tf_op jit(solution)/shard_map/ppermute | solution.py:595
  504.3 23.3 %collective-permute-start.34 = (bf16[256,2048]{1,0:T(8,128)(2,1)}, bf16[256,2048]{1,0:T(8,128)(2,1)}, u32[]{:S(2)}, u32[]{:S(2)}) collective-permute-start(bf16[256,2048]{1,0:T(8,128)(2,1)} %pad_maximum_fusion.10), channel_id=1, source_target_pairs={{0,2},{1,3},{2,0},{3,1},{4,6},{5,7},{6,4},{7,5},{8,10},{9,11},{10,... | collective-permute-start | bytes 3145736 | tf_op jit(solution)/shard_map/ppermute | solution.py:595
  506.1 23.1 %collective-permute-start.32 = (bf16[256,2048]{1,0:T(8,128)(2,1)}, bf16[256,2048]{1,0:T(8,128)(2,1)}, u32[]{:S(2)}, u32[]{:S(2)}) collective-permute-start(bf16[256,2048]{1,0:T(8,128)(2,1)} %pad_maximum_fusion.9), channel_id=1, source_target_pairs={{0,1},{1,0},{2,3},{3,2},{4,5},{5,4},{6,7},{7,6},{8,9},{9,8},{10,11... | collective-permute-start | bytes 3145736 | tf_op jit(solution)/shard_map/ppermute | solution.py:595
  532.0 14.4 %collective-permute-start.35 = (bf16[128,2048]{1,0:T(8,128)(2,1)S(1)}, bf16[128,2048]{1,0:T(8,128)(2,1)S(1)}, u32[]{:S(2)}, u32[]{:S(2)}) collective-permute-start(bf16[128,2048]{1,0:T(8,128)(2,1)S(1)} %add_convert_fusion.7), channel_id=1, source_target_pairs={{0,2},{1,3},{2,0},{3,1},{4,6},{5,7},{6,4},{7,5},{8,10},{9,11},{10,... | collective-permute-start | bytes 1572872 | tf_op jit(solution)/shard_map/ppermute | solution.py:595
  533.3 14.0 %collective-permute-start.36 = (bf16[128,2048]{1,0:T(8,128)(2,1)S(1)}, bf16[128,2048]{1,0:T(8,128)(2,1)S(1)}, u32[]{:S(2)}, u32[]{:S(2)}) collective-permute-start(bf16[128,2048]{1,0:T(8,128)(2,1)S(1)} %add_convert_fusion.6), channel_id=1, source_target_pairs={{0,1},{1,0},{2,3},{3,2},{4,5},{5,4},{6,7},{7,6},{8,9},{9,8},{10,11... | collective-permute-start | bytes 1572872 | tf_op jit(solution)/shard_map/ppermute | solution.py:595
  536.4 24.5 %collective-permute-start.46 = (bf16[1408,256]{1,0:T(8,128)(2,1)}, bf16[1408,256]{1,0:T(8,128)(2,1)}, u32[]{:S(2)}, u32[]{:S(2)}) collective-permute-start(bf16[1408,256]{1,0:T(8,128)(2,1)} %reduce-scatter.5.cloned.1.call-done), channel_id=1, source_target_pairs={{0,4},{4,0},{1,5},{5,1},{2,6},{6,2},{3,7},{7,3},{8,12},{12,8},{9,1... | collective-permute-start | bytes 2162696 | tf_op jit(solution)/shard_map/ppermute | solution.py:585
  554.9 37.2 %collective-permute-start.39 = (bf16[256,2048]{1,0:T(8,128)(2,1)}, bf16[256,2048]{1,0:T(8,128)(2,1)S(1)}, u32[]{:S(2)}, u32[]{:S(2)}) collective-permute-start(bf16[256,2048]{1,0:T(8,128)(2,1)} %add_convert_fusion.1.own_ref), channel_id=1, source_target_pairs={{0,1},{1,0},{2,3},{3,2},{4,5},{5,4},{6,7},{7,6},{8,9},{9,8},{10,11... | collective-permute-start | bytes 3145736 | tf_op jit(solution)/shard_map/ppermute | solution.py:595
  556.3 35.8 %collective-permute-start.40 = (bf16[256,2048]{1,0:T(8,128)(2,1)}, bf16[256,2048]{1,0:T(8,128)(2,1)S(1)}, u32[]{:S(2)}, u32[]{:S(2)}) collective-permute-start(bf16[256,2048]{1,0:T(8,128)(2,1)} %add_convert_fusion.1.own_ref), channel_id=1, source_target_pairs={{0,2},{1,3},{2,0},{3,1},{4,6},{5,7},{6,4},{7,5},{8,10},{9,11},{10,... | collective-permute-start | bytes 3145736 | tf_op jit(solution)/shard_map/ppermute | solution.py:595
  557.3 35.3 %collective-permute-start.44 = (bf16[256,1408]{1,0:T(8,128)(2,1)}, bf16[256,1408]{1,0:T(8,128)(2,1)S(1)}, u32[]{:S(2)}, u32[]{:S(2)}) collective-permute-start(bf16[256,1408]{1,0:T(8,128)(2,1)} %reduce-scatter.7.cloned.1.call-done.refs_10_), channel_id=1, source_target_pairs={{0,4},{4,0},{1,5},{5,1},{2,6},{6,2},{3,7},{7,3},{8,12},{12,8},{9,1... | collective-permute-start | bytes 2162696 | tf_op jit(solution)/shard_map/ppermute | solution.py:585
  558.5 33.5 %collective-permute-start.38 = (bf16[128,2048]{1,0:T(8,128)(2,1)S(1)}, bf16[128,2048]{1,0:T(8,128)(2,1)S(1)}, u32[]{:S(2)}, u32[]{:S(2)}) collective-permute-start(bf16[128,2048]{1,0:T(8,128)(2,1)S(1)} %slice.314), channel_id=1, source_target_pairs={{0,2},{1,3},{2,0},{3,1},{4,6},{5,7},{6,4},{7,5},{8,10},{9,11},{10,... | collective-permute-start | bytes 1572872 | tf_op jit(solution)/shard_map/ppermute | solution.py:595
  560.9 31.2 %collective-permute-start.37 = (bf16[128,2048]{1,0:T(8,128)(2,1)S(1)}, bf16[128,2048]{1,0:T(8,128)(2,1)S(1)}, u32[]{:S(2)}, u32[]{:S(2)}) collective-permute-start(bf16[128,2048]{1,0:T(8,128)(2,1)S(1)} %slice.313), channel_id=1, source_target_pairs={{0,1},{1,0},{2,3},{3,2},{4,5},{5,4},{6,7},{7,6},{8,9},{9,8},{10,11... | collective-permute-start | bytes 1572872 | tf_op jit(solution)/shard_map/ppermute | solution.py:595
  599.4 13.2 %collective-permute-start.41 = (bf16[128,2048]{1,0:T(8,128)(2,1)S(1)}, bf16[128,2048]{1,0:T(8,128)(2,1)S(1)}, u32[]{:S(2)}, u32[]{:S(2)}) collective-permute-start(bf16[128,2048]{1,0:T(8,128)(2,1)S(1)} %slice.315), channel_id=1, source_target_pairs={{0,1},{1,0},{2,3},{3,2},{4,5},{5,4},{6,7},{7,6},{8,9},{9,8},{10,11... | collective-permute-start | bytes 1572872 | tf_op jit(solution)/shard_map/ppermute | solution.py:595
  600.0 12.9 %collective-permute-start.42 = (bf16[128,2048]{1,0:T(8,128)(2,1)S(1)}, bf16[128,2048]{1,0:T(8,128)(2,1)S(1)}, u32[]{:S(2)}, u32[]{:S(2)}) collective-permute-start(bf16[128,2048]{1,0:T(8,128)(2,1)S(1)} %slice.316), channel_id=1, source_target_pairs={{0,2},{1,3},{2,0},{3,1},{4,6},{5,7},{6,4},{7,5},{8,10},{9,11},{10,... | collective-permute-start | bytes 1572872 | tf_op jit(solution)/shard_map/ppermute | solution.py:595
  600.8 19.2 %collective-permute-start.51 = (f32[38,128]{1,0:T(8,128)S(1)}, f32[38,128]{1,0:T(8,128)S(1)}, u32[]{:S(2)}, u32[]{:S(2)}) collective-permute-start(f32[38,128]{1,0:T(8,128)S(1)} %pad_maximum_fusion.11), channel_id=1, source_target_pairs={{0,8},{8,0},{16,24},{24,16},{1,9},{9,1},{17,25},{25,17},{2,10},{10... | collective-permute-start | bytes 58376 | tf_op jit(solution)/shard_map/ppermute | solution.py:571
  600.9 19.2 %collective-permute-start.52 = (f32[38,128]{1,0:T(8,128)S(1)}, f32[38,128]{1,0:T(8,128)S(1)}, u32[]{:S(2)}, u32[]{:S(2)}) collective-permute-start(f32[38,128]{1,0:T(8,128)S(1)} %pad_maximum_fusion.11), channel_id=1, source_target_pairs={{0,16},{8,24},{16,0},{24,8},{1,17},{9,25},{17,1},{25,9},{2,18},{10... | collective-permute-start | bytes 58376 | tf_op jit(solution)/shard_map/ppermute | solution.py:571
  602.5 17.6 %collective-permute-start.53 = (f32[38,128]{1,0:T(8,128)S(1)}, f32[38,128]{1,0:T(8,128)S(1)}, u32[]{:S(2)}, u32[]{:S(2)}) collective-permute-start(f32[38,128]{1,0:T(8,128)S(1)} %pad_maximum_fusion.11), channel_id=1, source_target_pairs={{0,24},{8,16},{16,8},{24,0},{1,25},{9,17},{17,9},{25,1},{2,26},{10... | collective-permute-start | bytes 58376 | tf_op jit(solution)/shard_map/ppermute | solution.py:571
  (66 other events, 654.1 us)
Sparse Core Ops, SparseCore 0:
  10.8 83.4 all-gather.4
  96.5 26.4 all-gather.6
  125.2 107.5 all-gather.8
  234.8 59.1 all-gather.10
  296.1 63.0 reduce-scatter.4
  361.4 63.2 reduce-scatter.6
  426.9 63.2 reduce-scatter.8
  529.3 93.3 reduce-scatter.10

commit v4 on v3

--- a/solution.py
+++ b/solution.py
@@ -393,10 +393,10 @@
 TN = ((0,), (0,))
 
 
-def product(a, b, dims, kind, rows=None, cols=None, a_half=None, parts=1, wait=()):
+def product(a, b, dims, kind, rows=None, cols=None, a_half=None, b_half=None, parts=1, wait=()):
     count = a.shape[1 - dims[0][0]] if a_half is None else a.shape[0] // 2
     depth = a.shape[dims[0][0]]
-    wide = b.shape[1 - dims[1][0]]
+    wide = b.shape[1 - dims[1][0]] // (1 if b_half is None else 2)
     tile_rows = rows or count
     tile_cols = cols or wide
     by_rows = rows is not None
@@ -407,15 +407,17 @@
 
     def at_col(i):
         return 0 if by_rows else i
+
+    b_shift = (b_half or 0) * (wide // tile_cols)
 
     if dims[0][0] == 1:
         a_spec = pl.BlockSpec((tile_rows, depth), lambda i: (at_row(i), 0))
     else:
         a_spec = pl.BlockSpec((depth, tile_rows), lambda i: (0, at_row(i)))
     if dims[1][0] == 0:
-        b_spec = pl.BlockSpec((depth, tile_cols), lambda i: (0, at_col(i)))
+        b_spec = pl.BlockSpec((depth, tile_cols), lambda i: (0, at_col(i) + b_shift))
     else:
-        b_spec = pl.BlockSpec((tile_cols, depth), lambda i: (at_col(i), 0))
+        b_spec = pl.BlockSpec((tile_cols, depth), lambda i: (at_col(i) + b_shift, 0))
     out_spec = pl.BlockSpec((tile_rows // parts, tile_cols), lambda i: (at_row(i) - shift, at_col(i)))
     out = pl.pallas_call(
         functools.partial(product_kernel, dims, parts),
@@ -430,6 +432,71 @@
         name="product",
     )(a, b, *wait)
     return out[0] if parts == 1 else out
+
+
+def gate_kernel(low_ref, weight_ref, pre_ref, hidden_ref):
+    half = hidden_ref.shape[1]
+    pre = dot_nn(low_ref[...], weight_ref[...])
+    pre_ref[...] = pre
+    gate = pre[:, :half]
+    hidden_ref[...] = (gate * sigmoid_pair(gate)[0] * pre[:, half:]).astype(BF16)
+
+
+def gate_product(low, weight, rows=256):
+    count, depth = low.shape
+    wide = weight.shape[1]
+    return pl.pallas_call(
+        gate_kernel,
+        grid=(count // rows,),
+        in_specs=[
+            pl.BlockSpec((rows, depth), lambda i: (i, 0)),
+            pl.BlockSpec((depth, wide), lambda i: (0, 0)),
+        ],
+        out_specs=[
+            pl.BlockSpec((rows, wide), lambda i: (i, 0)),
+            pl.BlockSpec((rows, wide // 2), lambda i: (i, 0)),
+        ],
+        out_shape=[
+            jax.ShapeDtypeStruct((count, wide), F32),
+            jax.ShapeDtypeStruct((count, wide // 2), BF16),
+        ],
+        compiler_params=pltpu.CompilerParams(
+            dimension_semantics=("arbitrary",), vmem_limit_bytes=VMEM
+        ),
+        cost_estimate=cost(2 * count * depth * wide),
+        name="gate_product",
+    )(low, weight)
+
+
+def hidden_back_kernel(grad_ref, weight_ref, pre_ref, out_ref):
+    half = out_ref.shape[1] // 2
+    grad = dot_nt(grad_ref[...], weight_ref[...])
+    gate, up = pre_ref[:, :half], pre_ref[:, half:]
+    sig, rest = sigmoid_pair(gate)
+    out_ref[:, :half] = (grad * up * sig * (1.0 + gate * rest)).astype(BF16)
+    out_ref[:, half:] = (grad * (gate * sig)).astype(BF16)
+
+
+def hidden_back(grad, weight, pre, rows=256, wait=()):
+    count, depth = grad.shape
+    wide = pre.shape[1]
+    return pl.pallas_call(
+        lambda *refs: hidden_back_kernel(*refs[:3], refs[-1]),
+        grid=(count // rows,),
+        in_specs=[
+            pl.BlockSpec((rows, depth), lambda i: (i, 0)),
+            pl.BlockSpec(weight.shape, lambda i: (0, 0)),
+            pl.BlockSpec((rows, wide), lambda i: (i, 0)),
+        ]
+        + [UNREAD] * len(wait),
+        out_specs=pl.BlockSpec((rows, wide), lambda i: (i, 0)),
+        out_shape=jax.ShapeDtypeStruct((count, wide), BF16),
+        compiler_params=pltpu.CompilerParams(
+            dimension_semantics=("arbitrary",), vmem_limit_bytes=VMEM
+        ),
+        cost_estimate=cost(count * depth * wide),
+        name="hidden_back",
+    )(grad, weight, pre, *wait)
 
 
 def weight_sum_kernel(own_ref, other_ref, b_ref, weight_ref, right_ref, *refs):
@@ -485,24 +552,50 @@
     return out, total[:, 0]
 
 
-def blocks_product_kernel(b_ref, *refs):
+def early_product_kernel(b_ref, *refs):
     out_ref = refs[-1]
-    start = 0
-    for ref in refs[:-1]:
-        size = ref.shape[0]
-        out_ref[start : start + size] = dot_nt(ref[...], b_ref[...])
-        start += size
-
-
-def blocks_product(blocks, b):
-    count = sum(block.shape[0] for block in blocks)
+    size = refs[0].shape[0]
+    for ref, block in zip(refs[:-1], (0, 1, 2, 4, 5, 6)):
+        out_ref[block * size : (block + 1) * size] = dot_nt(ref[...], b_ref[...])
+
+
+def late_product_kernel(b_ref, early_ref, *refs):
+    out_ref = refs[-1]
+    for step in range(2):
+
+        @pl.when(pl.program_id(0) == step)
+        def _(step=step):
+            half = refs[0].shape[0]
+            out_ref[:half] = dot_nt(refs[2 * step][...], b_ref[...])
+            out_ref[half:] = dot_nt(refs[2 * step + 1][...], b_ref[...])
+
+
+def early_product(blocks, b):
+    size = blocks[0].shape[0]
     return pl.pallas_call(
-        blocks_product_kernel,
-        out_shape=jax.ShapeDtypeStruct((count, b.shape[0]), F32),
+        early_product_kernel,
+        out_shape=jax.ShapeDtypeStruct((8 * size, b.shape[0]), F32),
         compiler_params=pltpu.CompilerParams(vmem_limit_bytes=VMEM),
-        cost_estimate=cost(2 * count * b.size),
-        name="blocks_product",
+        cost_estimate=cost(2 * 6 * size * b.size),
+        name="early_product",
     )(b, *blocks)
+
+
+def late_product(out, late, b):
+    size = 2 * late[0].shape[0]
+    width = b.shape[0]
+    whole = [pl.BlockSpec(part.shape, lambda i: (0, 0)) for part in late]
+    return pl.pallas_call(
+        late_product_kernel,
+        grid=(2,),
+        in_specs=[pl.BlockSpec(b.shape, lambda i: (0, 0)), UNREAD] + whole,
+        out_specs=pl.BlockSpec((size, width), lambda i: (4 * i + 3, 0)),
+        out_shape=jax.ShapeDtypeStruct(out.shape, F32),
+        input_output_aliases={1: 0},
+        compiler_params=pltpu.CompilerParams(vmem_limit_bytes=VMEM),
+        cost_estimate=cost(2 * 2 * size * b.size),
+        name="late_product",
+    )(b, out, *late)
 
 
 def joined_columns_kernel(width, at_ref, own_ref, other_ref, *out_refs):
@@ -553,6 +646,18 @@
     return lax.all_gather(part, axes, axis=dim, tiled=True)
 
 
+def gather_columns(part, axis):
+    count, at = lax.axis_size(axis), lax.axis_index(axis)
+    if count > 4:
+        return gather(part, axis, 1)
+    size = part.shape[1]
+    out = jnp.zeros((part.shape[0], count * size), part.dtype)
+    for m in range(count):
+        block = part if m == 0 else lax.ppermute(part, axis, [(i, i ^ m) for i in range(count)])
+        out = lax.dynamic_update_slice_in_dim(out, block, (at ^ m) * size, 1)
+    return out
+
+
 def scatter(whole, axes, dim):
     return lax.psum_scatter(whole, axes, scatter_dimension=dim, tiled=True)
 
@@ -602,22 +707,23 @@
     )
 
 
-def piece(parts, block, which):
-    half = parts[block].shape[0] // 2
-    return parts[block][which * half : (which + 1) * half]
+def parts_of(blocks):
+    half = blocks[0].shape[0] // 2
+    low, high = [block[:half] for block in blocks], [block[half:] for block in blocks]
+    near = jnp.concatenate([low[1], low[3]], axis=0)
+    far = jnp.concatenate([high[2], high[3]], axis=0)
+    return [near, far, blocks[0], low[2], high[1]]
 
 
 def sum_first(parts):
-    near = partner(jnp.concatenate([piece(parts, 1, 0), piece(parts, 3, 0)], axis=0), 1)
-    far = partner(jnp.concatenate([piece(parts, 2, 1), piece(parts, 3, 1)], axis=0), 2)
-    return near, far
+    return partner(parts[0], 1), partner(parts[1], 2)
 
 
 def sum_second(parts, near, far):
     half = near.shape[0] // 2
     near, far = together(near, far)
-    pass_far = (piece(parts, 2, 0).astype(F32) + near[half:].astype(F32)).astype(BF16)
-    pass_near = (piece(parts, 1, 1).astype(F32) + far[half:].astype(F32)).astype(BF16)
+    pass_far = (parts[3].astype(F32) + near[half:].astype(F32)).astype(BF16)
+    pass_near = (parts[4].astype(F32) + far[half:].astype(F32)).astype(BF16)
     pass_far, pass_near = together(pass_far, pass_near)
     return together(partner(pass_far, 2), partner(pass_near, 1))
 
@@ -625,7 +731,9 @@
 def sum_total(parts, first, second):
     half = second[0].shape[0]
     halves = [
-        piece(parts, 0, which).astype(F32) + first[which][:half].astype(F32) + second[which].astype(F32)
+        parts[2][which * half : (which + 1) * half].astype(F32)
+        + first[which][:half].astype(F32)
+        + second[which].astype(F32)
         for which in (0, 1)
     ]
     return jnp.concatenate(halves, axis=0)
@@ -640,11 +748,14 @@
     return partner(far[:half], 1), partner(near[half:], 2)
 
 
-def gather_blocks(own, first, second):
-    return [own, *first, jnp.concatenate(second, axis=0)]
-
-
-def placed_kernel(at_ref, own_ref, near_ref, far_ref, top_ref, bottom_ref, out_ref):
+def gathered_parts(own, first, second):
+    near, far = first
+    half = second[0].shape[0]
+    return [near[:half], second[0], far[half:], second[1], own, far[:half], near[half:]]
+
+
+def placed_kernel(at_ref, own_ref, near_ref, far_ref, top_ref, bottom_ref, *refs):
+    out_ref = refs[-1]
     step = pl.program_id(0)
     half = top_ref.shape[0]
     for which, ref in enumerate((own_ref, near_ref, far_ref)):
@@ -659,7 +770,7 @@
         out_ref[half:] = bottom_ref[...].astype(out_ref.dtype)
 
 
-def placed_blocks(own, near, far, top, bottom, at, kind):
+def placed_blocks(own, near, far, top, bottom, at, kind, wait=()):
     size, width = own.shape
     inputs = [own, near, far, top, bottom]
     return pl.pallas_call(
@@ -667,16 +778,16 @@
         grid_spec=pltpu.PrefetchScalarGridSpec(
             num_scalar_prefetch=1,
             grid=(4,),
-            in_specs=[pl.BlockSpec(part.shape, lambda i, at: (0, 0)) for part in inputs],
+            in_specs=[pl.BlockSpec(part.shape, lambda i, at: (0, 0)) for part in inputs] + [UNREAD] * len(wait),
             out_specs=pl.BlockSpec((size, width), lambda i, at: (i ^ at[0], 0)),
         ),
         out_shape=jax.ShapeDtypeStruct((4 * size, width), kind),
         compiler_params=pltpu.CompilerParams(
             dimension_semantics=("arbitrary",), vmem_limit_bytes=VMEM
         ),
-        cost_estimate=cost(1 << 20),
+        cost_estimate=cost(3 << 30),
         name="placed_blocks",
-    )(at.astype(jnp.int32).reshape(1), *inputs)
+    )(at.astype(jnp.int32).reshape(1), *inputs, *wait)
 
 
 def body(
@@ -710,11 +821,6 @@
         size = array.shape[dim] // ctx_count
         return lax.dynamic_slice_in_dim(array, ctx_at * size, size, dim)
 
-    def sum_over_chip(rows_in, right_side, dot):
-        other = swap(dot(rows_in[row_count:], right_side).astype(BF16))
-        own = dot(rows_in[:row_count], right_side)
-        return (own + other.astype(F32)).astype(BF16)
-
     blocks = ctx_count * tp_count
     order = lax.iota(jnp.int32, blocks) ^ (ctx_at * tp_count + tp_at)
 
@@ -725,7 +831,7 @@
         "dp",
         0,
     )
-    out_full = gather(own_half(out_proj, 0), "dp", 1)
+    out_full = gather_columns(own_half(out_proj, 0), "dp")
     ffn_full = gather(own_half(jnp.concatenate([ffn_gate, ffn_up], axis=1), 0), ("dp", "ctx"), 0)
     down_full = gather(own_half(ffn_down, 1), ("dp", "ctx"), 1)
 
@@ -740,10 +846,14 @@
     bound = jnp.sum(weights * counted, axis=0)
     bias = own_half(forget_bias, 0)
     gain = own_half(group_gain, 0)
-    pre = matmul(first_all, mix_full)
+    pre = product(first_all, mix_full, NN, F32, rows=512)
     gated, mixed, states = mixer_forward(pre, bias, bound, gain, second_start, order)
     inputs_own = inputs[:shard_rows]
-    out_part = blocks_of(sum_over_chip(gated, out_full, dot_nn), tp_count)
+    out_other = [
+        swap(block) for block in product(gated, out_full, NN, BF16, cols=512, a_half=1, parts=tp_count)
+    ]
+    out_own = product(gated, out_full, NN, BF16, cols=512, a_half=0, parts=tp_count)
+    out_part = parts_of([(a.astype(F32) + b.astype(F32)).astype(BF16) for a, b in zip(out_own, out_other)])
     first = sum_first(out_part)
     second = sum_second(out_part, *first)
     resid = inputs_own + sum_total(out_part, first, second)
@@ -751,43 +861,49 @@
     second_own = (resid * rms_rows(resid) * second_gain).astype(BF16)
     first = gather_first(second_own)
     second_low = jnp.concatenate(
-        gather_blocks(second_own, first, gather_second(*first)), axis=0
+        gathered_parts(second_own, first, gather_second(*first)), axis=0
     )
-    cotangent_rel = relative(cotangent, tp_count, tp_at)
-    gate_up = matmul(second_low, ffn_full)
-    pre_gate = gate_up[:, :hidden_width]
-    pre_up = gate_up[:, hidden_width:]
-    sig = jax.nn.sigmoid(pre_gate)
-    hidden = (pre_gate * sig * pre_up).astype(BF16)
-
-    down_grad = dot_tn(hidden, cotangent_rel).astype(BF16)
+    cotangent_blocks = blocks_of(relative(cotangent, tp_count, tp_at), tp_count)
+    cotangent_rel = jnp.concatenate(parts_of(cotangent_blocks), axis=0)
+    gate_up, hidden = gate_product(second_low, ffn_full)
+
+    down_grad = product(hidden, cotangent_rel, TN, BF16, cols=512)
     down_sum = scatter(down_grad, ("dp", "ctx"), 1)
-    hidden_grad = dot_nt(after(cotangent_rel, down_grad), down_full)
-    gate_grad = (hidden_grad * pre_up * sig * (1.0 + pre_gate * (1.0 - sig))).astype(BF16)
-    up_grad = (hidden_grad * (pre_gate * sig)).astype(BF16)
-    gate_up_grad = jnp.concatenate([gate_grad, up_grad], axis=1)
-    second_part = blocks_of(dot_nt(gate_up_grad, ffn_full).astype(BF16), tp_count)
-    first = sum_first(second_part)
-    ffn_part = matmul(after(hidden, *second_part), down_full).astype(BF16)
-    gate_weight_grad = product(second_low, gate_grad, TN, BF16, rows=256)
-    gate_sum = scatter(after(gate_weight_grad, *first), ("dp", "ctx"), 0)
+    gate_up_grad = hidden_back(cotangent_rel, down_full, gate_up, wait=[down_grad])
+    second_sent = product(gate_up_grad, ffn_full, NT, BF16, cols=512, a_half=0, parts=2)
+    first = sum_first(second_sent)
+    second_kept = product(gate_up_grad, ffn_full, NT, BF16, cols=512, a_half=1, wait=second_sent)
+    half_rows = shard_rows // 2
+    second_part = [
+        *second_sent,
+        second_kept[:shard_rows],
+        second_kept[shard_rows : shard_rows + half_rows],
+        second_kept[shard_rows + half_rows :],
+    ]
+    ffn_rows = product(hidden, down_full, NN, BF16, cols=256, parts=tp_count, wait=[second_kept])
+    gate_weight_grad = product(second_low, gate_up_grad, TN, BF16, rows=256, b_half=0)
+    gate_sum = scatter(after(gate_weight_grad, second_kept, *first), ("dp", "ctx"), 0)
     second = sum_second(second_part, *first)
     second_total = sum_total(second_part, first, second)
     resid_part, second_gain_grad = norm_back(
-        after(second_total, down_sum), resid, second_gain
+        after(second_total, down_sum, ffn_rows[0]), resid, second_gain
     )
-    resid_grad = cotangent_rel[:shard_rows].astype(F32) + resid_part
+    resid_grad = cotangent_blocks[0].astype(F32) + resid_part
     resid_own = resid_grad.astype(BF16)
     first = gather_first(resid_own)
-    up_weight_grad = product(second_low, up_grad, TN, BF16, rows=256)
+    up_weight_grad = product(second_low, gate_up_grad, TN, BF16, rows=256, b_half=1)
     up_sum = scatter(after(up_weight_grad, *first), ("dp", "ctx"), 0)
     resid_second = gather_second(*first)
-    resid_blocks = [resid_own, *first, *resid_second]
-    resid_blocks = resid_blocks + [swap(block) for block in resid_blocks]
-
-    ffn_part = blocks_of(after(ffn_part, *resid_second), tp_count)
+    resid_early = [resid_own, *first]
+    resid_early = resid_early + [swap(block) for block in resid_early]
+    early_grad = early_product(resid_early, out_full)
+    resid_late = [*resid_second, *[swap(after(block, early_grad)) for block in resid_second]]
+    resid_blocks = [*resid_early[:3], *resid_late[:2], *resid_early[3:], *resid_late[2:]]
+
+    ffn_rows = [after(part, *resid_second) for part in ffn_rows]
+    ffn_part = [*ffn_rows[:3], ffn_rows[3][:half_rows], ffn_rows[3][half_rows:]]
     ffn_first = sum_first(ffn_part)
-    gated_grad = blocks_product(resid_blocks, out_full)
+    gated_grad = late_product(early_grad, resid_late, out_full)
     proj_grad, sums = mixer_backward(pre, mixed, gated_grad, states, bias, bound, gain, second_start, order)
     first_other = product(proj_grad, mix_full, NT, BF16, cols=256, a_half=1, parts=tp_count, wait=ffn_first)
     ffn_second = sum_second([after(block, proj_grad) for block in ffn_part], *ffn_first)
@@ -797,36 +913,38 @@
     )
     block_first = gather_first(block_own)
     first_part = [
-        after((own.astype(F32) + swap(other).astype(F32)).astype(BF16), *block_first)
+        (own.astype(F32) + swap(other).astype(F32)).astype(BF16)
         for own, other in zip(first_own, first_other)
     ]
+    first_part = parts_of(first_part)
     first = sum_first(first_part)
     mix_grad, first_sum = weight_sum_product(
-        first_low, first_swapped, proj_grad, mix_full, resid_blocks, gated, wait=[gate_sum, up_sum]
+        first_low, first_swapped, proj_grad, mix_full, resid_blocks, gated, wait=block_first
     )
-    mix_sum = scatter(after(mix_grad, *first), "dp", 0)
+    mix_sum = scatter(after(mix_grad, gate_sum, up_sum, *first), "dp", 0)
     final_first = first
     second = sum_second(first_part, *first)
     input_part, _ = norm_back(sum_total(first_part, first, second), inputs_own, first_gain)
     input_own = (resid_grad + input_part).astype(BF16)
-    block_second = gather_second(*[after(block, input_own) for block in block_first])
-    first = together(*gather_first(input_own), *block_second)[:2]
-    input_grad = placed_blocks(input_own, *first, *gather_second(*first), tp_at, F32)
-    block_out = placed_blocks(block_own, *block_first, *after(block_second, *first), tp_at, BF16)
+    block_second = gather_second(*[after(block, *second) for block in block_first])
+    input_own = after(input_own, *block_second)
+    first = gather_first(input_own)
 
     gains = jnp.concatenate([first_sum / first_gain, second_gain_grad]).reshape(-1, HEAD)
-    gains = after(gains, *first)
-    gains = small_sum(gains + swap(gains), "tp")
-    heads = sums[:3].reshape(-1, HEAD)
-    small = small_sum(jnp.concatenate([heads, gains]), "dp")
-    cut = heads.shape[0]
+    gains = gains + swap(gains)
+    block_out = placed_blocks(block_own, *block_first, *block_second, tp_at, BF16, wait=[gains])
+    gains = small_sum(gains, "tp")
+    input_second = gather_second(*[after(block, block_out) for block in first])
+    small = small_sum(jnp.concatenate([sums[:3].reshape(-1, HEAD), gains]), "dp")
+    input_grad = placed_blocks(input_own, *first, *input_second, tp_at, F32, wait=[gains])
+    cut = 3 * width // HEAD
     head_sums = in_order(small[:cut].reshape(3, width), 1)
     gain_sums = small[cut:].reshape(-1)
     all_weights = jax.nn.softmax(bound_table, axis=0)
     all_bound = jnp.sum(all_weights * counted, axis=0)
     table_grad = all_weights * (counted - all_bound) * head_sums[2]
 
-    *mix_shards, out_shard = joined_columns(mix_sum, swap(mix_sum), ctx_at, width)
+    *mix_shards, out_shard = joined_columns(mix_sum, after(swap(mix_sum), small), ctx_at, width)
 
     return (
         block_out,

time: 648 us -> 635 us (0.980)
  Pallas kernels: 122 us -> 225 us
  matrix products: 95.7 us -> 0 us
  waiting for transfers between devices: 245 us -> 210 us
  local copies, waits for them, and re-layouts: 30.8 us -> 44.1 us
    dot_general x8 -> x0, matrix products: 95.7 us -> none  [the longest x3 41.9 us: matmul(): return jnp.dot(left_side, right_side, preferred_element_type=F32)]
    pallas_call x4 -> x11, Pallas kernels: 43.5 us -> 110 us  [product(): pl.pallas_call(functools.partial(product_kernel, dims, parts), grid=(coun...]
    all_gather x4 -> x3, waiting for transfers between devices: 89 us -> 37.9 us  [gather(): return lax.all_gather(part, axes, axis=dim, tiled=True)]
    pallas_call x1 -> x4, Pallas kernels: 8.02 us -> 44.8 us  [the longest x1 19.4 us: gate_product(): pl.pallas_call(gate_kernel, grid=(count // rows,), in_specs=[pl.BlockSpec...]
    ppermute x0 -> x3, waiting for transfers between devices: none -> 29.8 us  [gather_columns(): lax.ppermute(part, axis, [(i, i ^ m) for i in range(count)])]
    ppermute x32, waiting for transfers between devices: 143 us -> 128 us  [partner(): lax.ppermute(part, 'tp', [(i, i ^ mask) for i in range(lax.axis_size('tp'...]
    ppermute x17 -> x20, waiting for transfers between devices: 11.1 us -> 0.95 us  [swap(): return lax.ppermute(part, 'ctx', [(0, 1), (1, 0)])]
    ppermute x6, waiting for transfers between devices: 0.02 us -> 6.54 us  [small_sum(): lax.ppermute(part, axis, [(i, i ^ m) for i in range(count)])]
  transfers between devices with their start and end apart: 63 -> 68, of which waited for: 32 -> 31; matrix products, arithmetic and copies ran while one was open for 30% -> 18% of each run, Pallas kernels for 18% -> 35%
where the time goes in v4:
time: 635 us; the launch traced here: 623 us
  Pallas kernels  225 us (35%)
  waiting for transfers between devices  210 us (33%)
  other arithmetic  76.5 us (12%)
  starting transfers between devices  50.8 us (8%)
  local copies, waits for them, and re-layouts  44.1 us (7%)
  between operations  16.8 us (3%)
    ppermute x32, waiting for transfers between devices, partner(): lax.ppermute(part, 'tp', [(i, i ^ mask) for i in range(lax.axis_size('tp'...  128 us
    pallas_call x11, Pallas kernels, product(): pl.pallas_call(functools.partial(product_kernel, dims, parts), grid=(coun...  110 us
    all_gather x3, waiting for transfers between devices, gather(): return lax.all_gather(part, axes, axis=dim, tiled=True)  37.9 us
    ppermute x32, starting transfers between devices, partner(): lax.ppermute(part, 'tp', [(i, i ^ mask) for i in range(lax.axis_size('tp'...  32.8 us
    ppermute x3, waiting for transfers between devices, gather_columns(): lax.ppermute(part, axis, [(i, i ^ m) for i in range(count)])  29.8 us
    pallas_call x1, Pallas kernels, mixer_backward(): pl.pallas_call(functools.partial(backward_kernel, heads, chunks), grid_sp...  22.7 us
    pallas_call x1, Pallas kernels, gate_product(): pl.pallas_call(gate_kernel, grid=(count // rows,), in_specs=[pl.BlockSpec...  19.4 us
    pallas_call x1, Pallas kernels, weight_sum_product(): pl.pallas_call(weight_sum_kernel, grid=(count // rows,), in_specs=[a_spec...  18.7 us
  transfers between devices with their start and end apart: 68, of which 31 were waited for; matrix products, arithmetic and copies ran while one was open for 18% of the time, Pallas kernels for 35%

profile of v4, /device:TPU:0, one launch (start us, length us, event | category | flops | bytes accessed | tf_op | source)
XLA Modules:
  0.0 623.4 jit_solution(16405750499117402181)
XLA Ops:
  20.9 8.5 %multiply_convert_fusion.own_ref = bf16[1024,2048]{1,0:T(8,128)(2,1)} fusion(f32[2048]{0:T(1024)S(1)} %copy-done.38, f32[1024]{0:T(1024)S(1)} %add_rsqrt_fusion, bf16[256,2048]{1,0:T(8,128)(2,1)S(1)} %get-tuple-element.187, bf16[256,2048]{1,0:T(8,128)(2,1)S(1)} %get-tuple-element.188, bf16[256,2048]{1,0:T(8,128)(2,1)S(1)} %get-tuple-element.186, ...), kind=kLoop, calls=%fused_computation.1 | loop fusion | flops 23068672 | bytes 8400896 | tf_op jit(solution)/shard_map/convert_element_type | solution.py:839
  31.8 2.7 collective-permute-start.1
  34.5 2.6 collective-permute-start.2
  41.0 19.2 %collective-permute-done.1 = bf16[256,512]{1,0:T(8,128)(2,1)S(1)} collective-permute-done((bf16[256,512]{1,0:T(8,128)(2,1)}, bf16[256,512]{1,0:T(8,128)(2,1)S(1)}, u32[]{:S(2)}, u32[]{:S(2)}) %collective-permute-start.1) | collective-permute-done | bytes 262176 | tf_op jit(solution)/shard_map/ppermute | solution.py:656
  60.9 4.9 collective-permute-done.2
  66.5 5.7 collective-permute-done.3
  73.0 8.5 %pad_maximum_fusion.a_ref = bf16[2048,2048]{1,0:T(8,128)(2,1)} fusion(bf16[1024,2048]{1,0:T(8,128)(2,1)} %collective-permute-done.other_ref, bf16[1024,2048]{1,0:T(8,128)(2,1)} %multiply_convert_fusion.own_ref), kind=kLoop, calls=%fused_computation | loop fusion | flops 16777216 | bytes 16777216 | tf_op jit(solution)/shard_map/concatenate | solution.py:841
  81.5 34.9 %all-gather.4.cloned.1.call-done.b_ref.weight_ref = bf16[2048,1024]{1,0:T(8,128)(2,1)} async-done(((bf16[512,1024]{1,0:T(8,128)(2,1)}), bf16[2048,1024]{1,0:T(8,128)(2,1)}) %all-gather.4.cloned.1.call-update) | async-done | bytes 4194320 | tf_op jit(solution)/shard_map/all_gather | solution.py:646
  116.4 13.7 %product.11.pre_ref = f32[2048,1024]{1,0:T(8,128)} custom-call(bf16[2048,2048]{1,0:T(8,128)(2,1)} %pad_maximum_fusion.a_ref, bf16[2048,1024]{1,0:T(8,128)(2,1)} %all-gather.4.cloned.1.call-done.b_ref.weight_ref), custom_call_target="tpu_custom_call" | custom-call | flops 17179869184 | bytes 1048576 | tf_op jit(solution)/shard_map/product/pallas_call | solution.py:422
  130.2 14.3 %mixer_forward.1 = (bf16[2048,256]{1,0:T(8,128)(2,1)}, f32[2048,256]{1,0:T(8,128)}, f32[16,2,128,128]{3,2,1,0:T(8,128)}) custom-call(s32[8]{0:T(128)} %iota_xor_fusion.order_ref, s32[1]{0:T(128)S(6)} %copy.51.split_ref, f32[2048,1024]{1,0:T(8,128)} %product.11.pre_ref, f32[1,256]{1,0:T(1,128)} %bitcast.24, f32[1,256]{1,0:T(1,128)} %bitcast.22, f32[1,256]{1,0:T(1,128)} %bitcast.26), custom_call_target="tpu_custom_call" | custom-call | flops 14680064000 | bytes 1048576 | tf_op jit(solution)/shard_map/mixer_forward/pallas_call | solution.py:196
  144.5 4.6 product.13
  149.6 4.8 product.12
  165.3 2.6 maximum_convert_fusion
  167.9 16.5 %collective-permute-done.9 = bf16[256,2048]{1,0:T(8,128)(2,1)} collective-permute-done((bf16[256,2048]{1,0:T(8,128)(2,1)}, bf16[256,2048]{1,0:T(8,128)(2,1)}, u32[]{:S(2)}, u32[]{:S(2)}) %collective-permute-start.9) | collective-permute-done | bytes 1048608 | tf_op jit(solution)/shard_map/ppermute | solution.py:700
  184.4 3.7 collective-permute-done.7
  193.0 10.7 %collective-permute-done.10 = bf16[128,2048]{1,0:T(8,128)(2,1)S(1)} collective-permute-done((bf16[128,2048]{1,0:T(8,128)(2,1)S(1)}, bf16[128,2048]{1,0:T(8,128)(2,1)S(1)}, u32[]{:S(2)}, u32[]{:S(2)}) %collective-permute-start.10) | collective-permute-done | bytes 524320 | tf_op jit(solution)/shard_map/ppermute | solution.py:700
  212.5 18.7 %collective-permute-done.13 = bf16[256,2048]{1,0:T(8,128)(2,1)S(1)} collective-permute-done((bf16[256,2048]{1,0:T(8,128)(2,1)}, bf16[256,2048]{1,0:T(8,128)(2,1)S(1)}, u32[]{:S(2)}, u32[]{:S(2)}) %collective-permute-start.13) | collective-permute-done | bytes 1048608 | tf_op jit(solution)/shard_map/ppermute | solution.py:700
  238.3 5.3 collective-permute-done.14
  245.3 2.6 collective-permute-done.15
  252.8 19.4 %gate_product.1 = (f32[1024,2816]{1,0:T(8,128)}, bf16[1024,1408]{1,0:T(8,128)(2,1)}) custom-call(bf16[1024,2048]{1,0:T(8,128)(2,1)} %constant_dynamic-update-slice_fusion.low_ref.a_ref, bf16[2048,2816]{1,0:T(8,128)(2,1)} %all-gather.6.cloned.1.call-done.weight_ref.b_ref), custom_call_target="tpu_custom_call" | custom-call | flops 23622320128 | bytes 1048576 | tf_op jit(solution)/shard_map/gate_product/pallas_call | solution.py:448
  272.2 10.3 %product.14.refs_3_ = bf16[1408,2048]{1,0:T(8,128)(2,1)} custom-call(bf16[1024,1408]{1,0:T(8,128)(2,1)} %get-tuple-element.111.a_ref, bf16[1024,2048]{1,0:T(8,128)(2,1)} %dynamic-slice_dynamic-update-slice_fusion.1.b_ref.refs_0_), custom_call_target="tpu_custom_call" | custom-call | flops 11811160064 | bytes 1048576 | tf_op jit(solution)/shard_map/product/pallas_call | solution.py:422
  283.0 2.9 all-gather.8.cloned.1.call-done.refs_1_.b_ref
  285.9 14.7 %hidden_back.1.a_ref.b_ref = bf16[1024,2816]{1,0:T(8,128)(2,1)} custom-call(bf16[1024,2048]{1,0:T(8,128)(2,1)} %dynamic-slice_dynamic-update-slice_fusion.1.b_ref.refs_0_, bf16[1408,2048]{1,0:T(8,128)(2,1)} %all-gather.8.cloned.1.call-done.refs_1_.b_ref, f32[1024,2816]{1,0:T(8,128)} %get-tuple-element.112.refs_2_, bf16[1408,2048]{1,0:T(8,128)(2,1)} %product.14.refs_3_), custom_call_target="tpu_custom_call" | custom-call | flops 11811160064 | bytes 1048576 | tf_op jit(solution)/shard_map/hidden_back/pallas_call | solution.py:483
  300.6 10.5 %product.15 = (bf16[256,2048]{1,0:T(8,128)(2,1)}, bf16[256,2048]{1,0:T(8,128)(2,1)}) custom-call(bf16[1024,2816]{1,0:T(8,128)(2,1)} %hidden_back.1.a_ref.b_ref, bf16[2048,2816]{1,0:T(8,128)(2,1)} %all-gather.6.cloned.1.call-done.weight_ref.b_ref), custom_call_target="tpu_custom_call" | custom-call | flops 11811160064 | bytes 1048576 | tf_op jit(solution)/shard_map/product/pallas_call | solution.py:422
  314.1 12.0 %product.20 = bf16[2048,1408]{1,0:T(8,128)(2,1)} custom-call(bf16[1024,2048]{1,0:T(8,128)(2,1)} %constant_dynamic-update-slice_fusion.low_ref.a_ref, bf16[1024,2816]{1,0:T(8,128)(2,1)} %hidden_back.1.a_ref.b_ref), custom_call_target="tpu_custom_call" | custom-call | flops 11811160064 | bytes 1048576 | tf_op jit(solution)/shard_map/product/pallas_call | solution.py:422
  326.1 10.8 %product.16.refs_0_ = bf16[512,2048]{1,0:T(8,128)(2,1)} custom-call(bf16[1024,2816]{1,0:T(8,128)(2,1)} %hidden_back.1.a_ref.b_ref, bf16[2048,2816]{1,0:T(8,128)(2,1)} %all-gather.6.cloned.1.call-done.weight_ref.b_ref, bf16[256,2048]{1,0:T(8,128)(2,1)} %get-tuple-element.113.refs_0_, bf16[256,2048]{1,0:T(8,128)(2,1)} %get-tuple-element.114.refs_1_), custom_call_target="tpu_custom_call" | custom-call | flops 11811160064 | bytes 1048576 | tf_op jit(solution)/shard_map/product/pallas_call | solution.py:422
  338.1 2.7 add_convert_fusion.13
  342.9 11.3 %product.17 = (bf16[256,2048]{1,0:T(8,128)(2,1)}, bf16[256,2048]{1,0:T(8,128)(2,1)}, bf16[256,2048]{1,0:T(8,128)(2,1)}, bf16[256,2048]{1,0:T(8,128)(2,1)}) custom-call(bf16[1024,1408]{1,0:T(8,128)(2,1)} %get-tuple-element.111.a_ref, bf16[1408,2048]{1,0:T(8,128)(2,1)} %all-gather.8.cloned.1.call-done.refs_1_.b_ref, bf16[512,2048]{1,0:T(8,128)(2,1)} %product.16.refs_0_), custom_call_target="tpu_custom_call" | custom-call | flops 11811160064 | bytes 1048576 | tf_op jit(solution)/shard_map/product/pallas_call | solution.py:422
  364.5 22.0 %collective-permute-done.20.refs_2_ = bf16[256,2048]{1,0:T(8,128)(2,1)} collective-permute-done((bf16[256,2048]{1,0:T(8,128)(2,1)S(1)}, bf16[256,2048]{1,0:T(8,128)(2,1)}, u32[]{:S(2)}, u32[]{:S(2)}) %collective-permute-start.20) | collective-permute-done | bytes 1048608 | tf_op jit(solution)/shard_map/ppermute | solution.py:700
  392.0 12.0 %product.21 = bf16[2048,1408]{1,0:T(8,128)(2,1)} custom-call(bf16[1024,2048]{1,0:T(8,128)(2,1)} %constant_dynamic-update-slice_fusion.low_ref.a_ref, bf16[1024,2816]{1,0:T(8,128)(2,1)} %hidden_back.1.a_ref.b_ref), custom_call_target="tpu_custom_call" | custom-call | flops 11811160064 | bytes 1048576 | tf_op jit(solution)/shard_map/product/pallas_call | solution.py:422
  404.3 6.4 %early_product.1.early_ref = f32[2048,256]{1,0:T(8,128)} custom-call(bf16[256,2048]{1,0:T(8,128)(2,1)} %constant_dynamic-update-slice_fusion.5.b_ref, bf16[256,2048]{1,0:T(8,128)(2,1)} %copy-done.32, bf16[256,2048]{1,0:T(8,128)(2,1)} %collective-permute-done.22.refs_1_, bf16[256,2048]{1,0:T(8,128)(2,1)} %collective-permute-done.20.refs_2_, ...), custom_call_target="tpu_custom_call" | custom-call | flops 3221225472 | bytes 1048576 | tf_op jit(solution)/shard_map/early_product/pallas_call | solution.py:575
  416.3 4.2 late_product.1.grad_ref
  420.5 22.7 %mixer_backward.1 = (bf16[2048,1024]{1,0:T(8,128)(2,1)}, f32[8,256]{1,0:T(8,128)}) custom-call(s32[8]{0:T(128)} %iota_xor_fusion.order_ref, s32[1]{0:T(128)S(6)} %copy.51.split_ref, f32[2048,1024]{1,0:T(8,128)} %product.11.pre_ref, f32[2048,256]{1,0:T(8,128)} %get-tuple-element.128.mixed_ref, f32[2048,256]{1,0:T(8,128)} %late_product.1.grad_ref, ...), custom_call_target="tpu_custom_call" | custom-call | flops 23068672000 | bytes 1048576 | tf_op jit(solution)/shard_map/mixer_backward/pallas_call | solution.py:365
  446.5 9.7 %product.18 = (bf16[256,2048]{1,0:T(8,128)(2,1)}, bf16[256,2048]{1,0:T(8,128)(2,1)}, bf16[256,2048]{1,0:T(8,128)(2,1)}, bf16[256,2048]{1,0:T(8,128)(2,1)}) custom-call(bf16[2048,1024]{1,0:T(8,128)(2,1)} %get-tuple-element.132.a_ref.b_ref, bf16[2048,1024]{1,0:T(8,128)(2,1)} %all-gather.4.cloned.1.call-done.b_ref.weight_ref, bf16[256,2048]{1,0:T(8,128)(2,1)} %copy-done.27, ...), custom_call_target="tpu_custom_call" | custom-call | flops 8589934592 | bytes 1048576 | tf_op jit(solution)/shard_map/product/pallas_call | solution.py:422
  463.7 9.8 %product.19 = (bf16[256,2048]{1,0:T(8,128)(2,1)}, bf16[256,2048]{1,0:T(8,128)(2,1)}, bf16[256,2048]{1,0:T(8,128)(2,1)}, bf16[256,2048]{1,0:T(8,128)(2,1)}) custom-call(bf16[2048,1024]{1,0:T(8,128)(2,1)} %get-tuple-element.132.a_ref.b_ref, bf16[2048,1024]{1,0:T(8,128)(2,1)} %all-gather.4.cloned.1.call-done.b_ref.weight_ref, ...), custom_call_target="tpu_custom_call" | custom-call | flops 8589934592 | bytes 1048576 | tf_op jit(solution)/shard_map/product/pallas_call | solution.py:422
  481.8 5.7 collective-permute-done.33.refs_10_.near_ref
  488.5 18.7 %weight_sum_product.1 = (bf16[2048,1280]{1,0:T(8,128)(2,1)}, f32[2048,128]{1,0:T(8,128)}) custom-call(bf16[1024,2048]{1,0:T(8,128)(2,1)} %multiply_convert_fusion.own_ref, bf16[1024,2048]{1,0:T(8,128)(2,1)} %collective-permute-done.other_ref, bf16[2048,1024]{1,0:T(8,128)(2,1)} %get-tuple-element.132.a_ref.b_ref, ...), custom_call_target="tpu_custom_call" | custom-call | flops 21474836480 | bytes 1048576 | tf_op jit(solution)/shard_map/weight_sum_product/pallas_call | solution.py:526
  516.3 2.3 collective-permute-done.52
  519.5 3.6 collective-permute-start.56
  525.1 2.8 collective-permute-done.55
  533.4 12.4 %collective-permute-done.40 = bf16[128,2048]{1,0:T(8,128)(2,1)S(1)} collective-permute-done((bf16[128,2048]{1,0:T(8,128)(2,1)S(1)}, bf16[128,2048]{1,0:T(8,128)(2,1)S(1)}, u32[]{:S(2)}, u32[]{:S(2)}) %collective-permute-start.40) | collective-permute-done | bytes 524320 | tf_op jit(solution)/shard_map/ppermute | solution.py:700
  553.9 2.9 add_convert_fusion.own_ref
  556.9 3.7 collective-permute-done.43.bottom_ref
  564.2 4.6 placed_blocks.2
  568.8 17.6 %collective-permute-done.46.near_ref = bf16[256,2048]{1,0:T(8,128)(2,1)} collective-permute-done((bf16[256,2048]{1,0:T(8,128)(2,1)S(1)}, bf16[256,2048]{1,0:T(8,128)(2,1)}, u32[]{:S(2)}, u32[]{:S(2)}) %collective-permute-start.46) | collective-permute-done | bytes 1048608 | tf_op jit(solution)/shard_map/ppermute | solution.py:700
  594.2 7.1 %reduce-scatter.11.cloned.1.call-done.own_ref = bf16[512,1280]{1,0:T(8,128)(2,1)} async-done(((bf16[2048,1280]{1,0:T(8,128)(2,1)}), bf16[512,1280]{1,0:T(8,128)(2,1)}) %reduce-scatter.11.cloned.1.call-update) | async-done | bytes 1310736 | tf_op jit(solution)/shard_map/reduce_scatter | solution.py:662
  602.2 5.8 placed_blocks.3
  612.0 4.3 joined_columns.1
  (326 shorter events, 148.8 us)
Async XLA Ops:
  7.2 109.2 %all-gather.4.cloned.1.call-start = ((), (), s32[]{:S(2)}) async-start(), calls=%async_computation.4 | async-start | bytes 5242880 | tf_op jit(solution)/shard_map/all_gather | solution.py:646
  10.7 242.1 %all-gather.6.cloned.1.call-start = ((), (), s32[]{:S(2)}) async-start(), calls=%async_computation.5 | async-start | bytes 12976128 | tf_op jit(solution)/shard_map/all_gather | solution.py:646
  13.1 272.8 %all-gather.8.cloned.1.call-start = ((), (), s32[]{:S(2)}) async-start(), calls=%async_computation.6 | async-start | bytes 6488064 | tf_op jit(solution)/shard_map/all_gather | solution.py:646
  29.4 43.6 %collective-permute-start = (bf16[1024,2048]{1,0:T(8,128)(2,1)}, bf16[1024,2048]{1,0:T(8,128)(2,1)}, u32[]{:S(2)}, u32[]{:S(2)}) collective-permute-start(bf16[1024,2048]{1,0:T(8,128)(2,1)} %multiply_convert_fusion.own_ref), channel_id=1, source_target_pairs={{0,4},{4,0},{1,5},{5,1},{2,6},{6,2},{3,7},{7,3},{8,12},{12,8},{9,1... | collective-permute-start | bytes 12582920 | tf_op jit(solution)/shard_map/ppermute | solution.py:690
  31.8 28.4 %collective-permute-start.1 = (bf16[256,512]{1,0:T(8,128)(2,1)}, bf16[256,512]{1,0:T(8,128)(2,1)S(1)}, u32[]{:S(2)}, u32[]{:S(2)}) collective-permute-start(bf16[256,512]{1,0:T(8,128)(2,1)} %get-tuple-element.184), channel_id=1, source_target_pairs={{0,8},{8,0},{16,24},{24,16},{1,9},{9,1},{17,25},{25,17},{2,10},{10... | collective-permute-start | bytes 786440 | tf_op jit(solution)/shard_map/ppermute | solution.py:656
  34.5 31.3 %collective-permute-start.2 = (bf16[256,512]{1,0:T(8,128)(2,1)}, bf16[256,512]{1,0:T(8,128)(2,1)S(1)}, u32[]{:S(2)}, u32[]{:S(2)}) collective-permute-start(bf16[256,512]{1,0:T(8,128)(2,1)} %get-tuple-element.184), channel_id=1, source_target_pairs={{0,16},{8,24},{16,0},{24,8},{1,17},{9,25},{17,1},{25,9},{2,18},{10... | collective-permute-start | bytes 786440 | tf_op jit(solution)/shard_map/ppermute | solution.py:656
  37.1 35.1 %collective-permute-start.3 = (bf16[256,512]{1,0:T(8,128)(2,1)}, bf16[256,512]{1,0:T(8,128)(2,1)S(1)}, u32[]{:S(2)}, u32[]{:S(2)}) collective-permute-start(bf16[256,512]{1,0:T(8,128)(2,1)} %get-tuple-element.184), channel_id=1, source_target_pairs={{0,24},{8,16},{16,8},{24,0},{1,25},{9,17},{17,9},{25,1},{2,26},{10... | collective-permute-start | bytes 786440 | tf_op jit(solution)/shard_map/ppermute | solution.py:656
  158.5 25.8 %collective-permute-start.9 = (bf16[256,2048]{1,0:T(8,128)(2,1)}, bf16[256,2048]{1,0:T(8,128)(2,1)}, u32[]{:S(2)}, u32[]{:S(2)}) collective-permute-start(bf16[256,2048]{1,0:T(8,128)(2,1)} %pad_maximum_fusion.4), channel_id=1, source_target_pairs={{0,2},{1,3},{2,0},{3,1},{4,6},{5,7},{6,4},{7,5},{8,10},{9,11},{10,... | collective-permute-start | bytes 3145736 | tf_op jit(solution)/shard_map/ppermute | solution.py:700
  162.5 25.6 %collective-permute-start.7 = (bf16[256,2048]{1,0:T(8,128)(2,1)}, bf16[256,2048]{1,0:T(8,128)(2,1)}, u32[]{:S(2)}, u32[]{:S(2)}) collective-permute-start(bf16[256,2048]{1,0:T(8,128)(2,1)} %pad_maximum_fusion.3), channel_id=1, source_target_pairs={{0,1},{1,0},{2,3},{3,2},{4,5},{5,4},{6,7},{7,6},{8,9},{9,8},{10,11... | collective-permute-start | bytes 3145736 | tf_op jit(solution)/shard_map/ppermute | solution.py:700
  164.9 193.7 %reduce-scatter.5.cloned.1.call-start = ((), (), s32[]{:S(2)}) async-start(), calls=%async_computation.7 | async-start | bytes 6488064 | tf_op jit(solution)/shard_map/reduce_scatter | solution.py:662
  165.2 27.4 %collective-permute-start.4 = (bf16[256,2048]{1,0:T(8,128)(2,1)}, bf16[256,2048]{1,0:T(8,128)(2,1)S(1)}, u32[]{:S(2)}, u32[]{:S(2)}) collective-permute-start(bf16[256,2048]{1,0:T(8,128)(2,1)} %get-tuple-element.98), channel_id=1, source_target_pairs={{0,4},{4,0},{1,5},{5,1},{2,6},{6,2},{3,7},{7,3},{8,12},{12,8},{9,1... | collective-permute-start | bytes 3145736 | tf_op jit(solution)/shard_map/ppermute | solution.py:690
  190.4 13.3 %collective-permute-start.10 = (bf16[128,2048]{1,0:T(8,128)(2,1)S(1)}, bf16[128,2048]{1,0:T(8,128)(2,1)S(1)}, u32[]{:S(2)}, u32[]{:S(2)}) collective-permute-start(bf16[128,2048]{1,0:T(8,128)(2,1)S(1)} %add_convert_fusion.16), channel_id=1, source_target_pairs={{0,2},{1,3},{2,0},{3,1},{4,6},{5,7},{6,4},{7,5},{8,10},{9,11},{10,... | collective-permute-start | bytes 1572872 | tf_op jit(solution)/shard_map/ppermute | solution.py:700
  207.6 23.7 %collective-permute-start.13 = (bf16[256,2048]{1,0:T(8,128)(2,1)}, bf16[256,2048]{1,0:T(8,128)(2,1)S(1)}, u32[]{:S(2)}, u32[]{:S(2)}) collective-permute-start(bf16[256,2048]{1,0:T(8,128)(2,1)} %multiply_convert_fusion.1), channel_id=1, source_target_pairs={{0,2},{1,3},{2,0},{3,1},{4,6},{5,7},{6,4},{7,5},{8,10},{9,11},{10,... | collective-permute-start | bytes 3145736 | tf_op jit(solution)/shard_map/ppermute | solution.py:700
  209.1 25.6 %collective-permute-start.12 = (bf16[256,2048]{1,0:T(8,128)(2,1)}, bf16[256,2048]{1,0:T(8,128)(2,1)}, u32[]{:S(2)}, u32[]{:S(2)}) collective-permute-start(bf16[256,2048]{1,0:T(8,128)(2,1)} %multiply_convert_fusion.1), channel_id=1, source_target_pairs={{0,1},{1,0},{2,3},{3,2},{4,5},{5,4},{6,7},{7,6},{8,9},{9,8},{10,11... | collective-permute-start | bytes 3145736 | tf_op jit(solution)/shard_map/ppermute | solution.py:700
  282.5 224.7 %reduce-scatter.7.cloned.1.call-start = ((), (), s32[]{:S(2)}) async-start(), calls=%async_computation.8 | async-start | bytes 6488064 | tf_op jit(solution)/shard_map/reduce_scatter | solution.py:662
  311.1 25.7 %collective-permute-start.16 = (bf16[256,2048]{1,0:T(8,128)(2,1)}, bf16[256,2048]{1,0:T(8,128)(2,1)S(1)}, u32[]{:S(2)}, u32[]{:S(2)}) collective-permute-start(bf16[256,2048]{1,0:T(8,128)(2,1)} %get-tuple-element.113.refs_0_), channel_id=1, source_target_pairs={{0,1},{1,0},{2,3},{3,2},{4,5},{5,4},{6,7},{7,6},{8,9},{9,8},{10,11... | collective-permute-start | bytes 3145736 | tf_op jit(solution)/shard_map/ppermute | solution.py:700
  312.6 25.4 %collective-permute-start.17 = (bf16[256,2048]{1,0:T(8,128)(2,1)}, bf16[256,2048]{1,0:T(8,128)(2,1)}, u32[]{:S(2)}, u32[]{:S(2)}) collective-permute-start(bf16[256,2048]{1,0:T(8,128)(2,1)} %get-tuple-element.114.refs_1_), channel_id=1, source_target_pairs={{0,2},{1,3},{2,0},{3,1},{4,6},{5,7},{6,4},{7,5},{8,10},{9,11},{10,... | collective-permute-start | bytes 3145736 | tf_op jit(solution)/shard_map/ppermute | solution.py:700
  338.1 169.9 %reduce-scatter.9.cloned.1.call-start = ((), (), s32[]{:S(2)}) async-start(), calls=%async_computation.9 | async-start | bytes 6488064 | tf_op jit(solution)/shard_map/reduce_scatter | solution.py:662
  340.8 13.4 %collective-permute-start.18 = (bf16[128,2048]{1,0:T(8,128)(2,1)}, bf16[128,2048]{1,0:T(8,128)(2,1)S(1)}, u32[]{:S(2)}, u32[]{:S(2)}) collective-permute-start(bf16[128,2048]{1,0:T(8,128)(2,1)} %get-tuple-element.118), channel_id=1, source_target_pairs={{0,2},{1,3},{2,0},{3,1},{4,6},{5,7},{6,4},{7,5},{8,10},{9,11},{10,... | collective-permute-start | bytes 1572872 | tf_op jit(solution)/shard_map/ppermute | solution.py:700
  342.3 13.1 %collective-permute-start.19 = (bf16[128,2048]{1,0:T(8,128)(2,1)}, bf16[128,2048]{1,0:T(8,128)(2,1)}, u32[]{:S(2)}, u32[]{:S(2)}) collective-permute-start(bf16[128,2048]{1,0:T(8,128)(2,1)} %get-tuple-element.119), channel_id=1, source_target_pairs={{0,1},{1,0},{2,3},{3,2},{4,5},{5,4},{6,7},{7,6},{8,9},{9,8},{10,11... | collective-permute-start | bytes 1572872 | tf_op jit(solution)/shard_map/ppermute | solution.py:700
  362.8 23.7 %collective-permute-start.20 = (bf16[256,2048]{1,0:T(8,128)(2,1)S(1)}, bf16[256,2048]{1,0:T(8,128)(2,1)}, u32[]{:S(2)}, u32[]{:S(2)}) collective-permute-start(bf16[256,2048]{1,0:T(8,128)(2,1)S(1)} %fusion.8.refs_0_), channel_id=1, source_target_pairs={{0,2},{1,3},{2,0},{3,1},{4,6},{5,7},{6,4},{7,5},{8,10},{9,11},{10,... | collective-permute-start | bytes 3145736 | tf_op jit(solution)/shard_map/ppermute | solution.py:700
  363.5 25.5 %collective-permute-start.22 = (bf16[256,2048]{1,0:T(8,128)(2,1)S(1)}, bf16[256,2048]{1,0:T(8,128)(2,1)}, u32[]{:S(2)}, u32[]{:S(2)}) collective-permute-start(bf16[256,2048]{1,0:T(8,128)(2,1)S(1)} %fusion.8.refs_0_), channel_id=1, source_target_pairs={{0,1},{1,0},{2,3},{3,2},{4,5},{5,4},{6,7},{7,6},{8,9},{9,8},{10,11... | collective-permute-start | bytes 3145736 | tf_op jit(solution)/shard_map/ppermute | solution.py:700
  364.5 39.9 %collective-permute-start.25 = (bf16[256,2048]{1,0:T(8,128)(2,1)S(1)}, bf16[256,2048]{1,0:T(8,128)(2,1)}, u32[]{:S(2)}, u32[]{:S(2)}) collective-permute-start(bf16[256,2048]{1,0:T(8,128)(2,1)S(1)} %fusion.8.refs_0_), channel_id=1, source_target_pairs={{0,4},{4,0},{1,5},{5,1},{2,6},{6,2},{3,7},{7,3},{8,12},{12,8},{9,1... | collective-permute-start | bytes 3145736 | tf_op jit(solution)/shard_map/ppermute | solution.py:690
  388.4 22.4 %collective-permute-start.21 = (bf16[128,2048]{1,0:T(8,128)(2,1)}, bf16[128,2048]{1,0:T(8,128)(2,1)}, u32[]{:S(2)}, u32[]{:S(2)}) collective-permute-start(bf16[128,2048]{1,0:T(8,128)(2,1)} %slice.297), channel_id=1, source_target_pairs={{0,1},{1,0},{2,3},{3,2},{4,5},{5,4},{6,7},{7,6},{8,9},{9,8},{10,11... | collective-permute-start | bytes 1572872 | tf_op jit(solution)/shard_map/ppermute | solution.py:700
  390.9 19.9 %collective-permute-start.23 = (bf16[128,2048]{1,0:T(8,128)(2,1)}, bf16[128,2048]{1,0:T(8,128)(2,1)}, u32[]{:S(2)}, u32[]{:S(2)}) collective-permute-start(bf16[128,2048]{1,0:T(8,128)(2,1)} %slice.298), channel_id=1, source_target_pairs={{0,2},{1,3},{2,0},{3,1},{4,6},{5,7},{6,4},{7,5},{8,10},{9,11},{10,... | collective-permute-start | bytes 1572872 | tf_op jit(solution)/shard_map/ppermute | solution.py:700
  404.1 197.3 %reduce-scatter.11.cloned.1.call-start = ((), (), s32[]{:S(2)}) async-start(), calls=%async_computation.10 | async-start | bytes 6553600 | tf_op jit(solution)/shard_map/reduce_scatter | solution.py:662
  411.3 31.9 %collective-permute-start.30 = (bf16[256,2048]{1,0:T(8,128)(2,1)}, bf16[256,2048]{1,0:T(8,128)(2,1)S(1)}, u32[]{:S(2)}, u32[]{:S(2)}) collective-permute-start(bf16[256,2048]{1,0:T(8,128)(2,1)} %get-tuple-element.135), channel_id=1, source_target_pairs={{0,2},{1,3},{2,0},{3,1},{4,6},{5,7},{6,4},{7,5},{8,10},{9,11},{10,... | collective-permute-start | bytes 3145736 | tf_op jit(solution)/shard_map/ppermute | solution.py:700
  412.8 30.5 %collective-permute-start.24 = (bf16[256,2048]{1,0:T(8,128)(2,1)}, bf16[256,2048]{1,0:T(8,128)(2,1)S(1)}, u32[]{:S(2)}, u32[]{:S(2)}) collective-permute-start(bf16[256,2048]{1,0:T(8,128)(2,1)} %get-tuple-element.125), channel_id=1, source_target_pairs={{0,1},{1,0},{2,3},{3,2},{4,5},{5,4},{6,7},{7,6},{8,9},{9,8},{10,11... | collective-permute-start | bytes 3145736 | tf_op jit(solution)/shard_map/ppermute | solution.py:700
  445.3 13.6 %collective-permute-start.31 = (bf16[128,2048]{1,0:T(8,128)(2,1)}, bf16[128,2048]{1,0:T(8,128)(2,1)S(1)}, u32[]{:S(2)}, u32[]{:S(2)}) collective-permute-start(bf16[128,2048]{1,0:T(8,128)(2,1)} %add_convert_fusion.12), channel_id=1, source_target_pairs={{0,2},{1,3},{2,0},{3,1},{4,6},{5,7},{6,4},{7,5},{8,10},{9,11},{10,... | collective-permute-start | bytes 1572872 | tf_op jit(solution)/shard_map/ppermute | solution.py:700
  445.6 13.4 %collective-permute-start.32 = (bf16[128,2048]{1,0:T(8,128)(2,1)}, bf16[128,2048]{1,0:T(8,128)(2,1)}, u32[]{:S(2)}, u32[]{:S(2)}) collective-permute-start(bf16[128,2048]{1,0:T(8,128)(2,1)} %add_convert_fusion.11), channel_id=1, source_target_pairs={{0,1},{1,0},{2,3},{3,2},{4,5},{5,4},{6,7},{7,6},{8,9},{9,8},{10,11... | collective-permute-start | bytes 1572872 | tf_op jit(solution)/shard_map/ppermute | solution.py:700
  456.3 17.3 %collective-permute-start.37 = (bf16[256,2048]{1,0:T(8,128)(2,1)}, bf16[256,2048]{1,0:T(8,128)(2,1)}, u32[]{:S(2)}, u32[]{:S(2)}) collective-permute-start(bf16[256,2048]{1,0:T(8,128)(2,1)} %get-tuple-element.149), channel_id=1, source_target_pairs={{0,4},{4,0},{1,5},{5,1},{2,6},{6,2},{3,7},{7,3},{8,12},{12,8},{9,1... | collective-permute-start | bytes 3145736 | tf_op jit(solution)/shard_map/ppermute | solution.py:690
  456.3 19.3 %collective-permute-start.35 = (bf16[256,2048]{1,0:T(8,128)(2,1)}, bf16[256,2048]{1,0:T(8,128)(2,1)S(1)}, u32[]{:S(2)}, u32[]{:S(2)}) collective-permute-start(bf16[256,2048]{1,0:T(8,128)(2,1)} %get-tuple-element.145), channel_id=1, source_target_pairs={{0,4},{4,0},{1,5},{5,1},{2,6},{6,2},{3,7},{7,3},{8,12},{12,8},{9,1... | collective-permute-start | bytes 3145736 | tf_op jit(solution)/shard_map/ppermute | solution.py:690
  456.8 21.0 %collective-permute-start.36 = (bf16[256,2048]{1,0:T(8,128)(2,1)}, bf16[256,2048]{1,0:T(8,128)(2,1)S(1)}, u32[]{:S(2)}, u32[]{:S(2)}) collective-permute-start(bf16[256,2048]{1,0:T(8,128)(2,1)} %get-tuple-element.147), channel_id=1, source_target_pairs={{0,4},{4,0},{1,5},{5,1},{2,6},{6,2},{3,7},{7,3},{8,12},{12,8},{9,1... | collective-permute-start | bytes 3145736 | tf_op jit(solution)/shard_map/ppermute | solution.py:690
  461.3 26.3 %collective-permute-start.33 = (bf16[256,2048]{1,0:T(8,128)(2,1)S(1)}, bf16[256,2048]{1,0:T(8,128)(2,1)}, u32[]{:S(2)}, u32[]{:S(2)}) collective-permute-start(bf16[256,2048]{1,0:T(8,128)(2,1)S(1)} %fusion.refs_1_.own_ref), channel_id=1, source_target_pairs={{0,1},{1,0},{2,3},{3,2},{4,5},{5,4},{6,7},{7,6},{8,9},{9,8},{10,11... | collective-permute-start | bytes 3145736 | tf_op jit(solution)/shard_map/ppermute | solution.py:700
  462.3 26.2 %collective-permute-start.34 = (bf16[256,2048]{1,0:T(8,128)(2,1)S(1)}, bf16[256,2048]{1,0:T(8,128)(2,1)}, u32[]{:S(2)}, u32[]{:S(2)}) collective-permute-start(bf16[256,2048]{1,0:T(8,128)(2,1)S(1)} %fusion.refs_1_.own_ref), channel_id=1, source_target_pairs={{0,2},{1,3},{2,0},{3,1},{4,6},{5,7},{6,4},{7,5},{8,10},{9,11},{10,... | collective-permute-start | bytes 3145736 | tf_op jit(solution)/shard_map/ppermute | solution.py:700
  477.2 30.8 %collective-permute-start.39 = (bf16[256,2048]{1,0:T(8,128)(2,1)}, bf16[256,2048]{1,0:T(8,128)(2,1)S(1)}, u32[]{:S(2)}, u32[]{:S(2)}) collective-permute-start(bf16[256,2048]{1,0:T(8,128)(2,1)} %pad_maximum_fusion.6), channel_id=1, source_target_pairs={{0,2},{1,3},{2,0},{3,1},{4,6},{5,7},{6,4},{7,5},{8,10},{9,11},{10,... | collective-permute-start | bytes 3145736 | tf_op jit(solution)/shard_map/ppermute | solution.py:700
  480.4 27.6 %collective-permute-start.38 = (bf16[256,2048]{1,0:T(8,128)(2,1)}, bf16[256,2048]{1,0:T(8,128)(2,1)}, u32[]{:S(2)}, u32[]{:S(2)}) collective-permute-start(bf16[256,2048]{1,0:T(8,128)(2,1)} %pad_maximum_fusion.5), channel_id=1, source_target_pairs={{0,1},{1,0},{2,3},{3,2},{4,5},{5,4},{6,7},{7,6},{8,9},{9,8},{10,11... | collective-permute-start | bytes 3145736 | tf_op jit(solution)/shard_map/ppermute | solution.py:700
  508.1 15.0 %collective-permute-start.45 = (bf16[256,2048]{1,0:T(8,128)(2,1)}, bf16[256,2048]{1,0:T(8,128)(2,1)}, u32[]{:S(2)}, u32[]{:S(2)}) collective-permute-start(bf16[256,2048]{1,0:T(8,128)(2,1)} %get-tuple-element.143.refs_0_), channel_id=1, source_target_pairs={{0,4},{4,0},{1,5},{5,1},{2,6},{6,2},{3,7},{7,3},{8,12},{12,8},{9,1... | collective-permute-start | bytes 3145736 | tf_op jit(solution)/shard_map/ppermute | solution.py:690
  531.4 14.4 %collective-permute-start.40 = (bf16[128,2048]{1,0:T(8,128)(2,1)S(1)}, bf16[128,2048]{1,0:T(8,128)(2,1)S(1)}, u32[]{:S(2)}, u32[]{:S(2)}) collective-permute-start(bf16[128,2048]{1,0:T(8,128)(2,1)S(1)} %add_convert_fusion.10), channel_id=1, source_target_pairs={{0,2},{1,3},{2,0},{3,1},{4,6},{5,7},{6,4},{7,5},{8,10},{9,11},{10,... | collective-permute-start | bytes 1572872 | tf_op jit(solution)/shard_map/ppermute | solution.py:700
  531.4 14.4 %collective-permute-start.41 = (bf16[128,2048]{1,0:T(8,128)(2,1)S(1)}, bf16[128,2048]{1,0:T(8,128)(2,1)S(1)}, u32[]{:S(2)}, u32[]{:S(2)}) collective-permute-start(bf16[128,2048]{1,0:T(8,128)(2,1)S(1)} %add_convert_fusion.9), channel_id=1, source_target_pairs={{0,1},{1,0},{2,3},{3,2},{4,5},{5,4},{6,7},{7,6},{8,9},{9,8},{10,11... | collective-permute-start | bytes 1572872 | tf_op jit(solution)/shard_map/ppermute | solution.py:700
  532.8 24.0 %collective-permute-start.59 = (bf16[1408,256]{1,0:T(8,128)(2,1)S(1)}, bf16[1408,256]{1,0:T(8,128)(2,1)S(1)}, u32[]{:S(2)}, u32[]{:S(2)}) collective-permute-start(bf16[1408,256]{1,0:T(8,128)(2,1)S(1)} %copy-done.33), channel_id=1, source_target_pairs={{0,4},{4,0},{1,5},{5,1},{2,6},{6,2},{3,7},{7,3},{8,12},{12,8},{9,1... | collective-permute-start | bytes 2162696 | tf_op jit(solution)/shard_map/ppermute | solution.py:690
  533.3 30.7 %collective-permute-start.57 = (bf16[256,1408]{1,0:T(8,128)(2,1)S(1)}, bf16[256,1408]{1,0:T(8,128)(2,1)S(1)}, u32[]{:S(2)}, u32[]{:S(2)}) collective-permute-start(bf16[256,1408]{1,0:T(8,128)(2,1)S(1)} %copy-done.34), channel_id=1, source_target_pairs={{0,4},{4,0},{1,5},{5,1},{2,6},{6,2},{3,7},{7,3},{8,12},{12,8},{9,1... | collective-permute-start | bytes 2162696 | tf_op jit(solution)/shard_map/ppermute | solution.py:690
  546.9 13.7 %collective-permute-start.43 = (bf16[128,2048]{1,0:T(8,128)(2,1)S(1)}, bf16[128,2048]{1,0:T(8,128)(2,1)S(1)}, u32[]{:S(2)}, u32[]{:S(2)}) collective-permute-start(bf16[128,2048]{1,0:T(8,128)(2,1)S(1)} %slice.259), channel_id=1, source_target_pairs={{0,2},{1,3},{2,0},{3,1},{4,6},{5,7},{6,4},{7,5},{8,10},{9,11},{10,... | collective-permute-start | bytes 1572872 | tf_op jit(solution)/shard_map/ppermute | solution.py:700
  549.7 13.1 %collective-permute-start.42 = (bf16[128,2048]{1,0:T(8,128)(2,1)S(1)}, bf16[128,2048]{1,0:T(8,128)(2,1)S(1)}, u32[]{:S(2)}, u32[]{:S(2)}) collective-permute-start(bf16[128,2048]{1,0:T(8,128)(2,1)S(1)} %slice.258), channel_id=1, source_target_pairs={{0,1},{1,0},{2,3},{3,2},{4,5},{5,4},{6,7},{7,6},{8,9},{9,8},{10,11... | collective-permute-start | bytes 1572872 | tf_op jit(solution)/shard_map/ppermute | solution.py:700
  562.9 23.6 %collective-permute-start.46 = (bf16[256,2048]{1,0:T(8,128)(2,1)S(1)}, bf16[256,2048]{1,0:T(8,128)(2,1)}, u32[]{:S(2)}, u32[]{:S(2)}) collective-permute-start(bf16[256,2048]{1,0:T(8,128)(2,1)S(1)} %add_convert_fusion.own_ref), channel_id=1, source_target_pairs={{0,1},{1,0},{2,3},{3,2},{4,5},{5,4},{6,7},{7,6},{8,9},{9,8},{10,11... | collective-permute-start | bytes 3145736 | tf_op jit(solution)/shard_map/ppermute | solution.py:700
  563.5 25.1 %collective-permute-start.47 = (bf16[256,2048]{1,0:T(8,128)(2,1)S(1)}, bf16[256,2048]{1,0:T(8,128)(2,1)}, u32[]{:S(2)}, u32[]{:S(2)}) collective-permute-start(bf16[256,2048]{1,0:T(8,128)(2,1)S(1)} %add_convert_fusion.own_ref), channel_id=1, source_target_pairs={{0,2},{1,3},{2,0},{3,1},{4,6},{5,7},{6,4},{7,5},{8,10},{9,11},{10,... | collective-permute-start | bytes 3145736 | tf_op jit(solution)/shard_map/ppermute | solution.py:700
  587.5 13.8 %collective-permute-start.49 = (bf16[128,2048]{1,0:T(8,128)(2,1)S(1)}, bf16[128,2048]{1,0:T(8,128)(2,1)}, u32[]{:S(2)}, u32[]{:S(2)}) collective-permute-start(bf16[128,2048]{1,0:T(8,128)(2,1)S(1)} %slice.266), channel_id=1, source_target_pairs={{0,2},{1,3},{2,0},{3,1},{4,6},{5,7},{6,4},{7,5},{8,10},{9,11},{10,... | collective-permute-start | bytes 1572872 | tf_op jit(solution)/shard_map/ppermute | solution.py:700
  592.4 15.5 %collective-permute-start.58 = (bf16[256,1408]{1,0:T(8,128)(2,1)}, bf16[256,1408]{1,0:T(8,128)(2,1)S(1)}, u32[]{:S(2)}, u32[]{:S(2)}) collective-permute-start(bf16[256,1408]{1,0:T(8,128)(2,1)} %reduce-scatter.9.cloned.1.call-done), channel_id=1, source_target_pairs={{0,4},{4,0},{1,5},{5,1},{2,6},{6,2},{3,7},{7,3},{8,12},{12,8},{9,1... | collective-permute-start | bytes 2162696 | tf_op jit(solution)/shard_map/ppermute | solution.py:690
  (71 other events, 782.7 us)
Sparse Core Ops, SparseCore 0:
  10.8 105.5 all-gather.3
  118.6 106.4 all-gather.5
  226.7 59.1 all-gather.7
  288.1 63.0 reduce-scatter.4
  353.3 63.2 reduce-scatter.6
  418.7 63.2 reduce-scatter.8
  508.1 93.1 reduce-scatter.10

commit v5 on v4

--- a/solution.py
+++ b/solution.py
@@ -930,13 +930,14 @@
     input_own = after(input_own, *block_second)
     first = gather_first(input_own)
 
+    block_out = placed_blocks(block_own, *block_first, *block_second, tp_at, BF16)
+    input_second = gather_second(*[after(block, block_out) for block in first])
+    input_grad = placed_blocks(input_own, *first, *input_second, tp_at, F32)
+
     gains = jnp.concatenate([first_sum / first_gain, second_gain_grad]).reshape(-1, HEAD)
-    gains = gains + swap(gains)
-    block_out = placed_blocks(block_own, *block_first, *block_second, tp_at, BF16, wait=[gains])
-    gains = small_sum(gains, "tp")
-    input_second = gather_second(*[after(block, block_out) for block in first])
+    gains = after(gains, *input_second)
+    gains = small_sum(gains + swap(gains), "tp")
     small = small_sum(jnp.concatenate([sums[:3].reshape(-1, HEAD), gains]), "dp")
-    input_grad = placed_blocks(input_own, *first, *input_second, tp_at, F32, wait=[gains])
     cut = 3 * width // HEAD
     head_sums = in_order(small[:cut].reshape(3, width), 1)
     gain_sums = small[cut:].reshape(-1)
@@ -944,7 +945,7 @@
     all_bound = jnp.sum(all_weights * counted, axis=0)
     table_grad = all_weights * (counted - all_bound) * head_sums[2]
 
-    *mix_shards, out_shard = joined_columns(mix_sum, after(swap(mix_sum), small), ctx_at, width)
+    *mix_shards, out_shard = joined_columns(mix_sum, swap(mix_sum), ctx_at, width)
 
     return (
         block_out,

time: 635 us -> 629 us (level)
  waiting for transfers between devices: 210 us -> 194 us
    reduce_scatter x4, waiting for transfers between devices: 7.16 us -> 0.03 us  [scatter(): return lax.psum_scatter(whole, axes, scatter_dimension=dim, tiled=True)]
    unnamed x111 -> x125, local copies, waits for them, and re-layouts: 15.6 us -> 15.4 us
  transfers between devices with their start and end apart: 68 -> 68, of which waited for: 31 -> 28; matrix products, arithmetic and copies ran while one was open for 18% -> 19% of each run, Pallas kernels for 35% -> 36%
where the time goes in v5:
time: 629 us; the launch traced here: 617 us
  Pallas kernels  225 us (36%)
  waiting for transfers between devices  194 us (31%)
  other arithmetic  82.4 us (13%)
  starting transfers between devices  54.6 us (9%)
  local copies, waits for them, and re-layouts  44.7 us (7%)
  between operations  17.1 us (3%)
    ppermute x32, waiting for transfers between devices, partner(): lax.ppermute(part, 'tp', [(i, i ^ mask) for i in range(lax.axis_size('tp'...  130 us
    pallas_call x11, Pallas kernels, product(): pl.pallas_call(functools.partial(product_kernel, dims, parts), grid=(coun...  110 us
    all_gather x3, waiting for transfers between devices, gather(): return lax.all_gather(part, axes, axis=dim, tiled=True)  36.3 us
    ppermute x32, starting transfers between devices, partner(): lax.ppermute(part, 'tp', [(i, i ^ mask) for i in range(lax.axis_size('tp'...  36.2 us
    ppermute x3, waiting for transfers between devices, gather_columns(): lax.ppermute(part, axis, [(i, i ^ m) for i in range(count)])  25.3 us
    pallas_call x1, Pallas kernels, mixer_backward(): pl.pallas_call(functools.partial(backward_kernel, heads, chunks), grid_sp...  22.7 us
    pallas_call x1, Pallas kernels, gate_product(): pl.pallas_call(gate_kernel, grid=(count // rows,), in_specs=[pl.BlockSpec...  19.4 us
    pallas_call x1, Pallas kernels, weight_sum_product(): pl.pallas_call(weight_sum_kernel, grid=(count // rows,), in_specs=[a_spec...  18.8 us
  transfers between devices with their start and end apart: 68, of which 28 were waited for; matrix products, arithmetic and copies ran while one was open for 19% of the time, Pallas kernels for 36%

profile of v5, /device:TPU:0, one launch (start us, length us, event | category | flops | bytes accessed | tf_op | source)
XLA Modules:
  0.0 617.2 jit_solution(13545163156183470659)
XLA Ops:
  10.8 2.3 fusion.1
  20.8 8.5 %multiply_convert_fusion.own_ref = bf16[1024,2048]{1,0:T(8,128)(2,1)} fusion(f32[2048]{0:T(1024)S(1)} %copy-done.39, f32[1024]{0:T(1024)S(1)} %add_rsqrt_fusion, bf16[256,2048]{1,0:T(8,128)(2,1)S(1)} %get-tuple-element.187, bf16[256,2048]{1,0:T(8,128)(2,1)S(1)} %get-tuple-element.188, bf16[256,2048]{1,0:T(8,128)(2,1)S(1)} %get-tuple-element.186, ...), kind=kLoop, calls=%fused_computation.1 | loop fusion | flops 23068672 | bytes 8400896 | tf_op jit(solution)/shard_map/convert_element_type | solution.py:839
  32.6 2.7 collective-permute-start.1
  35.3 2.6 collective-permute-start.2
  44.5 15.8 %collective-permute-done.1 = bf16[256,512]{1,0:T(8,128)(2,1)} collective-permute-done((bf16[256,512]{1,0:T(8,128)(2,1)}, bf16[256,512]{1,0:T(8,128)(2,1)}, u32[]{:S(2)}, u32[]{:S(2)}) %collective-permute-start.1) | collective-permute-done | bytes 262176 | tf_op jit(solution)/shard_map/ppermute | solution.py:656
  62.0 3.2 collective-permute-done.2
  66.9 6.3 %collective-permute-done.3 = bf16[256,512]{1,0:T(8,128)(2,1)} collective-permute-done((bf16[256,512]{1,0:T(8,128)(2,1)}, bf16[256,512]{1,0:T(8,128)(2,1)}, u32[]{:S(2)}, u32[]{:S(2)}) %collective-permute-start.3) | collective-permute-done | bytes 262176 | tf_op jit(solution)/shard_map/ppermute | solution.py:656
  74.8 8.5 %pad_maximum_fusion.a_ref = bf16[2048,2048]{1,0:T(8,128)(2,1)} fusion(bf16[1024,2048]{1,0:T(8,128)(2,1)} %collective-permute-done.other_ref, bf16[1024,2048]{1,0:T(8,128)(2,1)} %multiply_convert_fusion.own_ref), kind=kLoop, calls=%fused_computation | loop fusion | flops 16777216 | bytes 16777216 | tf_op jit(solution)/shard_map/concatenate | solution.py:841
  83.4 33.1 %all-gather.4.cloned.1.call-done.b_ref.weight_ref = bf16[2048,1024]{1,0:T(8,128)(2,1)} async-done(((bf16[512,1024]{1,0:T(8,128)(2,1)}), bf16[2048,1024]{1,0:T(8,128)(2,1)}) %all-gather.4.cloned.1.call-update) | async-done | bytes 4194320 | tf_op jit(solution)/shard_map/all_gather | solution.py:646
  116.4 13.8 %product.11.pre_ref = f32[2048,1024]{1,0:T(8,128)} custom-call(bf16[2048,2048]{1,0:T(8,128)(2,1)} %pad_maximum_fusion.a_ref, bf16[2048,1024]{1,0:T(8,128)(2,1)} %all-gather.4.cloned.1.call-done.b_ref.weight_ref), custom_call_target="tpu_custom_call" | custom-call | flops 17179869184 | bytes 1048576 | tf_op jit(solution)/shard_map/product/pallas_call | solution.py:422
  130.2 14.3 %mixer_forward.1 = (bf16[2048,256]{1,0:T(8,128)(2,1)}, f32[2048,256]{1,0:T(8,128)}, f32[16,2,128,128]{3,2,1,0:T(8,128)}) custom-call(s32[8]{0:T(128)} %iota_xor_fusion.order_ref, s32[1]{0:T(128)S(6)} %copy.51.split_ref, f32[2048,1024]{1,0:T(8,128)} %product.11.pre_ref, f32[1,256]{1,0:T(1,128)} %bitcast.23, f32[1,256]{1,0:T(1,128)} %bitcast.21, f32[1,256]{1,0:T(1,128)} %bitcast.25), custom_call_target="tpu_custom_call" | custom-call | flops 14680064000 | bytes 1048576 | tf_op jit(solution)/shard_map/mixer_forward/pallas_call | solution.py:196
  144.5 4.6 product.13
  149.7 4.7 product.12
  165.5 4.9 maximum_convert_fusion
  170.5 13.9 %collective-permute-done.9 = bf16[256,2048]{1,0:T(8,128)(2,1)} collective-permute-done((bf16[256,2048]{1,0:T(8,128)(2,1)}, bf16[256,2048]{1,0:T(8,128)(2,1)}, u32[]{:S(2)}, u32[]{:S(2)}) %collective-permute-start.9) | collective-permute-done | bytes 1048608 | tf_op jit(solution)/shard_map/ppermute | solution.py:700
  184.3 3.7 collective-permute-done.7
  193.0 10.7 %collective-permute-done.10 = bf16[128,2048]{1,0:T(8,128)(2,1)S(1)} collective-permute-done((bf16[128,2048]{1,0:T(8,128)(2,1)S(1)}, bf16[128,2048]{1,0:T(8,128)(2,1)S(1)}, u32[]{:S(2)}, u32[]{:S(2)}) %collective-permute-start.10) | collective-permute-done | bytes 524320 | tf_op jit(solution)/shard_map/ppermute | solution.py:700
  212.5 18.8 %collective-permute-done.13 = bf16[256,2048]{1,0:T(8,128)(2,1)S(1)} collective-permute-done((bf16[256,2048]{1,0:T(8,128)(2,1)}, bf16[256,2048]{1,0:T(8,128)(2,1)S(1)}, u32[]{:S(2)}, u32[]{:S(2)}) %collective-permute-start.13) | collective-permute-done | bytes 1048608 | tf_op jit(solution)/shard_map/ppermute | solution.py:700
  238.3 5.4 collective-permute-done.14
  245.3 2.6 collective-permute-done.15
  252.8 19.4 %gate_product.1 = (f32[1024,2816]{1,0:T(8,128)}, bf16[1024,1408]{1,0:T(8,128)(2,1)}) custom-call(bf16[1024,2048]{1,0:T(8,128)(2,1)} %constant_dynamic-update-slice_fusion.low_ref.a_ref, bf16[2048,2816]{1,0:T(8,128)(2,1)} %all-gather.6.cloned.1.call-done.weight_ref.b_ref), custom_call_target="tpu_custom_call" | custom-call | flops 23622320128 | bytes 1048576 | tf_op jit(solution)/shard_map/gate_product/pallas_call | solution.py:448
  272.2 10.2 %product.14.refs_3_ = bf16[1408,2048]{1,0:T(8,128)(2,1)} custom-call(bf16[1024,1408]{1,0:T(8,128)(2,1)} %get-tuple-element.111.a_ref, bf16[1024,2048]{1,0:T(8,128)(2,1)} %dynamic-slice_dynamic-update-slice_fusion.1.b_ref.refs_0_), custom_call_target="tpu_custom_call" | custom-call | flops 11811160064 | bytes 1048576 | tf_op jit(solution)/shard_map/product/pallas_call | solution.py:422
  282.7 3.2 all-gather.8.cloned.1.call-done.refs_1_.b_ref
  285.9 14.7 %hidden_back.1.a_ref.b_ref = bf16[1024,2816]{1,0:T(8,128)(2,1)} custom-call(bf16[1024,2048]{1,0:T(8,128)(2,1)} %dynamic-slice_dynamic-update-slice_fusion.1.b_ref.refs_0_, bf16[1408,2048]{1,0:T(8,128)(2,1)} %all-gather.8.cloned.1.call-done.refs_1_.b_ref, f32[1024,2816]{1,0:T(8,128)} %get-tuple-element.112.refs_2_, bf16[1408,2048]{1,0:T(8,128)(2,1)} %product.14.refs_3_), custom_call_target="tpu_custom_call" | custom-call | flops 11811160064 | bytes 1048576 | tf_op jit(solution)/shard_map/hidden_back/pallas_call | solution.py:483
  300.6 10.5 %product.15 = (bf16[256,2048]{1,0:T(8,128)(2,1)}, bf16[256,2048]{1,0:T(8,128)(2,1)}) custom-call(bf16[1024,2816]{1,0:T(8,128)(2,1)} %hidden_back.1.a_ref.b_ref, bf16[2048,2816]{1,0:T(8,128)(2,1)} %all-gather.6.cloned.1.call-done.weight_ref.b_ref), custom_call_target="tpu_custom_call" | custom-call | flops 11811160064 | bytes 1048576 | tf_op jit(solution)/shard_map/product/pallas_call | solution.py:422
  314.1 12.0 %product.20 = bf16[2048,1408]{1,0:T(8,128)(2,1)} custom-call(bf16[1024,2048]{1,0:T(8,128)(2,1)} %constant_dynamic-update-slice_fusion.low_ref.a_ref, bf16[1024,2816]{1,0:T(8,128)(2,1)} %hidden_back.1.a_ref.b_ref), custom_call_target="tpu_custom_call" | custom-call | flops 11811160064 | bytes 1048576 | tf_op jit(solution)/shard_map/product/pallas_call | solution.py:422
  326.1 10.8 %product.16.refs_0_ = bf16[512,2048]{1,0:T(8,128)(2,1)} custom-call(bf16[1024,2816]{1,0:T(8,128)(2,1)} %hidden_back.1.a_ref.b_ref, bf16[2048,2816]{1,0:T(8,128)(2,1)} %all-gather.6.cloned.1.call-done.weight_ref.b_ref, bf16[256,2048]{1,0:T(8,128)(2,1)} %get-tuple-element.113.refs_0_, bf16[256,2048]{1,0:T(8,128)(2,1)} %get-tuple-element.114.refs_1_), custom_call_target="tpu_custom_call" | custom-call | flops 11811160064 | bytes 1048576 | tf_op jit(solution)/shard_map/product/pallas_call | solution.py:422
  338.1 2.7 add_convert_fusion.13
  342.9 11.3 %product.17 = (bf16[256,2048]{1,0:T(8,128)(2,1)}, bf16[256,2048]{1,0:T(8,128)(2,1)}, bf16[256,2048]{1,0:T(8,128)(2,1)}, bf16[256,2048]{1,0:T(8,128)(2,1)}) custom-call(bf16[1024,1408]{1,0:T(8,128)(2,1)} %get-tuple-element.111.a_ref, bf16[1408,2048]{1,0:T(8,128)(2,1)} %all-gather.8.cloned.1.call-done.refs_1_.b_ref, bf16[512,2048]{1,0:T(8,128)(2,1)} %product.16.refs_0_), custom_call_target="tpu_custom_call" | custom-call | flops 11811160064 | bytes 1048576 | tf_op jit(solution)/shard_map/product/pallas_call | solution.py:422
  358.8 2.3 multiply_reduce_fusion.1
  364.7 21.9 %collective-permute-done.20.refs_2_ = bf16[256,2048]{1,0:T(8,128)(2,1)} collective-permute-done((bf16[256,2048]{1,0:T(8,128)(2,1)S(1)}, bf16[256,2048]{1,0:T(8,128)(2,1)}, u32[]{:S(2)}, u32[]{:S(2)}) %collective-permute-start.20) | collective-permute-done | bytes 1048608 | tf_op jit(solution)/shard_map/ppermute | solution.py:700
  392.5 12.1 %product.21 = bf16[2048,1408]{1,0:T(8,128)(2,1)} custom-call(bf16[1024,2048]{1,0:T(8,128)(2,1)} %constant_dynamic-update-slice_fusion.low_ref.a_ref, bf16[1024,2816]{1,0:T(8,128)(2,1)} %hidden_back.1.a_ref.b_ref), custom_call_target="tpu_custom_call" | custom-call | flops 11811160064 | bytes 1048576 | tf_op jit(solution)/shard_map/product/pallas_call | solution.py:422
  404.9 6.4 %early_product.1.early_ref = f32[2048,256]{1,0:T(8,128)} custom-call(bf16[256,2048]{1,0:T(8,128)(2,1)} %constant_dynamic-update-slice_fusion.5.b_ref, bf16[256,2048]{1,0:T(8,128)(2,1)} %copy-done.31, bf16[256,2048]{1,0:T(8,128)(2,1)} %collective-permute-done.22.refs_1_, bf16[256,2048]{1,0:T(8,128)(2,1)} %collective-permute-done.20.refs_2_, ...), custom_call_target="tpu_custom_call" | custom-call | flops 3221225472 | bytes 1048576 | tf_op jit(solution)/shard_map/early_product/pallas_call | solution.py:575
  416.5 4.2 late_product.1.grad_ref
  420.7 22.7 %mixer_backward.1 = (bf16[2048,1024]{1,0:T(8,128)(2,1)}, f32[8,256]{1,0:T(8,128)}) custom-call(s32[8]{0:T(128)} %iota_xor_fusion.order_ref, s32[1]{0:T(128)S(6)} %copy.51.split_ref, f32[2048,1024]{1,0:T(8,128)} %product.11.pre_ref, f32[2048,256]{1,0:T(8,128)} %get-tuple-element.128.mixed_ref, f32[2048,256]{1,0:T(8,128)} %late_product.1.grad_ref, ...), custom_call_target="tpu_custom_call" | custom-call | flops 23068672000 | bytes 1048576 | tf_op jit(solution)/shard_map/mixer_backward/pallas_call | solution.py:365
  446.4 9.7 %product.18 = (bf16[256,2048]{1,0:T(8,128)(2,1)}, bf16[256,2048]{1,0:T(8,128)(2,1)}, bf16[256,2048]{1,0:T(8,128)(2,1)}, bf16[256,2048]{1,0:T(8,128)(2,1)}) custom-call(bf16[2048,1024]{1,0:T(8,128)(2,1)} %get-tuple-element.132.a_ref.b_ref, bf16[2048,1024]{1,0:T(8,128)(2,1)} %all-gather.4.cloned.1.call-done.b_ref.weight_ref, bf16[256,2048]{1,0:T(8,128)(2,1)} %copy-done.24, ...), custom_call_target="tpu_custom_call" | custom-call | flops 8589934592 | bytes 1048576 | tf_op jit(solution)/shard_map/product/pallas_call | solution.py:422
  463.8 9.8 %product.19 = (bf16[256,2048]{1,0:T(8,128)(2,1)}, bf16[256,2048]{1,0:T(8,128)(2,1)}, bf16[256,2048]{1,0:T(8,128)(2,1)}, bf16[256,2048]{1,0:T(8,128)(2,1)}) custom-call(bf16[2048,1024]{1,0:T(8,128)(2,1)} %get-tuple-element.132.a_ref.b_ref, bf16[2048,1024]{1,0:T(8,128)(2,1)} %all-gather.4.cloned.1.call-done.b_ref.weight_ref, ...), custom_call_target="tpu_custom_call" | custom-call | flops 8589934592 | bytes 1048576 | tf_op jit(solution)/shard_map/product/pallas_call | solution.py:422
  482.3 4.9 collective-permute-done.33.near_ref.refs_10_
  488.4 18.8 %weight_sum_product.1 = (bf16[2048,1280]{1,0:T(8,128)(2,1)}, f32[2048,128]{1,0:T(8,128)}) custom-call(bf16[1024,2048]{1,0:T(8,128)(2,1)} %multiply_convert_fusion.own_ref, bf16[1024,2048]{1,0:T(8,128)(2,1)} %collective-permute-done.other_ref, bf16[2048,1024]{1,0:T(8,128)(2,1)} %get-tuple-element.132.a_ref.b_ref, ...), custom_call_target="tpu_custom_call" | custom-call | flops 21474836480 | bytes 1048576 | tf_op jit(solution)/shard_map/weight_sum_product/pallas_call | solution.py:526
  517.5 9.2 %collective-permute-done.40 = bf16[128,2048]{1,0:T(8,128)(2,1)S(1)} collective-permute-done((bf16[128,2048]{1,0:T(8,128)(2,1)S(1)}, bf16[128,2048]{1,0:T(8,128)(2,1)S(1)}, u32[]{:S(2)}, u32[]{:S(2)}) %collective-permute-start.40) | collective-permute-done | bytes 524320 | tf_op jit(solution)/shard_map/ppermute | solution.py:700
  535.6 2.9 add_convert_fusion.own_ref
  538.6 4.1 collective-permute-done.43.bottom_ref
  546.5 4.7 placed_blocks.2
  551.3 16.7 %collective-permute-done.45.near_ref = bf16[256,2048]{1,0:T(8,128)(2,1)S(1)} collective-permute-done((bf16[256,2048]{1,0:T(8,128)(2,1)S(1)}, bf16[256,2048]{1,0:T(8,128)(2,1)S(1)}, u32[]{:S(2)}, u32[]{:S(2)}) %collective-permute-start.45) | collective-permute-done | bytes 1048608 | tf_op jit(solution)/shard_map/ppermute | solution.py:700
  571.7 8.2 %collective-permute-done.48.bottom_ref = bf16[128,2048]{1,0:T(8,128)(2,1)S(1)} collective-permute-done((bf16[128,2048]{1,0:T(8,128)(2,1)S(1)}, bf16[128,2048]{1,0:T(8,128)(2,1)S(1)}, u32[]{:S(2)}, u32[]{:S(2)}) %collective-permute-start.48) | collective-permute-done | bytes 524320 | tf_op jit(solution)/shard_map/ppermute | solution.py:700
  590.0 4.2 collective-permute-start.59
  594.2 5.8 placed_blocks.3
  605.6 4.3 joined_columns.1
  (340 shorter events, 152.0 us)
Async XLA Ops:
  7.2 109.2 %all-gather.4.cloned.1.call-start = ((), (), s32[]{:S(2)}) async-start(), calls=%async_computation.4 | async-start | bytes 5242880 | tf_op jit(solution)/shard_map/all_gather | solution.py:646
  10.7 242.1 %all-gather.6.cloned.1.call-start = ((), (), s32[]{:S(2)}) async-start(), calls=%async_computation.5 | async-start | bytes 12976128 | tf_op jit(solution)/shard_map/all_gather | solution.py:646
  13.1 272.8 %all-gather.8.cloned.1.call-start = ((), (), s32[]{:S(2)}) async-start(), calls=%async_computation.6 | async-start | bytes 6488064 | tf_op jit(solution)/shard_map/all_gather | solution.py:646
  29.2 45.6 %collective-permute-start = (bf16[1024,2048]{1,0:T(8,128)(2,1)}, bf16[1024,2048]{1,0:T(8,128)(2,1)}, u32[]{:S(2)}, u32[]{:S(2)}) collective-permute-start(bf16[1024,2048]{1,0:T(8,128)(2,1)} %multiply_convert_fusion.own_ref), channel_id=1, source_target_pairs={{0,4},{4,0},{1,5},{5,1},{2,6},{6,2},{3,7},{7,3},{8,12},{12,8},{9,1... | collective-permute-start | bytes 12582920 | tf_op jit(solution)/shard_map/ppermute | solution.py:690
  32.6 27.7 %collective-permute-start.1 = (bf16[256,512]{1,0:T(8,128)(2,1)}, bf16[256,512]{1,0:T(8,128)(2,1)}, u32[]{:S(2)}, u32[]{:S(2)}) collective-permute-start(bf16[256,512]{1,0:T(8,128)(2,1)} %get-tuple-element.184), channel_id=1, source_target_pairs={{0,8},{8,0},{16,24},{24,16},{1,9},{9,1},{17,25},{25,17},{2,10},{10... | collective-permute-start | bytes 786440 | tf_op jit(solution)/shard_map/ppermute | solution.py:656
  35.3 29.9 %collective-permute-start.2 = (bf16[256,512]{1,0:T(8,128)(2,1)}, bf16[256,512]{1,0:T(8,128)(2,1)}, u32[]{:S(2)}, u32[]{:S(2)}) collective-permute-start(bf16[256,512]{1,0:T(8,128)(2,1)} %get-tuple-element.184), channel_id=1, source_target_pairs={{0,16},{8,24},{16,0},{24,8},{1,17},{9,25},{17,1},{25,9},{2,18},{10... | collective-permute-start | bytes 786440 | tf_op jit(solution)/shard_map/ppermute | solution.py:656
  37.9 35.3 %collective-permute-start.3 = (bf16[256,512]{1,0:T(8,128)(2,1)}, bf16[256,512]{1,0:T(8,128)(2,1)}, u32[]{:S(2)}, u32[]{:S(2)}) collective-permute-start(bf16[256,512]{1,0:T(8,128)(2,1)} %get-tuple-element.184), channel_id=1, source_target_pairs={{0,24},{8,16},{16,8},{24,0},{1,25},{9,17},{17,9},{25,1},{2,26},{10... | collective-permute-start | bytes 786440 | tf_op jit(solution)/shard_map/ppermute | solution.py:656
  158.5 25.8 %collective-permute-start.9 = (bf16[256,2048]{1,0:T(8,128)(2,1)}, bf16[256,2048]{1,0:T(8,128)(2,1)}, u32[]{:S(2)}, u32[]{:S(2)}) collective-permute-start(bf16[256,2048]{1,0:T(8,128)(2,1)} %pad_maximum_fusion.4), channel_id=1, source_target_pairs={{0,2},{1,3},{2,0},{3,1},{4,6},{5,7},{6,4},{7,5},{8,10},{9,11},{10,... | collective-permute-start | bytes 3145736 | tf_op jit(solution)/shard_map/ppermute | solution.py:700
  162.5 25.6 %collective-permute-start.7 = (bf16[256,2048]{1,0:T(8,128)(2,1)}, bf16[256,2048]{1,0:T(8,128)(2,1)}, u32[]{:S(2)}, u32[]{:S(2)}) collective-permute-start(bf16[256,2048]{1,0:T(8,128)(2,1)} %pad_maximum_fusion.3), channel_id=1, source_target_pairs={{0,1},{1,0},{2,3},{3,2},{4,5},{5,4},{6,7},{7,6},{8,9},{9,8},{10,11... | collective-permute-start | bytes 3145736 | tf_op jit(solution)/shard_map/ppermute | solution.py:700
  164.9 193.9 %reduce-scatter.5.cloned.1.call-start = ((), (), s32[]{:S(2)}) async-start(), calls=%async_computation.7 | async-start | bytes 6488064 | tf_op jit(solution)/shard_map/reduce_scatter | solution.py:662
  165.4 27.1 %collective-permute-start.4 = (bf16[256,2048]{1,0:T(8,128)(2,1)}, bf16[256,2048]{1,0:T(8,128)(2,1)S(1)}, u32[]{:S(2)}, u32[]{:S(2)}) collective-permute-start(bf16[256,2048]{1,0:T(8,128)(2,1)} %get-tuple-element.98), channel_id=1, source_target_pairs={{0,4},{4,0},{1,5},{5,1},{2,6},{6,2},{3,7},{7,3},{8,12},{12,8},{9,1... | collective-permute-start | bytes 3145736 | tf_op jit(solution)/shard_map/ppermute | solution.py:690
  190.4 13.3 %collective-permute-start.10 = (bf16[128,2048]{1,0:T(8,128)(2,1)S(1)}, bf16[128,2048]{1,0:T(8,128)(2,1)S(1)}, u32[]{:S(2)}, u32[]{:S(2)}) collective-permute-start(bf16[128,2048]{1,0:T(8,128)(2,1)S(1)} %add_convert_fusion.16), channel_id=1, source_target_pairs={{0,2},{1,3},{2,0},{3,1},{4,6},{5,7},{6,4},{7,5},{8,10},{9,11},{10,... | collective-permute-start | bytes 1572872 | tf_op jit(solution)/shard_map/ppermute | solution.py:700
  191.0 12.9 %collective-permute-start.11 = (bf16[128,2048]{1,0:T(8,128)(2,1)S(1)}, bf16[128,2048]{1,0:T(8,128)(2,1)S(1)}, u32[]{:S(2)}, u32[]{:S(2)}) collective-permute-start(bf16[128,2048]{1,0:T(8,128)(2,1)S(1)} %add_convert_fusion.15), channel_id=1, source_target_pairs={{0,1},{1,0},{2,3},{3,2},{4,5},{5,4},{6,7},{7,6},{8,9},{9,8},{10,11... | collective-permute-start | bytes 1572872 | tf_op jit(solution)/shard_map/ppermute | solution.py:700
  207.6 23.7 %collective-permute-start.13 = (bf16[256,2048]{1,0:T(8,128)(2,1)}, bf16[256,2048]{1,0:T(8,128)(2,1)S(1)}, u32[]{:S(2)}, u32[]{:S(2)}) collective-permute-start(bf16[256,2048]{1,0:T(8,128)(2,1)} %multiply_convert_fusion.1), channel_id=1, source_target_pairs={{0,2},{1,3},{2,0},{3,1},{4,6},{5,7},{6,4},{7,5},{8,10},{9,11},{10,... | collective-permute-start | bytes 3145736 | tf_op jit(solution)/shard_map/ppermute | solution.py:700
  209.1 25.6 %collective-permute-start.12 = (bf16[256,2048]{1,0:T(8,128)(2,1)}, bf16[256,2048]{1,0:T(8,128)(2,1)}, u32[]{:S(2)}, u32[]{:S(2)}) collective-permute-start(bf16[256,2048]{1,0:T(8,128)(2,1)} %multiply_convert_fusion.1), channel_id=1, source_target_pairs={{0,1},{1,0},{2,3},{3,2},{4,5},{5,4},{6,7},{7,6},{8,9},{9,8},{10,11... | collective-permute-start | bytes 3145736 | tf_op jit(solution)/shard_map/ppermute | solution.py:700
  282.5 224.8 %reduce-scatter.7.cloned.1.call-start = ((), (), s32[]{:S(2)}) async-start(), calls=%async_computation.8 | async-start | bytes 6488064 | tf_op jit(solution)/shard_map/reduce_scatter | solution.py:662
  311.1 25.7 %collective-permute-start.16 = (bf16[256,2048]{1,0:T(8,128)(2,1)}, bf16[256,2048]{1,0:T(8,128)(2,1)S(1)}, u32[]{:S(2)}, u32[]{:S(2)}) collective-permute-start(bf16[256,2048]{1,0:T(8,128)(2,1)} %get-tuple-element.113.refs_0_), channel_id=1, source_target_pairs={{0,1},{1,0},{2,3},{3,2},{4,5},{5,4},{6,7},{7,6},{8,9},{9,8},{10,11... | collective-permute-start | bytes 3145736 | tf_op jit(solution)/shard_map/ppermute | solution.py:700
  312.6 25.4 %collective-permute-start.17 = (bf16[256,2048]{1,0:T(8,128)(2,1)}, bf16[256,2048]{1,0:T(8,128)(2,1)}, u32[]{:S(2)}, u32[]{:S(2)}) collective-permute-start(bf16[256,2048]{1,0:T(8,128)(2,1)} %get-tuple-element.114.refs_1_), channel_id=1, source_target_pairs={{0,2},{1,3},{2,0},{3,1},{4,6},{5,7},{6,4},{7,5},{8,10},{9,11},{10,... | collective-permute-start | bytes 3145736 | tf_op jit(solution)/shard_map/ppermute | solution.py:700
  338.1 169.7 %reduce-scatter.9.cloned.1.call-start = ((), (), s32[]{:S(2)}) async-start(), calls=%async_computation.9 | async-start | bytes 6488064 | tf_op jit(solution)/shard_map/reduce_scatter | solution.py:662
  340.8 13.3 %collective-permute-start.18 = (bf16[128,2048]{1,0:T(8,128)(2,1)}, bf16[128,2048]{1,0:T(8,128)(2,1)S(1)}, u32[]{:S(2)}, u32[]{:S(2)}) collective-permute-start(bf16[128,2048]{1,0:T(8,128)(2,1)} %get-tuple-element.118), channel_id=1, source_target_pairs={{0,2},{1,3},{2,0},{3,1},{4,6},{5,7},{6,4},{7,5},{8,10},{9,11},{10,... | collective-permute-start | bytes 1572872 | tf_op jit(solution)/shard_map/ppermute | solution.py:700
  342.3 13.1 %collective-permute-start.19 = (bf16[128,2048]{1,0:T(8,128)(2,1)}, bf16[128,2048]{1,0:T(8,128)(2,1)}, u32[]{:S(2)}, u32[]{:S(2)}) collective-permute-start(bf16[128,2048]{1,0:T(8,128)(2,1)} %get-tuple-element.119), channel_id=1, source_target_pairs={{0,1},{1,0},{2,3},{3,2},{4,5},{5,4},{6,7},{7,6},{8,9},{9,8},{10,11... | collective-permute-start | bytes 1572872 | tf_op jit(solution)/shard_map/ppermute | solution.py:700
  362.9 23.7 %collective-permute-start.20 = (bf16[256,2048]{1,0:T(8,128)(2,1)S(1)}, bf16[256,2048]{1,0:T(8,128)(2,1)}, u32[]{:S(2)}, u32[]{:S(2)}) collective-permute-start(bf16[256,2048]{1,0:T(8,128)(2,1)S(1)} %fusion.7.refs_0_), channel_id=1, source_target_pairs={{0,2},{1,3},{2,0},{3,1},{4,6},{5,7},{6,4},{7,5},{8,10},{9,11},{10,... | collective-permute-start | bytes 3145736 | tf_op jit(solution)/shard_map/ppermute | solution.py:700
  363.6 26.1 %collective-permute-start.22 = (bf16[256,2048]{1,0:T(8,128)(2,1)S(1)}, bf16[256,2048]{1,0:T(8,128)(2,1)}, u32[]{:S(2)}, u32[]{:S(2)}) collective-permute-start(bf16[256,2048]{1,0:T(8,128)(2,1)S(1)} %fusion.7.refs_0_), channel_id=1, source_target_pairs={{0,1},{1,0},{2,3},{3,2},{4,5},{5,4},{6,7},{7,6},{8,9},{9,8},{10,11... | collective-permute-start | bytes 3145736 | tf_op jit(solution)/shard_map/ppermute | solution.py:700
  364.7 40.1 %collective-permute-start.25 = (bf16[256,2048]{1,0:T(8,128)(2,1)S(1)}, bf16[256,2048]{1,0:T(8,128)(2,1)}, u32[]{:S(2)}, u32[]{:S(2)}) collective-permute-start(bf16[256,2048]{1,0:T(8,128)(2,1)S(1)} %fusion.7.refs_0_), channel_id=1, source_target_pairs={{0,4},{4,0},{1,5},{5,1},{2,6},{6,2},{3,7},{7,3},{8,12},{12,8},{9,1... | collective-permute-start | bytes 3145736 | tf_op jit(solution)/shard_map/ppermute | solution.py:690
  388.6 22.8 %collective-permute-start.21 = (bf16[128,2048]{1,0:T(8,128)(2,1)}, bf16[128,2048]{1,0:T(8,128)(2,1)}, u32[]{:S(2)}, u32[]{:S(2)}) collective-permute-start(bf16[128,2048]{1,0:T(8,128)(2,1)} %slice.297), channel_id=1, source_target_pairs={{0,1},{1,0},{2,3},{3,2},{4,5},{5,4},{6,7},{7,6},{8,9},{9,8},{10,11... | collective-permute-start | bytes 1572872 | tf_op jit(solution)/shard_map/ppermute | solution.py:700
  391.7 19.6 %collective-permute-start.23 = (bf16[128,2048]{1,0:T(8,128)(2,1)}, bf16[128,2048]{1,0:T(8,128)(2,1)}, u32[]{:S(2)}, u32[]{:S(2)}) collective-permute-start(bf16[128,2048]{1,0:T(8,128)(2,1)} %slice.298), channel_id=1, source_target_pairs={{0,2},{1,3},{2,0},{3,1},{4,6},{5,7},{6,4},{7,5},{8,10},{9,11},{10,... | collective-permute-start | bytes 1572872 | tf_op jit(solution)/shard_map/ppermute | solution.py:700
  392.0 12.9 %collective-permute-start.26 = (bf16[256,2048]{1,0:T(8,128)(2,1)}, bf16[256,2048]{1,0:T(8,128)(2,1)}, u32[]{:S(2)}, u32[]{:S(2)}) collective-permute-start(bf16[256,2048]{1,0:T(8,128)(2,1)} %collective-permute-done.22.refs_1_), channel_id=1, source_target_pairs={{0,4},{4,0},{1,5},{5,1},{2,6},{6,2},{3,7},{7,3},{8,12},{12,8},{9,1... | collective-permute-start | bytes 3145736 | tf_op jit(solution)/shard_map/ppermute | solution.py:690
  392.0 12.9 %collective-permute-start.27 = (bf16[256,2048]{1,0:T(8,128)(2,1)}, bf16[256,2048]{1,0:T(8,128)(2,1)}, u32[]{:S(2)}, u32[]{:S(2)}) collective-permute-start(bf16[256,2048]{1,0:T(8,128)(2,1)} %collective-permute-done.20.refs_2_), channel_id=1, source_target_pairs={{0,4},{4,0},{1,5},{5,1},{2,6},{6,2},{3,7},{7,3},{8,12},{12,8},{9,1... | collective-permute-start | bytes 3145736 | tf_op jit(solution)/shard_map/ppermute | solution.py:690
  404.6 196.6 %reduce-scatter.11.cloned.1.call-start = ((), (), s32[]{:S(2)}) async-start(), calls=%async_computation.10 | async-start | bytes 6553600 | tf_op jit(solution)/shard_map/reduce_scatter | solution.py:662
  411.8 31.6 %collective-permute-start.30 = (bf16[256,2048]{1,0:T(8,128)(2,1)}, bf16[256,2048]{1,0:T(8,128)(2,1)S(1)}, u32[]{:S(2)}, u32[]{:S(2)}) collective-permute-start(bf16[256,2048]{1,0:T(8,128)(2,1)} %get-tuple-element.135), channel_id=1, source_target_pairs={{0,2},{1,3},{2,0},{3,1},{4,6},{5,7},{6,4},{7,5},{8,10},{9,11},{10,... | collective-permute-start | bytes 3145736 | tf_op jit(solution)/shard_map/ppermute | solution.py:700
  413.5 29.9 %collective-permute-start.24 = (bf16[256,2048]{1,0:T(8,128)(2,1)}, bf16[256,2048]{1,0:T(8,128)(2,1)S(1)}, u32[]{:S(2)}, u32[]{:S(2)}) collective-permute-start(bf16[256,2048]{1,0:T(8,128)(2,1)} %get-tuple-element.125), channel_id=1, source_target_pairs={{0,1},{1,0},{2,3},{3,2},{4,5},{5,4},{6,7},{7,6},{8,9},{9,8},{10,11... | collective-permute-start | bytes 3145736 | tf_op jit(solution)/shard_map/ppermute | solution.py:700
  444.7 13.4 %collective-permute-start.31 = (bf16[128,2048]{1,0:T(8,128)(2,1)S(1)}, bf16[128,2048]{1,0:T(8,128)(2,1)S(1)}, u32[]{:S(2)}, u32[]{:S(2)}) collective-permute-start(bf16[128,2048]{1,0:T(8,128)(2,1)S(1)} %add_convert_fusion.12), channel_id=1, source_target_pairs={{0,2},{1,3},{2,0},{3,1},{4,6},{5,7},{6,4},{7,5},{8,10},{9,11},{10,... | collective-permute-start | bytes 1572872 | tf_op jit(solution)/shard_map/ppermute | solution.py:700
  445.2 13.4 %collective-permute-start.32 = (bf16[128,2048]{1,0:T(8,128)(2,1)}, bf16[128,2048]{1,0:T(8,128)(2,1)}, u32[]{:S(2)}, u32[]{:S(2)}) collective-permute-start(bf16[128,2048]{1,0:T(8,128)(2,1)} %add_convert_fusion.11), channel_id=1, source_target_pairs={{0,1},{1,0},{2,3},{3,2},{4,5},{5,4},{6,7},{7,6},{8,9},{9,8},{10,11... | collective-permute-start | bytes 1572872 | tf_op jit(solution)/shard_map/ppermute | solution.py:700
  456.1 17.5 %collective-permute-start.37 = (bf16[256,2048]{1,0:T(8,128)(2,1)}, bf16[256,2048]{1,0:T(8,128)(2,1)}, u32[]{:S(2)}, u32[]{:S(2)}) collective-permute-start(bf16[256,2048]{1,0:T(8,128)(2,1)} %get-tuple-element.149), channel_id=1, source_target_pairs={{0,4},{4,0},{1,5},{5,1},{2,6},{6,2},{3,7},{7,3},{8,12},{12,8},{9,1... | collective-permute-start | bytes 3145736 | tf_op jit(solution)/shard_map/ppermute | solution.py:690
  456.1 19.6 %collective-permute-start.35 = (bf16[256,2048]{1,0:T(8,128)(2,1)}, bf16[256,2048]{1,0:T(8,128)(2,1)}, u32[]{:S(2)}, u32[]{:S(2)}) collective-permute-start(bf16[256,2048]{1,0:T(8,128)(2,1)} %get-tuple-element.145), channel_id=1, source_target_pairs={{0,4},{4,0},{1,5},{5,1},{2,6},{6,2},{3,7},{7,3},{8,12},{12,8},{9,1... | collective-permute-start | bytes 3145736 | tf_op jit(solution)/shard_map/ppermute | solution.py:690
  456.6 22.3 %collective-permute-start.36 = (bf16[256,2048]{1,0:T(8,128)(2,1)}, bf16[256,2048]{1,0:T(8,128)(2,1)S(1)}, u32[]{:S(2)}, u32[]{:S(2)}) collective-permute-start(bf16[256,2048]{1,0:T(8,128)(2,1)} %get-tuple-element.147), channel_id=1, source_target_pairs={{0,4},{4,0},{1,5},{5,1},{2,6},{6,2},{3,7},{7,3},{8,12},{12,8},{9,1... | collective-permute-start | bytes 3145736 | tf_op jit(solution)/shard_map/ppermute | solution.py:690
  460.9 26.3 %collective-permute-start.33 = (bf16[256,2048]{1,0:T(8,128)(2,1)S(1)}, bf16[256,2048]{1,0:T(8,128)(2,1)}, u32[]{:S(2)}, u32[]{:S(2)}) collective-permute-start(bf16[256,2048]{1,0:T(8,128)(2,1)S(1)} %fusion.refs_1_.own_ref), channel_id=1, source_target_pairs={{0,1},{1,0},{2,3},{3,2},{4,5},{5,4},{6,7},{7,6},{8,9},{9,8},{10,11... | collective-permute-start | bytes 3145736 | tf_op jit(solution)/shard_map/ppermute | solution.py:700
  462.2 26.2 %collective-permute-start.34 = (bf16[256,2048]{1,0:T(8,128)(2,1)S(1)}, bf16[256,2048]{1,0:T(8,128)(2,1)}, u32[]{:S(2)}, u32[]{:S(2)}) collective-permute-start(bf16[256,2048]{1,0:T(8,128)(2,1)S(1)} %fusion.refs_1_.own_ref), channel_id=1, source_target_pairs={{0,2},{1,3},{2,0},{3,1},{4,6},{5,7},{6,4},{7,5},{8,10},{9,11},{10,... | collective-permute-start | bytes 3145736 | tf_op jit(solution)/shard_map/ppermute | solution.py:700
  478.6 29.2 %collective-permute-start.39 = (bf16[256,2048]{1,0:T(8,128)(2,1)}, bf16[256,2048]{1,0:T(8,128)(2,1)}, u32[]{:S(2)}, u32[]{:S(2)}) collective-permute-start(bf16[256,2048]{1,0:T(8,128)(2,1)} %pad_maximum_fusion.6), channel_id=1, source_target_pairs={{0,2},{1,3},{2,0},{3,1},{4,6},{5,7},{6,4},{7,5},{8,10},{9,11},{10,... | collective-permute-start | bytes 3145736 | tf_op jit(solution)/shard_map/ppermute | solution.py:700
  481.4 26.4 %collective-permute-start.38 = (bf16[256,2048]{1,0:T(8,128)(2,1)}, bf16[256,2048]{1,0:T(8,128)(2,1)}, u32[]{:S(2)}, u32[]{:S(2)}) collective-permute-start(bf16[256,2048]{1,0:T(8,128)(2,1)} %pad_maximum_fusion.5), channel_id=1, source_target_pairs={{0,1},{1,0},{2,3},{3,2},{4,5},{5,4},{6,7},{7,6},{8,9},{9,8},{10,11... | collective-permute-start | bytes 3145736 | tf_op jit(solution)/shard_map/ppermute | solution.py:700
  512.3 14.4 %collective-permute-start.40 = (bf16[128,2048]{1,0:T(8,128)(2,1)S(1)}, bf16[128,2048]{1,0:T(8,128)(2,1)S(1)}, u32[]{:S(2)}, u32[]{:S(2)}) collective-permute-start(bf16[128,2048]{1,0:T(8,128)(2,1)S(1)} %add_convert_fusion.10), channel_id=1, source_target_pairs={{0,2},{1,3},{2,0},{3,1},{4,6},{5,7},{6,4},{7,5},{8,10},{9,11},{10,... | collective-permute-start | bytes 1572872 | tf_op jit(solution)/shard_map/ppermute | solution.py:700
  514.0 14.1 %collective-permute-start.41 = (bf16[128,2048]{1,0:T(8,128)(2,1)S(1)}, bf16[128,2048]{1,0:T(8,128)(2,1)S(1)}, u32[]{:S(2)}, u32[]{:S(2)}) collective-permute-start(bf16[128,2048]{1,0:T(8,128)(2,1)S(1)} %add_convert_fusion.9), channel_id=1, source_target_pairs={{0,1},{1,0},{2,3},{3,2},{4,5},{5,4},{6,7},{7,6},{8,9},{9,8},{10,11... | collective-permute-start | bytes 1572872 | tf_op jit(solution)/shard_map/ppermute | solution.py:700
  516.9 29.4 %collective-permute-start.52 = (bf16[1408,256]{1,0:T(8,128)(2,1)S(1)}, bf16[1408,256]{1,0:T(8,128)(2,1)S(1)}, u32[]{:S(2)}, u32[]{:S(2)}) collective-permute-start(bf16[1408,256]{1,0:T(8,128)(2,1)S(1)} %copy-done.33), channel_id=1, source_target_pairs={{0,4},{4,0},{1,5},{5,1},{2,6},{6,2},{3,7},{7,3},{8,12},{12,8},{9,1... | collective-permute-start | bytes 2162696 | tf_op jit(solution)/shard_map/ppermute | solution.py:690
  517.0 53.4 %collective-permute-start.50 = (bf16[256,1408]{1,0:T(8,128)(2,1)S(1)}, bf16[256,1408]{1,0:T(8,128)(2,1)}, u32[]{:S(2)}, u32[]{:S(2)}) collective-permute-start(bf16[256,1408]{1,0:T(8,128)(2,1)S(1)} %copy-done.34), channel_id=1, source_target_pairs={{0,4},{4,0},{1,5},{5,1},{2,6},{6,2},{3,7},{7,3},{8,12},{12,8},{9,1... | collective-permute-start | bytes 2162696 | tf_op jit(solution)/shard_map/ppermute | solution.py:690
  529.2 13.5 %collective-permute-start.43 = (bf16[128,2048]{1,0:T(8,128)(2,1)S(1)}, bf16[128,2048]{1,0:T(8,128)(2,1)S(1)}, u32[]{:S(2)}, u32[]{:S(2)}) collective-permute-start(bf16[128,2048]{1,0:T(8,128)(2,1)S(1)} %slice.259), channel_id=1, source_target_pairs={{0,2},{1,3},{2,0},{3,1},{4,6},{5,7},{6,4},{7,5},{8,10},{9,11},{10,... | collective-permute-start | bytes 1572872 | tf_op jit(solution)/shard_map/ppermute | solution.py:700
  530.7 13.4 %collective-permute-start.42 = (bf16[128,2048]{1,0:T(8,128)(2,1)S(1)}, bf16[128,2048]{1,0:T(8,128)(2,1)S(1)}, u32[]{:S(2)}, u32[]{:S(2)}) collective-permute-start(bf16[128,2048]{1,0:T(8,128)(2,1)S(1)} %slice.258), channel_id=1, source_target_pairs={{0,1},{1,0},{2,3},{3,2},{4,5},{5,4},{6,7},{7,6},{8,9},{9,8},{10,11... | collective-permute-start | bytes 1572872 | tf_op jit(solution)/shard_map/ppermute | solution.py:700
  544.2 23.8 %collective-permute-start.45 = (bf16[256,2048]{1,0:T(8,128)(2,1)S(1)}, bf16[256,2048]{1,0:T(8,128)(2,1)S(1)}, u32[]{:S(2)}, u32[]{:S(2)}) collective-permute-start(bf16[256,2048]{1,0:T(8,128)(2,1)S(1)} %add_convert_fusion.own_ref), channel_id=1, source_target_pairs={{0,1},{1,0},{2,3},{3,2},{4,5},{5,4},{6,7},{7,6},{8,9},{9,8},{10,11... | collective-permute-start | bytes 3145736 | tf_op jit(solution)/shard_map/ppermute | solution.py:700
  544.9 24.4 %collective-permute-start.46 = (bf16[256,2048]{1,0:T(8,128)(2,1)S(1)}, bf16[256,2048]{1,0:T(8,128)(2,1)S(1)}, u32[]{:S(2)}, u32[]{:S(2)}) collective-permute-start(bf16[256,2048]{1,0:T(8,128)(2,1)S(1)} %add_convert_fusion.own_ref), channel_id=1, source_target_pairs={{0,2},{1,3},{2,0},{3,1},{4,6},{5,7},{6,4},{7,5},{8,10},{9,11},{10,... | collective-permute-start | bytes 3145736 | tf_op jit(solution)/shard_map/ppermute | solution.py:700
  (78 other events, 773.9 us)
Sparse Core Ops, SparseCore 0:
  10.8 105.5 all-gather.3
  118.6 106.4 all-gather.5
  226.7 59.1 all-gather.7
  288.0 63.0 reduce-scatter.4
  353.3 63.2 reduce-scatter.6
  418.7 63.1 reduce-scatter.8
  507.9 92.9 reduce-scatter.10

commit v6 on v5

--- a/solution.py
+++ b/solution.py
@@ -790,6 +790,51 @@
     )(at.astype(jnp.int32).reshape(1), *inputs, *wait)
 
 
+def resid_back_kernel(
+    own_ref, near_ref, far_ref, top_ref, bottom_ref, resid_ref, cot_ref, gain_ref, *refs
+):
+    grad_ref, low_ref, sum_ref = refs[-3:]
+    half = top_ref.shape[0]
+    gain = gain_ref[...]
+    total = jnp.zeros_like(gain)
+    for which, (first_ref, second_ref) in enumerate(((near_ref, top_ref), (far_ref, bottom_ref))):
+        rows = slice(which * half, (which + 1) * half)
+        grad = own_ref[rows].astype(F32) + first_ref[...].astype(F32) + second_ref[...].astype(F32)
+        resid = resid_ref[rows]
+        inv = rms_rows(resid)
+        u = grad * gain
+        moment = jnp.mean(u * resid, axis=-1, keepdims=True)
+        out = cot_ref[rows].astype(F32) + inv * u - resid * (inv * inv * inv * moment)
+        grad_ref[rows] = out
+        low_ref[rows] = out.astype(BF16)
+        total = total + jnp.sum(grad * resid * inv, axis=0, keepdims=True)
+    sum_ref[...] = total
+
+
+def resid_back(kept, first, second, resid, cot, gain, wait=()):
+    size, width = resid.shape
+    whole = pl.BlockSpec((size, width), lambda i: (0, 0))
+    half = pl.BlockSpec((size // 2, width), lambda i: (0, 0))
+    row = pl.BlockSpec((1, width), lambda i: (0, 0))
+    grad, low, total = pl.pallas_call(
+        resid_back_kernel,
+        grid=(1,),
+        in_specs=[whole] + [half] * 4 + [whole, whole, row] + [UNREAD] * len(wait),
+        out_specs=[whole, whole, row],
+        out_shape=[
+            jax.ShapeDtypeStruct((size, width), F32),
+            jax.ShapeDtypeStruct((size, width), BF16),
+            jax.ShapeDtypeStruct((1, width), F32),
+        ],
+        compiler_params=pltpu.CompilerParams(
+            dimension_semantics=("arbitrary",), vmem_limit_bytes=VMEM
+        ),
+        cost_estimate=cost(2 << 30),
+        name="resid_back",
+    )(kept, *first, *second, resid, cot, gain[None], *wait)
+    return grad, low, total[0]
+
+
 def body(
     block_in,
     query_proj,
@@ -884,12 +929,9 @@
     gate_weight_grad = product(second_low, gate_up_grad, TN, BF16, rows=256, b_half=0)
     gate_sum = scatter(after(gate_weight_grad, second_kept, *first), ("dp", "ctx"), 0)
     second = sum_second(second_part, *first)
-    second_total = sum_total(second_part, first, second)
-    resid_part, second_gain_grad = norm_back(
-        after(second_total, down_sum, ffn_rows[0]), resid, second_gain
+    resid_grad, resid_own, second_gain_grad = resid_back(
+        second_kept, first, second, resid, cotangent_blocks[0], second_gain, wait=[down_sum, ffn_rows[0]]
     )
-    resid_grad = cotangent_blocks[0].astype(F32) + resid_part
-    resid_own = resid_grad.astype(BF16)
     first = gather_first(resid_own)
     up_weight_grad = product(second_low, gate_up_grad, TN, BF16, rows=256, b_half=1)
     up_sum = scatter(after(up_weight_grad, *first), ("dp", "ctx"), 0)

time: 629 us -> 626 us (level)
  other arithmetic: 82.4 us -> 70 us
  local copies, waits for them, and re-layouts: 44.7 us -> 51.8 us
    unnamed x125 -> x112, local copies, waits for them, and re-layouts: 15.4 us -> 23.2 us
    pallas_call x0 -> x1, Pallas kernels: none -> 6.37 us  [resid_back(): pl.pallas_call(resid_back_kernel, grid=(1,), in_specs=[whole] + [half] *...]
  transfers between devices with their start and end apart: 68 -> 68, of which waited for: 28 -> 32; matrix products, arithmetic and copies ran while one was open for 19% -> 18% of each run, Pallas kernels for 36% -> 37%
where the time goes in v6:
time: 626 us; the launch traced here: 614 us
  Pallas kernels  231 us (37%)
  waiting for transfers between devices  193 us (31%)
  other arithmetic  70 us (11%)
  local copies, waits for them, and re-layouts  51.8 us (8%)
  starting transfers between devices  51.5 us (8%)
  between operations  17 us (3%)
    ppermute x32, waiting for transfers between devices, partner(): lax.ppermute(part, 'tp', [(i, i ^ mask) for i in range(lax.axis_size('tp'...  126 us
    pallas_call x11, Pallas kernels, product(): pl.pallas_call(functools.partial(product_kernel, dims, parts), grid=(coun...  110 us
    all_gather x3, waiting for transfers between devices, gather(): return lax.all_gather(part, axes, axis=dim, tiled=True)  39.8 us
    ppermute x32, starting transfers between devices, partner(): lax.ppermute(part, 'tp', [(i, i ^ mask) for i in range(lax.axis_size('tp'...  33.3 us
    ppermute x3, waiting for transfers between devices, gather_columns(): lax.ppermute(part, axis, [(i, i ^ m) for i in range(count)])  25.3 us
    unnamed x112, local copies, waits for them, and re-layouts  23.2 us
    pallas_call x1, Pallas kernels, mixer_backward(): pl.pallas_call(functools.partial(backward_kernel, heads, chunks), grid_sp...  22.7 us
    pallas_call x1, Pallas kernels, gate_product(): pl.pallas_call(gate_kernel, grid=(count // rows,), in_specs=[pl.BlockSpec...  19.3 us
  transfers between devices with their start and end apart: 68, of which 32 were waited for; matrix products, arithmetic and copies ran while one was open for 18% of the time, Pallas kernels for 37%

profile of v6, /device:TPU:0, one launch (start us, length us, event | category | flops | bytes accessed | tf_op | source)
XLA Modules:
  0.0 614.4 jit_solution(250656492178613871)
XLA Ops:
  10.8 2.3 fusion.1
  13.2 2.5 constant_dynamic-slice_fusion.10
  16.8 8.5 %multiply_convert_fusion.own_ref = bf16[1024,2048]{1,0:T(8,128)(2,1)} fusion(f32[2048]{0:T(1024)S(1)} %copy-done.35, f32[1024]{0:T(1024)S(1)} %add_rsqrt_fusion, bf16[256,2048]{1,0:T(8,128)(2,1)S(1)} %get-tuple-element.191, bf16[256,2048]{1,0:T(8,128)(2,1)S(1)} %get-tuple-element.192, bf16[256,2048]{1,0:T(8,128)(2,1)S(1)} %get-tuple-element.190, ...), kind=kLoop, calls=%fused_computation.1 | loop fusion | flops 23068672 | bytes 8400896 | tf_op jit(solution)/shard_map/convert_element_type | solution.py:884
  28.6 2.6 collective-permute-start.1
  31.1 2.6 collective-permute-start.2
  40.3 15.0 %collective-permute-done.1 = bf16[256,512]{1,0:T(8,128)(2,1)} collective-permute-done((bf16[256,512]{1,0:T(8,128)(2,1)}, bf16[256,512]{1,0:T(8,128)(2,1)}, u32[]{:S(2)}, u32[]{:S(2)}) %collective-permute-start.1) | collective-permute-done | bytes 262176 | tf_op jit(solution)/shard_map/ppermute | solution.py:656
  60.8 8.2 %collective-permute-done.3 = bf16[256,512]{1,0:T(8,128)(2,1)} collective-permute-done((bf16[256,512]{1,0:T(8,128)(2,1)}, bf16[256,512]{1,0:T(8,128)(2,1)}, u32[]{:S(2)}, u32[]{:S(2)}) %collective-permute-start.3) | collective-permute-done | bytes 262176 | tf_op jit(solution)/shard_map/ppermute | solution.py:656
  70.7 8.6 %pad_maximum_fusion.a_ref = bf16[2048,2048]{1,0:T(8,128)(2,1)} fusion(bf16[1024,2048]{1,0:T(8,128)(2,1)} %collective-permute-done.other_ref, bf16[1024,2048]{1,0:T(8,128)(2,1)} %multiply_convert_fusion.own_ref), kind=kLoop, calls=%fused_computation | loop fusion | flops 16777216 | bytes 16777216 | tf_op jit(solution)/shard_map/concatenate | solution.py:886
  79.3 37.1 %all-gather.4.cloned.1.call-done.b_ref.weight_ref = bf16[2048,1024]{1,0:T(8,128)(2,1)} async-done(((bf16[512,1024]{1,0:T(8,128)(2,1)}), bf16[2048,1024]{1,0:T(8,128)(2,1)}) %all-gather.4.cloned.1.call-update) | async-done | bytes 4194320 | tf_op jit(solution)/shard_map/all_gather | solution.py:646
  116.4 13.8 %product.11.pre_ref = f32[2048,1024]{1,0:T(8,128)} custom-call(bf16[2048,2048]{1,0:T(8,128)(2,1)} %pad_maximum_fusion.a_ref, bf16[2048,1024]{1,0:T(8,128)(2,1)} %all-gather.4.cloned.1.call-done.b_ref.weight_ref), custom_call_target="tpu_custom_call" | custom-call | flops 17179869184 | bytes 1048576 | tf_op jit(solution)/shard_map/product/pallas_call | solution.py:422
  130.2 14.3 %mixer_forward.1 = (bf16[2048,256]{1,0:T(8,128)(2,1)}, f32[2048,256]{1,0:T(8,128)}, f32[16,2,128,128]{3,2,1,0:T(8,128)}) custom-call(s32[8]{0:T(128)} %iota_xor_fusion.order_ref, s32[1]{0:T(128)S(6)} %copy.51.split_ref, f32[2048,1024]{1,0:T(8,128)} %product.11.pre_ref, f32[1,256]{1,0:T(1,128)} %bitcast.25, f32[1,256]{1,0:T(1,128)} %bitcast.23, f32[1,256]{1,0:T(1,128)} %bitcast.27), custom_call_target="tpu_custom_call" | custom-call | flops 14680064000 | bytes 1048576 | tf_op jit(solution)/shard_map/mixer_forward/pallas_call | solution.py:196
  144.5 4.6 product.13
  149.6 4.8 product.12
  165.4 4.9 maximum_convert_fusion
  170.5 2.8 dynamic-slice_dynamic-update-slice_fusion.5
  173.3 11.1 %collective-permute-done.9 = bf16[256,2048]{1,0:T(8,128)(2,1)} collective-permute-done((bf16[256,2048]{1,0:T(8,128)(2,1)}, bf16[256,2048]{1,0:T(8,128)(2,1)}, u32[]{:S(2)}, u32[]{:S(2)}) %collective-permute-start.9) | collective-permute-done | bytes 1048608 | tf_op jit(solution)/shard_map/ppermute | solution.py:700
  184.4 3.7 collective-permute-done.7
  193.0 10.7 %collective-permute-done.10 = bf16[128,2048]{1,0:T(8,128)(2,1)S(1)} collective-permute-done((bf16[128,2048]{1,0:T(8,128)(2,1)S(1)}, bf16[128,2048]{1,0:T(8,128)(2,1)S(1)}, u32[]{:S(2)}, u32[]{:S(2)}) %collective-permute-start.10) | collective-permute-done | bytes 524320 | tf_op jit(solution)/shard_map/ppermute | solution.py:700
  216.4 2.8 constant_dynamic-update-slice_fusion.5
  221.1 10.3 %collective-permute-done.13 = bf16[256,2048]{1,0:T(8,128)(2,1)S(1)} collective-permute-done((bf16[256,2048]{1,0:T(8,128)(2,1)}, bf16[256,2048]{1,0:T(8,128)(2,1)S(1)}, u32[]{:S(2)}, u32[]{:S(2)}) %collective-permute-start.13) | collective-permute-done | bytes 1048608 | tf_op jit(solution)/shard_map/ppermute | solution.py:700
  234.9 2.4 collective-permute-done.12
  239.4 6.3 %collective-permute-done.14 = bf16[128,2048]{1,0:T(8,128)(2,1)S(1)} collective-permute-done((bf16[128,2048]{1,0:T(8,128)(2,1)S(1)}, bf16[128,2048]{1,0:T(8,128)(2,1)S(1)}, u32[]{:S(2)}, u32[]{:S(2)}) %collective-permute-start.14) | collective-permute-done | bytes 524320 | tf_op jit(solution)/shard_map/ppermute | solution.py:700
  253.4 19.3 %gate_product.1 = (f32[1024,2816]{1,0:T(8,128)}, bf16[1024,1408]{1,0:T(8,128)(2,1)}) custom-call(bf16[1024,2048]{1,0:T(8,128)(2,1)} %constant_dynamic-update-slice_fusion.low_ref.a_ref, bf16[2048,2816]{1,0:T(8,128)(2,1)} %all-gather.6.cloned.1.call-done.weight_ref.b_ref), custom_call_target="tpu_custom_call" | custom-call | flops 23622320128 | bytes 1048576 | tf_op jit(solution)/shard_map/gate_product/pallas_call | solution.py:448
  272.7 10.2 %product.14.refs_3_ = bf16[1408,2048]{1,0:T(8,128)(2,1)} custom-call(bf16[1024,1408]{1,0:T(8,128)(2,1)} %get-tuple-element.113.a_ref, bf16[1024,2048]{1,0:T(8,128)(2,1)} %dynamic-slice_dynamic-update-slice_fusion.b_ref.refs_0_), custom_call_target="tpu_custom_call" | custom-call | flops 11811160064 | bytes 1048576 | tf_op jit(solution)/shard_map/product/pallas_call | solution.py:422
  283.2 2.7 all-gather.8.cloned.1.call-done.refs_1_.b_ref
  285.9 14.7 %hidden_back.1.a_ref.b_ref = bf16[1024,2816]{1,0:T(8,128)(2,1)} custom-call(bf16[1024,2048]{1,0:T(8,128)(2,1)} %dynamic-slice_dynamic-update-slice_fusion.b_ref.refs_0_, bf16[1408,2048]{1,0:T(8,128)(2,1)} %all-gather.8.cloned.1.call-done.refs_1_.b_ref, f32[1024,2816]{1,0:T(8,128)} %get-tuple-element.114.refs_2_, bf16[1408,2048]{1,0:T(8,128)(2,1)} %product.14.refs_3_), custom_call_target="tpu_custom_call" | custom-call | flops 11811160064 | bytes 1048576 | tf_op jit(solution)/shard_map/hidden_back/pallas_call | solution.py:483
  300.6 10.5 %product.15 = (bf16[256,2048]{1,0:T(8,128)(2,1)}, bf16[256,2048]{1,0:T(8,128)(2,1)}) custom-call(bf16[1024,2816]{1,0:T(8,128)(2,1)} %hidden_back.1.a_ref.b_ref, bf16[2048,2816]{1,0:T(8,128)(2,1)} %all-gather.6.cloned.1.call-done.weight_ref.b_ref), custom_call_target="tpu_custom_call" | custom-call | flops 11811160064 | bytes 1048576 | tf_op jit(solution)/shard_map/product/pallas_call | solution.py:422
  314.1 12.0 %product.20 = bf16[2048,1408]{1,0:T(8,128)(2,1)} custom-call(bf16[1024,2048]{1,0:T(8,128)(2,1)} %constant_dynamic-update-slice_fusion.low_ref.a_ref, bf16[1024,2816]{1,0:T(8,128)(2,1)} %hidden_back.1.a_ref.b_ref), custom_call_target="tpu_custom_call" | custom-call | flops 11811160064 | bytes 1048576 | tf_op jit(solution)/shard_map/product/pallas_call | solution.py:422
  326.1 10.8 %product.16.refs_0_.own_ref = bf16[512,2048]{1,0:T(8,128)(2,1)} custom-call(bf16[1024,2816]{1,0:T(8,128)(2,1)} %hidden_back.1.a_ref.b_ref, bf16[2048,2816]{1,0:T(8,128)(2,1)} %all-gather.6.cloned.1.call-done.weight_ref.b_ref, bf16[256,2048]{1,0:T(8,128)(2,1)} %get-tuple-element.115.refs_0_, bf16[256,2048]{1,0:T(8,128)(2,1)} %get-tuple-element.116.refs_1_), custom_call_target="tpu_custom_call" | custom-call | flops 11811160064 | bytes 1048576 | tf_op jit(solution)/shard_map/product/pallas_call | solution.py:422
  342.4 11.3 %product.17 = (bf16[256,2048]{1,0:T(8,128)(2,1)}, bf16[256,2048]{1,0:T(8,128)(2,1)}, bf16[256,2048]{1,0:T(8,128)(2,1)}, bf16[256,2048]{1,0:T(8,128)(2,1)}) custom-call(bf16[1024,1408]{1,0:T(8,128)(2,1)} %get-tuple-element.113.a_ref, bf16[1408,2048]{1,0:T(8,128)(2,1)} %all-gather.8.cloned.1.call-done.refs_1_.b_ref, bf16[512,2048]{1,0:T(8,128)(2,1)} %product.16.refs_0_.own_ref), custom_call_target="tpu_custom_call" | custom-call | flops 11811160064 | bytes 1048576 | tf_op jit(solution)/shard_map/product/pallas_call | solution.py:422
  355.1 6.4 %resid_back.1 = (f32[256,2048]{1,0:T(8,128)}, bf16[256,2048]{1,0:T(8,128)(2,1)}, f32[1,2048]{1,0:T(1,128)}) custom-call(bf16[512,2048]{1,0:T(8,128)(2,1)} %product.16.refs_0_.own_ref, bf16[256,2048]{1,0:T(8,128)(2,1)} %copy-done.34, bf16[256,2048]{1,0:T(8,128)(2,1)} %collective-permute-done.17.far_ref, bf16[128,2048]{1,0:T(8,128)(2,1)} %copy-done.49, ...), custom_call_target="tpu_custom_call" | custom-call | flops 4294967296 | bytes 1048576 | tf_op jit(solution)/shard_map/resid_back/pallas_call | solution.py:819
  363.0 22.4 %collective-permute-done.20.refs_2_ = bf16[256,2048]{1,0:T(8,128)(2,1)} collective-permute-done((bf16[256,2048]{1,0:T(8,128)(2,1)}, bf16[256,2048]{1,0:T(8,128)(2,1)}, u32[]{:S(2)}, u32[]{:S(2)}) %collective-permute-start.20) | collective-permute-done | bytes 1048608 | tf_op jit(solution)/shard_map/ppermute | solution.py:700
  390.4 12.1 %product.21 = bf16[2048,1408]{1,0:T(8,128)(2,1)} custom-call(bf16[1024,2048]{1,0:T(8,128)(2,1)} %constant_dynamic-update-slice_fusion.low_ref.a_ref, bf16[1024,2816]{1,0:T(8,128)(2,1)} %hidden_back.1.a_ref.b_ref), custom_call_target="tpu_custom_call" | custom-call | flops 11811160064 | bytes 1048576 | tf_op jit(solution)/shard_map/product/pallas_call | solution.py:422
  402.7 6.5 %early_product.1.early_ref = f32[2048,256]{1,0:T(8,128)} custom-call(bf16[256,2048]{1,0:T(8,128)(2,1)} %constant_dynamic-update-slice_fusion.6.b_ref, bf16[256,2048]{1,0:T(8,128)(2,1)} %get-tuple-element.125.refs_0_, bf16[256,2048]{1,0:T(8,128)(2,1)} %collective-permute-done.22.refs_1_, bf16[256,2048]{1,0:T(8,128)(2,1)} %collective-permute-done.20.refs_2_, ...), custom_call_target="tpu_custom_call" | custom-call | flops 3221225472 | bytes 1048576 | tf_op jit(solution)/shard_map/early_product/pallas_call | solution.py:575
  413.4 4.3 late_product.1.grad_ref
  417.7 22.7 %mixer_backward.1 = (bf16[2048,1024]{1,0:T(8,128)(2,1)}, f32[8,256]{1,0:T(8,128)}) custom-call(s32[8]{0:T(128)} %iota_xor_fusion.order_ref, s32[1]{0:T(128)S(6)} %copy.51.split_ref, f32[2048,1024]{1,0:T(8,128)} %product.11.pre_ref, f32[2048,256]{1,0:T(8,128)} %get-tuple-element.130.mixed_ref, f32[2048,256]{1,0:T(8,128)} %late_product.1.grad_ref, ...), custom_call_target="tpu_custom_call" | custom-call | flops 23068672000 | bytes 1048576 | tf_op jit(solution)/shard_map/mixer_backward/pallas_call | solution.py:365
  443.9 9.7 %product.18 = (bf16[256,2048]{1,0:T(8,128)(2,1)}, bf16[256,2048]{1,0:T(8,128)(2,1)}, bf16[256,2048]{1,0:T(8,128)(2,1)}, bf16[256,2048]{1,0:T(8,128)(2,1)}) custom-call(bf16[2048,1024]{1,0:T(8,128)(2,1)} %get-tuple-element.134.a_ref.b_ref, bf16[2048,1024]{1,0:T(8,128)(2,1)} %all-gather.4.cloned.1.call-done.b_ref.weight_ref, bf16[256,2048]{1,0:T(8,128)(2,1)} %copy-done.20, ...), custom_call_target="tpu_custom_call" | custom-call | flops 8589934592 | bytes 1048576 | tf_op jit(solution)/shard_map/product/pallas_call | solution.py:422
  460.9 9.8 %product.19 = (bf16[256,2048]{1,0:T(8,128)(2,1)}, bf16[256,2048]{1,0:T(8,128)(2,1)}, bf16[256,2048]{1,0:T(8,128)(2,1)}, bf16[256,2048]{1,0:T(8,128)(2,1)}) custom-call(bf16[2048,1024]{1,0:T(8,128)(2,1)} %get-tuple-element.134.a_ref.b_ref, bf16[2048,1024]{1,0:T(8,128)(2,1)} %all-gather.4.cloned.1.call-done.b_ref.weight_ref, ...), custom_call_target="tpu_custom_call" | custom-call | flops 8589934592 | bytes 1048576 | tf_op jit(solution)/shard_map/product/pallas_call | solution.py:422
  477.7 7.4 %collective-permute-done.33.near_ref.refs_10_ = bf16[256,2048]{1,0:T(8,128)(2,1)} collective-permute-done((bf16[256,2048]{1,0:T(8,128)(2,1)S(1)}, bf16[256,2048]{1,0:T(8,128)(2,1)}, u32[]{:S(2)}, u32[]{:S(2)}) %collective-permute-start.33) | collective-permute-done | bytes 1048608 | tf_op jit(solution)/shard_map/ppermute | solution.py:700
  485.9 18.7 %weight_sum_product.1 = (bf16[2048,1280]{1,0:T(8,128)(2,1)}, f32[2048,128]{1,0:T(8,128)}) custom-call(bf16[1024,2048]{1,0:T(8,128)(2,1)} %multiply_convert_fusion.own_ref, bf16[1024,2048]{1,0:T(8,128)(2,1)} %collective-permute-done.other_ref, bf16[2048,1024]{1,0:T(8,128)(2,1)} %get-tuple-element.134.a_ref.b_ref, ...), custom_call_target="tpu_custom_call" | custom-call | flops 21474836480 | bytes 1048576 | tf_op jit(solution)/shard_map/weight_sum_product/pallas_call | solution.py:526
  513.6 9.4 %collective-permute-done.40 = bf16[128,2048]{1,0:T(8,128)(2,1)S(1)} collective-permute-done((bf16[128,2048]{1,0:T(8,128)(2,1)S(1)}, bf16[128,2048]{1,0:T(8,128)(2,1)S(1)}, u32[]{:S(2)}, u32[]{:S(2)}) %collective-permute-start.40) | collective-permute-done | bytes 524320 | tf_op jit(solution)/shard_map/ppermute | solution.py:700
  534.1 4.7 collective-permute-done.43.bottom_ref
  542.2 4.6 placed_blocks.2
  546.8 17.2 %collective-permute-done.45.near_ref = bf16[256,2048]{1,0:T(8,128)(2,1)} collective-permute-done((bf16[256,2048]{1,0:T(8,128)(2,1)S(1)}, bf16[256,2048]{1,0:T(8,128)(2,1)}, u32[]{:S(2)}, u32[]{:S(2)}) %collective-permute-start.45) | collective-permute-done | bytes 1048608 | tf_op jit(solution)/shard_map/ppermute | solution.py:700
  568.1 8.6 %collective-permute-done.48.bottom_ref = bf16[128,2048]{1,0:T(8,128)(2,1)S(1)} collective-permute-done((bf16[128,2048]{1,0:T(8,128)(2,1)S(1)}, bf16[128,2048]{1,0:T(8,128)(2,1)S(1)}, u32[]{:S(2)}, u32[]{:S(2)}) %collective-permute-start.48) | collective-permute-done | bytes 524320 | tf_op jit(solution)/shard_map/ppermute | solution.py:700
  587.6 3.5 collective-permute-start.59
  591.1 5.8 placed_blocks.3
  602.9 4.3 joined_columns.1
  (323 shorter events, 147.7 us)
Async XLA Ops:
  7.2 109.2 %all-gather.4.cloned.1.call-start = ((), (), s32[]{:S(2)}) async-start(), calls=%async_computation.4 | async-start | bytes 5242880 | tf_op jit(solution)/shard_map/all_gather | solution.py:646
  10.7 242.7 %all-gather.6.cloned.1.call-start = ((), (), s32[]{:S(2)}) async-start(), calls=%async_computation.5 | async-start | bytes 12976128 | tf_op jit(solution)/shard_map/all_gather | solution.py:646
  13.1 272.8 %all-gather.8.cloned.1.call-start = ((), (), s32[]{:S(2)}) async-start(), calls=%async_computation.6 | async-start | bytes 6488064 | tf_op jit(solution)/shard_map/all_gather | solution.py:646
  25.2 45.4 %collective-permute-start = (bf16[1024,2048]{1,0:T(8,128)(2,1)}, bf16[1024,2048]{1,0:T(8,128)(2,1)}, u32[]{:S(2)}, u32[]{:S(2)}) collective-permute-start(bf16[1024,2048]{1,0:T(8,128)(2,1)} %multiply_convert_fusion.own_ref), channel_id=1, source_target_pairs={{0,4},{4,0},{1,5},{5,1},{2,6},{6,2},{3,7},{7,3},{8,12},{12,8},{9,1... | collective-permute-start | bytes 12582920 | tf_op jit(solution)/shard_map/ppermute | solution.py:690
  28.6 26.7 %collective-permute-start.1 = (bf16[256,512]{1,0:T(8,128)(2,1)}, bf16[256,512]{1,0:T(8,128)(2,1)}, u32[]{:S(2)}, u32[]{:S(2)}) collective-permute-start(bf16[256,512]{1,0:T(8,128)(2,1)} %get-tuple-element.188), channel_id=1, source_target_pairs={{0,8},{8,0},{16,24},{24,16},{1,9},{9,1},{17,25},{25,17},{2,10},{10... | collective-permute-start | bytes 786440 | tf_op jit(solution)/shard_map/ppermute | solution.py:656
  31.1 28.0 %collective-permute-start.2 = (bf16[256,512]{1,0:T(8,128)(2,1)}, bf16[256,512]{1,0:T(8,128)(2,1)}, u32[]{:S(2)}, u32[]{:S(2)}) collective-permute-start(bf16[256,512]{1,0:T(8,128)(2,1)} %get-tuple-element.188), channel_id=1, source_target_pairs={{0,16},{8,24},{16,0},{24,8},{1,17},{9,25},{17,1},{25,9},{2,18},{10... | collective-permute-start | bytes 786440 | tf_op jit(solution)/shard_map/ppermute | solution.py:656
  33.7 35.3 %collective-permute-start.3 = (bf16[256,512]{1,0:T(8,128)(2,1)}, bf16[256,512]{1,0:T(8,128)(2,1)}, u32[]{:S(2)}, u32[]{:S(2)}) collective-permute-start(bf16[256,512]{1,0:T(8,128)(2,1)} %get-tuple-element.188), channel_id=1, source_target_pairs={{0,24},{8,16},{16,8},{24,0},{1,25},{9,17},{17,9},{25,1},{2,26},{10... | collective-permute-start | bytes 786440 | tf_op jit(solution)/shard_map/ppermute | solution.py:656
  158.5 25.8 %collective-permute-start.9 = (bf16[256,2048]{1,0:T(8,128)(2,1)}, bf16[256,2048]{1,0:T(8,128)(2,1)}, u32[]{:S(2)}, u32[]{:S(2)}) collective-permute-start(bf16[256,2048]{1,0:T(8,128)(2,1)} %pad_maximum_fusion.3), channel_id=1, source_target_pairs={{0,2},{1,3},{2,0},{3,1},{4,6},{5,7},{6,4},{7,5},{8,10},{9,11},{10,... | collective-permute-start | bytes 3145736 | tf_op jit(solution)/shard_map/ppermute | solution.py:700
  162.5 25.6 %collective-permute-start.7 = (bf16[256,2048]{1,0:T(8,128)(2,1)}, bf16[256,2048]{1,0:T(8,128)(2,1)}, u32[]{:S(2)}, u32[]{:S(2)}) collective-permute-start(bf16[256,2048]{1,0:T(8,128)(2,1)} %pad_maximum_fusion.2), channel_id=1, source_target_pairs={{0,1},{1,0},{2,3},{3,2},{4,5},{5,4},{6,7},{7,6},{8,9},{9,8},{10,11... | collective-permute-start | bytes 3145736 | tf_op jit(solution)/shard_map/ppermute | solution.py:700
  164.9 189.4 %reduce-scatter.5.cloned.1.call-start = ((), (), s32[]{:S(2)}) async-start(), calls=%async_computation.7 | async-start | bytes 6488064 | tf_op jit(solution)/shard_map/reduce_scatter | solution.py:662
  170.4 22.2 %collective-permute-start.4 = (bf16[256,2048]{1,0:T(8,128)(2,1)S(1)}, bf16[256,2048]{1,0:T(8,128)(2,1)S(1)}, u32[]{:S(2)}, u32[]{:S(2)}) collective-permute-start(bf16[256,2048]{1,0:T(8,128)(2,1)S(1)} %copy-done.44), channel_id=1, source_target_pairs={{0,4},{4,0},{1,5},{5,1},{2,6},{6,2},{3,7},{7,3},{8,12},{12,8},{9,1... | collective-permute-start | bytes 3145736 | tf_op jit(solution)/shard_map/ppermute | solution.py:690
  190.5 13.3 %collective-permute-start.10 = (bf16[128,2048]{1,0:T(8,128)(2,1)S(1)}, bf16[128,2048]{1,0:T(8,128)(2,1)S(1)}, u32[]{:S(2)}, u32[]{:S(2)}) collective-permute-start(bf16[128,2048]{1,0:T(8,128)(2,1)S(1)} %add_convert_fusion.16), channel_id=1, source_target_pairs={{0,2},{1,3},{2,0},{3,1},{4,6},{5,7},{6,4},{7,5},{8,10},{9,11},{10,... | collective-permute-start | bytes 1572872 | tf_op jit(solution)/shard_map/ppermute | solution.py:700
  191.1 12.9 %collective-permute-start.11 = (bf16[128,2048]{1,0:T(8,128)(2,1)S(1)}, bf16[128,2048]{1,0:T(8,128)(2,1)S(1)}, u32[]{:S(2)}, u32[]{:S(2)}) collective-permute-start(bf16[128,2048]{1,0:T(8,128)(2,1)S(1)} %add_convert_fusion.15), channel_id=1, source_target_pairs={{0,1},{1,0},{2,3},{3,2},{4,5},{5,4},{6,7},{7,6},{8,9},{9,8},{10,11... | collective-permute-start | bytes 1572872 | tf_op jit(solution)/shard_map/ppermute | solution.py:700
  207.8 23.6 %collective-permute-start.13 = (bf16[256,2048]{1,0:T(8,128)(2,1)}, bf16[256,2048]{1,0:T(8,128)(2,1)S(1)}, u32[]{:S(2)}, u32[]{:S(2)}) collective-permute-start(bf16[256,2048]{1,0:T(8,128)(2,1)} %multiply_convert_fusion.1), channel_id=1, source_target_pairs={{0,2},{1,3},{2,0},{3,1},{4,6},{5,7},{6,4},{7,5},{8,10},{9,11},{10,... | collective-permute-start | bytes 3145736 | tf_op jit(solution)/shard_map/ppermute | solution.py:700
  211.2 26.2 %collective-permute-start.12 = (bf16[256,2048]{1,0:T(8,128)(2,1)}, bf16[256,2048]{1,0:T(8,128)(2,1)}, u32[]{:S(2)}, u32[]{:S(2)}) collective-permute-start(bf16[256,2048]{1,0:T(8,128)(2,1)} %multiply_convert_fusion.1), channel_id=1, source_target_pairs={{0,1},{1,0},{2,3},{3,2},{4,5},{5,4},{6,7},{7,6},{8,9},{9,8},{10,11... | collective-permute-start | bytes 3145736 | tf_op jit(solution)/shard_map/ppermute | solution.py:700
  231.4 14.3 %collective-permute-start.14 = (bf16[128,2048]{1,0:T(8,128)(2,1)S(1)}, bf16[128,2048]{1,0:T(8,128)(2,1)S(1)}, u32[]{:S(2)}, u32[]{:S(2)}) collective-permute-start(bf16[128,2048]{1,0:T(8,128)(2,1)S(1)} %slice.269), channel_id=1, source_target_pairs={{0,1},{1,0},{2,3},{3,2},{4,5},{5,4},{6,7},{7,6},{8,9},{9,8},{10,11... | collective-permute-start | bytes 1572872 | tf_op jit(solution)/shard_map/ppermute | solution.py:700
  283.0 221.6 %reduce-scatter.7.cloned.1.call-start = ((), (), s32[]{:S(2)}) async-start(), calls=%async_computation.8 | async-start | bytes 6488064 | tf_op jit(solution)/shard_map/reduce_scatter | solution.py:662
  311.2 25.7 %collective-permute-start.16 = (bf16[256,2048]{1,0:T(8,128)(2,1)}, bf16[256,2048]{1,0:T(8,128)(2,1)S(1)}, u32[]{:S(2)}, u32[]{:S(2)}) collective-permute-start(bf16[256,2048]{1,0:T(8,128)(2,1)} %get-tuple-element.115.refs_0_), channel_id=1, source_target_pairs={{0,1},{1,0},{2,3},{3,2},{4,5},{5,4},{6,7},{7,6},{8,9},{9,8},{10,11... | collective-permute-start | bytes 3145736 | tf_op jit(solution)/shard_map/ppermute | solution.py:700
  312.6 25.4 %collective-permute-start.17 = (bf16[256,2048]{1,0:T(8,128)(2,1)}, bf16[256,2048]{1,0:T(8,128)(2,1)}, u32[]{:S(2)}, u32[]{:S(2)}) collective-permute-start(bf16[256,2048]{1,0:T(8,128)(2,1)} %get-tuple-element.116.refs_1_), channel_id=1, source_target_pairs={{0,2},{1,3},{2,0},{3,1},{4,6},{5,7},{6,4},{7,5},{8,10},{9,11},{10,... | collective-permute-start | bytes 3145736 | tf_op jit(solution)/shard_map/ppermute | solution.py:700
  338.1 167.6 %reduce-scatter.9.cloned.1.call-start = ((), (), s32[]{:S(2)}) async-start(), calls=%async_computation.9 | async-start | bytes 6488064 | tf_op jit(solution)/shard_map/reduce_scatter | solution.py:662
  340.5 13.7 %collective-permute-start.18 = (bf16[128,2048]{1,0:T(8,128)(2,1)S(1)}, bf16[128,2048]{1,0:T(8,128)(2,1)S(1)}, u32[]{:S(2)}, u32[]{:S(2)}) collective-permute-start(bf16[128,2048]{1,0:T(8,128)(2,1)S(1)} %get-tuple-element.120), channel_id=1, source_target_pairs={{0,2},{1,3},{2,0},{3,1},{4,6},{5,7},{6,4},{7,5},{8,10},{9,11},{10,... | collective-permute-start | bytes 1572872 | tf_op jit(solution)/shard_map/ppermute | solution.py:700
  341.3 12.9 %collective-permute-start.19 = (bf16[128,2048]{1,0:T(8,128)(2,1)S(1)}, bf16[128,2048]{1,0:T(8,128)(2,1)S(1)}, u32[]{:S(2)}, u32[]{:S(2)}) collective-permute-start(bf16[128,2048]{1,0:T(8,128)(2,1)S(1)} %get-tuple-element.121), channel_id=1, source_target_pairs={{0,1},{1,0},{2,3},{3,2},{4,5},{5,4},{6,7},{7,6},{8,9},{9,8},{10,11... | collective-permute-start | bytes 1572872 | tf_op jit(solution)/shard_map/ppermute | solution.py:700
  361.5 24.0 %collective-permute-start.20 = (bf16[256,2048]{1,0:T(8,128)(2,1)}, bf16[256,2048]{1,0:T(8,128)(2,1)}, u32[]{:S(2)}, u32[]{:S(2)}) collective-permute-start(bf16[256,2048]{1,0:T(8,128)(2,1)} %get-tuple-element.125.refs_0_), channel_id=1, source_target_pairs={{0,2},{1,3},{2,0},{3,1},{4,6},{5,7},{6,4},{7,5},{8,10},{9,11},{10,... | collective-permute-start | bytes 3145736 | tf_op jit(solution)/shard_map/ppermute | solution.py:700
  362.8 24.6 %collective-permute-start.22 = (bf16[256,2048]{1,0:T(8,128)(2,1)}, bf16[256,2048]{1,0:T(8,128)(2,1)}, u32[]{:S(2)}, u32[]{:S(2)}) collective-permute-start(bf16[256,2048]{1,0:T(8,128)(2,1)} %get-tuple-element.125.refs_0_), channel_id=1, source_target_pairs={{0,1},{1,0},{2,3},{3,2},{4,5},{5,4},{6,7},{7,6},{8,9},{9,8},{10,11... | collective-permute-start | bytes 3145736 | tf_op jit(solution)/shard_map/ppermute | solution.py:700
  363.0 39.7 %collective-permute-start.25 = (bf16[256,2048]{1,0:T(8,128)(2,1)}, bf16[256,2048]{1,0:T(8,128)(2,1)}, u32[]{:S(2)}, u32[]{:S(2)}) collective-permute-start(bf16[256,2048]{1,0:T(8,128)(2,1)} %get-tuple-element.125.refs_0_), channel_id=1, source_target_pairs={{0,4},{4,0},{1,5},{5,1},{2,6},{6,2},{3,7},{7,3},{8,12},{12,8},{9,1... | collective-permute-start | bytes 3145736 | tf_op jit(solution)/shard_map/ppermute | solution.py:690
  386.6 22.6 %collective-permute-start.21 = (bf16[128,2048]{1,0:T(8,128)(2,1)S(1)}, bf16[128,2048]{1,0:T(8,128)(2,1)S(1)}, u32[]{:S(2)}, u32[]{:S(2)}) collective-permute-start(bf16[128,2048]{1,0:T(8,128)(2,1)S(1)} %slice.274), channel_id=1, source_target_pairs={{0,1},{1,0},{2,3},{3,2},{4,5},{5,4},{6,7},{7,6},{8,9},{9,8},{10,11... | collective-permute-start | bytes 1572872 | tf_op jit(solution)/shard_map/ppermute | solution.py:700
  388.5 20.7 %collective-permute-start.23 = (bf16[128,2048]{1,0:T(8,128)(2,1)S(1)}, bf16[128,2048]{1,0:T(8,128)(2,1)}, u32[]{:S(2)}, u32[]{:S(2)}) collective-permute-start(bf16[128,2048]{1,0:T(8,128)(2,1)S(1)} %slice.275), channel_id=1, source_target_pairs={{0,2},{1,3},{2,0},{3,1},{4,6},{5,7},{6,4},{7,5},{8,10},{9,11},{10,... | collective-permute-start | bytes 1572872 | tf_op jit(solution)/shard_map/ppermute | solution.py:700
  389.9 12.9 %collective-permute-start.27 = (bf16[256,2048]{1,0:T(8,128)(2,1)}, bf16[256,2048]{1,0:T(8,128)(2,1)}, u32[]{:S(2)}, u32[]{:S(2)}) collective-permute-start(bf16[256,2048]{1,0:T(8,128)(2,1)} %collective-permute-done.20.refs_2_), channel_id=1, source_target_pairs={{0,4},{4,0},{1,5},{5,1},{2,6},{6,2},{3,7},{7,3},{8,12},{12,8},{9,1... | collective-permute-start | bytes 3145736 | tf_op jit(solution)/shard_map/ppermute | solution.py:690
  402.5 196.1 %reduce-scatter.11.cloned.1.call-start = ((), (), s32[]{:S(2)}) async-start(), calls=%async_computation.10 | async-start | bytes 6553600 | tf_op jit(solution)/shard_map/reduce_scatter | solution.py:662
  409.7 30.7 %collective-permute-start.30 = (bf16[256,2048]{1,0:T(8,128)(2,1)}, bf16[256,2048]{1,0:T(8,128)(2,1)S(1)}, u32[]{:S(2)}, u32[]{:S(2)}) collective-permute-start(bf16[256,2048]{1,0:T(8,128)(2,1)} %get-tuple-element.137), channel_id=1, source_target_pairs={{0,2},{1,3},{2,0},{3,1},{4,6},{5,7},{6,4},{7,5},{8,10},{9,11},{10,... | collective-permute-start | bytes 3145736 | tf_op jit(solution)/shard_map/ppermute | solution.py:700
  410.4 30.0 %collective-permute-start.24 = (bf16[256,2048]{1,0:T(8,128)(2,1)}, bf16[256,2048]{1,0:T(8,128)(2,1)S(1)}, u32[]{:S(2)}, u32[]{:S(2)}) collective-permute-start(bf16[256,2048]{1,0:T(8,128)(2,1)} %get-tuple-element.127.refs_1_), channel_id=1, source_target_pairs={{0,1},{1,0},{2,3},{3,2},{4,5},{5,4},{6,7},{7,6},{8,9},{9,8},{10,11... | collective-permute-start | bytes 3145736 | tf_op jit(solution)/shard_map/ppermute | solution.py:700
  441.7 13.6 %collective-permute-start.31 = (bf16[128,2048]{1,0:T(8,128)(2,1)S(1)}, bf16[128,2048]{1,0:T(8,128)(2,1)S(1)}, u32[]{:S(2)}, u32[]{:S(2)}) collective-permute-start(bf16[128,2048]{1,0:T(8,128)(2,1)S(1)} %add_convert_fusion.12), channel_id=1, source_target_pairs={{0,2},{1,3},{2,0},{3,1},{4,6},{5,7},{6,4},{7,5},{8,10},{9,11},{10,... | collective-permute-start | bytes 1572872 | tf_op jit(solution)/shard_map/ppermute | solution.py:700
  443.1 13.3 %collective-permute-start.32 = (bf16[128,2048]{1,0:T(8,128)(2,1)}, bf16[128,2048]{1,0:T(8,128)(2,1)}, u32[]{:S(2)}, u32[]{:S(2)}) collective-permute-start(bf16[128,2048]{1,0:T(8,128)(2,1)} %add_convert_fusion.11), channel_id=1, source_target_pairs={{0,1},{1,0},{2,3},{3,2},{4,5},{5,4},{6,7},{7,6},{8,9},{9,8},{10,11... | collective-permute-start | bytes 1572872 | tf_op jit(solution)/shard_map/ppermute | solution.py:700
  453.5 17.2 %collective-permute-start.37 = (bf16[256,2048]{1,0:T(8,128)(2,1)}, bf16[256,2048]{1,0:T(8,128)(2,1)S(1)}, u32[]{:S(2)}, u32[]{:S(2)}) collective-permute-start(bf16[256,2048]{1,0:T(8,128)(2,1)} %get-tuple-element.151), channel_id=1, source_target_pairs={{0,4},{4,0},{1,5},{5,1},{2,6},{6,2},{3,7},{7,3},{8,12},{12,8},{9,1... | collective-permute-start | bytes 3145736 | tf_op jit(solution)/shard_map/ppermute | solution.py:690
  453.5 18.9 %collective-permute-start.35 = (bf16[256,2048]{1,0:T(8,128)(2,1)}, bf16[256,2048]{1,0:T(8,128)(2,1)S(1)}, u32[]{:S(2)}, u32[]{:S(2)}) collective-permute-start(bf16[256,2048]{1,0:T(8,128)(2,1)} %get-tuple-element.147), channel_id=1, source_target_pairs={{0,4},{4,0},{1,5},{5,1},{2,6},{6,2},{3,7},{7,3},{8,12},{12,8},{9,1... | collective-permute-start | bytes 3145736 | tf_op jit(solution)/shard_map/ppermute | solution.py:690
  454.0 20.9 %collective-permute-start.36 = (bf16[256,2048]{1,0:T(8,128)(2,1)}, bf16[256,2048]{1,0:T(8,128)(2,1)S(1)}, u32[]{:S(2)}, u32[]{:S(2)}) collective-permute-start(bf16[256,2048]{1,0:T(8,128)(2,1)} %get-tuple-element.149), channel_id=1, source_target_pairs={{0,4},{4,0},{1,5},{5,1},{2,6},{6,2},{3,7},{7,3},{8,12},{12,8},{9,1... | collective-permute-start | bytes 3145736 | tf_op jit(solution)/shard_map/ppermute | solution.py:690
  458.8 26.3 %collective-permute-start.33 = (bf16[256,2048]{1,0:T(8,128)(2,1)S(1)}, bf16[256,2048]{1,0:T(8,128)(2,1)}, u32[]{:S(2)}, u32[]{:S(2)}) collective-permute-start(bf16[256,2048]{1,0:T(8,128)(2,1)S(1)} %fusion.refs_1_.own_ref), channel_id=1, source_target_pairs={{0,1},{1,0},{2,3},{3,2},{4,5},{5,4},{6,7},{7,6},{8,9},{9,8},{10,11... | collective-permute-start | bytes 3145736 | tf_op jit(solution)/shard_map/ppermute | solution.py:700
  459.6 26.2 %collective-permute-start.34 = (bf16[256,2048]{1,0:T(8,128)(2,1)S(1)}, bf16[256,2048]{1,0:T(8,128)(2,1)}, u32[]{:S(2)}, u32[]{:S(2)}) collective-permute-start(bf16[256,2048]{1,0:T(8,128)(2,1)S(1)} %fusion.refs_1_.own_ref), channel_id=1, source_target_pairs={{0,2},{1,3},{2,0},{3,1},{4,6},{5,7},{6,4},{7,5},{8,10},{9,11},{10,... | collective-permute-start | bytes 3145736 | tf_op jit(solution)/shard_map/ppermute | solution.py:700
  474.1 31.6 %collective-permute-start.39 = (bf16[256,2048]{1,0:T(8,128)(2,1)}, bf16[256,2048]{1,0:T(8,128)(2,1)}, u32[]{:S(2)}, u32[]{:S(2)}) collective-permute-start(bf16[256,2048]{1,0:T(8,128)(2,1)} %pad_maximum_fusion.5), channel_id=1, source_target_pairs={{0,2},{1,3},{2,0},{3,1},{4,6},{5,7},{6,4},{7,5},{8,10},{9,11},{10,... | collective-permute-start | bytes 3145736 | tf_op jit(solution)/shard_map/ppermute | solution.py:700
  476.4 29.3 %collective-permute-start.38 = (bf16[256,2048]{1,0:T(8,128)(2,1)}, bf16[256,2048]{1,0:T(8,128)(2,1)}, u32[]{:S(2)}, u32[]{:S(2)}) collective-permute-start(bf16[256,2048]{1,0:T(8,128)(2,1)} %pad_maximum_fusion.4), channel_id=1, source_target_pairs={{0,1},{1,0},{2,3},{3,2},{4,5},{5,4},{6,7},{7,6},{8,9},{9,8},{10,11... | collective-permute-start | bytes 3145736 | tf_op jit(solution)/shard_map/ppermute | solution.py:700
  508.6 14.4 %collective-permute-start.40 = (bf16[128,2048]{1,0:T(8,128)(2,1)S(1)}, bf16[128,2048]{1,0:T(8,128)(2,1)S(1)}, u32[]{:S(2)}, u32[]{:S(2)}) collective-permute-start(bf16[128,2048]{1,0:T(8,128)(2,1)S(1)} %add_convert_fusion.10), channel_id=1, source_target_pairs={{0,2},{1,3},{2,0},{3,1},{4,6},{5,7},{6,4},{7,5},{8,10},{9,11},{10,... | collective-permute-start | bytes 1572872 | tf_op jit(solution)/shard_map/ppermute | solution.py:700
  510.3 14.0 %collective-permute-start.41 = (bf16[128,2048]{1,0:T(8,128)(2,1)S(1)}, bf16[128,2048]{1,0:T(8,128)(2,1)S(1)}, u32[]{:S(2)}, u32[]{:S(2)}) collective-permute-start(bf16[128,2048]{1,0:T(8,128)(2,1)S(1)} %add_convert_fusion.9), channel_id=1, source_target_pairs={{0,1},{1,0},{2,3},{3,2},{4,5},{5,4},{6,7},{7,6},{8,9},{9,8},{10,11... | collective-permute-start | bytes 1572872 | tf_op jit(solution)/shard_map/ppermute | solution.py:700
  513.0 29.0 %collective-permute-start.52 = (bf16[1408,256]{1,0:T(8,128)(2,1)S(1)}, bf16[1408,256]{1,0:T(8,128)(2,1)S(1)}, u32[]{:S(2)}, u32[]{:S(2)}) collective-permute-start(bf16[1408,256]{1,0:T(8,128)(2,1)S(1)} %copy-done.28), channel_id=1, source_target_pairs={{0,4},{4,0},{1,5},{5,1},{2,6},{6,2},{3,7},{7,3},{8,12},{12,8},{9,1... | collective-permute-start | bytes 2162696 | tf_op jit(solution)/shard_map/ppermute | solution.py:690
  513.1 54.8 %collective-permute-start.50 = (bf16[256,1408]{1,0:T(8,128)(2,1)S(1)}, bf16[256,1408]{1,0:T(8,128)(2,1)S(1)}, u32[]{:S(2)}, u32[]{:S(2)}) collective-permute-start(bf16[256,1408]{1,0:T(8,128)(2,1)S(1)} %copy-done.29), channel_id=1, source_target_pairs={{0,4},{4,0},{1,5},{5,1},{2,6},{6,2},{3,7},{7,3},{8,12},{12,8},{9,1... | collective-permute-start | bytes 2162696 | tf_op jit(solution)/shard_map/ppermute | solution.py:690
  525.4 13.4 %collective-permute-start.43 = (bf16[128,2048]{1,0:T(8,128)(2,1)S(1)}, bf16[128,2048]{1,0:T(8,128)(2,1)S(1)}, u32[]{:S(2)}, u32[]{:S(2)}) collective-permute-start(bf16[128,2048]{1,0:T(8,128)(2,1)S(1)} %slice.240), channel_id=1, source_target_pairs={{0,2},{1,3},{2,0},{3,1},{4,6},{5,7},{6,4},{7,5},{8,10},{9,11},{10,... | collective-permute-start | bytes 1572872 | tf_op jit(solution)/shard_map/ppermute | solution.py:700
  527.0 13.3 %collective-permute-start.42 = (bf16[128,2048]{1,0:T(8,128)(2,1)S(1)}, bf16[128,2048]{1,0:T(8,128)(2,1)S(1)}, u32[]{:S(2)}, u32[]{:S(2)}) collective-permute-start(bf16[128,2048]{1,0:T(8,128)(2,1)S(1)} %slice.239), channel_id=1, source_target_pairs={{0,1},{1,0},{2,3},{3,2},{4,5},{5,4},{6,7},{7,6},{8,9},{9,8},{10,11... | collective-permute-start | bytes 1572872 | tf_op jit(solution)/shard_map/ppermute | solution.py:700
  540.3 23.8 %collective-permute-start.45 = (bf16[256,2048]{1,0:T(8,128)(2,1)S(1)}, bf16[256,2048]{1,0:T(8,128)(2,1)}, u32[]{:S(2)}, u32[]{:S(2)}) collective-permute-start(bf16[256,2048]{1,0:T(8,128)(2,1)S(1)} %add_convert_fusion.own_ref), channel_id=1, source_target_pairs={{0,1},{1,0},{2,3},{3,2},{4,5},{5,4},{6,7},{7,6},{8,9},{9,8},{10,11... | collective-permute-start | bytes 3145736 | tf_op jit(solution)/shard_map/ppermute | solution.py:700
  541.0 25.5 %collective-permute-start.46 = (bf16[256,2048]{1,0:T(8,128)(2,1)S(1)}, bf16[256,2048]{1,0:T(8,128)(2,1)}, u32[]{:S(2)}, u32[]{:S(2)}) collective-permute-start(bf16[256,2048]{1,0:T(8,128)(2,1)S(1)} %add_convert_fusion.own_ref), channel_id=1, source_target_pairs={{0,2},{1,3},{2,0},{3,1},{4,6},{5,7},{6,4},{7,5},{8,10},{9,11},{10,... | collective-permute-start | bytes 3145736 | tf_op jit(solution)/shard_map/ppermute | solution.py:700
  (71 other events, 651.8 us)
Sparse Core Ops, SparseCore 0:
  10.8 105.5 all-gather.3
  118.6 106.5 all-gather.5
  226.8 59.1 all-gather.7
  288.1 63.0 reduce-scatter.4
  353.3 63.2 reduce-scatter.6
  418.8 63.2 reduce-scatter.8
  505.9 92.5 reduce-scatter.10
